TPU v7x, 128 devices: a whole 4x4x4 slice. The times are simulated.
128 devices in a mesh: qx: 16 (over z_hi, x, core), qy: 8 (over y, z_lo).
Axes of the slice: x: 4, y: 4, z: 4 (z_hi: 2, z_lo: 2; z = z_hi * 2 + z_lo), core: 2. Of those that a mesh axis runs over, the one named last changes fastest.
Arguments:
- image_tiles: bfloat16 [16, 8, 256, 64, 128], P('qx', 'qy'), may hold values from -6 to 6
- observed: bfloat16 [16, 8, 256, 64, 128], P('qx', 'qy'), may hold values from -6 to 6
- phases: float32 [16, 8, 256, 64, 128], P('qx', 'qy'), may hold values from -3.140625 to 3.140625
- interpolate: bfloat16 [64, 64], replicated, may hold values from -0.75 to 0.75
- local_weights: bfloat16 [16, 8, 2, 4, 4, 64, 64], P('qx', 'qy'), may hold values from -0.375 to 0.375
- merge_weights: bfloat16 [16, 8, 2, 4, 4, 64, 64], P('qx', 'qy'), may hold values from -0.375 to 0.375
- output_weight: bfloat16 [64, 64], replicated, may hold values from -0.75 to 0.75
Outputs:
- gradient: bfloat16 [16, 8, 256, 64, 128], P('qx', 'qy')
All inputs are finite; a program needn't handle non-finite values.
Results may differ from a plain program's by a relative error of at most 0.02.
Values may be sent and summed in bfloat16 or wider, within the bound.
A program may use at most 128 MiB of HBM per device.

v0:
```python
import math

import jax
import jax.numpy as jnp
from jax import lax
from jax.sharding import PartitionSpec as P

CHUNKS = 2


def mixing(weight, data, form):
    return jnp.einsum(form, weight, data, preferred_element_type=jnp.float32).astype(jnp.bfloat16)


def level_bit(axis_count, level_index, depth):
    total_bits = axis_count.bit_length() - 1
    return level_index * (total_bits - 1) // max(depth - 1, 1)


def xor_order(x, axis, x_bit, y_bit):
    moved = jnp.moveaxis(x, axis, 0)
    shape = moved.shape
    pairs = moved.reshape((2, 2) + shape[1:])
    pairs = jnp.where(y_bit == 1, jnp.flip(pairs, 1), pairs)
    pairs = jnp.where(x_bit == 1, jnp.flip(pairs, 0), pairs)
    return jnp.moveaxis(pairs.reshape(shape), 0, axis)


def flip_send(value, flip, x_shift, y_shift):
    n_x = lax.axis_size("qx")
    n_y = lax.axis_size("qy")
    if flip == 2:
        pairs = [(i, i ^ (1 << x_shift)) for i in range(n_x)]
        return lax.ppermute(value, "qx", pairs)
    if flip == 1:
        pairs = [(i, i ^ (1 << y_shift)) for i in range(n_y)]
        return lax.ppermute(value, "qy", pairs)
    pairs = [
        (t * n_y + u, (t ^ (1 << x_shift)) * n_y + (u ^ (1 << y_shift)))
        for t in range(n_x)
        for u in range(n_y)
    ]
    return lax.ppermute(value, ("qx", "qy"), pairs)


def exchange(relative, x_shift, y_shift):
    got = [relative[0]] + [flip_send(relative[f], f, x_shift, y_shift) for f in (1, 2, 3)]
    return jnp.stack(got)


def local(image_tiles, observed, phases, interpolate, local_weights, merge_weights, output_weight):
    groups = image_tiles.shape[2]
    rank_size = image_tiles.shape[3]
    inner_boxes = image_tiles.shape[4]
    local_depth = local_weights.shape[2]
    quarter = groups // 4
    part = quarter // CHUNKS
    levels = local_weights[0, 0]
    merges = merge_weights[0, 0]
    n_x = lax.axis_size("qx")
    n_y = lax.axis_size("qy")
    t = lax.axis_index("qx")
    u = lax.axis_index("qy")
    shifts = [(level_bit(n_x, j, 2), level_bit(n_y, j, 2)) for j in range(2)]
    bits = [
        (jnp.right_shift(t, xs) & 1, jnp.right_shift(u, ys) & 1) for xs, ys in shifts
    ]

    w0 = xor_order(xor_order(merges[0], 1, *bits[0]), 0, *bits[1])
    w1 = xor_order(merges[1], 1, *bits[1])

    shape5 = (4, CHUNKS, part, rank_size, inner_boxes)
    image = xor_order(image_tiles[0, 0].reshape(shape5), 0, *bits[0])
    obs = observed[0, 0].reshape(shape5)
    cas_all = jnp.float32(math.sqrt(2.0)) * jnp.sin(
        phases[0, 0].reshape(shape5) + jnp.float32(math.pi / 4)
    )

    results = []
    for m in range(CHUNKS):
        cur = mixing(interpolate, image[:, m], "op,qjpl->qjol")
        for i in range(local_depth):
            b = 4**i
            blk = cur.reshape(4, part // (4 * b), 4, b, rank_size, inner_boxes)
            cur = mixing(levels[i], blk, "kcor,qacerl->qakeol").reshape(
                4, part, rank_size, inner_boxes
            )
        pieces = exchange(cur, *shifts[0])
        cur = mixing(w0, pieces, "scor,cjrl->sjol")
        pieces = exchange(cur, *shifts[1])
        merged_y = mixing(w1, pieces, "scor,cjrl->sjol")
        cas_wave = cas_all[:, m]
        predicted = jnp.einsum(
            "or,sjrl->sjol", output_weight, merged_y, preferred_element_type=jnp.float32
        )
        residual = (cas_wave * predicted - obs[:, m].astype(jnp.float32)).astype(jnp.bfloat16)
        weighted = (cas_wave * residual.astype(jnp.float32)).astype(jnp.bfloat16)
        back = mixing(output_weight, weighted, "or,sjol->sjrl")
        terms = mixing(w1, back, "scor,sjol->cjrl")
        back = exchange(terms, *shifts[1])
        terms = mixing(w0, back, "scor,sjol->cjrl")
        cur = exchange(terms, *shifts[0])
        for i in reversed(range(local_depth)):
            b = 4**i
            blk = cur.reshape(4, part // (4 * b), 4, b, rank_size, inner_boxes)
            cur = mixing(levels[i], blk, "kcor,qakeol->qacerl").reshape(
                4, part, rank_size, inner_boxes
            )
        results.append(mixing(interpolate, cur, "op,qjol->qjpl"))
    gradient = xor_order(jnp.stack(results, 1), 0, *bits[0])
    return gradient.reshape(groups, rank_size, inner_boxes)[None, None]


def solution(mesh):
    placed = (
        P("qx", "qy", None, None, None),
        P("qx", "qy", None, None, None),
        P("qx", "qy", None, None, None),
        P(),
        P("qx", "qy", None, None, None, None, None),
        P("qx", "qy", None, None, None, None, None),
        P(),
    )
    return jax.shard_map(
        local,
        mesh=mesh,
        in_specs=placed,
        out_specs=P("qx", "qy", None, None, None),
        check_vma=False,
    )
```

profile of v0, /device:TPU:1, one launch (start us, length us, event | category | flops | bytes accessed | tf_op | source)
XLA Modules:
  0.0 229.8 jit_solution(2521348315309254862)
XLA Ops:
  0.0 3.2 %copy.161 = bf16[2,2,2,32,64,128]{5,4,3,1,0,2:T(8,128)(2,1)S(1)} copy(bf16[2,2,2,32,64,128]{5,4,3,2,1,0:T(8,128)(2,1)} %bitcast.500) | data formatting | bytes 8388608 | tf_op jit(solution)/shard_map/reshape;reshape;squeeze | solution.py:23
  20.8 29.4 %sine_multiply_fusion = f32[1,1,256,64,128]{4,3,2,1,0:T(8,128)} fusion(f32[1,1,256,64,128]{4,3,2,1,0:T(8,128)} %param.9), kind=kLoop, calls=%fused_computation | loop fusion | flops 4194304 | bytes 16777216 | tf_op jit(solution)/shard_map/mul | solution.py:75
  54.2 2.9 %collective-permute-start.15 = (bf16[32,64,128]{2,1,0:T(8,128)(2,1)S(1)}, bf16[32,64,128]{2,1,0:T(8,128)(2,1)S(1)}, u32[]{:S(2)}, u32[]{:S(2)}) collective-permute-start(bf16[32,64,128]{2,1,0:T(8,128)(2,1)S(1)} %get-tuple-element.30), channel_id=1, source_target_pairs={{0,4},{1,5},{2,6},{3,7},{4,0},{5,1},{6,2},{7,3},{8,12},{9,13},{10,... | collective-permute-start | bytes 1572872 | tf_op jit(solution)/shard_map/ppermute | solution.py:37
  57.1 3.1 %collective-permute-start.17 = (bf16[32,64,128]{2,1,0:T(8,128)(2,1)}, bf16[32,64,128]{2,1,0:T(8,128)(2,1)}, u32[]{:S(2)}, u32[]{:S(2)}) collective-permute-start(bf16[32,64,128]{2,1,0:T(8,128)(2,1)} %get-tuple-element.31), channel_id=1, source_target_pairs={{0,68},{1,69},{2,70},{3,71},{4,64},{5,65},{6,66},{7,67},{8,76},{9,... | collective-permute-start | bytes 1572872 | tf_op jit(solution)/shard_map/ppermute | solution.py:43
  60.4 4.6 %collective-permute-done.2 = bf16[32,64,128]{2,1,0:T(8,128)(2,1)S(1)} collective-permute-done((bf16[32,64,128]{2,1,0:T(8,128)(2,1)S(1)}, bf16[32,64,128]{2,1,0:T(8,128)(2,1)S(1)}, u32[]{:S(2)}, u32[]{:S(2)}) %collective-permute-start.2) | collective-permute-done | bytes 524320 | tf_op jit(solution)/shard_map/ppermute | solution.py:43
  67.1 3.0 %collective-permute-start.3 = (bf16[32,64,128]{2,1,0:T(8,128)(2,1)S(1)}, bf16[32,64,128]{2,1,0:T(8,128)(2,1)}, u32[]{:S(2)}, u32[]{:S(2)}) collective-permute-start(bf16[32,64,128]{2,1,0:T(8,128)(2,1)S(1)} %get-tuple-element.14), channel_id=1, source_target_pairs={{0,4},{1,5},{2,6},{3,7},{4,0},{5,1},{6,2},{7,3},{8,12},{9,13},{10,... | collective-permute-start | bytes 1572872 | tf_op jit(solution)/shard_map/ppermute | solution.py:37
  70.1 3.2 %collective-permute-start.5 = (bf16[32,64,128]{2,1,0:T(8,128)(2,1)S(1)}, bf16[32,64,128]{2,1,0:T(8,128)(2,1)}, u32[]{:S(2)}, u32[]{:S(2)}) collective-permute-start(bf16[32,64,128]{2,1,0:T(8,128)(2,1)S(1)} %get-tuple-element.15), channel_id=1, source_target_pairs={{0,68},{1,69},{2,70},{3,71},{4,64},{5,65},{6,66},{7,67},{8,76},{9,... | collective-permute-start | bytes 1572872 | tf_op jit(solution)/shard_map/ppermute | solution.py:43
  74.4 9.0 %collective-permute-done.17 = bf16[32,64,128]{2,1,0:T(8,128)(2,1)} collective-permute-done((bf16[32,64,128]{2,1,0:T(8,128)(2,1)}, bf16[32,64,128]{2,1,0:T(8,128)(2,1)}, u32[]{:S(2)}, u32[]{:S(2)}) %collective-permute-start.17) | collective-permute-done | bytes 524320 | tf_op jit(solution)/shard_map/ppermute | solution.py:43
  83.4 5.5 %collective-permute-done.16 = bf16[32,64,128]{2,1,0:T(8,128)(2,1)} collective-permute-done((bf16[32,64,128]{2,1,0:T(8,128)(2,1)}, bf16[32,64,128]{2,1,0:T(8,128)(2,1)}, u32[]{:S(2)}, u32[]{:S(2)}) %collective-permute-start.16) | collective-permute-done | bytes 524320 | tf_op jit(solution)/shard_map/ppermute | solution.py:34
  91.8 14.1 %collective-permute-done.5 = bf16[32,64,128]{2,1,0:T(8,128)(2,1)} collective-permute-done((bf16[32,64,128]{2,1,0:T(8,128)(2,1)S(1)}, bf16[32,64,128]{2,1,0:T(8,128)(2,1)}, u32[]{:S(2)}, u32[]{:S(2)}) %collective-permute-start.5) | collective-permute-done | bytes 524320 | tf_op jit(solution)/shard_map/ppermute | solution.py:43
  105.9 5.5 %collective-permute-done.4 = bf16[32,64,128]{2,1,0:T(8,128)(2,1)} collective-permute-done((bf16[32,64,128]{2,1,0:T(8,128)(2,1)S(1)}, bf16[32,64,128]{2,1,0:T(8,128)(2,1)}, u32[]{:S(2)}, u32[]{:S(2)}) %collective-permute-start.4) | collective-permute-done | bytes 524320 | tf_op jit(solution)/shard_map/ppermute | solution.py:34
  118.4 4.4 %fusion.77 = bf16[4,32,64,128]{3,2,0,1:T(8,128)(2,1)} fusion(bf16[4,4,64,64,1]{2,3,0,1,4:T(8,128)(2,1)S(1)} %bitcast.524, bf16[4,32,64,128]{3,2,1,0:T(8,128)(2,1)} %multiply_convert_fusion, bf16[64,64]{1,0:T(8,128)(2,1)S(1)} %copy-done), kind=kOutput, calls=%fused_computation.91 | convolution fusion | flops 673185792 | bytes 4333568 | tf_op jit(solution)/shard_map/scor,sjol->cjrl/dot_general | solution.py:12
  125.5 2.9 %collective-permute-start.18 = (bf16[32,64,128]{2,1,0:T(8,128)(2,1)}, bf16[32,64,128]{2,1,0:T(8,128)(2,1)}, u32[]{:S(2)}, u32[]{:S(2)}) collective-permute-start(bf16[32,64,128]{2,1,0:T(8,128)(2,1)} %get-tuple-element.26), channel_id=1, source_target_pairs={{0,4},{1,5},{2,6},{3,7},{4,0},{5,1},{6,2},{7,3},{8,12},{9,13},{10,... | collective-permute-start | bytes 1572872 | tf_op jit(solution)/shard_map/ppermute | solution.py:37
  131.2 3.7 %fusion.60 = bf16[4,32,64,128]{3,2,0,1:T(8,128)(2,1)} fusion(bf16[4,4,64,64,1]{2,3,0,1,4:T(8,128)(2,1)} %bitcast.525, bf16[4,32,64,128]{3,2,1,0:T(8,128)(2,1)S(1)} %multiply_convert_fusion.1, bf16[64,64]{1,0:T(8,128)(2,1)S(1)} %copy-done), kind=kOutput, calls=%fused_computation.86 | convolution fusion | flops 673185792 | bytes 4333568 | tf_op jit(solution)/shard_map/scor,sjol->cjrl/dot_general | solution.py:12
  136.6 3.0 %collective-permute-start.6 = (bf16[32,64,128]{2,1,0:T(8,128)(2,1)S(1)}, bf16[32,64,128]{2,1,0:T(8,128)(2,1)S(1)}, u32[]{:S(2)}, u32[]{:S(2)}) collective-permute-start(bf16[32,64,128]{2,1,0:T(8,128)(2,1)S(1)} %get-tuple-element.10), channel_id=1, source_target_pairs={{0,4},{1,5},{2,6},{3,7},{4,0},{5,1},{6,2},{7,3},{8,12},{9,13},{10,... | collective-permute-start | bytes 1572872 | tf_op jit(solution)/shard_map/ppermute | solution.py:37
  142.4 8.5 %collective-permute-done.20 = bf16[32,64,128]{2,1,0:T(8,128)(2,1)} collective-permute-done((bf16[32,64,128]{2,1,0:T(8,128)(2,1)}, bf16[32,64,128]{2,1,0:T(8,128)(2,1)}, u32[]{:S(2)}, u32[]{:S(2)}) %collective-permute-start.20) | collective-permute-done | bytes 524320 | tf_op jit(solution)/shard_map/ppermute | solution.py:43
  156.1 4.1 %collective-permute-start.23 = (bf16[32,64,128]{2,1,0:T(8,128)(2,1)S(1)}, bf16[32,64,128]{2,1,0:T(8,128)(2,1)S(1)}, u32[]{:S(2)}, u32[]{:S(2)}) collective-permute-start(bf16[32,64,128]{2,1,0:T(8,128)(2,1)S(1)} %get-tuple-element.22), channel_id=1, source_target_pairs={{0,9},{1,8},{2,11},{3,10},{4,13},{5,12},{6,15},{7,14},{8,1},{9,0},... | collective-permute-start | bytes 1572872 | tf_op jit(solution)/shard_map/ppermute | solution.py:43
  162.5 10.9 %collective-permute-done.8 = bf16[32,64,128]{2,1,0:T(8,128)(2,1)S(1)} collective-permute-done((bf16[32,64,128]{2,1,0:T(8,128)(2,1)S(1)}, bf16[32,64,128]{2,1,0:T(8,128)(2,1)S(1)}, u32[]{:S(2)}, u32[]{:S(2)}) %collective-permute-start.8) | collective-permute-done | bytes 524320 | tf_op jit(solution)/shard_map/ppermute | solution.py:43
  177.1 4.0 %collective-permute-start.11 = (bf16[32,64,128]{2,1,0:T(8,128)(2,1)S(1)}, bf16[32,64,128]{2,1,0:T(8,128)(2,1)S(1)}, u32[]{:S(2)}, u32[]{:S(2)}) collective-permute-start(bf16[32,64,128]{2,1,0:T(8,128)(2,1)S(1)} %get-tuple-element.6), channel_id=1, source_target_pairs={{0,9},{1,8},{2,11},{3,10},{4,13},{5,12},{6,15},{7,14},{8,1},{9,0},... | collective-permute-start | bytes 1572872 | tf_op jit(solution)/shard_map/ppermute | solution.py:43
  181.2 9.3 %collective-permute-done.23 = bf16[32,64,128]{2,1,0:T(8,128)(2,1)S(1)} collective-permute-done((bf16[32,64,128]{2,1,0:T(8,128)(2,1)S(1)}, bf16[32,64,128]{2,1,0:T(8,128)(2,1)S(1)}, u32[]{:S(2)}, u32[]{:S(2)}) %collective-permute-start.23) | collective-permute-done | bytes 524320 | tf_op jit(solution)/shard_map/ppermute | solution.py:43
  191.6 6.3 %collective-permute-done.21 = bf16[32,64,128]{2,1,0:T(8,128)(2,1)S(1)} collective-permute-done((bf16[32,64,128]{2,1,0:T(8,128)(2,1)S(1)}, bf16[32,64,128]{2,1,0:T(8,128)(2,1)S(1)}, u32[]{:S(2)}, u32[]{:S(2)}) %collective-permute-start.21) | collective-permute-done | bytes 524320 | tf_op jit(solution)/shard_map/ppermute | solution.py:37
  200.4 12.6 %collective-permute-done.11 = bf16[32,64,128]{2,1,0:T(8,128)(2,1)S(1)} collective-permute-done((bf16[32,64,128]{2,1,0:T(8,128)(2,1)S(1)}, bf16[32,64,128]{2,1,0:T(8,128)(2,1)S(1)}, u32[]{:S(2)}, u32[]{:S(2)}) %collective-permute-start.11) | collective-permute-done | bytes 524320 | tf_op jit(solution)/shard_map/ppermute | solution.py:43
  213.0 7.4 %collective-permute-done.9 = bf16[32,64,128]{2,1,0:T(8,128)(2,1)S(1)} collective-permute-done((bf16[32,64,128]{2,1,0:T(8,128)(2,1)S(1)}, bf16[32,64,128]{2,1,0:T(8,128)(2,1)S(1)}, u32[]{:S(2)}, u32[]{:S(2)}) %collective-permute-start.9) | collective-permute-done | bytes 524320 | tf_op jit(solution)/shard_map/ppermute | solution.py:37
  226.8 3.0 %copy.223 = bf16[2,2,2,32,64,128]{5,4,3,2,1,0:T(8,128)(2,1)} copy(bf16[2,2,2,32,64,128]{5,4,3,1,0,2:T(8,128)(2,1)S(1)} %reverse_select_fusion) | data formatting | bytes 8388608 | tf_op jit(solution)/shard_map/jit(_where)/select_n | solution.py:25
  (101 shorter events, 65.7 us)
Async XLA Ops:
  10.4 39.9 %collective-permute-start.12 = (bf16[32,64,128]{2,1,0:T(8,128)(2,1)}, bf16[32,64,128]{2,1,0:T(8,128)(2,1)}, u32[]{:S(2)}, u32[]{:S(2)}) collective-permute-start(bf16[32,64,128]{2,1,0:T(8,128)(2,1)} %bitcast.136), channel_id=1, source_target_pairs={{0,1},{1,0},{2,3},{3,2},{4,5},{5,4},{6,7},{7,6},{8,9},{9,8},{10,11... | collective-permute-start | bytes 1572872 | tf_op jit(solution)/shard_map/ppermute | solution.py:37
  13.7 37.2 %collective-permute-start.13 = (bf16[32,64,128]{2,1,0:T(8,128)(2,1)}, bf16[32,64,128]{2,1,0:T(8,128)(2,1)}, u32[]{:S(2)}, u32[]{:S(2)}) collective-permute-start(bf16[32,64,128]{2,1,0:T(8,128)(2,1)} %bitcast.138), channel_id=1, source_target_pairs={{0,8},{8,0},{16,24},{24,16},{32,40},{40,32},{48,56},{56,48},{64,72... | collective-permute-start | bytes 1572872 | tf_op jit(solution)/shard_map/ppermute | solution.py:34
  15.5 35.4 %collective-permute-start.14 = (bf16[32,64,128]{2,1,0:T(8,128)(2,1)}, bf16[32,64,128]{2,1,0:T(8,128)(2,1)}, u32[]{:S(2)}, u32[]{:S(2)}) collective-permute-start(bf16[32,64,128]{2,1,0:T(8,128)(2,1)} %bitcast.140), channel_id=1, source_target_pairs={{0,9},{1,8},{2,11},{3,10},{4,13},{5,12},{6,15},{7,14},{8,1},{9,0},... | collective-permute-start | bytes 1572872 | tf_op jit(solution)/shard_map/ppermute | solution.py:43
  17.9 42.3 %collective-permute-start = (bf16[32,64,128]{2,1,0:T(8,128)(2,1)S(1)}, bf16[32,64,128]{2,1,0:T(8,128)(2,1)}, u32[]{:S(2)}, u32[]{:S(2)}) collective-permute-start(bf16[32,64,128]{2,1,0:T(8,128)(2,1)S(1)} %bitcast.514), channel_id=1, source_target_pairs={{0,1},{1,0},{2,3},{3,2},{4,5},{5,4},{6,7},{7,6},{8,9},{9,8},{10,11... | collective-permute-start | bytes 1572872 | tf_op jit(solution)/shard_map/ppermute | solution.py:37
  19.4 41.0 %collective-permute-start.1 = (bf16[32,64,128]{2,1,0:T(8,128)(2,1)S(1)}, bf16[32,64,128]{2,1,0:T(8,128)(2,1)}, u32[]{:S(2)}, u32[]{:S(2)}) collective-permute-start(bf16[32,64,128]{2,1,0:T(8,128)(2,1)S(1)} %bitcast.513), channel_id=1, source_target_pairs={{0,8},{8,0},{16,24},{24,16},{32,40},{40,32},{48,56},{56,48},{64,72... | collective-permute-start | bytes 1572872 | tf_op jit(solution)/shard_map/ppermute | solution.py:34
  50.2 14.7 %collective-permute-start.2 = (bf16[32,64,128]{2,1,0:T(8,128)(2,1)S(1)}, bf16[32,64,128]{2,1,0:T(8,128)(2,1)S(1)}, u32[]{:S(2)}, u32[]{:S(2)}) collective-permute-start(bf16[32,64,128]{2,1,0:T(8,128)(2,1)S(1)} %bitcast.516), channel_id=1, source_target_pairs={{0,9},{1,8},{2,11},{3,10},{4,13},{5,12},{6,15},{7,14},{8,1},{9,0},... | collective-permute-start | bytes 1572872 | tf_op jit(solution)/shard_map/ppermute | solution.py:43
  54.2 19.2 %collective-permute-start.15 = (bf16[32,64,128]{2,1,0:T(8,128)(2,1)S(1)}, bf16[32,64,128]{2,1,0:T(8,128)(2,1)S(1)}, u32[]{:S(2)}, u32[]{:S(2)}) collective-permute-start(bf16[32,64,128]{2,1,0:T(8,128)(2,1)S(1)} %get-tuple-element.30), channel_id=1, source_target_pairs={{0,4},{1,5},{2,6},{3,7},{4,0},{5,1},{6,2},{7,3},{8,12},{9,13},{10,... | collective-permute-start | bytes 1572872 | tf_op jit(solution)/shard_map/ppermute | solution.py:37
  57.1 26.3 %collective-permute-start.17 = (bf16[32,64,128]{2,1,0:T(8,128)(2,1)}, bf16[32,64,128]{2,1,0:T(8,128)(2,1)}, u32[]{:S(2)}, u32[]{:S(2)}) collective-permute-start(bf16[32,64,128]{2,1,0:T(8,128)(2,1)} %get-tuple-element.31), channel_id=1, source_target_pairs={{0,68},{1,69},{2,70},{3,71},{4,64},{5,65},{6,66},{7,67},{8,76},{9,... | collective-permute-start | bytes 1572872 | tf_op jit(solution)/shard_map/ppermute | solution.py:43
  60.2 28.8 %collective-permute-start.16 = (bf16[32,64,128]{2,1,0:T(8,128)(2,1)}, bf16[32,64,128]{2,1,0:T(8,128)(2,1)}, u32[]{:S(2)}, u32[]{:S(2)}) collective-permute-start(bf16[32,64,128]{2,1,0:T(8,128)(2,1)} %get-tuple-element.32), channel_id=1, source_target_pairs={{0,64},{8,72},{16,80},{24,88},{32,96},{40,104},{48,112},{56,120},{... | collective-permute-start | bytes 1572872 | tf_op jit(solution)/shard_map/ppermute | solution.py:34
  67.1 24.7 %collective-permute-start.3 = (bf16[32,64,128]{2,1,0:T(8,128)(2,1)S(1)}, bf16[32,64,128]{2,1,0:T(8,128)(2,1)}, u32[]{:S(2)}, u32[]{:S(2)}) collective-permute-start(bf16[32,64,128]{2,1,0:T(8,128)(2,1)S(1)} %get-tuple-element.14), channel_id=1, source_target_pairs={{0,4},{1,5},{2,6},{3,7},{4,0},{5,1},{6,2},{7,3},{8,12},{9,13},{10,... | collective-permute-start | bytes 1572872 | tf_op jit(solution)/shard_map/ppermute | solution.py:37
  70.1 35.8 %collective-permute-start.5 = (bf16[32,64,128]{2,1,0:T(8,128)(2,1)S(1)}, bf16[32,64,128]{2,1,0:T(8,128)(2,1)}, u32[]{:S(2)}, u32[]{:S(2)}) collective-permute-start(bf16[32,64,128]{2,1,0:T(8,128)(2,1)S(1)} %get-tuple-element.15), channel_id=1, source_target_pairs={{0,68},{1,69},{2,70},{3,71},{4,64},{5,65},{6,66},{7,67},{8,76},{9,... | collective-permute-start | bytes 1572872 | tf_op jit(solution)/shard_map/ppermute | solution.py:43
  73.3 38.1 %collective-permute-start.4 = (bf16[32,64,128]{2,1,0:T(8,128)(2,1)S(1)}, bf16[32,64,128]{2,1,0:T(8,128)(2,1)}, u32[]{:S(2)}, u32[]{:S(2)}) collective-permute-start(bf16[32,64,128]{2,1,0:T(8,128)(2,1)S(1)} %get-tuple-element.16), channel_id=1, source_target_pairs={{0,64},{8,72},{16,80},{24,88},{32,96},{40,104},{48,112},{56,120},{... | collective-permute-start | bytes 1572872 | tf_op jit(solution)/shard_map/ppermute | solution.py:34
  125.5 14.6 %collective-permute-start.18 = (bf16[32,64,128]{2,1,0:T(8,128)(2,1)}, bf16[32,64,128]{2,1,0:T(8,128)(2,1)}, u32[]{:S(2)}, u32[]{:S(2)}) collective-permute-start(bf16[32,64,128]{2,1,0:T(8,128)(2,1)} %get-tuple-element.26), channel_id=1, source_target_pairs={{0,4},{1,5},{2,6},{3,7},{4,0},{5,1},{6,2},{7,3},{8,12},{9,13},{10,... | collective-permute-start | bytes 1572872 | tf_op jit(solution)/shard_map/ppermute | solution.py:37
  128.5 22.5 %collective-permute-start.20 = (bf16[32,64,128]{2,1,0:T(8,128)(2,1)}, bf16[32,64,128]{2,1,0:T(8,128)(2,1)}, u32[]{:S(2)}, u32[]{:S(2)}) collective-permute-start(bf16[32,64,128]{2,1,0:T(8,128)(2,1)} %get-tuple-element.27), channel_id=1, source_target_pairs={{0,68},{1,69},{2,70},{3,71},{4,64},{5,65},{6,66},{7,67},{8,76},{9,... | collective-permute-start | bytes 1572872 | tf_op jit(solution)/shard_map/ppermute | solution.py:43
  128.5 25.3 %collective-permute-start.19 = (bf16[32,64,128]{2,1,0:T(8,128)(2,1)S(1)}, bf16[32,64,128]{2,1,0:T(8,128)(2,1)}, u32[]{:S(2)}, u32[]{:S(2)}) collective-permute-start(bf16[32,64,128]{2,1,0:T(8,128)(2,1)S(1)} %get-tuple-element.28), channel_id=1, source_target_pairs={{0,64},{8,72},{16,80},{24,88},{32,96},{40,104},{48,112},{56,120},{... | collective-permute-start | bytes 1572872 | tf_op jit(solution)/shard_map/ppermute | solution.py:34
  136.6 25.9 %collective-permute-start.6 = (bf16[32,64,128]{2,1,0:T(8,128)(2,1)S(1)}, bf16[32,64,128]{2,1,0:T(8,128)(2,1)S(1)}, u32[]{:S(2)}, u32[]{:S(2)}) collective-permute-start(bf16[32,64,128]{2,1,0:T(8,128)(2,1)S(1)} %get-tuple-element.10), channel_id=1, source_target_pairs={{0,4},{1,5},{2,6},{3,7},{4,0},{5,1},{6,2},{7,3},{8,12},{9,13},{10,... | collective-permute-start | bytes 1572872 | tf_op jit(solution)/shard_map/ppermute | solution.py:37
  139.6 33.7 %collective-permute-start.8 = (bf16[32,64,128]{2,1,0:T(8,128)(2,1)S(1)}, bf16[32,64,128]{2,1,0:T(8,128)(2,1)S(1)}, u32[]{:S(2)}, u32[]{:S(2)}) collective-permute-start(bf16[32,64,128]{2,1,0:T(8,128)(2,1)S(1)} %get-tuple-element.11), channel_id=1, source_target_pairs={{0,68},{1,69},{2,70},{3,71},{4,64},{5,65},{6,66},{7,67},{8,76},{9,... | collective-permute-start | bytes 1572872 | tf_op jit(solution)/shard_map/ppermute | solution.py:43
  140.1 36.0 %collective-permute-start.7 = (bf16[32,64,128]{2,1,0:T(8,128)(2,1)S(1)}, bf16[32,64,128]{2,1,0:T(8,128)(2,1)S(1)}, u32[]{:S(2)}, u32[]{:S(2)}) collective-permute-start(bf16[32,64,128]{2,1,0:T(8,128)(2,1)S(1)} %get-tuple-element.12), channel_id=1, source_target_pairs={{0,64},{8,72},{16,80},{24,88},{32,96},{40,104},{48,112},{56,120},{... | collective-permute-start | bytes 1572872 | tf_op jit(solution)/shard_map/ppermute | solution.py:34
  156.1 34.4 %collective-permute-start.23 = (bf16[32,64,128]{2,1,0:T(8,128)(2,1)S(1)}, bf16[32,64,128]{2,1,0:T(8,128)(2,1)S(1)}, u32[]{:S(2)}, u32[]{:S(2)}) collective-permute-start(bf16[32,64,128]{2,1,0:T(8,128)(2,1)S(1)} %get-tuple-element.22), channel_id=1, source_target_pairs={{0,9},{1,8},{2,11},{3,10},{4,13},{5,12},{6,15},{7,14},{8,1},{9,0},... | collective-permute-start | bytes 1572872 | tf_op jit(solution)/shard_map/ppermute | solution.py:43
  160.2 31.4 %collective-permute-start.22 = (bf16[32,64,128]{2,1,0:T(8,128)(2,1)S(1)}, bf16[32,64,128]{2,1,0:T(8,128)(2,1)S(1)}, u32[]{:S(2)}, u32[]{:S(2)}) collective-permute-start(bf16[32,64,128]{2,1,0:T(8,128)(2,1)S(1)} %get-tuple-element.23), channel_id=1, source_target_pairs={{0,8},{8,0},{16,24},{24,16},{32,40},{40,32},{48,56},{56,48},{64,72... | collective-permute-start | bytes 1572872 | tf_op jit(solution)/shard_map/ppermute | solution.py:34
  162.5 35.4 %collective-permute-start.21 = (bf16[32,64,128]{2,1,0:T(8,128)(2,1)S(1)}, bf16[32,64,128]{2,1,0:T(8,128)(2,1)S(1)}, u32[]{:S(2)}, u32[]{:S(2)}) collective-permute-start(bf16[32,64,128]{2,1,0:T(8,128)(2,1)S(1)} %get-tuple-element.24), channel_id=1, source_target_pairs={{0,1},{1,0},{2,3},{3,2},{4,5},{5,4},{6,7},{7,6},{8,9},{9,8},{10,11... | collective-permute-start | bytes 1572872 | tf_op jit(solution)/shard_map/ppermute | solution.py:37
  177.1 35.8 %collective-permute-start.11 = (bf16[32,64,128]{2,1,0:T(8,128)(2,1)S(1)}, bf16[32,64,128]{2,1,0:T(8,128)(2,1)S(1)}, u32[]{:S(2)}, u32[]{:S(2)}) collective-permute-start(bf16[32,64,128]{2,1,0:T(8,128)(2,1)S(1)} %get-tuple-element.6), channel_id=1, source_target_pairs={{0,9},{1,8},{2,11},{3,10},{4,13},{5,12},{6,15},{7,14},{8,1},{9,0},... | collective-permute-start | bytes 1572872 | tf_op jit(solution)/shard_map/ppermute | solution.py:43
  181.2 31.8 %collective-permute-start.10 = (bf16[32,64,128]{2,1,0:T(8,128)(2,1)S(1)}, bf16[32,64,128]{2,1,0:T(8,128)(2,1)S(1)}, u32[]{:S(2)}, u32[]{:S(2)}) collective-permute-start(bf16[32,64,128]{2,1,0:T(8,128)(2,1)S(1)} %get-tuple-element.7), channel_id=1, source_target_pairs={{0,8},{8,0},{16,24},{24,16},{32,40},{40,32},{48,56},{56,48},{64,72... | collective-permute-start | bytes 1572872 | tf_op jit(solution)/shard_map/ppermute | solution.py:34
  190.5 29.8 %collective-permute-start.9 = (bf16[32,64,128]{2,1,0:T(8,128)(2,1)S(1)}, bf16[32,64,128]{2,1,0:T(8,128)(2,1)S(1)}, u32[]{:S(2)}, u32[]{:S(2)}) collective-permute-start(bf16[32,64,128]{2,1,0:T(8,128)(2,1)S(1)} %get-tuple-element.8), channel_id=1, source_target_pairs={{0,1},{1,0},{2,3},{3,2},{4,5},{5,4},{6,7},{7,6},{8,9},{9,8},{10,11... | collective-permute-start | bytes 1572872 | tf_op jit(solution)/shard_map/ppermute | solution.py:37
  (10 other events, 216.1 us)
where the time goes:
time: 231 us; the launch traced here: 230 us
  waiting for transfers between devices  103 us (45%)
  starting transfers between devices  39.3 us (17%)
  other arithmetic  37.2 us (16%)
  matrix products  31.5 us (14%)
  local copies, waits for them, and re-layouts  18.7 us (8%)
    ppermute x8, waiting for transfers between devices, flip_send(): return lax.ppermute(value, ('qx', 'qy'), pairs)  69 us
    mul x1, other arithmetic, local(): jnp.float32(math.sqrt(2.0))  29.4 us
    dot_general x20, matrix products, mixing(): jnp.einsum(form, weight, data, preferred_element_type=jnp.float32)  28.5 us
    ppermute x8, waiting for transfers between devices, flip_send(): return lax.ppermute(value, 'qy', pairs)  17 us
    ppermute x8, starting transfers between devices, flip_send(): return lax.ppermute(value, 'qy', pairs)  16.8 us
    ppermute x8, waiting for transfers between devices, flip_send(): return lax.ppermute(value, 'qx', pairs)  16.6 us
    ppermute x8, starting transfers between devices, flip_send(): return lax.ppermute(value, ('qx', 'qy'), pairs)  15.1 us
    unnamed x24, local copies, waits for them, and re-layouts  8.3 us
  transfers between devices with their start and end apart: 24, of which 16 were waited for; matrix products, arithmetic and copies ran while one was open for 23% of the time, Pallas kernels for 0%

commit v1 on v0

--- a/solution.py
+++ b/solution.py
@@ -70,22 +70,40 @@
     w1 = xor_order(merges[1], 1, *bits[1])
 
     shape5 = (4, CHUNKS, part, rank_size, inner_boxes)
-    image = xor_order(image_tiles[0, 0].reshape(shape5), 0, *bits[0])
+    image = image_tiles[0, 0].reshape(shape5)
     obs = observed[0, 0].reshape(shape5)
     cas_all = jnp.float32(math.sqrt(2.0)) * jnp.sin(
         phases[0, 0].reshape(shape5) + jnp.float32(math.pi / 4)
     )
+    k0 = 2 * bits[0][0] + bits[0][1]
 
-    results = []
-    for m in range(CHUNKS):
-        cur = mixing(interpolate, image[:, m], "op,qjpl->qjol")
+    def local_forward(tiles):
+        cur = mixing(interpolate, tiles, "op,jpl->jol")
         for i in range(local_depth):
             b = 4**i
-            blk = cur.reshape(4, part // (4 * b), 4, b, rank_size, inner_boxes)
-            cur = mixing(levels[i], blk, "kcor,qacerl->qakeol").reshape(
-                4, part, rank_size, inner_boxes
+            blk = cur.reshape(part // (4 * b), 4, b, rank_size, inner_boxes)
+            cur = mixing(levels[i], blk, "kcor,acerl->akeol").reshape(
+                part, rank_size, inner_boxes
             )
-        pieces = exchange(cur, *shifts[0])
+        return cur
+
+    def local_adjoint(cur):
+        for i in reversed(range(local_depth)):
+            b = 4**i
+            blk = cur.reshape(part // (4 * b), 4, b, rank_size, inner_boxes)
+            cur = mixing(levels[i], blk, "kcor,akeol->acerl").reshape(
+                part, rank_size, inner_boxes
+            )
+        return mixing(interpolate, cur, "op,jol->jpl")
+
+    gradient = jnp.zeros(shape5, jnp.bfloat16)
+    for m in range(CHUNKS):
+        chunk = image[:, m]
+        coef = [
+            local_forward(lax.dynamic_index_in_dim(chunk, k0 ^ f, 0, keepdims=False))
+            for f in range(4)
+        ]
+        pieces = exchange(jnp.stack(coef), *shifts[0])
         cur = mixing(w0, pieces, "scor,cjrl->sjol")
         pieces = exchange(cur, *shifts[1])
         merged_y = mixing(w1, pieces, "scor,cjrl->sjol")
@@ -99,15 +117,12 @@
         terms = mixing(w1, back, "scor,sjol->cjrl")
         back = exchange(terms, *shifts[1])
         terms = mixing(w0, back, "scor,sjol->cjrl")
-        cur = exchange(terms, *shifts[0])
-        for i in reversed(range(local_depth)):
-            b = 4**i
-            blk = cur.reshape(4, part // (4 * b), 4, b, rank_size, inner_boxes)
-            cur = mixing(levels[i], blk, "kcor,qakeol->qacerl").reshape(
-                4, part, rank_size, inner_boxes
+        back = exchange(terms, *shifts[0])
+        for f in range(4):
+            piece = local_adjoint(back[f])
+            gradient = lax.dynamic_update_slice(
+                gradient, piece[None, None], (k0 ^ f, m, 0, 0, 0)
             )
-        results.append(mixing(interpolate, cur, "op,qjol->qjpl"))
-    gradient = xor_order(jnp.stack(results, 1), 0, *bits[0])
     return gradient.reshape(groups, rank_size, inner_boxes)[None, None]
 
 

time: 231 us -> 220 us (0.952)
  waiting for transfers between devices: 103 us -> 85.5 us
  matrix products: 31.5 us -> 42 us
  other arithmetic: 37.2 us -> 29 us
  local copies, waits for them, and re-layouts: 18.7 us -> 23.3 us
    ppermute x8, waiting for transfers between devices: 69 us -> 24.1 us  [flip_send(): return lax.ppermute(value, ('qx', 'qy'), pairs)]
    ppermute x8, waiting for transfers between devices: 16.6 us -> 47.9 us  [flip_send(): return lax.ppermute(value, 'qx', pairs)]
    dot_general x20 -> x56, matrix products: 28.5 us -> 40.3 us  [mixing(): jnp.einsum(form, weight, data, preferred_element_type=jnp.float32)]
    unnamed x24 -> x46, local copies, waits for them, and re-layouts: 8.3 us -> 12.9 us
    ppermute x8, starting transfers between devices: 15.1 us -> 10.7 us  [flip_send(): return lax.ppermute(value, ('qx', 'qy'), pairs)]
    select_n x5 -> x3, other arithmetic: 3.7 us -> 0.19 us  [xor_order(): pairs = jnp.where(x_bit == 1, jnp.flip(pairs, 0), pairs)]
    ppermute x8, waiting for transfers between devices: 17 us -> 13.5 us  [flip_send(): return lax.ppermute(value, 'qy', pairs)]
    select_n x4 -> x2, other arithmetic: 3.68 us -> 0.21 us  [xor_order(): pairs = jnp.where(y_bit == 1, jnp.flip(pairs, 1), pairs)]
  transfers between devices with their start and end apart: 24 -> 24, of which waited for: 16 -> 9; matrix products, arithmetic and copies ran while one was open for 23% -> 34% of each run, Pallas kernels for 0% -> 0%
where the time goes in v1:
time: 220 us; the launch traced here: 219 us
  waiting for transfers between devices  85.5 us (39%)
  matrix products  42 us (19%)
  starting transfers between devices  38.4 us (17%)
  other arithmetic  29 us (13%)
  local copies, waits for them, and re-layouts  23.3 us (11%)
    ppermute x8, waiting for transfers between devices, flip_send(): return lax.ppermute(value, 'qx', pairs)  47.9 us
    dot_general x56, matrix products, mixing(): jnp.einsum(form, weight, data, preferred_element_type=jnp.float32)  40.3 us
    mul x1, other arithmetic, local(): jnp.float32(math.sqrt(2.0))  28.6 us
    ppermute x8, waiting for transfers between devices, flip_send(): return lax.ppermute(value, ('qx', 'qy'), pairs)  24.1 us
    ppermute x8, starting transfers between devices, flip_send(): return lax.ppermute(value, 'qy', pairs)  17.1 us
    ppermute x8, waiting for transfers between devices, flip_send(): return lax.ppermute(value, 'qy', pairs)  13.5 us
    unnamed x46, local copies, waits for them, and re-layouts  12.9 us
    ppermute x8, starting transfers between devices, flip_send(): return lax.ppermute(value, ('qx', 'qy'), pairs)  10.7 us
  transfers between devices with their start and end apart: 24, of which 9 were waited for; matrix products, arithmetic and copies ran while one was open for 34% of the time, Pallas kernels for 0%

profile of v1, /device:TPU:1, one launch (start us, length us, event | category | flops | bytes accessed | tf_op | source)
XLA Modules:
  0.0 219.0 jit_solution(1627843088749051785)
XLA Ops:
  0.0 5.0 %fusion.236 = (bf16[4,1,32,64,128]{4,3,2,1,0:T(8,128)(2,1)}, bf16[4,1,32,64,128]{4,3,2,1,0:T(8,128)(2,1)S(1)}) fusion(bf16[4,2,32,64,128]{4,3,2,1,0:T(8,128)(2,1)} %bitcast.1009), kind=kLoop, calls=%fused_computation.306 | loop fusion | bytes 8388608 | tf_op jit(solution)/shard_map/slice | solution.py:101
  30.5 28.6 %sine_multiply_fusion = f32[1,1,256,64,128]{4,3,2,1,0:T(8,128)S(1)} fusion(f32[1,1,256,64,128]{4,3,2,1,0:T(8,128)} %param.9), kind=kLoop, calls=%fused_computation | loop fusion | flops 4194304 | bytes 16777216 | tf_op jit(solution)/shard_map/mul | solution.py:75
  59.4 3.3 %fusion.43 = bf16[4,32,64,128]{3,2,0,1:T(8,128)(2,1)S(1)} fusion(bf16[4,4,64,64,1]{3,2,0,1,4:T(8,128)(2,1)S(1)} %bitcast.1047, bf16[1,32,64,128]{3,2,0,1:T(8,128)(2,1)} %bitcast.271, bf16[1,32,64,128]{3,2,0,1:T(8,128)(2,1)} %bitcast.255, bf16[1,32,64,128]{3,2,0,1:T(8,128)(2,1)} %bitcast.239, bf16[1,32,64,128]{3,2,0,1:T(8,128)(2,1)S(1)} %bitcast.1018), kind=kOutput, calls=%fused_computation.56 | convolution fusion | flops 546308096 | bytes 4325376 | tf_op jit(solution)/shard_map/scor,cjrl->sjol/dot_general | solution.py:12
  62.9 3.0 %collective-permute-start.15 = (bf16[32,64,128]{2,1,0:T(8,128)(2,1)S(1)}, bf16[32,64,128]{2,1,0:T(8,128)(2,1)S(1)}, u32[]{:S(2)}, u32[]{:S(2)}) collective-permute-start(bf16[32,64,128]{2,1,0:T(8,128)(2,1)S(1)} %get-tuple-element.16), channel_id=1, source_target_pairs={{0,4},{1,5},{2,6},{3,7},{4,0},{5,1},{6,2},{7,3},{8,12},{9,13},{10,... | collective-permute-start | bytes 1572872 | tf_op jit(solution)/shard_map/ppermute | solution.py:37
  65.9 3.3 %collective-permute-start.16 = (bf16[32,64,128]{2,1,0:T(8,128)(2,1)S(1)}, bf16[32,64,128]{2,1,0:T(8,128)(2,1)S(1)}, u32[]{:S(2)}, u32[]{:S(2)}) collective-permute-start(bf16[32,64,128]{2,1,0:T(8,128)(2,1)S(1)} %get-tuple-element.18), channel_id=1, source_target_pairs={{0,64},{8,72},{16,80},{24,88},{32,96},{40,104},{48,112},{56,120},{... | collective-permute-start | bytes 1572872 | tf_op jit(solution)/shard_map/ppermute | solution.py:34
  69.2 4.7 %collective-permute-done.2 = bf16[32,64,128]{2,1,0:T(8,128)(2,1)S(1)} collective-permute-done((bf16[32,64,128]{2,1,0:T(8,128)(2,1)S(1)}, bf16[32,64,128]{2,1,0:T(8,128)(2,1)S(1)}, u32[]{:S(2)}, u32[]{:S(2)}) %collective-permute-start.2) | collective-permute-done | bytes 524320 | tf_op jit(solution)/shard_map/ppermute | solution.py:43
  77.1 2.9 %collective-permute-start.3 = (bf16[32,64,128]{2,1,0:T(8,128)(2,1)}, bf16[32,64,128]{2,1,0:T(8,128)(2,1)}, u32[]{:S(2)}, u32[]{:S(2)}) collective-permute-start(bf16[32,64,128]{2,1,0:T(8,128)(2,1)} %get-tuple-element.28), channel_id=1, source_target_pairs={{0,4},{1,5},{2,6},{3,7},{4,0},{5,1},{6,2},{7,3},{8,12},{9,13},{10,... | collective-permute-start | bytes 1572872 | tf_op jit(solution)/shard_map/ppermute | solution.py:37
  80.0 3.3 %collective-permute-start.4 = (bf16[32,64,128]{2,1,0:T(8,128)(2,1)}, bf16[32,64,128]{2,1,0:T(8,128)(2,1)}, u32[]{:S(2)}, u32[]{:S(2)}) collective-permute-start(bf16[32,64,128]{2,1,0:T(8,128)(2,1)} %get-tuple-element.30), channel_id=1, source_target_pairs={{0,64},{8,72},{16,80},{24,88},{32,96},{40,104},{48,112},{56,120},{... | collective-permute-start | bytes 1572872 | tf_op jit(solution)/shard_map/ppermute | solution.py:34
  83.4 13.7 %collective-permute-done.16 = bf16[32,64,128]{2,1,0:T(8,128)(2,1)S(1)} collective-permute-done((bf16[32,64,128]{2,1,0:T(8,128)(2,1)S(1)}, bf16[32,64,128]{2,1,0:T(8,128)(2,1)S(1)}, u32[]{:S(2)}, u32[]{:S(2)}) %collective-permute-start.16) | collective-permute-done | bytes 524320 | tf_op jit(solution)/shard_map/ppermute | solution.py:34
  100.3 2.8 %fusion.60 = bf16[4,32,64,128]{3,2,0,1:T(8,128)(2,1)} fusion(bf16[4,4,64,64,1]{2,3,0,1,4:T(8,128)(2,1)S(1)} %bitcast.1051, bf16[4,32,64,128]{3,2,1,0:T(8,128)(2,1)S(1)} %multiply_convert_fusion, bf16[64,64]{1,0:T(8,128)(2,1)S(1)} %copy-done.12), kind=kOutput, calls=%fused_computation.61 | convolution fusion | flops 673185792 | bytes 4333568 | tf_op jit(solution)/shard_map/scor,sjol->cjrl/dot_general | solution.py:12
  103.0 2.8 %slice_bitcast_fusion.10 = (bf16[1,32,64,128]{3,2,1,0:T(8,128)(2,1)S(1)}, bf16[32,64,128]{2,1,0:T(8,128)(2,1)}, bf16[32,64,128]{2,1,0:T(8,128)(2,1)}, bf16[32,64,128]{2,1,0:T(8,128)(2,1)}) fusion(bf16[4,32,64,128]{3,2,0,1:T(8,128)(2,1)} %fusion.60), kind=kLoop, calls=%fused_computation.181 | loop fusion | bytes 4194304
  105.9 2.8 %collective-permute-start.18 = (bf16[32,64,128]{2,1,0:T(8,128)(2,1)}, bf16[32,64,128]{2,1,0:T(8,128)(2,1)}, u32[]{:S(2)}, u32[]{:S(2)}) collective-permute-start(bf16[32,64,128]{2,1,0:T(8,128)(2,1)} %get-tuple-element.12), channel_id=1, source_target_pairs={{0,4},{1,5},{2,6},{3,7},{4,0},{5,1},{6,2},{7,3},{8,12},{9,13},{10,... | collective-permute-start | bytes 1572872 | tf_op jit(solution)/shard_map/ppermute | solution.py:37
  108.8 2.8 %collective-permute-start.20 = (bf16[32,64,128]{2,1,0:T(8,128)(2,1)}, bf16[32,64,128]{2,1,0:T(8,128)(2,1)}, u32[]{:S(2)}, u32[]{:S(2)}) collective-permute-start(bf16[32,64,128]{2,1,0:T(8,128)(2,1)} %get-tuple-element.13), channel_id=1, source_target_pairs={{0,68},{1,69},{2,70},{3,71},{4,64},{5,65},{6,66},{7,67},{8,76},{9,... | collective-permute-start | bytes 1572872 | tf_op jit(solution)/shard_map/ppermute | solution.py:43
  111.5 8.1 %collective-permute-done.4 = bf16[32,64,128]{2,1,0:T(8,128)(2,1)} collective-permute-done((bf16[32,64,128]{2,1,0:T(8,128)(2,1)}, bf16[32,64,128]{2,1,0:T(8,128)(2,1)}, u32[]{:S(2)}, u32[]{:S(2)}) %collective-permute-start.4) | collective-permute-done | bytes 524320 | tf_op jit(solution)/shard_map/ppermute | solution.py:34
  124.5 2.8 %fusion.49 = bf16[4,32,64,128]{3,2,0,1:T(8,128)(2,1)} fusion(bf16[4,4,64,64,1]{2,3,0,1,4:T(8,128)(2,1)S(1)} %bitcast.1052, bf16[4,32,64,128]{3,2,1,0:T(8,128)(2,1)S(1)} %multiply_convert_fusion.1, bf16[64,64]{1,0:T(8,128)(2,1)S(1)} %copy-done.12), kind=kOutput, calls=%fused_computation.58 | convolution fusion | flops 673185792 | bytes 4333568 | tf_op jit(solution)/shard_map/scor,sjol->cjrl/dot_general | solution.py:12
  129.0 3.0 %collective-permute-start.6 = (bf16[32,64,128]{2,1,0:T(8,128)(2,1)S(1)}, bf16[32,64,128]{2,1,0:T(8,128)(2,1)S(1)}, u32[]{:S(2)}, u32[]{:S(2)}) collective-permute-start(bf16[32,64,128]{2,1,0:T(8,128)(2,1)S(1)} %get-tuple-element.24), channel_id=1, source_target_pairs={{0,4},{1,5},{2,6},{3,7},{4,0},{5,1},{6,2},{7,3},{8,12},{9,13},{10,... | collective-permute-start | bytes 1572872 | tf_op jit(solution)/shard_map/ppermute | solution.py:37
  132.0 2.8 %collective-permute-start.8 = (bf16[32,64,128]{2,1,0:T(8,128)(2,1)S(1)}, bf16[32,64,128]{2,1,0:T(8,128)(2,1)S(1)}, u32[]{:S(2)}, u32[]{:S(2)}) collective-permute-start(bf16[32,64,128]{2,1,0:T(8,128)(2,1)S(1)} %get-tuple-element.25), channel_id=1, source_target_pairs={{0,68},{1,69},{2,70},{3,71},{4,64},{5,65},{6,66},{7,67},{8,76},{9,... | collective-permute-start | bytes 1572872 | tf_op jit(solution)/shard_map/ppermute | solution.py:43
  134.7 7.3 %collective-permute-done.19 = bf16[32,64,128]{2,1,0:T(8,128)(2,1)} collective-permute-done((bf16[32,64,128]{2,1,0:T(8,128)(2,1)}, bf16[32,64,128]{2,1,0:T(8,128)(2,1)}, u32[]{:S(2)}, u32[]{:S(2)}) %collective-permute-start.19) | collective-permute-done | bytes 524320 | tf_op jit(solution)/shard_map/ppermute | solution.py:34
  145.6 18.8 %collective-permute-done.7 = bf16[32,64,128]{2,1,0:T(8,128)(2,1)S(1)} collective-permute-done((bf16[32,64,128]{2,1,0:T(8,128)(2,1)S(1)}, bf16[32,64,128]{2,1,0:T(8,128)(2,1)S(1)}, u32[]{:S(2)}, u32[]{:S(2)}) %collective-permute-start.7) | collective-permute-done | bytes 524320 | tf_op jit(solution)/shard_map/ppermute | solution.py:34
  172.4 5.8 %collective-permute-done.9 = bf16[32,64,128]{2,1,0:T(8,128)(2,1)S(1)} collective-permute-done((bf16[32,64,128]{2,1,0:T(8,128)(2,1)S(1)}, bf16[32,64,128]{2,1,0:T(8,128)(2,1)S(1)}, u32[]{:S(2)}, u32[]{:S(2)}) %collective-permute-start.9) | collective-permute-done | bytes 524320 | tf_op jit(solution)/shard_map/ppermute | solution.py:37
  178.2 4.1 %collective-permute-start.23 = (bf16[32,64,128]{2,1,0:T(8,128)(2,1)S(1)}, bf16[32,64,128]{2,1,0:T(8,128)(2,1)S(1)}, u32[]{:S(2)}, u32[]{:S(2)}) collective-permute-start(bf16[32,64,128]{2,1,0:T(8,128)(2,1)S(1)} %get-tuple-element.7), channel_id=1, source_target_pairs={{0,9},{1,8},{2,11},{3,10},{4,13},{5,12},{6,15},{7,14},{8,1},{9,0},... | collective-permute-start | bytes 1572872 | tf_op jit(solution)/shard_map/ppermute | solution.py:43
  183.9 8.4 %collective-permute-done.11 = bf16[32,64,128]{2,1,0:T(8,128)(2,1)S(1)} collective-permute-done((bf16[32,64,128]{2,1,0:T(8,128)(2,1)S(1)}, bf16[32,64,128]{2,1,0:T(8,128)(2,1)S(1)}, u32[]{:S(2)}, u32[]{:S(2)}) %collective-permute-start.11) | collective-permute-done | bytes 524320 | tf_op jit(solution)/shard_map/ppermute | solution.py:43
  193.0 7.7 %collective-permute-done.21 = bf16[32,64,128]{2,1,0:T(8,128)(2,1)S(1)} collective-permute-done((bf16[32,64,128]{2,1,0:T(8,128)(2,1)S(1)}, bf16[32,64,128]{2,1,0:T(8,128)(2,1)S(1)}, u32[]{:S(2)}, u32[]{:S(2)}) %collective-permute-start.21) | collective-permute-done | bytes 524320 | tf_op jit(solution)/shard_map/ppermute | solution.py:37
  202.2 11.0 %collective-permute-done.23 = bf16[32,64,128]{2,1,0:T(8,128)(2,1)S(1)} collective-permute-done((bf16[32,64,128]{2,1,0:T(8,128)(2,1)S(1)}, bf16[32,64,128]{2,1,0:T(8,128)(2,1)S(1)}, u32[]{:S(2)}, u32[]{:S(2)}) %collective-permute-start.23) | collective-permute-done | bytes 524320 | tf_op jit(solution)/shard_map/ppermute | solution.py:43
  (158 shorter events, 59.7 us)
Async XLA Ops:
  7.1 52.0 %collective-permute-start.12 = (bf16[32,64,128]{2,1,0:T(8,128)(2,1)S(1)}, bf16[32,64,128]{2,1,0:T(8,128)(2,1)}, u32[]{:S(2)}, u32[]{:S(2)}) collective-permute-start(bf16[32,64,128]{2,1,0:T(8,128)(2,1)S(1)} %bitcast.1016), channel_id=1, source_target_pairs={{0,1},{1,0},{2,3},{3,2},{4,5},{5,4},{6,7},{7,6},{8,9},{9,8},{10,11... | collective-permute-start | bytes 1572872 | tf_op jit(solution)/shard_map/ppermute | solution.py:37
  11.8 47.7 %collective-permute-start.13 = (bf16[32,64,128]{2,1,0:T(8,128)(2,1)S(1)}, bf16[32,64,128]{2,1,0:T(8,128)(2,1)}, u32[]{:S(2)}, u32[]{:S(2)}) collective-permute-start(bf16[32,64,128]{2,1,0:T(8,128)(2,1)S(1)} %bitcast.1017), channel_id=1, source_target_pairs={{0,8},{8,0},{16,24},{24,16},{32,40},{40,32},{48,56},{56,48},{64,72... | collective-permute-start | bytes 1572872 | tf_op jit(solution)/shard_map/ppermute | solution.py:34
  16.7 42.7 %collective-permute-start.14 = (bf16[32,64,128]{2,1,0:T(8,128)(2,1)}, bf16[32,64,128]{2,1,0:T(8,128)(2,1)}, u32[]{:S(2)}, u32[]{:S(2)}) collective-permute-start(bf16[32,64,128]{2,1,0:T(8,128)(2,1)} %bitcast.270), channel_id=1, source_target_pairs={{0,9},{1,8},{2,11},{3,10},{4,13},{5,12},{6,15},{7,14},{8,1},{9,0},... | collective-permute-start | bytes 1572872 | tf_op jit(solution)/shard_map/ppermute | solution.py:43
  18.6 50.6 %collective-permute-start = (bf16[32,64,128]{2,1,0:T(8,128)(2,1)}, bf16[32,64,128]{2,1,0:T(8,128)(2,1)}, u32[]{:S(2)}, u32[]{:S(2)}) collective-permute-start(bf16[32,64,128]{2,1,0:T(8,128)(2,1)} %bitcast.42), channel_id=1, source_target_pairs={{0,1},{1,0},{2,3},{3,2},{4,5},{5,4},{6,7},{7,6},{8,9},{9,8},{10,11... | collective-permute-start | bytes 1572872 | tf_op jit(solution)/shard_map/ppermute | solution.py:37
  21.8 47.4 %collective-permute-start.1 = (bf16[32,64,128]{2,1,0:T(8,128)(2,1)}, bf16[32,64,128]{2,1,0:T(8,128)(2,1)}, u32[]{:S(2)}, u32[]{:S(2)}) collective-permute-start(bf16[32,64,128]{2,1,0:T(8,128)(2,1)} %bitcast.58), channel_id=1, source_target_pairs={{0,8},{8,0},{16,24},{24,16},{32,40},{40,32},{48,56},{56,48},{64,72... | collective-permute-start | bytes 1572872 | tf_op jit(solution)/shard_map/ppermute | solution.py:34
  59.1 14.7 %collective-permute-start.2 = (bf16[32,64,128]{2,1,0:T(8,128)(2,1)S(1)}, bf16[32,64,128]{2,1,0:T(8,128)(2,1)S(1)}, u32[]{:S(2)}, u32[]{:S(2)}) collective-permute-start(bf16[32,64,128]{2,1,0:T(8,128)(2,1)S(1)} %bitcast.1020), channel_id=1, source_target_pairs={{0,9},{1,8},{2,11},{3,10},{4,13},{5,12},{6,15},{7,14},{8,1},{9,0},... | collective-permute-start | bytes 1572872 | tf_op jit(solution)/shard_map/ppermute | solution.py:43
  62.9 20.4 %collective-permute-start.15 = (bf16[32,64,128]{2,1,0:T(8,128)(2,1)S(1)}, bf16[32,64,128]{2,1,0:T(8,128)(2,1)S(1)}, u32[]{:S(2)}, u32[]{:S(2)}) collective-permute-start(bf16[32,64,128]{2,1,0:T(8,128)(2,1)S(1)} %get-tuple-element.16), channel_id=1, source_target_pairs={{0,4},{1,5},{2,6},{3,7},{4,0},{5,1},{6,2},{7,3},{8,12},{9,13},{10,... | collective-permute-start | bytes 1572872 | tf_op jit(solution)/shard_map/ppermute | solution.py:37
  65.9 31.2 %collective-permute-start.16 = (bf16[32,64,128]{2,1,0:T(8,128)(2,1)S(1)}, bf16[32,64,128]{2,1,0:T(8,128)(2,1)S(1)}, u32[]{:S(2)}, u32[]{:S(2)}) collective-permute-start(bf16[32,64,128]{2,1,0:T(8,128)(2,1)S(1)} %get-tuple-element.18), channel_id=1, source_target_pairs={{0,64},{8,72},{16,80},{24,88},{32,96},{40,104},{48,112},{56,120},{... | collective-permute-start | bytes 1572872 | tf_op jit(solution)/shard_map/ppermute | solution.py:34
  69.2 27.9 %collective-permute-start.17 = (bf16[32,64,128]{2,1,0:T(8,128)(2,1)S(1)}, bf16[32,64,128]{2,1,0:T(8,128)(2,1)S(1)}, u32[]{:S(2)}, u32[]{:S(2)}) collective-permute-start(bf16[32,64,128]{2,1,0:T(8,128)(2,1)S(1)} %get-tuple-element.17), channel_id=1, source_target_pairs={{0,68},{1,69},{2,70},{3,71},{4,64},{5,65},{6,66},{7,67},{8,76},{9,... | collective-permute-start | bytes 1572872 | tf_op jit(solution)/shard_map/ppermute | solution.py:43
  77.1 31.6 %collective-permute-start.3 = (bf16[32,64,128]{2,1,0:T(8,128)(2,1)}, bf16[32,64,128]{2,1,0:T(8,128)(2,1)}, u32[]{:S(2)}, u32[]{:S(2)}) collective-permute-start(bf16[32,64,128]{2,1,0:T(8,128)(2,1)} %get-tuple-element.28), channel_id=1, source_target_pairs={{0,4},{1,5},{2,6},{3,7},{4,0},{5,1},{6,2},{7,3},{8,12},{9,13},{10,... | collective-permute-start | bytes 1572872 | tf_op jit(solution)/shard_map/ppermute | solution.py:37
  80.0 39.6 %collective-permute-start.4 = (bf16[32,64,128]{2,1,0:T(8,128)(2,1)}, bf16[32,64,128]{2,1,0:T(8,128)(2,1)}, u32[]{:S(2)}, u32[]{:S(2)}) collective-permute-start(bf16[32,64,128]{2,1,0:T(8,128)(2,1)} %get-tuple-element.30), channel_id=1, source_target_pairs={{0,64},{8,72},{16,80},{24,88},{32,96},{40,104},{48,112},{56,120},{... | collective-permute-start | bytes 1572872 | tf_op jit(solution)/shard_map/ppermute | solution.py:34
  83.3 36.3 %collective-permute-start.5 = (bf16[32,64,128]{2,1,0:T(8,128)(2,1)}, bf16[32,64,128]{2,1,0:T(8,128)(2,1)}, u32[]{:S(2)}, u32[]{:S(2)}) collective-permute-start(bf16[32,64,128]{2,1,0:T(8,128)(2,1)} %get-tuple-element.29), channel_id=1, source_target_pairs={{0,68},{1,69},{2,70},{3,71},{4,64},{5,65},{6,66},{7,67},{8,76},{9,... | collective-permute-start | bytes 1572872 | tf_op jit(solution)/shard_map/ppermute | solution.py:43
  105.9 26.1 %collective-permute-start.18 = (bf16[32,64,128]{2,1,0:T(8,128)(2,1)}, bf16[32,64,128]{2,1,0:T(8,128)(2,1)}, u32[]{:S(2)}, u32[]{:S(2)}) collective-permute-start(bf16[32,64,128]{2,1,0:T(8,128)(2,1)} %get-tuple-element.12), channel_id=1, source_target_pairs={{0,4},{1,5},{2,6},{3,7},{4,0},{5,1},{6,2},{7,3},{8,12},{9,13},{10,... | collective-permute-start | bytes 1572872 | tf_op jit(solution)/shard_map/ppermute | solution.py:37
  108.6 33.4 %collective-permute-start.19 = (bf16[32,64,128]{2,1,0:T(8,128)(2,1)}, bf16[32,64,128]{2,1,0:T(8,128)(2,1)}, u32[]{:S(2)}, u32[]{:S(2)}) collective-permute-start(bf16[32,64,128]{2,1,0:T(8,128)(2,1)} %get-tuple-element.14), channel_id=1, source_target_pairs={{0,64},{8,72},{16,80},{24,88},{32,96},{40,104},{48,112},{56,120},{... | collective-permute-start | bytes 1572872 | tf_op jit(solution)/shard_map/ppermute | solution.py:34
  108.8 33.3 %collective-permute-start.20 = (bf16[32,64,128]{2,1,0:T(8,128)(2,1)}, bf16[32,64,128]{2,1,0:T(8,128)(2,1)}, u32[]{:S(2)}, u32[]{:S(2)}) collective-permute-start(bf16[32,64,128]{2,1,0:T(8,128)(2,1)} %get-tuple-element.13), channel_id=1, source_target_pairs={{0,68},{1,69},{2,70},{3,71},{4,64},{5,65},{6,66},{7,67},{8,76},{9,... | collective-permute-start | bytes 1572872 | tf_op jit(solution)/shard_map/ppermute | solution.py:43
  129.0 16.6 %collective-permute-start.6 = (bf16[32,64,128]{2,1,0:T(8,128)(2,1)S(1)}, bf16[32,64,128]{2,1,0:T(8,128)(2,1)S(1)}, u32[]{:S(2)}, u32[]{:S(2)}) collective-permute-start(bf16[32,64,128]{2,1,0:T(8,128)(2,1)S(1)} %get-tuple-element.24), channel_id=1, source_target_pairs={{0,4},{1,5},{2,6},{3,7},{4,0},{5,1},{6,2},{7,3},{8,12},{9,13},{10,... | collective-permute-start | bytes 1572872 | tf_op jit(solution)/shard_map/ppermute | solution.py:37
  131.9 32.5 %collective-permute-start.7 = (bf16[32,64,128]{2,1,0:T(8,128)(2,1)S(1)}, bf16[32,64,128]{2,1,0:T(8,128)(2,1)S(1)}, u32[]{:S(2)}, u32[]{:S(2)}) collective-permute-start(bf16[32,64,128]{2,1,0:T(8,128)(2,1)S(1)} %get-tuple-element.26), channel_id=1, source_target_pairs={{0,64},{8,72},{16,80},{24,88},{32,96},{40,104},{48,112},{56,120},{... | collective-permute-start | bytes 1572872 | tf_op jit(solution)/shard_map/ppermute | solution.py:34
  132.0 32.5 %collective-permute-start.8 = (bf16[32,64,128]{2,1,0:T(8,128)(2,1)S(1)}, bf16[32,64,128]{2,1,0:T(8,128)(2,1)S(1)}, u32[]{:S(2)}, u32[]{:S(2)}) collective-permute-start(bf16[32,64,128]{2,1,0:T(8,128)(2,1)S(1)} %get-tuple-element.25), channel_id=1, source_target_pairs={{0,68},{1,69},{2,70},{3,71},{4,64},{5,65},{6,66},{7,67},{8,76},{9,... | collective-permute-start | bytes 1572872 | tf_op jit(solution)/shard_map/ppermute | solution.py:43
  165.8 12.5 %collective-permute-start.9 = (bf16[32,64,128]{2,1,0:T(8,128)(2,1)S(1)}, bf16[32,64,128]{2,1,0:T(8,128)(2,1)S(1)}, u32[]{:S(2)}, u32[]{:S(2)}) collective-permute-start(bf16[32,64,128]{2,1,0:T(8,128)(2,1)S(1)} %get-tuple-element.21), channel_id=1, source_target_pairs={{0,1},{1,0},{2,3},{3,2},{4,5},{5,4},{6,7},{7,6},{8,9},{9,8},{10,11... | collective-permute-start | bytes 1572872 | tf_op jit(solution)/shard_map/ppermute | solution.py:37
  166.9 15.8 %collective-permute-start.10 = (bf16[32,64,128]{2,1,0:T(8,128)(2,1)S(1)}, bf16[32,64,128]{2,1,0:T(8,128)(2,1)S(1)}, u32[]{:S(2)}, u32[]{:S(2)}) collective-permute-start(bf16[32,64,128]{2,1,0:T(8,128)(2,1)S(1)} %get-tuple-element.20), channel_id=1, source_target_pairs={{0,8},{8,0},{16,24},{24,16},{32,40},{40,32},{48,56},{56,48},{64,72... | collective-permute-start | bytes 1572872 | tf_op jit(solution)/shard_map/ppermute | solution.py:34
  168.3 24.0 %collective-permute-start.11 = (bf16[32,64,128]{2,1,0:T(8,128)(2,1)S(1)}, bf16[32,64,128]{2,1,0:T(8,128)(2,1)S(1)}, u32[]{:S(2)}, u32[]{:S(2)}) collective-permute-start(bf16[32,64,128]{2,1,0:T(8,128)(2,1)S(1)} %get-tuple-element.19), channel_id=1, source_target_pairs={{0,9},{1,8},{2,11},{3,10},{4,13},{5,12},{6,15},{7,14},{8,1},{9,0},... | collective-permute-start | bytes 1572872 | tf_op jit(solution)/shard_map/ppermute | solution.py:43
  169.0 31.7 %collective-permute-start.21 = (bf16[32,64,128]{2,1,0:T(8,128)(2,1)S(1)}, bf16[32,64,128]{2,1,0:T(8,128)(2,1)S(1)}, u32[]{:S(2)}, u32[]{:S(2)}) collective-permute-start(bf16[32,64,128]{2,1,0:T(8,128)(2,1)S(1)} %get-tuple-element.9), channel_id=1, source_target_pairs={{0,1},{1,0},{2,3},{3,2},{4,5},{5,4},{6,7},{7,6},{8,9},{9,8},{10,11... | collective-permute-start | bytes 1572872 | tf_op jit(solution)/shard_map/ppermute | solution.py:37
  169.8 31.3 %collective-permute-start.22 = (bf16[32,64,128]{2,1,0:T(8,128)(2,1)S(1)}, bf16[32,64,128]{2,1,0:T(8,128)(2,1)S(1)}, u32[]{:S(2)}, u32[]{:S(2)}) collective-permute-start(bf16[32,64,128]{2,1,0:T(8,128)(2,1)S(1)} %get-tuple-element.8), channel_id=1, source_target_pairs={{0,8},{8,0},{16,24},{24,16},{32,40},{40,32},{48,56},{56,48},{64,72... | collective-permute-start | bytes 1572872 | tf_op jit(solution)/shard_map/ppermute | solution.py:34
  178.2 35.0 %collective-permute-start.23 = (bf16[32,64,128]{2,1,0:T(8,128)(2,1)S(1)}, bf16[32,64,128]{2,1,0:T(8,128)(2,1)S(1)}, u32[]{:S(2)}, u32[]{:S(2)}) collective-permute-start(bf16[32,64,128]{2,1,0:T(8,128)(2,1)S(1)} %get-tuple-element.7), channel_id=1, source_target_pairs={{0,9},{1,8},{2,11},{3,10},{4,13},{5,12},{6,15},{7,14},{8,1},{9,0},... | collective-permute-start | bytes 1572872 | tf_op jit(solution)/shard_map/ppermute | solution.py:43
  (21 other events, 157.1 us)

commit v2 on v1

--- a/solution.py
+++ b/solution.py
@@ -24,6 +24,24 @@
     pairs = jnp.where(y_bit == 1, jnp.flip(pairs, 1), pairs)
     pairs = jnp.where(x_bit == 1, jnp.flip(pairs, 0), pairs)
     return jnp.moveaxis(pairs.reshape(shape), 0, axis)
+
+
+PI_HI = 3.140625
+PI_LO = math.pi - 3.140625
+
+
+def cas(phase):
+    x = phase + jnp.float32(math.pi / 4)
+    n = jnp.round(x * jnp.float32(1 / math.pi))
+    y = (x - n * jnp.float32(PI_HI)) - n * jnp.float32(PI_LO)
+    y2 = y * y
+    poly = jnp.float32(-1 / 39916800)
+    for k in (9, 7, 5, 3):
+        poly = poly * y2 + jnp.float32((-1) ** ((k - 1) // 2) / math.factorial(k))
+    sine = y + y * y2 * poly
+    odd = jnp.abs(n) == 1
+    scale = jnp.where(odd, jnp.float32(-math.sqrt(2.0)), jnp.float32(math.sqrt(2.0)))
+    return scale * sine
 
 
 def flip_send(value, flip, x_shift, y_shift):
@@ -72,9 +90,7 @@
     shape5 = (4, CHUNKS, part, rank_size, inner_boxes)
     image = image_tiles[0, 0].reshape(shape5)
     obs = observed[0, 0].reshape(shape5)
-    cas_all = jnp.float32(math.sqrt(2.0)) * jnp.sin(
-        phases[0, 0].reshape(shape5) + jnp.float32(math.pi / 4)
-    )
+    wave = phases[0, 0].reshape(shape5)
     k0 = 2 * bits[0][0] + bits[0][1]
 
     def local_forward(tiles):
@@ -107,7 +123,7 @@
         cur = mixing(w0, pieces, "scor,cjrl->sjol")
         pieces = exchange(cur, *shifts[1])
         merged_y = mixing(w1, pieces, "scor,cjrl->sjol")
-        cas_wave = cas_all[:, m]
+        cas_wave = cas(wave[:, m])
         predicted = jnp.einsum(
             "or,sjrl->sjol", output_weight, merged_y, preferred_element_type=jnp.float32
         )

time: 220 us -> 203 us (0.923)
  other arithmetic: 29 us -> 0.4 us
  matrix products: 42 us -> 54.9 us
  starting transfers between devices: 38.4 us -> 44.2 us
  waiting for transfers between devices: 85.5 us -> 81.7 us
  local copies, waits for them, and re-layouts: 23.3 us -> 20.5 us
    mul x1 -> x0, other arithmetic: 28.6 us -> none  [local(): jnp.float32(math.sqrt(2.0))]
    ppermute x8, waiting for transfers between devices: 47.9 us -> 30 us  [flip_send(): return lax.ppermute(value, 'qx', pairs)]
    ppermute x8, waiting for transfers between devices: 24.1 us -> 38.9 us  [flip_send(): return lax.ppermute(value, ('qx', 'qy'), pairs)]
    dot_general x2, matrix products: 1.73 us -> 10.4 us  [local(): jnp.einsum('or,sjrl->sjol', output_weight, merged_y, preferred_element_ty...]
    ppermute x8, starting transfers between devices: 10.7 us -> 17.3 us  [flip_send(): return lax.ppermute(value, ('qx', 'qy'), pairs)]
    dot_general x56, matrix products: 40.3 us -> 44.5 us  [mixing(): jnp.einsum(form, weight, data, preferred_element_type=jnp.float32)]
    unnamed x46 -> x42, local copies, waits for them, and re-layouts: 12.9 us -> 10.1 us
  transfers between devices with their start and end apart: 24 -> 24, of which waited for: 9 -> 10; matrix products, arithmetic and copies ran while one was open for 34% -> 28% of each run, Pallas kernels for 0% -> 0%
where the time goes in v2:
time: 203 us; the launch traced here: 202 us
  waiting for transfers between devices  81.7 us (40%)
  matrix products  54.9 us (27%)
  starting transfers between devices  44.2 us (22%)
  local copies, waits for them, and re-layouts  20.5 us (10%)
    dot_general x56, matrix products, mixing(): jnp.einsum(form, weight, data, preferred_element_type=jnp.float32)  44.5 us
    ppermute x8, waiting for transfers between devices, flip_send(): return lax.ppermute(value, ('qx', 'qy'), pairs)  38.9 us
    ppermute x8, waiting for transfers between devices, flip_send(): return lax.ppermute(value, 'qx', pairs)  30 us
    ppermute x8, starting transfers between devices, flip_send(): return lax.ppermute(value, ('qx', 'qy'), pairs)  17.3 us
    ppermute x8, starting transfers between devices, flip_send(): return lax.ppermute(value, 'qy', pairs)  15.9 us
    ppermute x8, waiting for transfers between devices, flip_send(): return lax.ppermute(value, 'qy', pairs)  12.8 us
    ppermute x8, starting transfers between devices, flip_send(): return lax.ppermute(value, 'qx', pairs)  11 us
    dot_general x2, matrix products, local(): jnp.einsum('or,sjrl->sjol', output_weight, merged_y, preferred_element_ty...  10.4 us
  transfers between devices with their start and end apart: 24, of which 10 were waited for; matrix products, arithmetic and copies ran while one was open for 28% of the time, Pallas kernels for 0%

profile of v2, /device:TPU:1, one launch (start us, length us, event | category | flops | bytes accessed | tf_op | source)
XLA Modules:
  0.0 202.5 jit_solution(7784714720018020633)
XLA Ops:
  0.0 5.0 %fusion.254 = (bf16[4,1,32,64,128]{4,3,2,1,0:T(8,128)(2,1)}, bf16[4,1,32,64,128]{4,3,2,1,0:T(8,128)(2,1)S(1)}) fusion(bf16[4,2,32,64,128]{4,3,2,1,0:T(8,128)(2,1)} %bitcast.1015), kind=kLoop, calls=%fused_computation.335 | loop fusion | bytes 8388608 | tf_op jit(solution)/shard_map/slice | solution.py:117
  37.2 3.0 %collective-permute-start.15 = (bf16[32,64,128]{2,1,0:T(8,128)(2,1)S(1)}, bf16[32,64,128]{2,1,0:T(8,128)(2,1)S(1)}, u32[]{:S(2)}, u32[]{:S(2)}) collective-permute-start(bf16[32,64,128]{2,1,0:T(8,128)(2,1)S(1)} %get-tuple-element.16), channel_id=1, source_target_pairs={{0,4},{1,5},{2,6},{3,7},{4,0},{5,1},{6,2},{7,3},{8,12},{9,13},{10,... | collective-permute-start | bytes 1572872 | tf_op jit(solution)/shard_map/ppermute | solution.py:55
  40.2 3.3 %collective-permute-start.16 = (bf16[32,64,128]{2,1,0:T(8,128)(2,1)S(1)}, bf16[32,64,128]{2,1,0:T(8,128)(2,1)S(1)}, u32[]{:S(2)}, u32[]{:S(2)}) collective-permute-start(bf16[32,64,128]{2,1,0:T(8,128)(2,1)S(1)} %get-tuple-element.18), channel_id=1, source_target_pairs={{0,64},{8,72},{16,80},{24,88},{32,96},{40,104},{48,112},{56,120},{... | collective-permute-start | bytes 1572872 | tf_op jit(solution)/shard_map/ppermute | solution.py:52
  43.9 5.8 %collective-permute-start.17 = (bf16[32,64,128]{2,1,0:T(8,128)(2,1)S(1)}, bf16[32,64,128]{2,1,0:T(8,128)(2,1)S(1)}, u32[]{:S(2)}, u32[]{:S(2)}) collective-permute-start(bf16[32,64,128]{2,1,0:T(8,128)(2,1)S(1)} %get-tuple-element.17), channel_id=1, source_target_pairs={{0,68},{1,69},{2,70},{3,71},{4,64},{5,65},{6,66},{7,67},{8,76},{9,... | collective-permute-start | bytes 1572872 | tf_op jit(solution)/shard_map/ppermute | solution.py:61
  49.6 18.0 %collective-permute-done.2 = bf16[32,64,128]{2,1,0:T(8,128)(2,1)S(1)} collective-permute-done((bf16[32,64,128]{2,1,0:T(8,128)(2,1)S(1)}, bf16[32,64,128]{2,1,0:T(8,128)(2,1)S(1)}, u32[]{:S(2)}, u32[]{:S(2)}) %collective-permute-start.2) | collective-permute-done | bytes 524320 | tf_op jit(solution)/shard_map/ppermute | solution.py:61
  70.8 3.0 %collective-permute-start.3 = (bf16[32,64,128]{2,1,0:T(8,128)(2,1)}, bf16[32,64,128]{2,1,0:T(8,128)(2,1)}, u32[]{:S(2)}, u32[]{:S(2)}) collective-permute-start(bf16[32,64,128]{2,1,0:T(8,128)(2,1)} %get-tuple-element.28), channel_id=1, source_target_pairs={{0,4},{1,5},{2,6},{3,7},{4,0},{5,1},{6,2},{7,3},{8,12},{9,13},{10,... | collective-permute-start | bytes 1572872 | tf_op jit(solution)/shard_map/ppermute | solution.py:55
  73.9 3.9 %collective-permute-start.4 = (bf16[32,64,128]{2,1,0:T(8,128)(2,1)}, bf16[32,64,128]{2,1,0:T(8,128)(2,1)}, u32[]{:S(2)}, u32[]{:S(2)}) collective-permute-start(bf16[32,64,128]{2,1,0:T(8,128)(2,1)} %get-tuple-element.30), channel_id=1, source_target_pairs={{0,64},{8,72},{16,80},{24,88},{32,96},{40,104},{48,112},{56,120},{... | collective-permute-start | bytes 1572872 | tf_op jit(solution)/shard_map/ppermute | solution.py:52
  77.8 2.8 %collective-permute-done.16 = bf16[32,64,128]{2,1,0:T(8,128)(2,1)S(1)} collective-permute-done((bf16[32,64,128]{2,1,0:T(8,128)(2,1)S(1)}, bf16[32,64,128]{2,1,0:T(8,128)(2,1)S(1)}, u32[]{:S(2)}, u32[]{:S(2)}) %collective-permute-start.16) | collective-permute-done | bytes 524320 | tf_op jit(solution)/shard_map/ppermute | solution.py:52
  84.1 5.2 %multiply_convert_fusion = bf16[4,32,64,128]{3,2,1,0:T(8,128)(2,1)} fusion(f32[4,2,32,64,128]{4,3,2,1,0:T(8,128)S(1)} %bitcast.1060, bf16[4,2,32,64,128]{4,3,2,1,0:T(8,128)(2,1)S(1)} %bitcast.1064, bf16[4,32,64,128]{3,2,0,1:T(8,128)(2,1)S(1)} %fusion.75, bf16[64,64]{1,0:T(8,128)(2,1)S(1)} %copy-done.14), kind=kOutput, calls=%fused_computation.44 | convolution fusion | flops 165675008 | bytes 10493952 | tf_op jit(solution)/shard_map/or,sjrl->sjol/dot_general | solution.py:127
  89.2 3.0 %fusion.78 = bf16[4,32,64,128]{3,2,0,1:T(8,128)(2,1)S(1)} fusion(bf16[4,4,64,64,1]{2,3,0,1,4:T(8,128)(2,1)S(1)} %bitcast.1056, bf16[4,32,64,128]{3,2,1,0:T(8,128)(2,1)} %multiply_convert_fusion, bf16[64,64]{1,0:T(8,128)(2,1)S(1)} %copy-done.14), kind=kOutput, calls=%fused_computation.90 | convolution fusion | flops 673185792 | bytes 4333568 | tf_op jit(solution)/shard_map/scor,sjol->cjrl/dot_general | solution.py:12
  93.4 2.8 %collective-permute-start.18 = (bf16[32,64,128]{2,1,0:T(8,128)(2,1)}, bf16[32,64,128]{2,1,0:T(8,128)(2,1)}, u32[]{:S(2)}, u32[]{:S(2)}) collective-permute-start(bf16[32,64,128]{2,1,0:T(8,128)(2,1)} %get-tuple-element.12), channel_id=1, source_target_pairs={{0,4},{1,5},{2,6},{3,7},{4,0},{5,1},{6,2},{7,3},{8,12},{9,13},{10,... | collective-permute-start | bytes 1572872 | tf_op jit(solution)/shard_map/ppermute | solution.py:55
  96.3 2.8 %collective-permute-start.20 = (bf16[32,64,128]{2,1,0:T(8,128)(2,1)}, bf16[32,64,128]{2,1,0:T(8,128)(2,1)}, u32[]{:S(2)}, u32[]{:S(2)}) collective-permute-start(bf16[32,64,128]{2,1,0:T(8,128)(2,1)} %get-tuple-element.13), channel_id=1, source_target_pairs={{0,68},{1,69},{2,70},{3,71},{4,64},{5,65},{6,66},{7,67},{8,76},{9,... | collective-permute-start | bytes 1572872 | tf_op jit(solution)/shard_map/ppermute | solution.py:61
  99.1 4.0 %collective-permute-done.4 = bf16[32,64,128]{2,1,0:T(8,128)(2,1)} collective-permute-done((bf16[32,64,128]{2,1,0:T(8,128)(2,1)}, bf16[32,64,128]{2,1,0:T(8,128)(2,1)}, u32[]{:S(2)}, u32[]{:S(2)}) %collective-permute-start.4) | collective-permute-done | bytes 524320 | tf_op jit(solution)/shard_map/ppermute | solution.py:52
  107.0 5.2 %multiply_convert_fusion.1 = bf16[4,32,64,128]{3,2,1,0:T(8,128)(2,1)} fusion(f32[4,2,32,64,128]{4,3,2,1,0:T(8,128)S(1)} %bitcast.1063, bf16[4,2,32,64,128]{4,3,2,1,0:T(8,128)(2,1)S(1)} %bitcast.1065, bf16[4,32,64,128]{3,2,0,1:T(8,128)(2,1)S(1)} %fusion.64, bf16[64,64]{1,0:T(8,128)(2,1)S(1)} %copy-done.14), kind=kOutput, calls=%fused_computation.46 | convolution fusion | flops 165675008 | bytes 10493952 | tf_op jit(solution)/shard_map/or,sjrl->sjol/dot_general | solution.py:127
  112.2 3.0 %fusion.67 = bf16[4,32,64,128]{3,2,0,1:T(8,128)(2,1)S(1)} fusion(bf16[4,4,64,64,1]{2,3,0,1,4:T(8,128)(2,1)S(1)} %bitcast.1057, bf16[4,32,64,128]{3,2,1,0:T(8,128)(2,1)} %multiply_convert_fusion.1, bf16[64,64]{1,0:T(8,128)(2,1)S(1)} %copy-done.14), kind=kOutput, calls=%fused_computation.87 | convolution fusion | flops 673185792 | bytes 4333568 | tf_op jit(solution)/shard_map/scor,sjol->cjrl/dot_general | solution.py:12
  115.4 3.0 %collective-permute-start.6 = (bf16[32,64,128]{2,1,0:T(8,128)(2,1)S(1)}, bf16[32,64,128]{2,1,0:T(8,128)(2,1)S(1)}, u32[]{:S(2)}, u32[]{:S(2)}) collective-permute-start(bf16[32,64,128]{2,1,0:T(8,128)(2,1)S(1)} %get-tuple-element.24), channel_id=1, source_target_pairs={{0,4},{1,5},{2,6},{3,7},{4,0},{5,1},{6,2},{7,3},{8,12},{9,13},{10,... | collective-permute-start | bytes 1572872 | tf_op jit(solution)/shard_map/ppermute | solution.py:55
  118.4 2.8 %collective-permute-start.8 = (bf16[32,64,128]{2,1,0:T(8,128)(2,1)S(1)}, bf16[32,64,128]{2,1,0:T(8,128)(2,1)S(1)}, u32[]{:S(2)}, u32[]{:S(2)}) collective-permute-start(bf16[32,64,128]{2,1,0:T(8,128)(2,1)S(1)} %get-tuple-element.25), channel_id=1, source_target_pairs={{0,68},{1,69},{2,70},{3,71},{4,64},{5,65},{6,66},{7,67},{8,76},{9,... | collective-permute-start | bytes 1572872 | tf_op jit(solution)/shard_map/ppermute | solution.py:61
  121.2 4.3 %collective-permute-done.19 = bf16[32,64,128]{2,1,0:T(8,128)(2,1)} collective-permute-done((bf16[32,64,128]{2,1,0:T(8,128)(2,1)}, bf16[32,64,128]{2,1,0:T(8,128)(2,1)}, u32[]{:S(2)}, u32[]{:S(2)}) %collective-permute-start.19) | collective-permute-done | bytes 524320 | tf_op jit(solution)/shard_map/ppermute | solution.py:52
  129.1 18.8 %collective-permute-done.7 = bf16[32,64,128]{2,1,0:T(8,128)(2,1)S(1)} collective-permute-done((bf16[32,64,128]{2,1,0:T(8,128)(2,1)S(1)}, bf16[32,64,128]{2,1,0:T(8,128)(2,1)S(1)}, u32[]{:S(2)}, u32[]{:S(2)}) %collective-permute-start.7) | collective-permute-done | bytes 524320 | tf_op jit(solution)/shard_map/ppermute | solution.py:52
  155.4 5.8 %collective-permute-done.9 = bf16[32,64,128]{2,1,0:T(8,128)(2,1)S(1)} collective-permute-done((bf16[32,64,128]{2,1,0:T(8,128)(2,1)S(1)}, bf16[32,64,128]{2,1,0:T(8,128)(2,1)S(1)}, u32[]{:S(2)}, u32[]{:S(2)}) %collective-permute-start.9) | collective-permute-done | bytes 524320 | tf_op jit(solution)/shard_map/ppermute | solution.py:55
  161.2 4.1 %collective-permute-start.23 = (bf16[32,64,128]{2,1,0:T(8,128)(2,1)S(1)}, bf16[32,64,128]{2,1,0:T(8,128)(2,1)S(1)}, u32[]{:S(2)}, u32[]{:S(2)}) collective-permute-start(bf16[32,64,128]{2,1,0:T(8,128)(2,1)S(1)} %get-tuple-element.7), channel_id=1, source_target_pairs={{0,9},{1,8},{2,11},{3,10},{4,13},{5,12},{6,15},{7,14},{8,1},{9,0},... | collective-permute-start | bytes 1572872 | tf_op jit(solution)/shard_map/ppermute | solution.py:61
  166.9 9.4 %collective-permute-done.11 = bf16[32,64,128]{2,1,0:T(8,128)(2,1)S(1)} collective-permute-done((bf16[32,64,128]{2,1,0:T(8,128)(2,1)S(1)}, bf16[32,64,128]{2,1,0:T(8,128)(2,1)S(1)}, u32[]{:S(2)}, u32[]{:S(2)}) %collective-permute-start.11) | collective-permute-done | bytes 524320 | tf_op jit(solution)/shard_map/ppermute | solution.py:61
  177.0 6.6 %collective-permute-done.21 = bf16[32,64,128]{2,1,0:T(8,128)(2,1)S(1)} collective-permute-done((bf16[32,64,128]{2,1,0:T(8,128)(2,1)S(1)}, bf16[32,64,128]{2,1,0:T(8,128)(2,1)S(1)}, u32[]{:S(2)}, u32[]{:S(2)}) %collective-permute-start.21) | collective-permute-done | bytes 524320 | tf_op jit(solution)/shard_map/ppermute | solution.py:55
  185.2 11.5 %collective-permute-done.23 = bf16[32,64,128]{2,1,0:T(8,128)(2,1)S(1)} collective-permute-done((bf16[32,64,128]{2,1,0:T(8,128)(2,1)S(1)}, bf16[32,64,128]{2,1,0:T(8,128)(2,1)S(1)}, u32[]{:S(2)}, u32[]{:S(2)}) %collective-permute-start.23) | collective-permute-done | bytes 524320 | tf_op jit(solution)/shard_map/ppermute | solution.py:61
  (154 shorter events, 64.5 us)
Async XLA Ops:
  7.1 27.6 %collective-permute-start.12 = (bf16[32,64,128]{2,1,0:T(8,128)(2,1)S(1)}, bf16[32,64,128]{2,1,0:T(8,128)(2,1)}, u32[]{:S(2)}, u32[]{:S(2)}) collective-permute-start(bf16[32,64,128]{2,1,0:T(8,128)(2,1)S(1)} %bitcast.1022), channel_id=1, source_target_pairs={{0,1},{1,0},{2,3},{3,2},{4,5},{5,4},{6,7},{7,6},{8,9},{9,8},{10,11... | collective-permute-start | bytes 1572872 | tf_op jit(solution)/shard_map/ppermute | solution.py:55
  12.6 22.3 %collective-permute-start.13 = (bf16[32,64,128]{2,1,0:T(8,128)(2,1)}, bf16[32,64,128]{2,1,0:T(8,128)(2,1)}, u32[]{:S(2)}, u32[]{:S(2)}) collective-permute-start(bf16[32,64,128]{2,1,0:T(8,128)(2,1)} %bitcast.254), channel_id=1, source_target_pairs={{0,8},{8,0},{16,24},{24,16},{32,40},{40,32},{48,56},{56,48},{64,72... | collective-permute-start | bytes 1572872 | tf_op jit(solution)/shard_map/ppermute | solution.py:52
  16.4 18.4 %collective-permute-start.14 = (bf16[32,64,128]{2,1,0:T(8,128)(2,1)}, bf16[32,64,128]{2,1,0:T(8,128)(2,1)}, u32[]{:S(2)}, u32[]{:S(2)}) collective-permute-start(bf16[32,64,128]{2,1,0:T(8,128)(2,1)} %bitcast.270), channel_id=1, source_target_pairs={{0,9},{1,8},{2,11},{3,10},{4,13},{5,12},{6,15},{7,14},{8,1},{9,0},... | collective-permute-start | bytes 1572872 | tf_op jit(solution)/shard_map/ppermute | solution.py:61
  18.2 25.6 %collective-permute-start = (bf16[32,64,128]{2,1,0:T(8,128)(2,1)}, bf16[32,64,128]{2,1,0:T(8,128)(2,1)}, u32[]{:S(2)}, u32[]{:S(2)}) collective-permute-start(bf16[32,64,128]{2,1,0:T(8,128)(2,1)} %bitcast.42), channel_id=1, source_target_pairs={{0,1},{1,0},{2,3},{3,2},{4,5},{5,4},{6,7},{7,6},{8,9},{9,8},{10,11... | collective-permute-start | bytes 1572872 | tf_op jit(solution)/shard_map/ppermute | solution.py:55
  21.4 28.2 %collective-permute-start.1 = (bf16[32,64,128]{2,1,0:T(8,128)(2,1)}, bf16[32,64,128]{2,1,0:T(8,128)(2,1)}, u32[]{:S(2)}, u32[]{:S(2)}) collective-permute-start(bf16[32,64,128]{2,1,0:T(8,128)(2,1)} %bitcast.58), channel_id=1, source_target_pairs={{0,8},{8,0},{16,24},{24,16},{32,40},{40,32},{48,56},{56,48},{64,72... | collective-permute-start | bytes 1572872 | tf_op jit(solution)/shard_map/ppermute | solution.py:52
  34.7 32.9 %collective-permute-start.2 = (bf16[32,64,128]{2,1,0:T(8,128)(2,1)S(1)}, bf16[32,64,128]{2,1,0:T(8,128)(2,1)S(1)}, u32[]{:S(2)}, u32[]{:S(2)}) collective-permute-start(bf16[32,64,128]{2,1,0:T(8,128)(2,1)S(1)} %bitcast.1024), channel_id=1, source_target_pairs={{0,9},{1,8},{2,11},{3,10},{4,13},{5,12},{6,15},{7,14},{8,1},{9,0},... | collective-permute-start | bytes 1572872 | tf_op jit(solution)/shard_map/ppermute | solution.py:61
  37.2 40.6 %collective-permute-start.15 = (bf16[32,64,128]{2,1,0:T(8,128)(2,1)S(1)}, bf16[32,64,128]{2,1,0:T(8,128)(2,1)S(1)}, u32[]{:S(2)}, u32[]{:S(2)}) collective-permute-start(bf16[32,64,128]{2,1,0:T(8,128)(2,1)S(1)} %get-tuple-element.16), channel_id=1, source_target_pairs={{0,4},{1,5},{2,6},{3,7},{4,0},{5,1},{6,2},{7,3},{8,12},{9,13},{10,... | collective-permute-start | bytes 1572872 | tf_op jit(solution)/shard_map/ppermute | solution.py:55
  40.2 40.4 %collective-permute-start.16 = (bf16[32,64,128]{2,1,0:T(8,128)(2,1)S(1)}, bf16[32,64,128]{2,1,0:T(8,128)(2,1)S(1)}, u32[]{:S(2)}, u32[]{:S(2)}) collective-permute-start(bf16[32,64,128]{2,1,0:T(8,128)(2,1)S(1)} %get-tuple-element.18), channel_id=1, source_target_pairs={{0,64},{8,72},{16,80},{24,88},{32,96},{40,104},{48,112},{56,120},{... | collective-permute-start | bytes 1572872 | tf_op jit(solution)/shard_map/ppermute | solution.py:52
  43.9 36.7 %collective-permute-start.17 = (bf16[32,64,128]{2,1,0:T(8,128)(2,1)S(1)}, bf16[32,64,128]{2,1,0:T(8,128)(2,1)S(1)}, u32[]{:S(2)}, u32[]{:S(2)}) collective-permute-start(bf16[32,64,128]{2,1,0:T(8,128)(2,1)S(1)} %get-tuple-element.17), channel_id=1, source_target_pairs={{0,68},{1,69},{2,70},{3,71},{4,64},{5,65},{6,66},{7,67},{8,76},{9,... | collective-permute-start | bytes 1572872 | tf_op jit(solution)/shard_map/ppermute | solution.py:61
  70.8 25.4 %collective-permute-start.3 = (bf16[32,64,128]{2,1,0:T(8,128)(2,1)}, bf16[32,64,128]{2,1,0:T(8,128)(2,1)}, u32[]{:S(2)}, u32[]{:S(2)}) collective-permute-start(bf16[32,64,128]{2,1,0:T(8,128)(2,1)} %get-tuple-element.28), channel_id=1, source_target_pairs={{0,4},{1,5},{2,6},{3,7},{4,0},{5,1},{6,2},{7,3},{8,12},{9,13},{10,... | collective-permute-start | bytes 1572872 | tf_op jit(solution)/shard_map/ppermute | solution.py:55
  73.9 29.2 %collective-permute-start.4 = (bf16[32,64,128]{2,1,0:T(8,128)(2,1)}, bf16[32,64,128]{2,1,0:T(8,128)(2,1)}, u32[]{:S(2)}, u32[]{:S(2)}) collective-permute-start(bf16[32,64,128]{2,1,0:T(8,128)(2,1)} %get-tuple-element.30), channel_id=1, source_target_pairs={{0,64},{8,72},{16,80},{24,88},{32,96},{40,104},{48,112},{56,120},{... | collective-permute-start | bytes 1572872 | tf_op jit(solution)/shard_map/ppermute | solution.py:52
  77.8 25.3 %collective-permute-start.5 = (bf16[32,64,128]{2,1,0:T(8,128)(2,1)}, bf16[32,64,128]{2,1,0:T(8,128)(2,1)}, u32[]{:S(2)}, u32[]{:S(2)}) collective-permute-start(bf16[32,64,128]{2,1,0:T(8,128)(2,1)} %get-tuple-element.29), channel_id=1, source_target_pairs={{0,68},{1,69},{2,70},{3,71},{4,64},{5,65},{6,66},{7,67},{8,76},{9,... | collective-permute-start | bytes 1572872 | tf_op jit(solution)/shard_map/ppermute | solution.py:61
  93.4 25.0 %collective-permute-start.18 = (bf16[32,64,128]{2,1,0:T(8,128)(2,1)}, bf16[32,64,128]{2,1,0:T(8,128)(2,1)}, u32[]{:S(2)}, u32[]{:S(2)}) collective-permute-start(bf16[32,64,128]{2,1,0:T(8,128)(2,1)} %get-tuple-element.12), channel_id=1, source_target_pairs={{0,4},{1,5},{2,6},{3,7},{4,0},{5,1},{6,2},{7,3},{8,12},{9,13},{10,... | collective-permute-start | bytes 1572872 | tf_op jit(solution)/shard_map/ppermute | solution.py:55
  96.2 29.3 %collective-permute-start.19 = (bf16[32,64,128]{2,1,0:T(8,128)(2,1)}, bf16[32,64,128]{2,1,0:T(8,128)(2,1)}, u32[]{:S(2)}, u32[]{:S(2)}) collective-permute-start(bf16[32,64,128]{2,1,0:T(8,128)(2,1)} %get-tuple-element.14), channel_id=1, source_target_pairs={{0,64},{8,72},{16,80},{24,88},{32,96},{40,104},{48,112},{56,120},{... | collective-permute-start | bytes 1572872 | tf_op jit(solution)/shard_map/ppermute | solution.py:52
  96.3 29.3 %collective-permute-start.20 = (bf16[32,64,128]{2,1,0:T(8,128)(2,1)}, bf16[32,64,128]{2,1,0:T(8,128)(2,1)}, u32[]{:S(2)}, u32[]{:S(2)}) collective-permute-start(bf16[32,64,128]{2,1,0:T(8,128)(2,1)} %get-tuple-element.13), channel_id=1, source_target_pairs={{0,68},{1,69},{2,70},{3,71},{4,64},{5,65},{6,66},{7,67},{8,76},{9,... | collective-permute-start | bytes 1572872 | tf_op jit(solution)/shard_map/ppermute | solution.py:61
  115.4 13.7 %collective-permute-start.6 = (bf16[32,64,128]{2,1,0:T(8,128)(2,1)S(1)}, bf16[32,64,128]{2,1,0:T(8,128)(2,1)S(1)}, u32[]{:S(2)}, u32[]{:S(2)}) collective-permute-start(bf16[32,64,128]{2,1,0:T(8,128)(2,1)S(1)} %get-tuple-element.24), channel_id=1, source_target_pairs={{0,4},{1,5},{2,6},{3,7},{4,0},{5,1},{6,2},{7,3},{8,12},{9,13},{10,... | collective-permute-start | bytes 1572872 | tf_op jit(solution)/shard_map/ppermute | solution.py:55
  118.4 29.5 %collective-permute-start.7 = (bf16[32,64,128]{2,1,0:T(8,128)(2,1)S(1)}, bf16[32,64,128]{2,1,0:T(8,128)(2,1)S(1)}, u32[]{:S(2)}, u32[]{:S(2)}) collective-permute-start(bf16[32,64,128]{2,1,0:T(8,128)(2,1)S(1)} %get-tuple-element.26), channel_id=1, source_target_pairs={{0,64},{8,72},{16,80},{24,88},{32,96},{40,104},{48,112},{56,120},{... | collective-permute-start | bytes 1572872 | tf_op jit(solution)/shard_map/ppermute | solution.py:52
  118.4 29.5 %collective-permute-start.8 = (bf16[32,64,128]{2,1,0:T(8,128)(2,1)S(1)}, bf16[32,64,128]{2,1,0:T(8,128)(2,1)S(1)}, u32[]{:S(2)}, u32[]{:S(2)}) collective-permute-start(bf16[32,64,128]{2,1,0:T(8,128)(2,1)S(1)} %get-tuple-element.25), channel_id=1, source_target_pairs={{0,68},{1,69},{2,70},{3,71},{4,64},{5,65},{6,66},{7,67},{8,76},{9,... | collective-permute-start | bytes 1572872 | tf_op jit(solution)/shard_map/ppermute | solution.py:61
  149.2 12.0 %collective-permute-start.9 = (bf16[32,64,128]{2,1,0:T(8,128)(2,1)S(1)}, bf16[32,64,128]{2,1,0:T(8,128)(2,1)S(1)}, u32[]{:S(2)}, u32[]{:S(2)}) collective-permute-start(bf16[32,64,128]{2,1,0:T(8,128)(2,1)S(1)} %get-tuple-element.21), channel_id=1, source_target_pairs={{0,1},{1,0},{2,3},{3,2},{4,5},{5,4},{6,7},{7,6},{8,9},{9,8},{10,11... | collective-permute-start | bytes 1572872 | tf_op jit(solution)/shard_map/ppermute | solution.py:55
  149.7 16.0 %collective-permute-start.10 = (bf16[32,64,128]{2,1,0:T(8,128)(2,1)S(1)}, bf16[32,64,128]{2,1,0:T(8,128)(2,1)S(1)}, u32[]{:S(2)}, u32[]{:S(2)}) collective-permute-start(bf16[32,64,128]{2,1,0:T(8,128)(2,1)S(1)} %get-tuple-element.20), channel_id=1, source_target_pairs={{0,8},{8,0},{16,24},{24,16},{32,40},{40,32},{48,56},{56,48},{64,72... | collective-permute-start | bytes 1572872 | tf_op jit(solution)/shard_map/ppermute | solution.py:52
  151.3 25.0 %collective-permute-start.11 = (bf16[32,64,128]{2,1,0:T(8,128)(2,1)S(1)}, bf16[32,64,128]{2,1,0:T(8,128)(2,1)S(1)}, u32[]{:S(2)}, u32[]{:S(2)}) collective-permute-start(bf16[32,64,128]{2,1,0:T(8,128)(2,1)S(1)} %get-tuple-element.19), channel_id=1, source_target_pairs={{0,9},{1,8},{2,11},{3,10},{4,13},{5,12},{6,15},{7,14},{8,1},{9,0},... | collective-permute-start | bytes 1572872 | tf_op jit(solution)/shard_map/ppermute | solution.py:61
  153.0 30.6 %collective-permute-start.21 = (bf16[32,64,128]{2,1,0:T(8,128)(2,1)S(1)}, bf16[32,64,128]{2,1,0:T(8,128)(2,1)S(1)}, u32[]{:S(2)}, u32[]{:S(2)}) collective-permute-start(bf16[32,64,128]{2,1,0:T(8,128)(2,1)S(1)} %get-tuple-element.9), channel_id=1, source_target_pairs={{0,1},{1,0},{2,3},{3,2},{4,5},{5,4},{6,7},{7,6},{8,9},{9,8},{10,11... | collective-permute-start | bytes 1572872 | tf_op jit(solution)/shard_map/ppermute | solution.py:55
  153.1 30.9 %collective-permute-start.22 = (bf16[32,64,128]{2,1,0:T(8,128)(2,1)S(1)}, bf16[32,64,128]{2,1,0:T(8,128)(2,1)S(1)}, u32[]{:S(2)}, u32[]{:S(2)}) collective-permute-start(bf16[32,64,128]{2,1,0:T(8,128)(2,1)S(1)} %get-tuple-element.8), channel_id=1, source_target_pairs={{0,8},{8,0},{16,24},{24,16},{32,40},{40,32},{48,56},{56,48},{64,72... | collective-permute-start | bytes 1572872 | tf_op jit(solution)/shard_map/ppermute | solution.py:52
  161.2 35.5 %collective-permute-start.23 = (bf16[32,64,128]{2,1,0:T(8,128)(2,1)S(1)}, bf16[32,64,128]{2,1,0:T(8,128)(2,1)S(1)}, u32[]{:S(2)}, u32[]{:S(2)}) collective-permute-start(bf16[32,64,128]{2,1,0:T(8,128)(2,1)S(1)} %get-tuple-element.7), channel_id=1, source_target_pairs={{0,9},{1,8},{2,11},{3,10},{4,13},{5,12},{6,15},{7,14},{8,1},{9,0},... | collective-permute-start | bytes 1572872 | tf_op jit(solution)/shard_map/ppermute | solution.py:61
  (19 other events, 180.6 us)

commit v3 on v2

--- a/solution.py
+++ b/solution.py
@@ -3,6 +3,8 @@
 import jax
 import jax.numpy as jnp
 from jax import lax
+from jax.experimental import pallas as pl
+from jax.experimental.pallas import tpu as pltpu
 from jax.sharding import PartitionSpec as P
 
 CHUNKS = 2
@@ -62,8 +64,70 @@
 
 
 def exchange(relative, x_shift, y_shift):
-    got = [relative[0]] + [flip_send(relative[f], f, x_shift, y_shift) for f in (1, 2, 3)]
-    return jnp.stack(got)
+    return [relative[0]] + [flip_send(relative[f], f, x_shift, y_shift) for f in (1, 2, 3)]
+
+
+def cas_kernel(phase):
+    x = phase + jnp.float32(math.pi / 4)
+    n = jnp.floor(x * jnp.float32(1 / math.pi) + jnp.float32(0.5))
+    y = (x - n * jnp.float32(PI_HI)) - n * jnp.float32(PI_LO)
+    y2 = y * y
+    poly = jnp.float32(-1 / 39916800)
+    for k in (9, 7, 5, 3):
+        poly = poly * y2 + jnp.float32((-1) ** ((k - 1) // 2) / math.factorial(k))
+    sine = y + y * y2 * poly
+    half = n * jnp.float32(0.5)
+    odd = half != jnp.floor(half)
+    scale = jnp.where(odd, jnp.float32(-math.sqrt(2.0)), jnp.float32(math.sqrt(2.0)))
+    return scale * sine
+
+
+def output_stage_kernel(p0, p1, p2, p3, ph_ref, obs_ref, w_ref, wt_ref, o_ref, ot_ref,
+                        t0, t1, t2, t3):
+    rows = 4 * p0.shape[1]
+    pieces = (p0, p1, p2, p3)
+    terms = (t0, t1, t2, t3)
+
+    def body(j, carry):
+        stacked = jnp.concatenate([p[j] for p in pieces], axis=0)
+        merged = jnp.dot(w_ref[...], stacked, preferred_element_type=jnp.float32)
+        merged = merged.astype(jnp.bfloat16)
+        predicted = jnp.dot(o_ref[...], merged, preferred_element_type=jnp.float32)
+        wave = cas_kernel(ph_ref[:, j].reshape(rows, -1))
+        seen = obs_ref[:, j].reshape(rows, -1).astype(jnp.float32)
+        residual = (wave * predicted - seen).astype(jnp.bfloat16)
+        weighted = (wave * residual.astype(jnp.float32)).astype(jnp.bfloat16)
+        back = jnp.dot(ot_ref[...], weighted, preferred_element_type=jnp.float32)
+        back = back.astype(jnp.bfloat16)
+        out = jnp.dot(wt_ref[...], back, preferred_element_type=jnp.float32)
+        out = out.astype(jnp.bfloat16)
+        size = p0.shape[1]
+        for f in range(4):
+            terms[f][j] = out[f * size:(f + 1) * size]
+        return carry
+
+    lax.fori_loop(0, p0.shape[0], body, 0)
+
+
+def output_stage(pieces, wave, obs, chunk, w_mat, w_t, o_mat, o_t, step=8):
+    part, rank_size, inner_boxes = pieces[0].shape
+    piece_spec = pl.BlockSpec((step, rank_size, inner_boxes), lambda i: (i, 0, 0))
+    field_spec = pl.BlockSpec(
+        (4, None, step, rank_size, inner_boxes), lambda i: (0, chunk, i, 0, 0)
+    )
+    square = pl.BlockSpec(w_mat.shape, lambda i: (0, 0))
+    flops = 4 * 2 * part * inner_boxes * w_mat.shape[0] * w_mat.shape[1]
+    moved = part * rank_size * inner_boxes * 4 * (2 + 4 + 2 + 2)
+    return pl.pallas_call(
+        output_stage_kernel,
+        grid=(part // step,),
+        in_specs=[piece_spec] * 4 + [field_spec, field_spec] + [square] * 4,
+        out_specs=[piece_spec] * 4,
+        out_shape=[jax.ShapeDtypeStruct(pieces[0].shape, jnp.bfloat16)] * 4,
+        cost_estimate=pl.CostEstimate(
+            flops=flops, bytes_accessed=moved, transcendentals=0
+        ),
+    )(*pieces, wave, obs, w_mat, w_t, o_mat, o_t)
 
 
 def local(image_tiles, observed, phases, interpolate, local_weights, merge_weights, output_weight):
@@ -86,6 +150,11 @@
 
     w0 = xor_order(xor_order(merges[0], 1, *bits[0]), 0, *bits[1])
     w1 = xor_order(merges[1], 1, *bits[1])
+    w1_mat = jnp.transpose(w1, (0, 2, 1, 3)).reshape(4 * rank_size, 4 * rank_size)
+    w1_t = w1_mat.T
+    eye = jnp.eye(4, dtype=output_weight.dtype)
+    ow_mat = jnp.einsum("st,or->sotr", eye, output_weight).reshape(4 * rank_size, 4 * rank_size)
+    ow_t = ow_mat.T
 
     shape5 = (4, CHUNKS, part, rank_size, inner_boxes)
     image = image_tiles[0, 0].reshape(shape5)
@@ -119,20 +188,12 @@
             local_forward(lax.dynamic_index_in_dim(chunk, k0 ^ f, 0, keepdims=False))
             for f in range(4)
         ]
-        pieces = exchange(jnp.stack(coef), *shifts[0])
-        cur = mixing(w0, pieces, "scor,cjrl->sjol")
+        pieces = exchange(coef, *shifts[0])
+        cur = mixing(w0, jnp.stack(pieces), "scor,cjrl->sjol")
         pieces = exchange(cur, *shifts[1])
-        merged_y = mixing(w1, pieces, "scor,cjrl->sjol")
-        cas_wave = cas(wave[:, m])
-        predicted = jnp.einsum(
-            "or,sjrl->sjol", output_weight, merged_y, preferred_element_type=jnp.float32
-        )
-        residual = (cas_wave * predicted - obs[:, m].astype(jnp.float32)).astype(jnp.bfloat16)
-        weighted = (cas_wave * residual.astype(jnp.float32)).astype(jnp.bfloat16)
-        back = mixing(output_weight, weighted, "or,sjol->sjrl")
-        terms = mixing(w1, back, "scor,sjol->cjrl")
+        terms = output_stage(pieces, wave, obs, m, w1_mat, w1_t, ow_mat, ow_t)
         back = exchange(terms, *shifts[1])
-        terms = mixing(w0, back, "scor,sjol->cjrl")
+        terms = mixing(w0, jnp.stack(back), "scor,sjol->cjrl")
         back = exchange(terms, *shifts[0])
         for f in range(4):
             piece = local_adjoint(back[f])

time: 203 us -> 223 us (1.099)
  Pallas kernels: 0 us -> 54.4 us
  waiting for transfers between devices: 81.7 us -> 60.4 us
  matrix products: 54.9 us -> 35.3 us
  starting transfers between devices: 44.2 us -> 51.8 us
    pallas_call x0 -> x2, Pallas kernels: none -> 54.4 us  [output_stage(): pl.pallas_call(output_stage_kernel, grid=(part // step,), in_specs=[piece...]
    ppermute x8, waiting for transfers between devices: 30 us -> 5.84 us  [flip_send(): return lax.ppermute(value, 'qx', pairs)]
    dot_general x2 -> x0, matrix products: 10.4 us -> none  [local(): jnp.einsum('or,sjrl->sjol', output_weight, merged_y, preferred_element_ty...]
    ppermute x8, waiting for transfers between devices: 38.9 us -> 49.3 us  [flip_send(): return lax.ppermute(value, ('qx', 'qy'), pairs)]
    dot_general x56 -> x52, matrix products: 44.5 us -> 35.3 us  [mixing(): jnp.einsum(form, weight, data, preferred_element_type=jnp.float32)]
    ppermute x8, waiting for transfers between devices: 12.8 us -> 5.31 us  [flip_send(): return lax.ppermute(value, 'qy', pairs)]
    unnamed x42 -> x33, local copies, waits for them, and re-layouts: 10.1 us -> 4.79 us
    ppermute x8, starting transfers between devices: 15.9 us -> 18.9 us  [flip_send(): return lax.ppermute(value, 'qy', pairs)]
  transfers between devices with their start and end apart: 24 -> 24, of which waited for: 10 -> 9; matrix products, arithmetic and copies ran while one was open for 28% -> 17% of each run, Pallas kernels for 0% -> 24%
where the time goes in v3:
time: 223 us; the launch traced here: 222 us
  waiting for transfers between devices  60.4 us (27%)
  Pallas kernels  54.4 us (24%)
  starting transfers between devices  51.8 us (23%)
  matrix products  35.3 us (16%)
  local copies, waits for them, and re-layouts  18.8 us (8%)
    pallas_call x2, Pallas kernels, output_stage(): pl.pallas_call(output_stage_kernel, grid=(part // step,), in_specs=[piece...  54.4 us
    ppermute x8, waiting for transfers between devices, flip_send(): return lax.ppermute(value, ('qx', 'qy'), pairs)  49.3 us
    dot_general x52, matrix products, mixing(): jnp.einsum(form, weight, data, preferred_element_type=jnp.float32)  35.3 us
    ppermute x8, starting transfers between devices, flip_send(): return lax.ppermute(value, ('qx', 'qy'), pairs)  19 us
    ppermute x8, starting transfers between devices, flip_send(): return lax.ppermute(value, 'qy', pairs)  18.9 us
    ppermute x8, starting transfers between devices, flip_send(): return lax.ppermute(value, 'qx', pairs)  13.8 us
    ppermute x8, waiting for transfers between devices, flip_send(): return lax.ppermute(value, 'qx', pairs)  5.84 us
    ppermute x8, waiting for transfers between devices, flip_send(): return lax.ppermute(value, 'qy', pairs)  5.31 us
  transfers between devices with their start and end apart: 24, of which 9 were waited for; matrix products, arithmetic and copies ran while one was open for 17% of the time, Pallas kernels for 24%

profile of v3, /device:TPU:1, one launch (start us, length us, event | category | flops | bytes accessed | tf_op | source)
XLA Modules:
  0.0 222.1 jit_solution(13231898926836936247)
XLA Ops:
  0.0 5.0 %fusion.185 = (bf16[4,1,32,64,128]{4,3,2,1,0:T(8,128)(2,1)}, bf16[4,1,32,64,128]{4,3,2,1,0:T(8,128)(2,1)S(1)}) fusion(bf16[4,2,32,64,128]{4,3,2,1,0:T(8,128)(2,1)} %bitcast.837), kind=kLoop, calls=%fused_computation.260 | loop fusion | bytes 8388608 | tf_op jit(solution)/shard_map/slice | solution.py:186
  7.1 2.5 %collective-permute-start.12 = (bf16[32,64,128]{2,1,0:T(8,128)(2,1)S(1)}, bf16[32,64,128]{2,1,0:T(8,128)(2,1)}, u32[]{:S(2)}, u32[]{:S(2)}) collective-permute-start(bf16[32,64,128]{2,1,0:T(8,128)(2,1)S(1)} %bitcast.850), channel_id=1, source_target_pairs={{0,1},{1,0},{2,3},{3,2},{4,5},{5,4},{6,7},{7,6},{8,9},{9,8},{10,11... | collective-permute-start | bytes 1572872 | tf_op jit(solution)/shard_map/ppermute | solution.py:57
  36.5 2.1 fusion.15
  39.6 2.9 %collective-permute-start.15 = (bf16[32,64,128]{2,1,0:T(8,128)(2,1)S(1)}, bf16[32,64,128]{2,1,0:T(8,128)(2,1)}, u32[]{:S(2)}, u32[]{:S(2)}) collective-permute-start(bf16[32,64,128]{2,1,0:T(8,128)(2,1)S(1)} %get-tuple-element.29), channel_id=1, source_target_pairs={{0,4},{1,5},{2,6},{3,7},{4,0},{5,1},{6,2},{7,3},{8,12},{9,13},{10,... | collective-permute-start | bytes 1572872 | tf_op jit(solution)/shard_map/ppermute | solution.py:57
  42.5 3.3 %collective-permute-start.16 = (bf16[32,64,128]{2,1,0:T(8,128)(2,1)S(1)}, bf16[32,64,128]{2,1,0:T(8,128)(2,1)}, u32[]{:S(2)}, u32[]{:S(2)}) collective-permute-start(bf16[32,64,128]{2,1,0:T(8,128)(2,1)S(1)} %get-tuple-element.28), channel_id=1, source_target_pairs={{0,64},{8,72},{16,80},{24,88},{32,96},{40,104},{48,112},{56,120},{... | collective-permute-start | bytes 1572872 | tf_op jit(solution)/shard_map/ppermute | solution.py:54
  45.8 4.2 %collective-permute-start.17 = (bf16[32,64,128]{2,1,0:T(8,128)(2,1)S(1)}, bf16[32,64,128]{2,1,0:T(8,128)(2,1)}, u32[]{:S(2)}, u32[]{:S(2)}) collective-permute-start(bf16[32,64,128]{2,1,0:T(8,128)(2,1)S(1)} %get-tuple-element.27), channel_id=1, source_target_pairs={{0,68},{1,69},{2,70},{3,71},{4,64},{5,65},{6,66},{7,67},{8,76},{9,... | collective-permute-start | bytes 1572872 | tf_op jit(solution)/shard_map/ppermute | solution.py:63
  50.0 17.8 %collective-permute-done.2 = bf16[32,64,128]{2,1,0:T(8,128)(2,1)S(1)} collective-permute-done((bf16[32,64,128]{2,1,0:T(8,128)(2,1)S(1)}, bf16[32,64,128]{2,1,0:T(8,128)(2,1)S(1)}, u32[]{:S(2)}, u32[]{:S(2)}) %collective-permute-start.2) | collective-permute-done | bytes 524320 | tf_op jit(solution)/shard_map/ppermute | solution.py:63
  71.0 2.9 %collective-permute-start.3 = (bf16[32,64,128]{2,1,0:T(8,128)(2,1)}, bf16[32,64,128]{2,1,0:T(8,128)(2,1)}, u32[]{:S(2)}, u32[]{:S(2)}) collective-permute-start(bf16[32,64,128]{2,1,0:T(8,128)(2,1)} %get-tuple-element.37), channel_id=1, source_target_pairs={{0,4},{1,5},{2,6},{3,7},{4,0},{5,1},{6,2},{7,3},{8,12},{9,13},{10,... | collective-permute-start | bytes 1572872 | tf_op jit(solution)/shard_map/ppermute | solution.py:57
  75.1 3.5 %collective-permute-start.4 = (bf16[32,64,128]{2,1,0:T(8,128)(2,1)S(1)}, bf16[32,64,128]{2,1,0:T(8,128)(2,1)}, u32[]{:S(2)}, u32[]{:S(2)}) collective-permute-start(bf16[32,64,128]{2,1,0:T(8,128)(2,1)S(1)} %get-tuple-element.36), channel_id=1, source_target_pairs={{0,64},{8,72},{16,80},{24,88},{32,96},{40,104},{48,112},{56,120},{... | collective-permute-start | bytes 1572872 | tf_op jit(solution)/shard_map/ppermute | solution.py:54
  80.6 27.2 %shard_map.74 = (bf16[32,64,128]{2,1,0:T(8,128)(2,1)}, bf16[32,64,128]{2,1,0:T(8,128)(2,1)}, bf16[32,64,128]{2,1,0:T(8,128)(2,1)}, bf16[32,64,128]{2,1,0:T(8,128)(2,1)}) custom-call(bf16[32,64,128]{2,1,0:T(8,128)(2,1)} %get-tuple-element.30.p0, bf16[32,64,128]{2,1,0:T(8,128)(2,1)} %collective-permute-done.15.p1, ...), custom_call_target="tpu_custom_call" | custom-call | flops 2147483648 | bytes 10485760 | tf_op jit(solution)/shard_map/pallas_call | solution.py:121
  107.8 3.0 %collective-permute-start.18 = (bf16[32,64,128]{2,1,0:T(8,128)(2,1)}, bf16[32,64,128]{2,1,0:T(8,128)(2,1)S(1)}, u32[]{:S(2)}, u32[]{:S(2)}) collective-permute-start(bf16[32,64,128]{2,1,0:T(8,128)(2,1)} %get-tuple-element.18), channel_id=1, source_target_pairs={{0,4},{1,5},{2,6},{3,7},{4,0},{5,1},{6,2},{7,3},{8,12},{9,13},{10,... | collective-permute-start | bytes 1572872 | tf_op jit(solution)/shard_map/ppermute | solution.py:57
  111.5 2.0 collective-permute-start.20
  114.4 27.2 %shard_map.73 = (bf16[32,64,128]{2,1,0:T(8,128)(2,1)}, bf16[32,64,128]{2,1,0:T(8,128)(2,1)}, bf16[32,64,128]{2,1,0:T(8,128)(2,1)}, bf16[32,64,128]{2,1,0:T(8,128)(2,1)}) custom-call(bf16[32,64,128]{2,1,0:T(8,128)(2,1)} %get-tuple-element.38.p0, bf16[32,64,128]{2,1,0:T(8,128)(2,1)} %collective-permute-done.3.p1, ...), custom_call_target="tpu_custom_call" | custom-call | flops 2147483648 | bytes 10485760 | tf_op jit(solution)/shard_map/pallas_call | solution.py:121
  141.6 3.0 %collective-permute-start.6 = (bf16[32,64,128]{2,1,0:T(8,128)(2,1)}, bf16[32,64,128]{2,1,0:T(8,128)(2,1)S(1)}, u32[]{:S(2)}, u32[]{:S(2)}) collective-permute-start(bf16[32,64,128]{2,1,0:T(8,128)(2,1)} %get-tuple-element.14), channel_id=1, source_target_pairs={{0,4},{1,5},{2,6},{3,7},{4,0},{5,1},{6,2},{7,3},{8,12},{9,13},{10,... | collective-permute-start | bytes 1572872 | tf_op jit(solution)/shard_map/ppermute | solution.py:57
  145.3 2.0 collective-permute-start.8
  150.7 2.6 %collective-permute-done.6 = bf16[32,64,128]{2,1,0:T(8,128)(2,1)S(1)} collective-permute-done((bf16[32,64,128]{2,1,0:T(8,128)(2,1)}, bf16[32,64,128]{2,1,0:T(8,128)(2,1)S(1)}, u32[]{:S(2)}, u32[]{:S(2)}) %collective-permute-start.6) | collective-permute-done | bytes 524320 | tf_op jit(solution)/shard_map/ppermute | solution.py:57
  153.4 3.9 %collective-permute-done.7 = bf16[32,64,128]{2,1,0:T(8,128)(2,1)S(1)} collective-permute-done((bf16[32,64,128]{2,1,0:T(8,128)(2,1)}, bf16[32,64,128]{2,1,0:T(8,128)(2,1)S(1)}, u32[]{:S(2)}, u32[]{:S(2)}) %collective-permute-start.7) | collective-permute-done | bytes 524320 | tf_op jit(solution)/shard_map/ppermute | solution.py:54
  157.2 8.6 %collective-permute-done.8 = bf16[32,64,128]{2,1,0:T(8,128)(2,1)S(1)} collective-permute-done((bf16[32,64,128]{2,1,0:T(8,128)(2,1)}, bf16[32,64,128]{2,1,0:T(8,128)(2,1)S(1)}, u32[]{:S(2)}, u32[]{:S(2)}) %collective-permute-start.8) | collective-permute-done | bytes 524320 | tf_op jit(solution)/shard_map/ppermute | solution.py:63
  167.3 3.1 %collective-permute-start.9 = (bf16[32,64,128]{2,1,0:T(8,128)(2,1)S(1)}, bf16[32,64,128]{2,1,0:T(8,128)(2,1)S(1)}, u32[]{:S(2)}, u32[]{:S(2)}) collective-permute-start(bf16[32,64,128]{2,1,0:T(8,128)(2,1)S(1)} %get-tuple-element.33), channel_id=1, source_target_pairs={{0,1},{1,0},{2,3},{3,2},{4,5},{5,4},{6,7},{7,6},{8,9},{9,8},{10,11... | collective-permute-start | bytes 1572872 | tf_op jit(solution)/shard_map/ppermute | solution.py:57
  170.7 3.2 %collective-permute-start.10 = (bf16[32,64,128]{2,1,0:T(8,128)(2,1)S(1)}, bf16[32,64,128]{2,1,0:T(8,128)(2,1)S(1)}, u32[]{:S(2)}, u32[]{:S(2)}) collective-permute-start(bf16[32,64,128]{2,1,0:T(8,128)(2,1)S(1)} %get-tuple-element.32), channel_id=1, source_target_pairs={{0,8},{8,0},{16,24},{24,16},{32,40},{40,32},{48,56},{56,48},{64,72... | collective-permute-start | bytes 1572872 | tf_op jit(solution)/shard_map/ppermute | solution.py:54
  178.8 9.1 %collective-permute-start.23 = (bf16[32,64,128]{2,1,0:T(8,128)(2,1)S(1)}, bf16[32,64,128]{2,1,0:T(8,128)(2,1)S(1)}, u32[]{:S(2)}, u32[]{:S(2)}) collective-permute-start(bf16[32,64,128]{2,1,0:T(8,128)(2,1)S(1)} %get-tuple-element.23), channel_id=1, source_target_pairs={{0,9},{1,8},{2,11},{3,10},{4,13},{5,12},{6,15},{7,14},{8,1},{9,0},... | collective-permute-start | bytes 1572872 | tf_op jit(solution)/shard_map/ppermute | solution.py:63
  189.4 9.3 %collective-permute-done.11 = bf16[32,64,128]{2,1,0:T(8,128)(2,1)S(1)} collective-permute-done((bf16[32,64,128]{2,1,0:T(8,128)(2,1)S(1)}, bf16[32,64,128]{2,1,0:T(8,128)(2,1)S(1)}, u32[]{:S(2)}, u32[]{:S(2)}) %collective-permute-start.11) | collective-permute-done | bytes 524320 | tf_op jit(solution)/shard_map/ppermute | solution.py:63
  202.8 13.5 %collective-permute-done.23 = bf16[32,64,128]{2,1,0:T(8,128)(2,1)S(1)} collective-permute-done((bf16[32,64,128]{2,1,0:T(8,128)(2,1)S(1)}, bf16[32,64,128]{2,1,0:T(8,128)(2,1)S(1)}, u32[]{:S(2)}, u32[]{:S(2)}) %collective-permute-start.23) | collective-permute-done | bytes 524320 | tf_op jit(solution)/shard_map/ppermute | solution.py:63
  220.1 2.0 copy-done.1
  (148 shorter events, 57.2 us)
Async XLA Ops:
  7.1 29.3 %collective-permute-start.12 = (bf16[32,64,128]{2,1,0:T(8,128)(2,1)S(1)}, bf16[32,64,128]{2,1,0:T(8,128)(2,1)}, u32[]{:S(2)}, u32[]{:S(2)}) collective-permute-start(bf16[32,64,128]{2,1,0:T(8,128)(2,1)S(1)} %bitcast.850), channel_id=1, source_target_pairs={{0,1},{1,0},{2,3},{3,2},{4,5},{5,4},{6,7},{7,6},{8,9},{9,8},{10,11... | collective-permute-start | bytes 1572872 | tf_op jit(solution)/shard_map/ppermute | solution.py:57
  13.6 22.9 %collective-permute-start.13 = (bf16[32,64,128]{2,1,0:T(8,128)(2,1)S(1)}, bf16[32,64,128]{2,1,0:T(8,128)(2,1)}, u32[]{:S(2)}, u32[]{:S(2)}) collective-permute-start(bf16[32,64,128]{2,1,0:T(8,128)(2,1)S(1)} %bitcast.851), channel_id=1, source_target_pairs={{0,8},{8,0},{16,24},{24,16},{32,40},{40,32},{48,56},{56,48},{64,72... | collective-permute-start | bytes 1572872 | tf_op jit(solution)/shard_map/ppermute | solution.py:54
  18.6 17.9 %collective-permute-start.14 = (bf16[32,64,128]{2,1,0:T(8,128)(2,1)}, bf16[32,64,128]{2,1,0:T(8,128)(2,1)}, u32[]{:S(2)}, u32[]{:S(2)}) collective-permute-start(bf16[32,64,128]{2,1,0:T(8,128)(2,1)} %bitcast.246), channel_id=1, source_target_pairs={{0,9},{1,8},{2,11},{3,10},{4,13},{5,12},{6,15},{7,14},{8,1},{9,0},... | collective-permute-start | bytes 1572872 | tf_op jit(solution)/shard_map/ppermute | solution.py:63
  20.5 25.4 %collective-permute-start = (bf16[32,64,128]{2,1,0:T(8,128)(2,1)}, bf16[32,64,128]{2,1,0:T(8,128)(2,1)}, u32[]{:S(2)}, u32[]{:S(2)}) collective-permute-start(bf16[32,64,128]{2,1,0:T(8,128)(2,1)} %bitcast.40), channel_id=1, source_target_pairs={{0,1},{1,0},{2,3},{3,2},{4,5},{5,4},{6,7},{7,6},{8,9},{9,8},{10,11... | collective-permute-start | bytes 1572872 | tf_op jit(solution)/shard_map/ppermute | solution.py:57
  23.7 26.3 %collective-permute-start.1 = (bf16[32,64,128]{2,1,0:T(8,128)(2,1)}, bf16[32,64,128]{2,1,0:T(8,128)(2,1)}, u32[]{:S(2)}, u32[]{:S(2)}) collective-permute-start(bf16[32,64,128]{2,1,0:T(8,128)(2,1)} %bitcast.56), channel_id=1, source_target_pairs={{0,8},{8,0},{16,24},{24,16},{32,40},{40,32},{48,56},{56,48},{64,72... | collective-permute-start | bytes 1572872 | tf_op jit(solution)/shard_map/ppermute | solution.py:54
  36.4 31.4 %collective-permute-start.2 = (bf16[32,64,128]{2,1,0:T(8,128)(2,1)S(1)}, bf16[32,64,128]{2,1,0:T(8,128)(2,1)S(1)}, u32[]{:S(2)}, u32[]{:S(2)}) collective-permute-start(bf16[32,64,128]{2,1,0:T(8,128)(2,1)S(1)} %bitcast.853), channel_id=1, source_target_pairs={{0,9},{1,8},{2,11},{3,10},{4,13},{5,12},{6,15},{7,14},{8,1},{9,0},... | collective-permute-start | bytes 1572872 | tf_op jit(solution)/shard_map/ppermute | solution.py:63
  39.6 39.0 %collective-permute-start.15 = (bf16[32,64,128]{2,1,0:T(8,128)(2,1)S(1)}, bf16[32,64,128]{2,1,0:T(8,128)(2,1)}, u32[]{:S(2)}, u32[]{:S(2)}) collective-permute-start(bf16[32,64,128]{2,1,0:T(8,128)(2,1)S(1)} %get-tuple-element.29), channel_id=1, source_target_pairs={{0,4},{1,5},{2,6},{3,7},{4,0},{5,1},{6,2},{7,3},{8,12},{9,13},{10,... | collective-permute-start | bytes 1572872 | tf_op jit(solution)/shard_map/ppermute | solution.py:57
  42.5 38.1 %collective-permute-start.16 = (bf16[32,64,128]{2,1,0:T(8,128)(2,1)S(1)}, bf16[32,64,128]{2,1,0:T(8,128)(2,1)}, u32[]{:S(2)}, u32[]{:S(2)}) collective-permute-start(bf16[32,64,128]{2,1,0:T(8,128)(2,1)S(1)} %get-tuple-element.28), channel_id=1, source_target_pairs={{0,64},{8,72},{16,80},{24,88},{32,96},{40,104},{48,112},{56,120},{... | collective-permute-start | bytes 1572872 | tf_op jit(solution)/shard_map/ppermute | solution.py:54
  45.8 34.8 %collective-permute-start.17 = (bf16[32,64,128]{2,1,0:T(8,128)(2,1)S(1)}, bf16[32,64,128]{2,1,0:T(8,128)(2,1)}, u32[]{:S(2)}, u32[]{:S(2)}) collective-permute-start(bf16[32,64,128]{2,1,0:T(8,128)(2,1)S(1)} %get-tuple-element.27), channel_id=1, source_target_pairs={{0,68},{1,69},{2,70},{3,71},{4,64},{5,65},{6,66},{7,67},{8,76},{9,... | collective-permute-start | bytes 1572872 | tf_op jit(solution)/shard_map/ppermute | solution.py:63
  71.0 40.6 %collective-permute-start.3 = (bf16[32,64,128]{2,1,0:T(8,128)(2,1)}, bf16[32,64,128]{2,1,0:T(8,128)(2,1)}, u32[]{:S(2)}, u32[]{:S(2)}) collective-permute-start(bf16[32,64,128]{2,1,0:T(8,128)(2,1)} %get-tuple-element.37), channel_id=1, source_target_pairs={{0,4},{1,5},{2,6},{3,7},{4,0},{5,1},{6,2},{7,3},{8,12},{9,13},{10,... | collective-permute-start | bytes 1572872 | tf_op jit(solution)/shard_map/ppermute | solution.py:57
  75.1 38.5 %collective-permute-start.4 = (bf16[32,64,128]{2,1,0:T(8,128)(2,1)S(1)}, bf16[32,64,128]{2,1,0:T(8,128)(2,1)}, u32[]{:S(2)}, u32[]{:S(2)}) collective-permute-start(bf16[32,64,128]{2,1,0:T(8,128)(2,1)S(1)} %get-tuple-element.36), channel_id=1, source_target_pairs={{0,64},{8,72},{16,80},{24,88},{32,96},{40,104},{48,112},{56,120},{... | collective-permute-start | bytes 1572872 | tf_op jit(solution)/shard_map/ppermute | solution.py:54
  78.6 35.0 %collective-permute-start.5 = (bf16[32,64,128]{2,1,0:T(8,128)(2,1)S(1)}, bf16[32,64,128]{2,1,0:T(8,128)(2,1)S(1)}, u32[]{:S(2)}, u32[]{:S(2)}) collective-permute-start(bf16[32,64,128]{2,1,0:T(8,128)(2,1)S(1)} %get-tuple-element.35), channel_id=1, source_target_pairs={{0,68},{1,69},{2,70},{3,71},{4,64},{5,65},{6,66},{7,67},{8,76},{9,... | collective-permute-start | bytes 1572872 | tf_op jit(solution)/shard_map/ppermute | solution.py:63
  107.8 37.6 %collective-permute-start.18 = (bf16[32,64,128]{2,1,0:T(8,128)(2,1)}, bf16[32,64,128]{2,1,0:T(8,128)(2,1)S(1)}, u32[]{:S(2)}, u32[]{:S(2)}) collective-permute-start(bf16[32,64,128]{2,1,0:T(8,128)(2,1)} %get-tuple-element.18), channel_id=1, source_target_pairs={{0,4},{1,5},{2,6},{3,7},{4,0},{5,1},{6,2},{7,3},{8,12},{9,13},{10,... | collective-permute-start | bytes 1572872 | tf_op jit(solution)/shard_map/ppermute | solution.py:57
  110.8 36.6 %collective-permute-start.19 = (bf16[32,64,128]{2,1,0:T(8,128)(2,1)}, bf16[32,64,128]{2,1,0:T(8,128)(2,1)}, u32[]{:S(2)}, u32[]{:S(2)}) collective-permute-start(bf16[32,64,128]{2,1,0:T(8,128)(2,1)} %get-tuple-element.19), channel_id=1, source_target_pairs={{0,64},{8,72},{16,80},{24,88},{32,96},{40,104},{48,112},{56,120},{... | collective-permute-start | bytes 1572872 | tf_op jit(solution)/shard_map/ppermute | solution.py:54
  111.5 35.8 %collective-permute-start.20 = (bf16[32,64,128]{2,1,0:T(8,128)(2,1)}, bf16[32,64,128]{2,1,0:T(8,128)(2,1)}, u32[]{:S(2)}, u32[]{:S(2)}) collective-permute-start(bf16[32,64,128]{2,1,0:T(8,128)(2,1)} %get-tuple-element.20), channel_id=1, source_target_pairs={{0,68},{1,69},{2,70},{3,71},{4,64},{5,65},{6,66},{7,67},{8,76},{9,... | collective-permute-start | bytes 1572872 | tf_op jit(solution)/shard_map/ppermute | solution.py:63
  141.6 11.8 %collective-permute-start.6 = (bf16[32,64,128]{2,1,0:T(8,128)(2,1)}, bf16[32,64,128]{2,1,0:T(8,128)(2,1)S(1)}, u32[]{:S(2)}, u32[]{:S(2)}) collective-permute-start(bf16[32,64,128]{2,1,0:T(8,128)(2,1)} %get-tuple-element.14), channel_id=1, source_target_pairs={{0,4},{1,5},{2,6},{3,7},{4,0},{5,1},{6,2},{7,3},{8,12},{9,13},{10,... | collective-permute-start | bytes 1572872 | tf_op jit(solution)/shard_map/ppermute | solution.py:57
  144.6 12.6 %collective-permute-start.7 = (bf16[32,64,128]{2,1,0:T(8,128)(2,1)}, bf16[32,64,128]{2,1,0:T(8,128)(2,1)S(1)}, u32[]{:S(2)}, u32[]{:S(2)}) collective-permute-start(bf16[32,64,128]{2,1,0:T(8,128)(2,1)} %get-tuple-element.15), channel_id=1, source_target_pairs={{0,64},{8,72},{16,80},{24,88},{32,96},{40,104},{48,112},{56,120},{... | collective-permute-start | bytes 1572872 | tf_op jit(solution)/shard_map/ppermute | solution.py:54
  145.3 20.5 %collective-permute-start.8 = (bf16[32,64,128]{2,1,0:T(8,128)(2,1)}, bf16[32,64,128]{2,1,0:T(8,128)(2,1)S(1)}, u32[]{:S(2)}, u32[]{:S(2)}) collective-permute-start(bf16[32,64,128]{2,1,0:T(8,128)(2,1)} %get-tuple-element.16), channel_id=1, source_target_pairs={{0,68},{1,69},{2,70},{3,71},{4,64},{5,65},{6,66},{7,67},{8,76},{9,... | collective-permute-start | bytes 1572872 | tf_op jit(solution)/shard_map/ppermute | solution.py:63
  167.3 11.6 %collective-permute-start.9 = (bf16[32,64,128]{2,1,0:T(8,128)(2,1)S(1)}, bf16[32,64,128]{2,1,0:T(8,128)(2,1)S(1)}, u32[]{:S(2)}, u32[]{:S(2)}) collective-permute-start(bf16[32,64,128]{2,1,0:T(8,128)(2,1)S(1)} %get-tuple-element.33), channel_id=1, source_target_pairs={{0,1},{1,0},{2,3},{3,2},{4,5},{5,4},{6,7},{7,6},{8,9},{9,8},{10,11... | collective-permute-start | bytes 1572872 | tf_op jit(solution)/shard_map/ppermute | solution.py:57
  170.7 17.5 %collective-permute-start.10 = (bf16[32,64,128]{2,1,0:T(8,128)(2,1)S(1)}, bf16[32,64,128]{2,1,0:T(8,128)(2,1)S(1)}, u32[]{:S(2)}, u32[]{:S(2)}) collective-permute-start(bf16[32,64,128]{2,1,0:T(8,128)(2,1)S(1)} %get-tuple-element.32), channel_id=1, source_target_pairs={{0,8},{8,0},{16,24},{24,16},{32,40},{40,32},{48,56},{56,48},{64,72... | collective-permute-start | bytes 1572872 | tf_op jit(solution)/shard_map/ppermute | solution.py:54
  173.9 24.8 %collective-permute-start.11 = (bf16[32,64,128]{2,1,0:T(8,128)(2,1)S(1)}, bf16[32,64,128]{2,1,0:T(8,128)(2,1)S(1)}, u32[]{:S(2)}, u32[]{:S(2)}) collective-permute-start(bf16[32,64,128]{2,1,0:T(8,128)(2,1)S(1)} %get-tuple-element.31), channel_id=1, source_target_pairs={{0,9},{1,8},{2,11},{3,10},{4,13},{5,12},{6,15},{7,14},{8,1},{9,0},... | collective-permute-start | bytes 1572872 | tf_op jit(solution)/shard_map/ppermute | solution.py:63
  175.5 25.8 %collective-permute-start.21 = (bf16[32,64,128]{2,1,0:T(8,128)(2,1)S(1)}, bf16[32,64,128]{2,1,0:T(8,128)(2,1)S(1)}, u32[]{:S(2)}, u32[]{:S(2)}) collective-permute-start(bf16[32,64,128]{2,1,0:T(8,128)(2,1)S(1)} %get-tuple-element.25), channel_id=1, source_target_pairs={{0,1},{1,0},{2,3},{3,2},{4,5},{5,4},{6,7},{7,6},{8,9},{9,8},{10,11... | collective-permute-start | bytes 1572872 | tf_op jit(solution)/shard_map/ppermute | solution.py:57
  175.5 26.1 %collective-permute-start.22 = (bf16[32,64,128]{2,1,0:T(8,128)(2,1)S(1)}, bf16[32,64,128]{2,1,0:T(8,128)(2,1)S(1)}, u32[]{:S(2)}, u32[]{:S(2)}) collective-permute-start(bf16[32,64,128]{2,1,0:T(8,128)(2,1)S(1)} %get-tuple-element.24), channel_id=1, source_target_pairs={{0,8},{8,0},{16,24},{24,16},{32,40},{40,32},{48,56},{56,48},{64,72... | collective-permute-start | bytes 1572872 | tf_op jit(solution)/shard_map/ppermute | solution.py:54
  178.8 37.5 %collective-permute-start.23 = (bf16[32,64,128]{2,1,0:T(8,128)(2,1)S(1)}, bf16[32,64,128]{2,1,0:T(8,128)(2,1)S(1)}, u32[]{:S(2)}, u32[]{:S(2)}) collective-permute-start(bf16[32,64,128]{2,1,0:T(8,128)(2,1)S(1)} %get-tuple-element.23), channel_id=1, source_target_pairs={{0,9},{1,8},{2,11},{3,10},{4,13},{5,12},{6,15},{7,14},{8,1},{9,0},... | collective-permute-start | bytes 1572872 | tf_op jit(solution)/shard_map/ppermute | solution.py:63
  (16 other events, 91.1 us)

commit v4 on v3

--- a/solution.py
+++ b/solution.py
@@ -84,29 +84,31 @@
 
 def output_stage_kernel(p0, p1, p2, p3, ph_ref, obs_ref, w_ref, wt_ref, o_ref, ot_ref,
                         t0, t1, t2, t3):
-    rows = 4 * p0.shape[1]
+    size = p0.shape[1]
+    rows = 4 * size
+    step = p0.shape[0]
     pieces = (p0, p1, p2, p3)
     terms = (t0, t1, t2, t3)
 
-    def body(j, carry):
-        stacked = jnp.concatenate([p[j] for p in pieces], axis=0)
-        merged = jnp.dot(w_ref[...], stacked, preferred_element_type=jnp.float32)
-        merged = merged.astype(jnp.bfloat16)
-        predicted = jnp.dot(o_ref[...], merged, preferred_element_type=jnp.float32)
-        wave = cas_kernel(ph_ref[:, j].reshape(rows, -1))
-        seen = obs_ref[:, j].reshape(rows, -1).astype(jnp.float32)
-        residual = (wave * predicted - seen).astype(jnp.bfloat16)
-        weighted = (wave * residual.astype(jnp.float32)).astype(jnp.bfloat16)
-        back = jnp.dot(ot_ref[...], weighted, preferred_element_type=jnp.float32)
-        back = back.astype(jnp.bfloat16)
-        out = jnp.dot(wt_ref[...], back, preferred_element_type=jnp.float32)
-        out = out.astype(jnp.bfloat16)
-        size = p0.shape[1]
-        for f in range(4):
-            terms[f][j] = out[f * size:(f + 1) * size]
-        return carry
-
-    lax.fori_loop(0, p0.shape[0], body, 0)
+    def wide(parts):
+        return jnp.concatenate(parts, axis=1)
+
+    stacked = wide([jnp.concatenate([p[j] for p in pieces], axis=0) for j in range(step)])
+    merged = jnp.dot(w_ref[...], stacked, preferred_element_type=jnp.float32)
+    merged = merged.astype(jnp.bfloat16)
+    predicted = jnp.dot(o_ref[...], merged, preferred_element_type=jnp.float32)
+    wave = cas_kernel(wide([ph_ref[:, j].reshape(rows, -1) for j in range(step)]))
+    seen = wide([obs_ref[:, j].reshape(rows, -1) for j in range(step)]).astype(jnp.float32)
+    residual = (wave * predicted - seen).astype(jnp.bfloat16)
+    weighted = (wave * residual.astype(jnp.float32)).astype(jnp.bfloat16)
+    back = jnp.dot(ot_ref[...], weighted, preferred_element_type=jnp.float32)
+    back = back.astype(jnp.bfloat16)
+    out = jnp.dot(wt_ref[...], back, preferred_element_type=jnp.float32)
+    out = out.astype(jnp.bfloat16)
+    lanes = p0.shape[2]
+    for f in range(4):
+        for j in range(step):
+            terms[f][j] = out[f * size:(f + 1) * size, j * lanes:(j + 1) * lanes]
 
 
 def output_stage(pieces, wave, obs, chunk, w_mat, w_t, o_mat, o_t, step=8):

time: 223 us -> 203 us (0.910)
  Pallas kernels: 54.4 us -> 19.8 us
  waiting for transfers between devices: 60.4 us -> 84.9 us
  starting transfers between devices: 51.8 us -> 42.3 us
    pallas_call x2, Pallas kernels: 54.4 us -> 19.8 us  [output_stage(): pl.pallas_call(output_stage_kernel, grid=(part // step,), in_specs=[piece...]
    ppermute x8, waiting for transfers between devices: 5.84 us -> 32.1 us  [flip_send(): return lax.ppermute(value, 'qx', pairs)]
    ppermute x8, waiting for transfers between devices: 49.3 us -> 38.8 us  [flip_send(): return lax.ppermute(value, ('qx', 'qy'), pairs)]
    ppermute x8, waiting for transfers between devices: 5.31 us -> 14 us  [flip_send(): return lax.ppermute(value, 'qy', pairs)]
    ppermute x8, starting transfers between devices: 19 us -> 14.9 us  [flip_send(): return lax.ppermute(value, ('qx', 'qy'), pairs)]
    ppermute x8, starting transfers between devices: 13.8 us -> 11 us  [flip_send(): return lax.ppermute(value, 'qx', pairs)]
    ppermute x8, starting transfers between devices: 18.9 us -> 16.5 us  [flip_send(): return lax.ppermute(value, 'qy', pairs)]
  transfers between devices with their start and end apart: 24 -> 24, of which waited for: 9 -> 10; matrix products, arithmetic and copies ran while one was open for 17% -> 19% of each run, Pallas kernels for 24% -> 10%
where the time goes in v4:
time: 203 us
  waiting for transfers between devices  84.9 us (42%)
  starting transfers between devices  42.3 us (21%)
  matrix products  35.3 us (17%)
  Pallas kernels  19.8 us (10%)
  local copies, waits for them, and re-layouts  18.8 us (9%)
    ppermute x8, waiting for transfers between devices, flip_send(): return lax.ppermute(value, ('qx', 'qy'), pairs)  38.8 us
    dot_general x52, matrix products, mixing(): jnp.einsum(form, weight, data, preferred_element_type=jnp.float32)  35.3 us
    ppermute x8, waiting for transfers between devices, flip_send(): return lax.ppermute(value, 'qx', pairs)  32.1 us
    pallas_call x2, Pallas kernels, output_stage(): pl.pallas_call(output_stage_kernel, grid=(part // step,), in_specs=[piece...  19.8 us
    ppermute x8, starting transfers between devices, flip_send(): return lax.ppermute(value, 'qy', pairs)  16.5 us
    ppermute x8, starting transfers between devices, flip_send(): return lax.ppermute(value, ('qx', 'qy'), pairs)  14.9 us
    ppermute x8, waiting for transfers between devices, flip_send(): return lax.ppermute(value, 'qy', pairs)  14 us
    ppermute x8, starting transfers between devices, flip_send(): return lax.ppermute(value, 'qx', pairs)  11 us
  transfers between devices with their start and end apart: 24, of which 10 were waited for; matrix products, arithmetic and copies ran while one was open for 19% of the time, Pallas kernels for 10%

profile of v4, /device:TPU:1, one launch (start us, length us, event | category | flops | bytes accessed | tf_op | source)
XLA Modules:
  0.0 202.5 jit_solution(14984038449845528900)
XLA Ops:
  0.0 5.0 %fusion.185 = (bf16[4,1,32,64,128]{4,3,2,1,0:T(8,128)(2,1)}, bf16[4,1,32,64,128]{4,3,2,1,0:T(8,128)(2,1)S(1)}) fusion(bf16[4,2,32,64,128]{4,3,2,1,0:T(8,128)(2,1)} %bitcast.837), kind=kLoop, calls=%fused_computation.260 | loop fusion | bytes 8388608 | tf_op jit(solution)/shard_map/slice | solution.py:188
  7.1 2.5 %collective-permute-start.12 = (bf16[32,64,128]{2,1,0:T(8,128)(2,1)S(1)}, bf16[32,64,128]{2,1,0:T(8,128)(2,1)}, u32[]{:S(2)}, u32[]{:S(2)}) collective-permute-start(bf16[32,64,128]{2,1,0:T(8,128)(2,1)S(1)} %bitcast.850), channel_id=1, source_target_pairs={{0,1},{1,0},{2,3},{3,2},{4,5},{5,4},{6,7},{7,6},{8,9},{9,8},{10,11... | collective-permute-start | bytes 1572872 | tf_op jit(solution)/shard_map/ppermute | solution.py:57
  36.5 2.1 %fusion.15 = bf16[4,32,64,128]{3,2,1,0:T(8,128)(2,1)S(1)} fusion(bf16[4,4,64,64,1]{2,3,1,4,0:T(8,128)(2,1)S(1)} %copy.151, bf16[1,32,64,128]{3,2,0,1:T(8,128)(2,1)} %bitcast.247, bf16[1,32,64,128]{3,2,0,1:T(8,128)(2,1)} %bitcast.231, bf16[1,32,64,128]{3,2,0,1:T(8,128)(2,1)} %bitcast.215, bf16[1,32,64,128]{3,2,0,1:T(8,128)(2,1)S(1)} %bitcast.854), kind=kOutput, calls=%fused_computation.23 | convolution fusion | flops 546308096 | bytes 4325376 | tf_op jit(solution)/shard_map/scor,cjrl->sjol/dot_general | solution.py:14
  39.6 2.9 %collective-permute-start.15 = (bf16[32,64,128]{2,1,0:T(8,128)(2,1)S(1)}, bf16[32,64,128]{2,1,0:T(8,128)(2,1)}, u32[]{:S(2)}, u32[]{:S(2)}) collective-permute-start(bf16[32,64,128]{2,1,0:T(8,128)(2,1)S(1)} %get-tuple-element.29), channel_id=1, source_target_pairs={{0,4},{1,5},{2,6},{3,7},{4,0},{5,1},{6,2},{7,3},{8,12},{9,13},{10,... | collective-permute-start | bytes 1572872 | tf_op jit(solution)/shard_map/ppermute | solution.py:57
  42.5 3.3 %collective-permute-start.16 = (bf16[32,64,128]{2,1,0:T(8,128)(2,1)S(1)}, bf16[32,64,128]{2,1,0:T(8,128)(2,1)}, u32[]{:S(2)}, u32[]{:S(2)}) collective-permute-start(bf16[32,64,128]{2,1,0:T(8,128)(2,1)S(1)} %get-tuple-element.28), channel_id=1, source_target_pairs={{0,64},{8,72},{16,80},{24,88},{32,96},{40,104},{48,112},{56,120},{... | collective-permute-start | bytes 1572872 | tf_op jit(solution)/shard_map/ppermute | solution.py:54
  45.8 4.2 %collective-permute-start.17 = (bf16[32,64,128]{2,1,0:T(8,128)(2,1)S(1)}, bf16[32,64,128]{2,1,0:T(8,128)(2,1)}, u32[]{:S(2)}, u32[]{:S(2)}) collective-permute-start(bf16[32,64,128]{2,1,0:T(8,128)(2,1)S(1)} %get-tuple-element.27), channel_id=1, source_target_pairs={{0,68},{1,69},{2,70},{3,71},{4,64},{5,65},{6,66},{7,67},{8,76},{9,... | collective-permute-start | bytes 1572872 | tf_op jit(solution)/shard_map/ppermute | solution.py:63
  50.0 17.8 %collective-permute-done.2 = bf16[32,64,128]{2,1,0:T(8,128)(2,1)S(1)} collective-permute-done((bf16[32,64,128]{2,1,0:T(8,128)(2,1)S(1)}, bf16[32,64,128]{2,1,0:T(8,128)(2,1)S(1)}, u32[]{:S(2)}, u32[]{:S(2)}) %collective-permute-start.2) | collective-permute-done | bytes 524320 | tf_op jit(solution)/shard_map/ppermute | solution.py:63
  71.0 2.9 %collective-permute-start.3 = (bf16[32,64,128]{2,1,0:T(8,128)(2,1)}, bf16[32,64,128]{2,1,0:T(8,128)(2,1)}, u32[]{:S(2)}, u32[]{:S(2)}) collective-permute-start(bf16[32,64,128]{2,1,0:T(8,128)(2,1)} %get-tuple-element.37), channel_id=1, source_target_pairs={{0,4},{1,5},{2,6},{3,7},{4,0},{5,1},{6,2},{7,3},{8,12},{9,13},{10,... | collective-permute-start | bytes 1572872 | tf_op jit(solution)/shard_map/ppermute | solution.py:57
  75.1 3.5 %collective-permute-start.4 = (bf16[32,64,128]{2,1,0:T(8,128)(2,1)S(1)}, bf16[32,64,128]{2,1,0:T(8,128)(2,1)}, u32[]{:S(2)}, u32[]{:S(2)}) collective-permute-start(bf16[32,64,128]{2,1,0:T(8,128)(2,1)S(1)} %get-tuple-element.36), channel_id=1, source_target_pairs={{0,64},{8,72},{16,80},{24,88},{32,96},{40,104},{48,112},{56,120},{... | collective-permute-start | bytes 1572872 | tf_op jit(solution)/shard_map/ppermute | solution.py:54
  80.6 9.9 %shard_map.74 = (bf16[32,64,128]{2,1,0:T(8,128)(2,1)}, bf16[32,64,128]{2,1,0:T(8,128)(2,1)}, bf16[32,64,128]{2,1,0:T(8,128)(2,1)}, bf16[32,64,128]{2,1,0:T(8,128)(2,1)}) custom-call(bf16[32,64,128]{2,1,0:T(8,128)(2,1)} %get-tuple-element.30.p0, bf16[32,64,128]{2,1,0:T(8,128)(2,1)} %collective-permute-done.15.p1, ...), custom_call_target="tpu_custom_call" | custom-call | flops 2147483648 | bytes 10485760 | tf_op jit(solution)/shard_map/pallas_call | solution.py:123
  90.5 3.0 %collective-permute-start.18 = (bf16[32,64,128]{2,1,0:T(8,128)(2,1)}, bf16[32,64,128]{2,1,0:T(8,128)(2,1)S(1)}, u32[]{:S(2)}, u32[]{:S(2)}) collective-permute-start(bf16[32,64,128]{2,1,0:T(8,128)(2,1)} %get-tuple-element.18), channel_id=1, source_target_pairs={{0,4},{1,5},{2,6},{3,7},{4,0},{5,1},{6,2},{7,3},{8,12},{9,13},{10,... | collective-permute-start | bytes 1572872 | tf_op jit(solution)/shard_map/ppermute | solution.py:57
  94.3 2.0 %collective-permute-start.20 = (bf16[32,64,128]{2,1,0:T(8,128)(2,1)}, bf16[32,64,128]{2,1,0:T(8,128)(2,1)}, u32[]{:S(2)}, u32[]{:S(2)}) collective-permute-start(bf16[32,64,128]{2,1,0:T(8,128)(2,1)} %get-tuple-element.20), channel_id=1, source_target_pairs={{0,68},{1,69},{2,70},{3,71},{4,64},{5,65},{6,66},{7,67},{8,76},{9,... | collective-permute-start | bytes 1572872 | tf_op jit(solution)/shard_map/ppermute | solution.py:63
  96.3 6.8 %collective-permute-done.4.p2 = bf16[32,64,128]{2,1,0:T(8,128)(2,1)} collective-permute-done((bf16[32,64,128]{2,1,0:T(8,128)(2,1)S(1)}, bf16[32,64,128]{2,1,0:T(8,128)(2,1)}, u32[]{:S(2)}, u32[]{:S(2)}) %collective-permute-start.4) | collective-permute-done | bytes 524320 | tf_op jit(solution)/shard_map/ppermute | solution.py:54
  103.9 9.9 %shard_map.73 = (bf16[32,64,128]{2,1,0:T(8,128)(2,1)}, bf16[32,64,128]{2,1,0:T(8,128)(2,1)}, bf16[32,64,128]{2,1,0:T(8,128)(2,1)}, bf16[32,64,128]{2,1,0:T(8,128)(2,1)}) custom-call(bf16[32,64,128]{2,1,0:T(8,128)(2,1)} %get-tuple-element.38.p0, bf16[32,64,128]{2,1,0:T(8,128)(2,1)} %collective-permute-done.3.p1, ...), custom_call_target="tpu_custom_call" | custom-call | flops 2147483648 | bytes 10485760 | tf_op jit(solution)/shard_map/pallas_call | solution.py:123
  113.8 3.0 %collective-permute-start.6 = (bf16[32,64,128]{2,1,0:T(8,128)(2,1)}, bf16[32,64,128]{2,1,0:T(8,128)(2,1)S(1)}, u32[]{:S(2)}, u32[]{:S(2)}) collective-permute-start(bf16[32,64,128]{2,1,0:T(8,128)(2,1)} %get-tuple-element.14), channel_id=1, source_target_pairs={{0,4},{1,5},{2,6},{3,7},{4,0},{5,1},{6,2},{7,3},{8,12},{9,13},{10,... | collective-permute-start | bytes 1572872 | tf_op jit(solution)/shard_map/ppermute | solution.py:57
  116.8 2.8 %collective-permute-start.8 = (bf16[32,64,128]{2,1,0:T(8,128)(2,1)}, bf16[32,64,128]{2,1,0:T(8,128)(2,1)S(1)}, u32[]{:S(2)}, u32[]{:S(2)}) collective-permute-start(bf16[32,64,128]{2,1,0:T(8,128)(2,1)} %get-tuple-element.16), channel_id=1, source_target_pairs={{0,68},{1,69},{2,70},{3,71},{4,64},{5,65},{6,66},{7,67},{8,76},{9,... | collective-permute-start | bytes 1572872 | tf_op jit(solution)/shard_map/ppermute | solution.py:63
  119.6 5.9 %collective-permute-done.19 = bf16[32,64,128]{2,1,0:T(8,128)(2,1)} collective-permute-done((bf16[32,64,128]{2,1,0:T(8,128)(2,1)}, bf16[32,64,128]{2,1,0:T(8,128)(2,1)}, u32[]{:S(2)}, u32[]{:S(2)}) %collective-permute-start.19) | collective-permute-done | bytes 524320 | tf_op jit(solution)/shard_map/ppermute | solution.py:54
  130.4 17.4 %collective-permute-done.7 = bf16[32,64,128]{2,1,0:T(8,128)(2,1)S(1)} collective-permute-done((bf16[32,64,128]{2,1,0:T(8,128)(2,1)}, bf16[32,64,128]{2,1,0:T(8,128)(2,1)S(1)}, u32[]{:S(2)}, u32[]{:S(2)}) %collective-permute-start.7) | collective-permute-done | bytes 524320 | tf_op jit(solution)/shard_map/ppermute | solution.py:54
  155.4 5.8 %collective-permute-done.9 = bf16[32,64,128]{2,1,0:T(8,128)(2,1)S(1)} collective-permute-done((bf16[32,64,128]{2,1,0:T(8,128)(2,1)S(1)}, bf16[32,64,128]{2,1,0:T(8,128)(2,1)S(1)}, u32[]{:S(2)}, u32[]{:S(2)}) %collective-permute-start.9) | collective-permute-done | bytes 524320 | tf_op jit(solution)/shard_map/ppermute | solution.py:57
  161.2 4.1 %collective-permute-start.23 = (bf16[32,64,128]{2,1,0:T(8,128)(2,1)S(1)}, bf16[32,64,128]{2,1,0:T(8,128)(2,1)S(1)}, u32[]{:S(2)}, u32[]{:S(2)}) collective-permute-start(bf16[32,64,128]{2,1,0:T(8,128)(2,1)S(1)} %get-tuple-element.23), channel_id=1, source_target_pairs={{0,9},{1,8},{2,11},{3,10},{4,13},{5,12},{6,15},{7,14},{8,1},{9,0},... | collective-permute-start | bytes 1572872 | tf_op jit(solution)/shard_map/ppermute | solution.py:63
  166.9 9.5 %collective-permute-done.11 = bf16[32,64,128]{2,1,0:T(8,128)(2,1)S(1)} collective-permute-done((bf16[32,64,128]{2,1,0:T(8,128)(2,1)S(1)}, bf16[32,64,128]{2,1,0:T(8,128)(2,1)S(1)}, u32[]{:S(2)}, u32[]{:S(2)}) %collective-permute-start.11) | collective-permute-done | bytes 524320 | tf_op jit(solution)/shard_map/ppermute | solution.py:63
  177.1 6.6 %collective-permute-done.21 = bf16[32,64,128]{2,1,0:T(8,128)(2,1)S(1)} collective-permute-done((bf16[32,64,128]{2,1,0:T(8,128)(2,1)S(1)}, bf16[32,64,128]{2,1,0:T(8,128)(2,1)S(1)}, u32[]{:S(2)}, u32[]{:S(2)}) %collective-permute-start.21) | collective-permute-done | bytes 524320 | tf_op jit(solution)/shard_map/ppermute | solution.py:57
  185.2 11.5 %collective-permute-done.23 = bf16[32,64,128]{2,1,0:T(8,128)(2,1)S(1)} collective-permute-done((bf16[32,64,128]{2,1,0:T(8,128)(2,1)S(1)}, bf16[32,64,128]{2,1,0:T(8,128)(2,1)S(1)}, u32[]{:S(2)}, u32[]{:S(2)}) %collective-permute-start.23) | collective-permute-done | bytes 524320 | tf_op jit(solution)/shard_map/ppermute | solution.py:63
  200.5 2.0 copy-done.1
  (148 shorter events, 57.1 us)
Async XLA Ops:
  7.1 29.3 %collective-permute-start.12 = (bf16[32,64,128]{2,1,0:T(8,128)(2,1)S(1)}, bf16[32,64,128]{2,1,0:T(8,128)(2,1)}, u32[]{:S(2)}, u32[]{:S(2)}) collective-permute-start(bf16[32,64,128]{2,1,0:T(8,128)(2,1)S(1)} %bitcast.850), channel_id=1, source_target_pairs={{0,1},{1,0},{2,3},{3,2},{4,5},{5,4},{6,7},{7,6},{8,9},{9,8},{10,11... | collective-permute-start | bytes 1572872 | tf_op jit(solution)/shard_map/ppermute | solution.py:57
  13.6 22.9 %collective-permute-start.13 = (bf16[32,64,128]{2,1,0:T(8,128)(2,1)S(1)}, bf16[32,64,128]{2,1,0:T(8,128)(2,1)}, u32[]{:S(2)}, u32[]{:S(2)}) collective-permute-start(bf16[32,64,128]{2,1,0:T(8,128)(2,1)S(1)} %bitcast.851), channel_id=1, source_target_pairs={{0,8},{8,0},{16,24},{24,16},{32,40},{40,32},{48,56},{56,48},{64,72... | collective-permute-start | bytes 1572872 | tf_op jit(solution)/shard_map/ppermute | solution.py:54
  18.6 17.9 %collective-permute-start.14 = (bf16[32,64,128]{2,1,0:T(8,128)(2,1)}, bf16[32,64,128]{2,1,0:T(8,128)(2,1)}, u32[]{:S(2)}, u32[]{:S(2)}) collective-permute-start(bf16[32,64,128]{2,1,0:T(8,128)(2,1)} %bitcast.246), channel_id=1, source_target_pairs={{0,9},{1,8},{2,11},{3,10},{4,13},{5,12},{6,15},{7,14},{8,1},{9,0},... | collective-permute-start | bytes 1572872 | tf_op jit(solution)/shard_map/ppermute | solution.py:63
  20.5 25.4 %collective-permute-start = (bf16[32,64,128]{2,1,0:T(8,128)(2,1)}, bf16[32,64,128]{2,1,0:T(8,128)(2,1)}, u32[]{:S(2)}, u32[]{:S(2)}) collective-permute-start(bf16[32,64,128]{2,1,0:T(8,128)(2,1)} %bitcast.40), channel_id=1, source_target_pairs={{0,1},{1,0},{2,3},{3,2},{4,5},{5,4},{6,7},{7,6},{8,9},{9,8},{10,11... | collective-permute-start | bytes 1572872 | tf_op jit(solution)/shard_map/ppermute | solution.py:57
  23.7 26.3 %collective-permute-start.1 = (bf16[32,64,128]{2,1,0:T(8,128)(2,1)}, bf16[32,64,128]{2,1,0:T(8,128)(2,1)}, u32[]{:S(2)}, u32[]{:S(2)}) collective-permute-start(bf16[32,64,128]{2,1,0:T(8,128)(2,1)} %bitcast.56), channel_id=1, source_target_pairs={{0,8},{8,0},{16,24},{24,16},{32,40},{40,32},{48,56},{56,48},{64,72... | collective-permute-start | bytes 1572872 | tf_op jit(solution)/shard_map/ppermute | solution.py:54
  36.4 31.4 %collective-permute-start.2 = (bf16[32,64,128]{2,1,0:T(8,128)(2,1)S(1)}, bf16[32,64,128]{2,1,0:T(8,128)(2,1)S(1)}, u32[]{:S(2)}, u32[]{:S(2)}) collective-permute-start(bf16[32,64,128]{2,1,0:T(8,128)(2,1)S(1)} %bitcast.853), channel_id=1, source_target_pairs={{0,9},{1,8},{2,11},{3,10},{4,13},{5,12},{6,15},{7,14},{8,1},{9,0},... | collective-permute-start | bytes 1572872 | tf_op jit(solution)/shard_map/ppermute | solution.py:63
  39.6 39.0 %collective-permute-start.15 = (bf16[32,64,128]{2,1,0:T(8,128)(2,1)S(1)}, bf16[32,64,128]{2,1,0:T(8,128)(2,1)}, u32[]{:S(2)}, u32[]{:S(2)}) collective-permute-start(bf16[32,64,128]{2,1,0:T(8,128)(2,1)S(1)} %get-tuple-element.29), channel_id=1, source_target_pairs={{0,4},{1,5},{2,6},{3,7},{4,0},{5,1},{6,2},{7,3},{8,12},{9,13},{10,... | collective-permute-start | bytes 1572872 | tf_op jit(solution)/shard_map/ppermute | solution.py:57
  42.5 38.1 %collective-permute-start.16 = (bf16[32,64,128]{2,1,0:T(8,128)(2,1)S(1)}, bf16[32,64,128]{2,1,0:T(8,128)(2,1)}, u32[]{:S(2)}, u32[]{:S(2)}) collective-permute-start(bf16[32,64,128]{2,1,0:T(8,128)(2,1)S(1)} %get-tuple-element.28), channel_id=1, source_target_pairs={{0,64},{8,72},{16,80},{24,88},{32,96},{40,104},{48,112},{56,120},{... | collective-permute-start | bytes 1572872 | tf_op jit(solution)/shard_map/ppermute | solution.py:54
  45.8 34.8 %collective-permute-start.17 = (bf16[32,64,128]{2,1,0:T(8,128)(2,1)S(1)}, bf16[32,64,128]{2,1,0:T(8,128)(2,1)}, u32[]{:S(2)}, u32[]{:S(2)}) collective-permute-start(bf16[32,64,128]{2,1,0:T(8,128)(2,1)S(1)} %get-tuple-element.27), channel_id=1, source_target_pairs={{0,68},{1,69},{2,70},{3,71},{4,64},{5,65},{6,66},{7,67},{8,76},{9,... | collective-permute-start | bytes 1572872 | tf_op jit(solution)/shard_map/ppermute | solution.py:63
  71.0 23.3 %collective-permute-start.3 = (bf16[32,64,128]{2,1,0:T(8,128)(2,1)}, bf16[32,64,128]{2,1,0:T(8,128)(2,1)}, u32[]{:S(2)}, u32[]{:S(2)}) collective-permute-start(bf16[32,64,128]{2,1,0:T(8,128)(2,1)} %get-tuple-element.37), channel_id=1, source_target_pairs={{0,4},{1,5},{2,6},{3,7},{4,0},{5,1},{6,2},{7,3},{8,12},{9,13},{10,... | collective-permute-start | bytes 1572872 | tf_op jit(solution)/shard_map/ppermute | solution.py:57
  75.1 28.0 %collective-permute-start.4 = (bf16[32,64,128]{2,1,0:T(8,128)(2,1)S(1)}, bf16[32,64,128]{2,1,0:T(8,128)(2,1)}, u32[]{:S(2)}, u32[]{:S(2)}) collective-permute-start(bf16[32,64,128]{2,1,0:T(8,128)(2,1)S(1)} %get-tuple-element.36), channel_id=1, source_target_pairs={{0,64},{8,72},{16,80},{24,88},{32,96},{40,104},{48,112},{56,120},{... | collective-permute-start | bytes 1572872 | tf_op jit(solution)/shard_map/ppermute | solution.py:54
  78.6 24.4 %collective-permute-start.5 = (bf16[32,64,128]{2,1,0:T(8,128)(2,1)S(1)}, bf16[32,64,128]{2,1,0:T(8,128)(2,1)S(1)}, u32[]{:S(2)}, u32[]{:S(2)}) collective-permute-start(bf16[32,64,128]{2,1,0:T(8,128)(2,1)S(1)} %get-tuple-element.35), channel_id=1, source_target_pairs={{0,68},{1,69},{2,70},{3,71},{4,64},{5,65},{6,66},{7,67},{8,76},{9,... | collective-permute-start | bytes 1572872 | tf_op jit(solution)/shard_map/ppermute | solution.py:63
  90.5 26.4 %collective-permute-start.18 = (bf16[32,64,128]{2,1,0:T(8,128)(2,1)}, bf16[32,64,128]{2,1,0:T(8,128)(2,1)S(1)}, u32[]{:S(2)}, u32[]{:S(2)}) collective-permute-start(bf16[32,64,128]{2,1,0:T(8,128)(2,1)} %get-tuple-element.18), channel_id=1, source_target_pairs={{0,4},{1,5},{2,6},{3,7},{4,0},{5,1},{6,2},{7,3},{8,12},{9,13},{10,... | collective-permute-start | bytes 1572872 | tf_op jit(solution)/shard_map/ppermute | solution.py:57
  93.5 32.0 %collective-permute-start.19 = (bf16[32,64,128]{2,1,0:T(8,128)(2,1)}, bf16[32,64,128]{2,1,0:T(8,128)(2,1)}, u32[]{:S(2)}, u32[]{:S(2)}) collective-permute-start(bf16[32,64,128]{2,1,0:T(8,128)(2,1)} %get-tuple-element.19), channel_id=1, source_target_pairs={{0,64},{8,72},{16,80},{24,88},{32,96},{40,104},{48,112},{56,120},{... | collective-permute-start | bytes 1572872 | tf_op jit(solution)/shard_map/ppermute | solution.py:54
  94.3 31.3 %collective-permute-start.20 = (bf16[32,64,128]{2,1,0:T(8,128)(2,1)}, bf16[32,64,128]{2,1,0:T(8,128)(2,1)}, u32[]{:S(2)}, u32[]{:S(2)}) collective-permute-start(bf16[32,64,128]{2,1,0:T(8,128)(2,1)} %get-tuple-element.20), channel_id=1, source_target_pairs={{0,68},{1,69},{2,70},{3,71},{4,64},{5,65},{6,66},{7,67},{8,76},{9,... | collective-permute-start | bytes 1572872 | tf_op jit(solution)/shard_map/ppermute | solution.py:63
  113.8 16.6 %collective-permute-start.6 = (bf16[32,64,128]{2,1,0:T(8,128)(2,1)}, bf16[32,64,128]{2,1,0:T(8,128)(2,1)S(1)}, u32[]{:S(2)}, u32[]{:S(2)}) collective-permute-start(bf16[32,64,128]{2,1,0:T(8,128)(2,1)} %get-tuple-element.14), channel_id=1, source_target_pairs={{0,4},{1,5},{2,6},{3,7},{4,0},{5,1},{6,2},{7,3},{8,12},{9,13},{10,... | collective-permute-start | bytes 1572872 | tf_op jit(solution)/shard_map/ppermute | solution.py:57
  116.8 31.1 %collective-permute-start.7 = (bf16[32,64,128]{2,1,0:T(8,128)(2,1)}, bf16[32,64,128]{2,1,0:T(8,128)(2,1)S(1)}, u32[]{:S(2)}, u32[]{:S(2)}) collective-permute-start(bf16[32,64,128]{2,1,0:T(8,128)(2,1)} %get-tuple-element.15), channel_id=1, source_target_pairs={{0,64},{8,72},{16,80},{24,88},{32,96},{40,104},{48,112},{56,120},{... | collective-permute-start | bytes 1572872 | tf_op jit(solution)/shard_map/ppermute | solution.py:54
  116.8 31.1 %collective-permute-start.8 = (bf16[32,64,128]{2,1,0:T(8,128)(2,1)}, bf16[32,64,128]{2,1,0:T(8,128)(2,1)S(1)}, u32[]{:S(2)}, u32[]{:S(2)}) collective-permute-start(bf16[32,64,128]{2,1,0:T(8,128)(2,1)} %get-tuple-element.16), channel_id=1, source_target_pairs={{0,68},{1,69},{2,70},{3,71},{4,64},{5,65},{6,66},{7,67},{8,76},{9,... | collective-permute-start | bytes 1572872 | tf_op jit(solution)/shard_map/ppermute | solution.py:63
  149.3 11.9 %collective-permute-start.9 = (bf16[32,64,128]{2,1,0:T(8,128)(2,1)S(1)}, bf16[32,64,128]{2,1,0:T(8,128)(2,1)S(1)}, u32[]{:S(2)}, u32[]{:S(2)}) collective-permute-start(bf16[32,64,128]{2,1,0:T(8,128)(2,1)S(1)} %get-tuple-element.33), channel_id=1, source_target_pairs={{0,1},{1,0},{2,3},{3,2},{4,5},{5,4},{6,7},{7,6},{8,9},{9,8},{10,11... | collective-permute-start | bytes 1572872 | tf_op jit(solution)/shard_map/ppermute | solution.py:57
  150.2 15.4 %collective-permute-start.10 = (bf16[32,64,128]{2,1,0:T(8,128)(2,1)S(1)}, bf16[32,64,128]{2,1,0:T(8,128)(2,1)S(1)}, u32[]{:S(2)}, u32[]{:S(2)}) collective-permute-start(bf16[32,64,128]{2,1,0:T(8,128)(2,1)S(1)} %get-tuple-element.32), channel_id=1, source_target_pairs={{0,8},{8,0},{16,24},{24,16},{32,40},{40,32},{48,56},{56,48},{64,72... | collective-permute-start | bytes 1572872 | tf_op jit(solution)/shard_map/ppermute | solution.py:54
  151.4 25.0 %collective-permute-start.11 = (bf16[32,64,128]{2,1,0:T(8,128)(2,1)S(1)}, bf16[32,64,128]{2,1,0:T(8,128)(2,1)S(1)}, u32[]{:S(2)}, u32[]{:S(2)}) collective-permute-start(bf16[32,64,128]{2,1,0:T(8,128)(2,1)S(1)} %get-tuple-element.31), channel_id=1, source_target_pairs={{0,9},{1,8},{2,11},{3,10},{4,13},{5,12},{6,15},{7,14},{8,1},{9,0},... | collective-permute-start | bytes 1572872 | tf_op jit(solution)/shard_map/ppermute | solution.py:63
  153.1 30.6 %collective-permute-start.21 = (bf16[32,64,128]{2,1,0:T(8,128)(2,1)S(1)}, bf16[32,64,128]{2,1,0:T(8,128)(2,1)S(1)}, u32[]{:S(2)}, u32[]{:S(2)}) collective-permute-start(bf16[32,64,128]{2,1,0:T(8,128)(2,1)S(1)} %get-tuple-element.25), channel_id=1, source_target_pairs={{0,1},{1,0},{2,3},{3,2},{4,5},{5,4},{6,7},{7,6},{8,9},{9,8},{10,11... | collective-permute-start | bytes 1572872 | tf_op jit(solution)/shard_map/ppermute | solution.py:57
  153.1 30.9 %collective-permute-start.22 = (bf16[32,64,128]{2,1,0:T(8,128)(2,1)S(1)}, bf16[32,64,128]{2,1,0:T(8,128)(2,1)S(1)}, u32[]{:S(2)}, u32[]{:S(2)}) collective-permute-start(bf16[32,64,128]{2,1,0:T(8,128)(2,1)S(1)} %get-tuple-element.24), channel_id=1, source_target_pairs={{0,8},{8,0},{16,24},{24,16},{32,40},{40,32},{48,56},{56,48},{64,72... | collective-permute-start | bytes 1572872 | tf_op jit(solution)/shard_map/ppermute | solution.py:54
  161.2 35.5 %collective-permute-start.23 = (bf16[32,64,128]{2,1,0:T(8,128)(2,1)S(1)}, bf16[32,64,128]{2,1,0:T(8,128)(2,1)S(1)}, u32[]{:S(2)}, u32[]{:S(2)}) collective-permute-start(bf16[32,64,128]{2,1,0:T(8,128)(2,1)S(1)} %get-tuple-element.23), channel_id=1, source_target_pairs={{0,9},{1,8},{2,11},{3,10},{4,13},{5,12},{6,15},{7,14},{8,1},{9,0},... | collective-permute-start | bytes 1572872 | tf_op jit(solution)/shard_map/ppermute | solution.py:63
  (16 other events, 83.6 us)

commit v5 on v4

--- a/solution.py
+++ b/solution.py
@@ -1,3 +1,4 @@
+import functools
 import math
 
 import jax
@@ -111,6 +112,55 @@
             terms[f][j] = out[f * size:(f + 1) * size, j * lanes:(j + 1) * lanes]
 
 
+def chain_stage(cur, matrix, sets):
+    size = cur[0].shape[0]
+    lanes = cur[0].shape[1]
+    wide = jnp.concatenate(
+        [jnp.concatenate([cur[g] for g in group], axis=0) for group in sets], axis=1
+    )
+    mixed = jnp.dot(matrix, wide, preferred_element_type=jnp.float32).astype(jnp.bfloat16)
+    out = list(cur)
+    for b, group in enumerate(sets):
+        for c, g in enumerate(group):
+            out[g] = mixed[c * size:(c + 1) * size, b * lanes:(b + 1) * lanes]
+    return out
+
+
+def chain_sets(count, stride):
+    return [
+        [a * 4 * stride + c * stride + e for c in range(4)]
+        for a in range(count // (4 * stride))
+        for e in range(stride)
+    ]
+
+
+def chain_kernel(plan, k_ref, x_ref, m_ref, *rest):
+    o_ref = rest[-1]
+    cur = [x_ref[g] for g in range(x_ref.shape[0])]
+    for index, sets in enumerate(plan):
+        cur = chain_stage(cur, m_ref[index], sets)
+    for g in range(len(cur)):
+        o_ref[g] = cur[g]
+
+
+def chain_call(plan, k0, data, mats, data_spec, out_shape, out_spec, target=None):
+    in_specs = [data_spec, pl.BlockSpec(mats.shape, lambda i, k: (0, 0, 0))]
+    operands = [k0, data, mats]
+    aliases = {}
+    if target is not None:
+        in_specs.append(pl.BlockSpec(memory_space=pl.ANY))
+        operands.append(target)
+        aliases = {3: 0}
+    return pl.pallas_call(
+        functools.partial(chain_kernel, plan),
+        grid_spec=pltpu.PrefetchScalarGridSpec(
+            num_scalar_prefetch=1, grid=(1,), in_specs=in_specs, out_specs=out_spec
+        ),
+        out_shape=out_shape,
+        input_output_aliases=aliases,
+    )(*operands)
+
+
 def output_stage(pieces, wave, obs, chunk, w_mat, w_t, o_mat, o_t, step=8):
     part, rank_size, inner_boxes = pieces[0].shape
     piece_spec = pl.BlockSpec((step, rank_size, inner_boxes), lambda i: (i, 0, 0))
@@ -154,8 +204,7 @@
     w1 = xor_order(merges[1], 1, *bits[1])
     w1_mat = jnp.transpose(w1, (0, 2, 1, 3)).reshape(4 * rank_size, 4 * rank_size)
     w1_t = w1_mat.T
-    eye = jnp.eye(4, dtype=output_weight.dtype)
-    ow_mat = jnp.einsum("st,or->sotr", eye, output_weight).reshape(4 * rank_size, 4 * rank_size)
+    ow_mat = jnp.einsum("st,or->sotr", jnp.eye(4, dtype=output_weight.dtype), output_weight).reshape(4 * rank_size, 4 * rank_size)
     ow_t = ow_mat.T
 
     shape5 = (4, CHUNKS, part, rank_size, inner_boxes)
@@ -164,32 +213,48 @@
     wave = phases[0, 0].reshape(shape5)
     k0 = 2 * bits[0][0] + bits[0][1]
 
-    def local_forward(tiles):
-        cur = mixing(interpolate, tiles, "op,jpl->jol")
-        for i in range(local_depth):
-            b = 4**i
-            blk = cur.reshape(part // (4 * b), 4, b, rank_size, inner_boxes)
-            cur = mixing(levels[i], blk, "kcor,acerl->akeol").reshape(
-                part, rank_size, inner_boxes
-            )
-        return cur
-
-    def local_adjoint(cur):
-        for i in reversed(range(local_depth)):
-            b = 4**i
-            blk = cur.reshape(part // (4 * b), 4, b, rank_size, inner_boxes)
-            cur = mixing(levels[i], blk, "kcor,akeol->acerl").reshape(
-                part, rank_size, inner_boxes
-            )
-        return mixing(interpolate, cur, "op,jol->jpl")
+    eye = jnp.eye(4, dtype=interpolate.dtype)
+    spread = jnp.einsum("st,op->sotp", eye, interpolate).reshape(4 * rank_size, 4 * rank_size)
+    forward_levels = [
+        jnp.transpose(levels[i], (0, 2, 1, 3)).reshape(4 * rank_size, 4 * rank_size)
+        for i in range(local_depth)
+    ]
+    forward_mats = jnp.stack([spread] + forward_levels)
+    adjoint_mats = jnp.stack([w.T for w in reversed(forward_levels)] + [spread.T])
+    forward_plan = [chain_sets(part, 1)] + [chain_sets(part, 4**i) for i in range(local_depth)]
+    adjoint_plan = [chain_sets(part, 4**i) for i in reversed(range(local_depth))] + [
+        chain_sets(part, 1)
+    ]
+    k0_ref = jnp.reshape(k0, (1,)).astype(jnp.int32)
+    piece_shape = jax.ShapeDtypeStruct((part, rank_size, inner_boxes), jnp.bfloat16)
+    whole_piece = pl.BlockSpec((part, rank_size, inner_boxes), lambda i, k: (0, 0, 0))
+
+    def in_place(m, f):
+        return pl.BlockSpec(
+            (None, None, part, rank_size, inner_boxes),
+            lambda i, k: (jnp.bitwise_xor(k[0], f), m, 0, 0, 0),
+        )
+
+    def local_forward(m, f):
+        return chain_call(
+            forward_plan, k0_ref, image, forward_mats, in_place(m, f), piece_shape, whole_piece
+        )
+
+    def local_adjoint(gradient, piece, m, f):
+        return chain_call(
+            adjoint_plan,
+            k0_ref,
+            piece,
+            adjoint_mats,
+            whole_piece,
+            jax.ShapeDtypeStruct(shape5, jnp.bfloat16),
+            in_place(m, f),
+            target=gradient,
+        )
 
     gradient = jnp.zeros(shape5, jnp.bfloat16)
     for m in range(CHUNKS):
-        chunk = image[:, m]
-        coef = [
-            local_forward(lax.dynamic_index_in_dim(chunk, k0 ^ f, 0, keepdims=False))
-            for f in range(4)
-        ]
+        coef = [local_forward(m, f) for f in range(4)]
         pieces = exchange(coef, *shifts[0])
         cur = mixing(w0, jnp.stack(pieces), "scor,cjrl->sjol")
         pieces = exchange(cur, *shifts[1])
@@ -198,10 +263,7 @@
         terms = mixing(w0, jnp.stack(back), "scor,sjol->cjrl")
         back = exchange(terms, *shifts[0])
         for f in range(4):
-            piece = local_adjoint(back[f])
-            gradient = lax.dynamic_update_slice(
-                gradient, piece[None, None], (k0 ^ f, m, 0, 0, 0)
-            )
+            gradient = local_adjoint(gradient, back[f], m, f)
     return gradient.reshape(groups, rank_size, inner_boxes)[None, None]
 
 

time: 203 us -> 195 us (0.961)
  Pallas kernels: 19.8 us -> 62.7 us
  waiting for transfers between devices: 84.9 us -> 50.7 us
  matrix products: 35.3 us -> 6.8 us
  starting transfers between devices: 42.3 us -> 53.6 us
    pallas_call x0 -> x16, Pallas kernels: none -> 42.9 us  [chain_call(): pl.pallas_call(functools.partial(chain_kernel, plan), grid_spec=pltpu.Pre...]
    ppermute x8, waiting for transfers between devices: 38.8 us -> 6.05 us  [flip_send(): return lax.ppermute(value, ('qx', 'qy'), pairs)]
    dot_general x52 -> x4, matrix products: 35.3 us -> 6.8 us  [mixing(): jnp.einsum(form, weight, data, preferred_element_type=jnp.float32)]
    ppermute x8, starting transfers between devices: 14.9 us -> 23 us  [flip_send(): return lax.ppermute(value, ('qx', 'qy'), pairs)]
    ppermute x8, starting transfers between devices: 11 us -> 16.3 us  [flip_send(): return lax.ppermute(value, 'qx', pairs)]
    slice x1 -> x0, local copies, waits for them, and re-layouts: 5.02 us -> none  [local(): chunk = image[:, m]]
    ppermute x8, waiting for transfers between devices: 32.1 us -> 28.8 us  [flip_send(): return lax.ppermute(value, 'qx', pairs)]
    convert_element_type x16 -> x0, local copies, waits for them, and re-layouts: 3.04 us -> none  [mixing(): jnp.einsum(form, weight, data, preferred_element_type=jnp.float32)]
  transfers between devices with their start and end apart: 24 -> 24, of which waited for: 10 -> 9; matrix products, arithmetic and copies ran while one was open for 19% -> 10% of each run, Pallas kernels for 10% -> 30%
where the time goes in v5:
time: 195 us; the launch traced here: 194 us
  Pallas kernels  62.7 us (32%)
  starting transfers between devices  53.6 us (27%)
  waiting for transfers between devices  50.7 us (26%)
  local copies, waits for them, and re-layouts  17.7 us (9%)
  matrix products  6.8 us (3%)
  other arithmetic  2.27 us (1%)
    pallas_call x16, Pallas kernels, chain_call(): pl.pallas_call(functools.partial(chain_kernel, plan), grid_spec=pltpu.Pre...  42.9 us
    ppermute x8, waiting for transfers between devices, flip_send(): return lax.ppermute(value, 'qx', pairs)  28.8 us
    ppermute x8, starting transfers between devices, flip_send(): return lax.ppermute(value, ('qx', 'qy'), pairs)  23 us
    pallas_call x2, Pallas kernels, output_stage(): pl.pallas_call(output_stage_kernel, grid=(part // step,), in_specs=[piece...  19.9 us
    ppermute x8, starting transfers between devices, flip_send(): return lax.ppermute(value, 'qx', pairs)  16.3 us
    ppermute x8, waiting for transfers between devices, flip_send(): return lax.ppermute(value, 'qy', pairs)  15.8 us
    ppermute x8, starting transfers between devices, flip_send(): return lax.ppermute(value, 'qy', pairs)  14.3 us
    dot_general x4, matrix products, mixing(): jnp.einsum(form, weight, data, preferred_element_type=jnp.float32)  6.8 us
  transfers between devices with their start and end apart: 24, of which 9 were waited for; matrix products, arithmetic and copies ran while one was open for 10% of the time, Pallas kernels for 30%

profile of v5, /device:TPU:1, one launch (start us, length us, event | category | flops | bytes accessed | tf_op | source)
XLA Modules:
  0.0 194.1 jit_solution(4825279951947929879)
XLA Ops:
  12.4 2.7 %shard_map.81 = bf16[32,64,128]{2,1,0:T(8,128)(2,1)} custom-call(s32[1]{0:T(128)} %bitcast.k_ref, bf16[4,2,32,64,128]{4,3,2,1,0:T(8,128)(2,1)} %bitcast.167, bf16[3,256,256]{2,1,0:T(8,128)(2,1)} %pad_maximum_fusion.4.m_ref), custom_call_target="tpu_custom_call" | custom-call | tf_op jit(solution)/shard_map/pallas_call | solution.py:154
  19.6 2.7 %shard_map.74 = bf16[32,64,128]{2,1,0:T(8,128)(2,1)} custom-call(s32[1]{0:T(128)} %bitcast.k_ref, bf16[4,2,32,64,128]{4,3,2,1,0:T(8,128)(2,1)} %bitcast.169, bf16[3,256,256]{2,1,0:T(8,128)(2,1)} %pad_maximum_fusion.4.m_ref), custom_call_target="tpu_custom_call" | custom-call | tf_op jit(solution)/shard_map/pallas_call | solution.py:154
  22.5 2.7 %shard_map.78 = bf16[32,64,128]{2,1,0:T(8,128)(2,1)} custom-call(s32[1]{0:T(128)} %bitcast.k_ref, bf16[4,2,32,64,128]{4,3,2,1,0:T(8,128)(2,1)} %bitcast.170, bf16[3,256,256]{2,1,0:T(8,128)(2,1)} %pad_maximum_fusion.4.m_ref), custom_call_target="tpu_custom_call" | custom-call | tf_op jit(solution)/shard_map/pallas_call | solution.py:154
  37.0 3.0 %collective-permute-start.15 = (bf16[32,64,128]{2,1,0:T(8,128)(2,1)}, bf16[32,64,128]{2,1,0:T(8,128)(2,1)}, u32[]{:S(2)}, u32[]{:S(2)}) collective-permute-start(bf16[32,64,128]{2,1,0:T(8,128)(2,1)} %get-tuple-element.27), channel_id=1, source_target_pairs={{0,4},{1,5},{2,6},{3,7},{4,0},{5,1},{6,2},{7,3},{8,12},{9,13},{10,... | collective-permute-start | bytes 1572872 | tf_op jit(solution)/shard_map/ppermute | solution.py:58
  40.0 3.6 %collective-permute-start.16 = (bf16[32,64,128]{2,1,0:T(8,128)(2,1)}, bf16[32,64,128]{2,1,0:T(8,128)(2,1)}, u32[]{:S(2)}, u32[]{:S(2)}) collective-permute-start(bf16[32,64,128]{2,1,0:T(8,128)(2,1)} %get-tuple-element.26), channel_id=1, source_target_pairs={{0,64},{8,72},{16,80},{24,88},{32,96},{40,104},{48,112},{56,120},{... | collective-permute-start | bytes 1572872 | tf_op jit(solution)/shard_map/ppermute | solution.py:55
  44.9 6.3 %collective-permute-start.17 = (bf16[32,64,128]{2,1,0:T(8,128)(2,1)S(1)}, bf16[32,64,128]{2,1,0:T(8,128)(2,1)}, u32[]{:S(2)}, u32[]{:S(2)}) collective-permute-start(bf16[32,64,128]{2,1,0:T(8,128)(2,1)S(1)} %get-tuple-element.25), channel_id=1, source_target_pairs={{0,68},{1,69},{2,70},{3,71},{4,64},{5,65},{6,66},{7,67},{8,76},{9,... | collective-permute-start | bytes 1572872 | tf_op jit(solution)/shard_map/ppermute | solution.py:64
  51.2 14.4 %collective-permute-done = bf16[32,64,128]{2,1,0:T(8,128)(2,1)} collective-permute-done((bf16[32,64,128]{2,1,0:T(8,128)(2,1)}, bf16[32,64,128]{2,1,0:T(8,128)(2,1)}, u32[]{:S(2)}, u32[]{:S(2)}) %collective-permute-start) | collective-permute-done | bytes 524320 | tf_op jit(solution)/shard_map/ppermute | solution.py:58
  68.8 2.8 %collective-permute-start.3 = (bf16[32,64,128]{2,1,0:T(8,128)(2,1)}, bf16[32,64,128]{2,1,0:T(8,128)(2,1)}, u32[]{:S(2)}, u32[]{:S(2)}) collective-permute-start(bf16[32,64,128]{2,1,0:T(8,128)(2,1)} %get-tuple-element.35), channel_id=1, source_target_pairs={{0,4},{1,5},{2,6},{3,7},{4,0},{5,1},{6,2},{7,3},{8,12},{9,13},{10,... | collective-permute-start | bytes 1572872 | tf_op jit(solution)/shard_map/ppermute | solution.py:58
  73.8 3.2 %collective-permute-start.4 = (bf16[32,64,128]{2,1,0:T(8,128)(2,1)}, bf16[32,64,128]{2,1,0:T(8,128)(2,1)S(1)}, u32[]{:S(2)}, u32[]{:S(2)}) collective-permute-start(bf16[32,64,128]{2,1,0:T(8,128)(2,1)} %get-tuple-element.34), channel_id=1, source_target_pairs={{0,64},{8,72},{16,80},{24,88},{32,96},{40,104},{48,112},{56,120},{... | collective-permute-start | bytes 1572872 | tf_op jit(solution)/shard_map/ppermute | solution.py:55
  77.1 2.8 %collective-permute-done.16.p2 = bf16[32,64,128]{2,1,0:T(8,128)(2,1)} collective-permute-done((bf16[32,64,128]{2,1,0:T(8,128)(2,1)}, bf16[32,64,128]{2,1,0:T(8,128)(2,1)}, u32[]{:S(2)}, u32[]{:S(2)}) %collective-permute-start.16) | collective-permute-done | bytes 524320 | tf_op jit(solution)/shard_map/ppermute | solution.py:55
  79.9 9.9 %shard_map.82 = (bf16[32,64,128]{2,1,0:T(8,128)(2,1)}, bf16[32,64,128]{2,1,0:T(8,128)(2,1)}, bf16[32,64,128]{2,1,0:T(8,128)(2,1)}, bf16[32,64,128]{2,1,0:T(8,128)(2,1)}) custom-call(bf16[32,64,128]{2,1,0:T(8,128)(2,1)} %get-tuple-element.28.p0, bf16[32,64,128]{2,1,0:T(8,128)(2,1)} %collective-permute-done.15.p1, ...), custom_call_target="tpu_custom_call" | custom-call | flops 2147483648 | bytes 10485760 | tf_op jit(solution)/shard_map/pallas_call | solution.py:173
  89.8 3.0 %collective-permute-start.18 = (bf16[32,64,128]{2,1,0:T(8,128)(2,1)}, bf16[32,64,128]{2,1,0:T(8,128)(2,1)S(1)}, u32[]{:S(2)}, u32[]{:S(2)}) collective-permute-start(bf16[32,64,128]{2,1,0:T(8,128)(2,1)} %get-tuple-element.18), channel_id=1, source_target_pairs={{0,4},{1,5},{2,6},{3,7},{4,0},{5,1},{6,2},{7,3},{8,12},{9,13},{10,... | collective-permute-start | bytes 1572872 | tf_op jit(solution)/shard_map/ppermute | solution.py:58
  92.8 2.8 %collective-permute-start.20 = (bf16[32,64,128]{2,1,0:T(8,128)(2,1)}, bf16[32,64,128]{2,1,0:T(8,128)(2,1)}, u32[]{:S(2)}, u32[]{:S(2)}) collective-permute-start(bf16[32,64,128]{2,1,0:T(8,128)(2,1)} %get-tuple-element.20), channel_id=1, source_target_pairs={{0,68},{1,69},{2,70},{3,71},{4,64},{5,65},{6,66},{7,67},{8,76},{9,... | collective-permute-start | bytes 1572872 | tf_op jit(solution)/shard_map/ppermute | solution.py:64
  95.6 6.6 %collective-permute-done.4.p2 = bf16[32,64,128]{2,1,0:T(8,128)(2,1)S(1)} collective-permute-done((bf16[32,64,128]{2,1,0:T(8,128)(2,1)}, bf16[32,64,128]{2,1,0:T(8,128)(2,1)S(1)}, u32[]{:S(2)}, u32[]{:S(2)}) %collective-permute-start.4) | collective-permute-done | bytes 524320 | tf_op jit(solution)/shard_map/ppermute | solution.py:55
  103.0 9.9 %shard_map.77 = (bf16[32,64,128]{2,1,0:T(8,128)(2,1)}, bf16[32,64,128]{2,1,0:T(8,128)(2,1)}, bf16[32,64,128]{2,1,0:T(8,128)(2,1)}, bf16[32,64,128]{2,1,0:T(8,128)(2,1)}) custom-call(bf16[32,64,128]{2,1,0:T(8,128)(2,1)} %get-tuple-element.36.p0, bf16[32,64,128]{2,1,0:T(8,128)(2,1)} %collective-permute-done.3.p1, bf16[32,64,128]{2,1,0:T(8,128)(2,1)} %copy-done.10, ...), custom_call_target="tpu_custom_call" | custom-call | flops 2147483648 | bytes 10485760 | tf_op jit(solution)/shard_map/pallas_call | solution.py:173
  113.0 3.0 %collective-permute-start.6 = (bf16[32,64,128]{2,1,0:T(8,128)(2,1)}, bf16[32,64,128]{2,1,0:T(8,128)(2,1)S(1)}, u32[]{:S(2)}, u32[]{:S(2)}) collective-permute-start(bf16[32,64,128]{2,1,0:T(8,128)(2,1)} %get-tuple-element.14), channel_id=1, source_target_pairs={{0,4},{1,5},{2,6},{3,7},{4,0},{5,1},{6,2},{7,3},{8,12},{9,13},{10,... | collective-permute-start | bytes 1572872 | tf_op jit(solution)/shard_map/ppermute | solution.py:58
  116.0 2.8 %collective-permute-start.8 = (bf16[32,64,128]{2,1,0:T(8,128)(2,1)}, bf16[32,64,128]{2,1,0:T(8,128)(2,1)S(1)}, u32[]{:S(2)}, u32[]{:S(2)}) collective-permute-start(bf16[32,64,128]{2,1,0:T(8,128)(2,1)} %get-tuple-element.16), channel_id=1, source_target_pairs={{0,68},{1,69},{2,70},{3,71},{4,64},{5,65},{6,66},{7,67},{8,76},{9,... | collective-permute-start | bytes 1572872 | tf_op jit(solution)/shard_map/ppermute | solution.py:64
  118.7 6.1 %collective-permute-done.19 = bf16[32,64,128]{2,1,0:T(8,128)(2,1)} collective-permute-done((bf16[32,64,128]{2,1,0:T(8,128)(2,1)}, bf16[32,64,128]{2,1,0:T(8,128)(2,1)}, u32[]{:S(2)}, u32[]{:S(2)}) %collective-permute-start.19) | collective-permute-done | bytes 524320 | tf_op jit(solution)/shard_map/ppermute | solution.py:55
  128.0 4.0 %collective-permute-start.22 = (bf16[32,64,128]{2,1,0:T(8,128)(2,1)}, bf16[32,64,128]{2,1,0:T(8,128)(2,1)S(1)}, u32[]{:S(2)}, u32[]{:S(2)}) collective-permute-start(bf16[32,64,128]{2,1,0:T(8,128)(2,1)} %get-tuple-element.23), channel_id=1, source_target_pairs={{0,8},{8,0},{16,24},{24,16},{32,40},{40,32},{48,56},{56,48},{64,72... | collective-permute-start | bytes 1572872 | tf_op jit(solution)/shard_map/ppermute | solution.py:55
  133.8 13.3 %collective-permute-done.7 = bf16[32,64,128]{2,1,0:T(8,128)(2,1)S(1)} collective-permute-done((bf16[32,64,128]{2,1,0:T(8,128)(2,1)}, bf16[32,64,128]{2,1,0:T(8,128)(2,1)S(1)}, u32[]{:S(2)}, u32[]{:S(2)}) %collective-permute-start.7) | collective-permute-done | bytes 524320 | tf_op jit(solution)/shard_map/ppermute | solution.py:55
  149.3 4.0 %collective-permute-start.10 = (bf16[32,64,128]{2,1,0:T(8,128)(2,1)}, bf16[32,64,128]{2,1,0:T(8,128)(2,1)S(1)}, u32[]{:S(2)}, u32[]{:S(2)}) collective-permute-start(bf16[32,64,128]{2,1,0:T(8,128)(2,1)} %get-tuple-element.31), channel_id=1, source_target_pairs={{0,8},{8,0},{16,24},{24,16},{32,40},{40,32},{48,56},{56,48},{64,72... | collective-permute-start | bytes 1572872 | tf_op jit(solution)/shard_map/ppermute | solution.py:55
  154.7 7.5 %collective-permute-start.9 = (bf16[32,64,128]{2,1,0:T(8,128)(2,1)}, bf16[32,64,128]{2,1,0:T(8,128)(2,1)}, u32[]{:S(2)}, u32[]{:S(2)}) collective-permute-start(bf16[32,64,128]{2,1,0:T(8,128)(2,1)} %get-tuple-element.32), channel_id=1, source_target_pairs={{0,9},{1,8},{2,11},{3,10},{4,13},{5,12},{6,15},{7,14},{8,1},{9,0},... | collective-permute-start | bytes 1572872 | tf_op jit(solution)/shard_map/ppermute | solution.py:64
  164.0 3.1 %broadcast_in_dim.3.rest_0_ = bf16[4,2,32,64,128]{4,3,2,1,0:T(8,128)(2,1)} broadcast(bf16[]{:T(256)} %constant.18.clone.1), dimensions={} | broadcast | bytes 4194306 | tf_op jit(solution)/shard_map/broadcast_in_dim | solution.py:255
  188.2 3.2 %collective-permute-done.9.x_ref = bf16[32,64,128]{2,1,0:T(8,128)(2,1)} collective-permute-done((bf16[32,64,128]{2,1,0:T(8,128)(2,1)}, bf16[32,64,128]{2,1,0:T(8,128)(2,1)}, u32[]{:S(2)}, u32[]{:S(2)}) %collective-permute-start.9) | collective-permute-done | bytes 524320 | tf_op jit(solution)/shard_map/ppermute | solution.py:64
  (112 shorter events, 70.3 us)
Async XLA Ops:
  6.3 24.7 %collective-permute-start.12 = (bf16[32,64,128]{2,1,0:T(8,128)(2,1)}, bf16[32,64,128]{2,1,0:T(8,128)(2,1)}, u32[]{:S(2)}, u32[]{:S(2)}) collective-permute-start(bf16[32,64,128]{2,1,0:T(8,128)(2,1)} %shard_map.79), channel_id=1, source_target_pairs={{0,1},{1,0},{2,3},{3,2},{4,5},{5,4},{6,7},{7,6},{8,9},{9,8},{10,11... | collective-permute-start | bytes 1572872 | tf_op jit(solution)/shard_map/ppermute | solution.py:58
  11.4 20.6 %collective-permute-start.13 = (bf16[32,64,128]{2,1,0:T(8,128)(2,1)}, bf16[32,64,128]{2,1,0:T(8,128)(2,1)}, u32[]{:S(2)}, u32[]{:S(2)}) collective-permute-start(bf16[32,64,128]{2,1,0:T(8,128)(2,1)} %shard_map.80), channel_id=1, source_target_pairs={{0,8},{8,0},{16,24},{24,16},{32,40},{40,32},{48,56},{56,48},{64,72... | collective-permute-start | bytes 1572872 | tf_op jit(solution)/shard_map/ppermute | solution.py:55
  15.1 18.5 %collective-permute-start.14 = (bf16[32,64,128]{2,1,0:T(8,128)(2,1)}, bf16[32,64,128]{2,1,0:T(8,128)(2,1)}, u32[]{:S(2)}, u32[]{:S(2)}) collective-permute-start(bf16[32,64,128]{2,1,0:T(8,128)(2,1)} %shard_map.81), channel_id=1, source_target_pairs={{0,9},{1,8},{2,11},{3,10},{4,13},{5,12},{6,15},{7,14},{8,1},{9,0},... | collective-permute-start | bytes 1572872 | tf_op jit(solution)/shard_map/ppermute | solution.py:64
  17.8 27.1 %collective-permute-start.2 = (bf16[32,64,128]{2,1,0:T(8,128)(2,1)}, bf16[32,64,128]{2,1,0:T(8,128)(2,1)}, u32[]{:S(2)}, u32[]{:S(2)}) collective-permute-start(bf16[32,64,128]{2,1,0:T(8,128)(2,1)} %shard_map.76), channel_id=1, source_target_pairs={{0,9},{1,8},{2,11},{3,10},{4,13},{5,12},{6,15},{7,14},{8,1},{9,0},... | collective-permute-start | bytes 1572872 | tf_op jit(solution)/shard_map/ppermute | solution.py:64
  22.3 43.3 %collective-permute-start = (bf16[32,64,128]{2,1,0:T(8,128)(2,1)}, bf16[32,64,128]{2,1,0:T(8,128)(2,1)}, u32[]{:S(2)}, u32[]{:S(2)}) collective-permute-start(bf16[32,64,128]{2,1,0:T(8,128)(2,1)} %shard_map.74), channel_id=1, source_target_pairs={{0,1},{1,0},{2,3},{3,2},{4,5},{5,4},{6,7},{7,6},{8,9},{9,8},{10,11... | collective-permute-start | bytes 1572872 | tf_op jit(solution)/shard_map/ppermute | solution.py:58
  31.6 34.0 %collective-permute-start.1 = (bf16[32,64,128]{2,1,0:T(8,128)(2,1)S(1)}, bf16[32,64,128]{2,1,0:T(8,128)(2,1)S(1)}, u32[]{:S(2)}, u32[]{:S(2)}) collective-permute-start(bf16[32,64,128]{2,1,0:T(8,128)(2,1)S(1)} %copy-done.8), channel_id=1, source_target_pairs={{0,8},{8,0},{16,24},{24,16},{32,40},{40,32},{48,56},{56,48},{64,72... | collective-permute-start | bytes 1572872 | tf_op jit(solution)/shard_map/ppermute | solution.py:55
  37.0 40.1 %collective-permute-start.15 = (bf16[32,64,128]{2,1,0:T(8,128)(2,1)}, bf16[32,64,128]{2,1,0:T(8,128)(2,1)}, u32[]{:S(2)}, u32[]{:S(2)}) collective-permute-start(bf16[32,64,128]{2,1,0:T(8,128)(2,1)} %get-tuple-element.27), channel_id=1, source_target_pairs={{0,4},{1,5},{2,6},{3,7},{4,0},{5,1},{6,2},{7,3},{8,12},{9,13},{10,... | collective-permute-start | bytes 1572872 | tf_op jit(solution)/shard_map/ppermute | solution.py:58
  40.0 39.9 %collective-permute-start.16 = (bf16[32,64,128]{2,1,0:T(8,128)(2,1)}, bf16[32,64,128]{2,1,0:T(8,128)(2,1)}, u32[]{:S(2)}, u32[]{:S(2)}) collective-permute-start(bf16[32,64,128]{2,1,0:T(8,128)(2,1)} %get-tuple-element.26), channel_id=1, source_target_pairs={{0,64},{8,72},{16,80},{24,88},{32,96},{40,104},{48,112},{56,120},{... | collective-permute-start | bytes 1572872 | tf_op jit(solution)/shard_map/ppermute | solution.py:55
  44.9 35.0 %collective-permute-start.17 = (bf16[32,64,128]{2,1,0:T(8,128)(2,1)S(1)}, bf16[32,64,128]{2,1,0:T(8,128)(2,1)}, u32[]{:S(2)}, u32[]{:S(2)}) collective-permute-start(bf16[32,64,128]{2,1,0:T(8,128)(2,1)S(1)} %get-tuple-element.25), channel_id=1, source_target_pairs={{0,68},{1,69},{2,70},{3,71},{4,64},{5,65},{6,66},{7,67},{8,76},{9,... | collective-permute-start | bytes 1572872 | tf_op jit(solution)/shard_map/ppermute | solution.py:64
  68.8 24.0 %collective-permute-start.3 = (bf16[32,64,128]{2,1,0:T(8,128)(2,1)}, bf16[32,64,128]{2,1,0:T(8,128)(2,1)}, u32[]{:S(2)}, u32[]{:S(2)}) collective-permute-start(bf16[32,64,128]{2,1,0:T(8,128)(2,1)} %get-tuple-element.35), channel_id=1, source_target_pairs={{0,4},{1,5},{2,6},{3,7},{4,0},{5,1},{6,2},{7,3},{8,12},{9,13},{10,... | collective-permute-start | bytes 1572872 | tf_op jit(solution)/shard_map/ppermute | solution.py:58
  73.8 28.4 %collective-permute-start.4 = (bf16[32,64,128]{2,1,0:T(8,128)(2,1)}, bf16[32,64,128]{2,1,0:T(8,128)(2,1)S(1)}, u32[]{:S(2)}, u32[]{:S(2)}) collective-permute-start(bf16[32,64,128]{2,1,0:T(8,128)(2,1)} %get-tuple-element.34), channel_id=1, source_target_pairs={{0,64},{8,72},{16,80},{24,88},{32,96},{40,104},{48,112},{56,120},{... | collective-permute-start | bytes 1572872 | tf_op jit(solution)/shard_map/ppermute | solution.py:55
  77.1 25.2 %collective-permute-start.5 = (bf16[32,64,128]{2,1,0:T(8,128)(2,1)S(1)}, bf16[32,64,128]{2,1,0:T(8,128)(2,1)}, u32[]{:S(2)}, u32[]{:S(2)}) collective-permute-start(bf16[32,64,128]{2,1,0:T(8,128)(2,1)S(1)} %get-tuple-element.33), channel_id=1, source_target_pairs={{0,68},{1,69},{2,70},{3,71},{4,64},{5,65},{6,66},{7,67},{8,76},{9,... | collective-permute-start | bytes 1572872 | tf_op jit(solution)/shard_map/ppermute | solution.py:64
  89.8 26.2 %collective-permute-start.18 = (bf16[32,64,128]{2,1,0:T(8,128)(2,1)}, bf16[32,64,128]{2,1,0:T(8,128)(2,1)S(1)}, u32[]{:S(2)}, u32[]{:S(2)}) collective-permute-start(bf16[32,64,128]{2,1,0:T(8,128)(2,1)} %get-tuple-element.18), channel_id=1, source_target_pairs={{0,4},{1,5},{2,6},{3,7},{4,0},{5,1},{6,2},{7,3},{8,12},{9,13},{10,... | collective-permute-start | bytes 1572872 | tf_op jit(solution)/shard_map/ppermute | solution.py:58
  92.8 32.0 %collective-permute-start.19 = (bf16[32,64,128]{2,1,0:T(8,128)(2,1)}, bf16[32,64,128]{2,1,0:T(8,128)(2,1)}, u32[]{:S(2)}, u32[]{:S(2)}) collective-permute-start(bf16[32,64,128]{2,1,0:T(8,128)(2,1)} %get-tuple-element.19), channel_id=1, source_target_pairs={{0,64},{8,72},{16,80},{24,88},{32,96},{40,104},{48,112},{56,120},{... | collective-permute-start | bytes 1572872 | tf_op jit(solution)/shard_map/ppermute | solution.py:55
  92.8 32.0 %collective-permute-start.20 = (bf16[32,64,128]{2,1,0:T(8,128)(2,1)}, bf16[32,64,128]{2,1,0:T(8,128)(2,1)}, u32[]{:S(2)}, u32[]{:S(2)}) collective-permute-start(bf16[32,64,128]{2,1,0:T(8,128)(2,1)} %get-tuple-element.20), channel_id=1, source_target_pairs={{0,68},{1,69},{2,70},{3,71},{4,64},{5,65},{6,66},{7,67},{8,76},{9,... | collective-permute-start | bytes 1572872 | tf_op jit(solution)/shard_map/ppermute | solution.py:64
  113.0 19.0 %collective-permute-start.6 = (bf16[32,64,128]{2,1,0:T(8,128)(2,1)}, bf16[32,64,128]{2,1,0:T(8,128)(2,1)S(1)}, u32[]{:S(2)}, u32[]{:S(2)}) collective-permute-start(bf16[32,64,128]{2,1,0:T(8,128)(2,1)} %get-tuple-element.14), channel_id=1, source_target_pairs={{0,4},{1,5},{2,6},{3,7},{4,0},{5,1},{6,2},{7,3},{8,12},{9,13},{10,... | collective-permute-start | bytes 1572872 | tf_op jit(solution)/shard_map/ppermute | solution.py:58
  116.0 31.2 %collective-permute-start.7 = (bf16[32,64,128]{2,1,0:T(8,128)(2,1)}, bf16[32,64,128]{2,1,0:T(8,128)(2,1)S(1)}, u32[]{:S(2)}, u32[]{:S(2)}) collective-permute-start(bf16[32,64,128]{2,1,0:T(8,128)(2,1)} %get-tuple-element.15), channel_id=1, source_target_pairs={{0,64},{8,72},{16,80},{24,88},{32,96},{40,104},{48,112},{56,120},{... | collective-permute-start | bytes 1572872 | tf_op jit(solution)/shard_map/ppermute | solution.py:55
  116.0 31.2 %collective-permute-start.8 = (bf16[32,64,128]{2,1,0:T(8,128)(2,1)}, bf16[32,64,128]{2,1,0:T(8,128)(2,1)S(1)}, u32[]{:S(2)}, u32[]{:S(2)}) collective-permute-start(bf16[32,64,128]{2,1,0:T(8,128)(2,1)} %get-tuple-element.16), channel_id=1, source_target_pairs={{0,68},{1,69},{2,70},{3,71},{4,64},{5,65},{6,66},{7,67},{8,76},{9,... | collective-permute-start | bytes 1572872 | tf_op jit(solution)/shard_map/ppermute | solution.py:64
  128.0 26.7 %collective-permute-start.23 = (bf16[32,64,128]{2,1,0:T(8,128)(2,1)S(1)}, bf16[32,64,128]{2,1,0:T(8,128)(2,1)S(1)}, u32[]{:S(2)}, u32[]{:S(2)}) collective-permute-start(bf16[32,64,128]{2,1,0:T(8,128)(2,1)S(1)} %get-tuple-element.22), channel_id=1, source_target_pairs={{0,1},{1,0},{2,3},{3,2},{4,5},{5,4},{6,7},{7,6},{8,9},{9,8},{10,11... | collective-permute-start | bytes 1572872 | tf_op jit(solution)/shard_map/ppermute | solution.py:58
  128.0 44.5 %collective-permute-start.22 = (bf16[32,64,128]{2,1,0:T(8,128)(2,1)}, bf16[32,64,128]{2,1,0:T(8,128)(2,1)S(1)}, u32[]{:S(2)}, u32[]{:S(2)}) collective-permute-start(bf16[32,64,128]{2,1,0:T(8,128)(2,1)} %get-tuple-element.23), channel_id=1, source_target_pairs={{0,8},{8,0},{16,24},{24,16},{32,40},{40,32},{48,56},{56,48},{64,72... | collective-permute-start | bytes 1572872 | tf_op jit(solution)/shard_map/ppermute | solution.py:55
  132.0 44.0 %collective-permute-start.21 = (bf16[32,64,128]{2,1,0:T(8,128)(2,1)}, bf16[32,64,128]{2,1,0:T(8,128)(2,1)S(1)}, u32[]{:S(2)}, u32[]{:S(2)}) collective-permute-start(bf16[32,64,128]{2,1,0:T(8,128)(2,1)} %get-tuple-element.24), channel_id=1, source_target_pairs={{0,9},{1,8},{2,11},{3,10},{4,13},{5,12},{6,15},{7,14},{8,1},{9,0},... | collective-permute-start | bytes 1572872 | tf_op jit(solution)/shard_map/ppermute | solution.py:64
  149.3 32.7 %collective-permute-start.11 = (bf16[32,64,128]{2,1,0:T(8,128)(2,1)}, bf16[32,64,128]{2,1,0:T(8,128)(2,1)}, u32[]{:S(2)}, u32[]{:S(2)}) collective-permute-start(bf16[32,64,128]{2,1,0:T(8,128)(2,1)} %get-tuple-element.30), channel_id=1, source_target_pairs={{0,1},{1,0},{2,3},{3,2},{4,5},{5,4},{6,7},{7,6},{8,9},{9,8},{10,11... | collective-permute-start | bytes 1572872 | tf_op jit(solution)/shard_map/ppermute | solution.py:58
  149.3 35.4 %collective-permute-start.10 = (bf16[32,64,128]{2,1,0:T(8,128)(2,1)}, bf16[32,64,128]{2,1,0:T(8,128)(2,1)S(1)}, u32[]{:S(2)}, u32[]{:S(2)}) collective-permute-start(bf16[32,64,128]{2,1,0:T(8,128)(2,1)} %get-tuple-element.31), channel_id=1, source_target_pairs={{0,8},{8,0},{16,24},{24,16},{32,40},{40,32},{48,56},{56,48},{64,72... | collective-permute-start | bytes 1572872 | tf_op jit(solution)/shard_map/ppermute | solution.py:55
  154.7 36.7 %collective-permute-start.9 = (bf16[32,64,128]{2,1,0:T(8,128)(2,1)}, bf16[32,64,128]{2,1,0:T(8,128)(2,1)}, u32[]{:S(2)}, u32[]{:S(2)}) collective-permute-start(bf16[32,64,128]{2,1,0:T(8,128)(2,1)} %get-tuple-element.32), channel_id=1, source_target_pairs={{0,9},{1,8},{2,11},{3,10},{4,13},{5,12},{6,15},{7,14},{8,1},{9,0},... | collective-permute-start | bytes 1572872 | tf_op jit(solution)/shard_map/ppermute | solution.py:64
  (15 other events, 114.9 us)

commit v6 on v5

--- a/solution.py
+++ b/solution.py
@@ -143,7 +143,7 @@
         o_ref[g] = cur[g]
 
 
-def chain_call(plan, k0, data, mats, data_spec, out_shape, out_spec, target=None):
+def chain_call(plan, k0, data, mats, data_spec, out_shape, out_spec, steps, target=None):
     in_specs = [data_spec, pl.BlockSpec(mats.shape, lambda i, k: (0, 0, 0))]
     operands = [k0, data, mats]
     aliases = {}
@@ -154,7 +154,7 @@
     return pl.pallas_call(
         functools.partial(chain_kernel, plan),
         grid_spec=pltpu.PrefetchScalarGridSpec(
-            num_scalar_prefetch=1, grid=(1,), in_specs=in_specs, out_specs=out_spec
+            num_scalar_prefetch=1, grid=(steps,), in_specs=in_specs, out_specs=out_spec
         ),
         out_shape=out_shape,
         input_output_aliases=aliases,
@@ -221,23 +221,26 @@
     ]
     forward_mats = jnp.stack([spread] + forward_levels)
     adjoint_mats = jnp.stack([w.T for w in reversed(forward_levels)] + [spread.T])
-    forward_plan = [chain_sets(part, 1)] + [chain_sets(part, 4**i) for i in range(local_depth)]
-    adjoint_plan = [chain_sets(part, 4**i) for i in reversed(range(local_depth))] + [
-        chain_sets(part, 1)
+    steps = 2
+    block = part // steps
+    forward_plan = [chain_sets(block, 1)] + [chain_sets(block, 4**i) for i in range(local_depth)]
+    adjoint_plan = [chain_sets(block, 4**i) for i in reversed(range(local_depth))] + [
+        chain_sets(block, 1)
     ]
     k0_ref = jnp.reshape(k0, (1,)).astype(jnp.int32)
     piece_shape = jax.ShapeDtypeStruct((part, rank_size, inner_boxes), jnp.bfloat16)
-    whole_piece = pl.BlockSpec((part, rank_size, inner_boxes), lambda i, k: (0, 0, 0))
+    whole_piece = pl.BlockSpec((block, rank_size, inner_boxes), lambda i, k: (i, 0, 0))
 
     def in_place(m, f):
         return pl.BlockSpec(
-            (None, None, part, rank_size, inner_boxes),
-            lambda i, k: (jnp.bitwise_xor(k[0], f), m, 0, 0, 0),
+            (None, None, block, rank_size, inner_boxes),
+            lambda i, k: (jnp.bitwise_xor(k[0], f), m, i, 0, 0),
         )
 
     def local_forward(m, f):
         return chain_call(
-            forward_plan, k0_ref, image, forward_mats, in_place(m, f), piece_shape, whole_piece
+            forward_plan, k0_ref, image, forward_mats, in_place(m, f), piece_shape, whole_piece,
+            steps,
         )
 
     def local_adjoint(gradient, piece, m, f):
@@ -249,10 +252,11 @@
             whole_piece,
             jax.ShapeDtypeStruct(shape5, jnp.bfloat16),
             in_place(m, f),
+            steps,
             target=gradient,
         )
 
-    gradient = jnp.zeros(shape5, jnp.bfloat16)
+    gradient = None
     for m in range(CHUNKS):
         coef = [local_forward(m, f) for f in range(4)]
         pieces = exchange(coef, *shifts[0])

time: 195 us -> 198 us (1.015)
  waiting for transfers between devices: 50.7 us -> 40.8 us
  starting transfers between devices: 53.6 us -> 63.5 us
  Pallas kernels: 62.7 us -> 69.3 us
  local copies, waits for them, and re-layouts: 17.7 us -> 14.6 us
    ppermute x8, waiting for transfers between devices: 15.8 us -> 4.58 us  [flip_send(): return lax.ppermute(value, 'qy', pairs)]
    ppermute x8, starting transfers between devices: 16.3 us -> 24.9 us  [flip_send(): return lax.ppermute(value, 'qx', pairs)]
    pallas_call x16, Pallas kernels: 42.9 us -> 49.4 us  [chain_call(): pl.pallas_call(functools.partial(chain_kernel, plan), grid_spec=pltpu.Pre...]
    ppermute x8, starting transfers between devices: 14.3 us -> 19.7 us  [flip_send(): return lax.ppermute(value, 'qy', pairs)]
    ppermute x8, starting transfers between devices: 23 us -> 18.9 us  [flip_send(): return lax.ppermute(value, ('qx', 'qy'), pairs)]
    broadcast_in_dim x1 -> x0, local copies, waits for them, and re-layouts: 3.08 us -> none  [local(): gradient = jnp.zeros(shape5, jnp.bfloat16)]
  transfers between devices with their start and end apart: 24 -> 24, of which waited for: 9 -> 8; matrix products, arithmetic and copies ran while one was open for 10% -> 8% of each run, Pallas kernels for 30% -> 32%
where the time goes in v6:
time: 198 us
  Pallas kernels  69.3 us (35%)
  starting transfers between devices  63.5 us (32%)
  waiting for transfers between devices  40.8 us (21%)
  local copies, waits for them, and re-layouts  14.6 us (7%)
  matrix products  6.8 us (3%)
  other arithmetic  2.27 us (1%)
    pallas_call x16, Pallas kernels, chain_call(): pl.pallas_call(functools.partial(chain_kernel, plan), grid_spec=pltpu.Pre...  49.4 us
    ppermute x8, waiting for transfers between devices, flip_send(): return lax.ppermute(value, 'qx', pairs)  30.7 us
    ppermute x8, starting transfers between devices, flip_send(): return lax.ppermute(value, 'qx', pairs)  24.9 us
    pallas_call x2, Pallas kernels, output_stage(): pl.pallas_call(output_stage_kernel, grid=(part // step,), in_specs=[piece...  19.9 us
    ppermute x8, starting transfers between devices, flip_send(): return lax.ppermute(value, 'qy', pairs)  19.7 us
    ppermute x8, starting transfers between devices, flip_send(): return lax.ppermute(value, ('qx', 'qy'), pairs)  18.9 us
    dot_general x4, matrix products, mixing(): jnp.einsum(form, weight, data, preferred_element_type=jnp.float32)  6.8 us
    ppermute x8, waiting for transfers between devices, flip_send(): return lax.ppermute(value, ('qx', 'qy'), pairs)  5.55 us
  transfers between devices with their start and end apart: 24, of which 8 were waited for; matrix products, arithmetic and copies ran while one was open for 8% of the time, Pallas kernels for 32%

profile of v6, /device:TPU:1, one launch (start us, length us, event | category | flops | bytes accessed | tf_op | source)
XLA Modules:
  0.0 197.6 jit_solution(9614435137438456373)
XLA Ops:
  3.6 3.1 %shard_map.79 = bf16[32,64,128]{2,1,0:T(8,128)(2,1)} custom-call(s32[1]{0:T(128)} %bitcast.k_ref, bf16[4,2,32,64,128]{4,3,2,1,0:T(8,128)(2,1)} %bitcast.165, bf16[3,256,256]{2,1,0:T(8,128)(2,1)} %pad_maximum_fusion.4.m_ref), custom_call_target="tpu_custom_call" | custom-call | tf_op jit(solution)/shard_map/pallas_call | solution.py:154
  9.1 3.1 %shard_map.80 = bf16[32,64,128]{2,1,0:T(8,128)(2,1)} custom-call(s32[1]{0:T(128)} %bitcast.k_ref, bf16[4,2,32,64,128]{4,3,2,1,0:T(8,128)(2,1)} %bitcast.166, bf16[3,256,256]{2,1,0:T(8,128)(2,1)} %pad_maximum_fusion.4.m_ref), custom_call_target="tpu_custom_call" | custom-call | tf_op jit(solution)/shard_map/pallas_call | solution.py:154
  13.2 3.1 %shard_map.81 = bf16[32,64,128]{2,1,0:T(8,128)(2,1)} custom-call(s32[1]{0:T(128)} %bitcast.k_ref, bf16[4,2,32,64,128]{4,3,2,1,0:T(8,128)(2,1)} %bitcast.167, bf16[3,256,256]{2,1,0:T(8,128)(2,1)} %pad_maximum_fusion.4.m_ref), custom_call_target="tpu_custom_call" | custom-call | tf_op jit(solution)/shard_map/pallas_call | solution.py:154
  16.3 3.1 %shard_map.76 = bf16[32,64,128]{2,1,0:T(8,128)(2,1)} custom-call(s32[1]{0:T(128)} %bitcast.k_ref, bf16[4,2,32,64,128]{4,3,2,1,0:T(8,128)(2,1)} %bitcast.168, bf16[3,256,256]{2,1,0:T(8,128)(2,1)} %pad_maximum_fusion.4.m_ref), custom_call_target="tpu_custom_call" | custom-call | tf_op jit(solution)/shard_map/pallas_call | solution.py:154
  21.1 3.1 %shard_map.74 = bf16[32,64,128]{2,1,0:T(8,128)(2,1)} custom-call(s32[1]{0:T(128)} %bitcast.k_ref, bf16[4,2,32,64,128]{4,3,2,1,0:T(8,128)(2,1)} %bitcast.169, bf16[3,256,256]{2,1,0:T(8,128)(2,1)} %pad_maximum_fusion.4.m_ref), custom_call_target="tpu_custom_call" | custom-call | tf_op jit(solution)/shard_map/pallas_call | solution.py:154
  24.4 3.1 %shard_map.78 = bf16[32,64,128]{2,1,0:T(8,128)(2,1)} custom-call(s32[1]{0:T(128)} %bitcast.k_ref, bf16[4,2,32,64,128]{4,3,2,1,0:T(8,128)(2,1)} %bitcast.170, bf16[3,256,256]{2,1,0:T(8,128)(2,1)} %pad_maximum_fusion.4.m_ref), custom_call_target="tpu_custom_call" | custom-call | tf_op jit(solution)/shard_map/pallas_call | solution.py:154
  27.6 3.1 %shard_map.75 = bf16[32,64,128]{2,1,0:T(8,128)(2,1)} custom-call(s32[1]{0:T(128)} %bitcast.k_ref, bf16[4,2,32,64,128]{4,3,2,1,0:T(8,128)(2,1)} %bitcast.171, bf16[3,256,256]{2,1,0:T(8,128)(2,1)} %pad_maximum_fusion.4.m_ref), custom_call_target="tpu_custom_call" | custom-call | tf_op jit(solution)/shard_map/pallas_call | solution.py:154
  30.7 3.1 %shard_map.73 = bf16[32,64,128]{2,1,0:T(8,128)(2,1)} custom-call(s32[1]{0:T(128)} %bitcast.k_ref, bf16[4,2,32,64,128]{4,3,2,1,0:T(8,128)(2,1)} %bitcast.172, bf16[3,256,256]{2,1,0:T(8,128)(2,1)} %pad_maximum_fusion.4.m_ref), custom_call_target="tpu_custom_call" | custom-call | tf_op jit(solution)/shard_map/pallas_call | solution.py:154
  41.5 3.3 %collective-permute-start.16 = (bf16[32,64,128]{2,1,0:T(8,128)(2,1)}, bf16[32,64,128]{2,1,0:T(8,128)(2,1)}, u32[]{:S(2)}, u32[]{:S(2)}) collective-permute-start(bf16[32,64,128]{2,1,0:T(8,128)(2,1)} %get-tuple-element.26), channel_id=1, source_target_pairs={{0,64},{8,72},{16,80},{24,88},{32,96},{40,104},{48,112},{56,120},{... | collective-permute-start | bytes 1572872 | tf_op jit(solution)/shard_map/ppermute | solution.py:55
  45.3 6.3 %collective-permute-start.17 = (bf16[32,64,128]{2,1,0:T(8,128)(2,1)S(1)}, bf16[32,64,128]{2,1,0:T(8,128)(2,1)}, u32[]{:S(2)}, u32[]{:S(2)}) collective-permute-start(bf16[32,64,128]{2,1,0:T(8,128)(2,1)S(1)} %get-tuple-element.25), channel_id=1, source_target_pairs={{0,68},{1,69},{2,70},{3,71},{4,64},{5,65},{6,66},{7,67},{8,76},{9,... | collective-permute-start | bytes 1572872 | tf_op jit(solution)/shard_map/ppermute | solution.py:64
  51.6 3.2 %collective-permute-done = bf16[32,64,128]{2,1,0:T(8,128)(2,1)} collective-permute-done((bf16[32,64,128]{2,1,0:T(8,128)(2,1)}, bf16[32,64,128]{2,1,0:T(8,128)(2,1)}, u32[]{:S(2)}, u32[]{:S(2)}) %collective-permute-start) | collective-permute-done | bytes 524320 | tf_op jit(solution)/shard_map/ppermute | solution.py:58
  63.0 3.2 %collective-permute-start.4 = (bf16[32,64,128]{2,1,0:T(8,128)(2,1)}, bf16[32,64,128]{2,1,0:T(8,128)(2,1)S(1)}, u32[]{:S(2)}, u32[]{:S(2)}) collective-permute-start(bf16[32,64,128]{2,1,0:T(8,128)(2,1)} %get-tuple-element.34), channel_id=1, source_target_pairs={{0,64},{8,72},{16,80},{24,88},{32,96},{40,104},{48,112},{56,120},{... | collective-permute-start | bytes 1572872 | tf_op jit(solution)/shard_map/ppermute | solution.py:55
  66.3 19.6 %collective-permute-done.16.p2 = bf16[32,64,128]{2,1,0:T(8,128)(2,1)} collective-permute-done((bf16[32,64,128]{2,1,0:T(8,128)(2,1)}, bf16[32,64,128]{2,1,0:T(8,128)(2,1)}, u32[]{:S(2)}, u32[]{:S(2)}) %collective-permute-start.16) | collective-permute-done | bytes 524320 | tf_op jit(solution)/shard_map/ppermute | solution.py:55
  85.9 9.9 %shard_map.82 = (bf16[32,64,128]{2,1,0:T(8,128)(2,1)}, bf16[32,64,128]{2,1,0:T(8,128)(2,1)}, bf16[32,64,128]{2,1,0:T(8,128)(2,1)}, bf16[32,64,128]{2,1,0:T(8,128)(2,1)}) custom-call(bf16[32,64,128]{2,1,0:T(8,128)(2,1)} %get-tuple-element.28.p0, bf16[32,64,128]{2,1,0:T(8,128)(2,1)} %collective-permute-done.15.p1, ...), custom_call_target="tpu_custom_call" | custom-call | flops 2147483648 | bytes 10485760 | tf_op jit(solution)/shard_map/pallas_call | solution.py:173
  95.8 8.6 %collective-permute-start.18 = (bf16[32,64,128]{2,1,0:T(8,128)(2,1)}, bf16[32,64,128]{2,1,0:T(8,128)(2,1)S(1)}, u32[]{:S(2)}, u32[]{:S(2)}) collective-permute-start(bf16[32,64,128]{2,1,0:T(8,128)(2,1)} %get-tuple-element.18), channel_id=1, source_target_pairs={{0,4},{1,5},{2,6},{3,7},{4,0},{5,1},{6,2},{7,3},{8,12},{9,13},{10,... | collective-permute-start | bytes 1572872 | tf_op jit(solution)/shard_map/ppermute | solution.py:58
  108.0 9.9 %shard_map.77 = (bf16[32,64,128]{2,1,0:T(8,128)(2,1)}, bf16[32,64,128]{2,1,0:T(8,128)(2,1)}, bf16[32,64,128]{2,1,0:T(8,128)(2,1)}, bf16[32,64,128]{2,1,0:T(8,128)(2,1)}) custom-call(bf16[32,64,128]{2,1,0:T(8,128)(2,1)} %get-tuple-element.36.p0, bf16[32,64,128]{2,1,0:T(8,128)(2,1)} %collective-permute-done.3.p1, bf16[32,64,128]{2,1,0:T(8,128)(2,1)} %copy-done.10, ...), custom_call_target="tpu_custom_call" | custom-call | flops 2147483648 | bytes 10485760 | tf_op jit(solution)/shard_map/pallas_call | solution.py:173
  127.8 10.3 %collective-permute-start.22 = (bf16[32,64,128]{2,1,0:T(8,128)(2,1)}, bf16[32,64,128]{2,1,0:T(8,128)(2,1)S(1)}, u32[]{:S(2)}, u32[]{:S(2)}) collective-permute-start(bf16[32,64,128]{2,1,0:T(8,128)(2,1)} %get-tuple-element.23), channel_id=1, source_target_pairs={{0,8},{8,0},{16,24},{24,16},{32,40},{40,32},{48,56},{56,48},{64,72... | collective-permute-start | bytes 1572872 | tf_op jit(solution)/shard_map/ppermute | solution.py:55
  139.7 11.0 %collective-permute-done.7 = bf16[32,64,128]{2,1,0:T(8,128)(2,1)S(1)} collective-permute-done((bf16[32,64,128]{2,1,0:T(8,128)(2,1)}, bf16[32,64,128]{2,1,0:T(8,128)(2,1)S(1)}, u32[]{:S(2)}, u32[]{:S(2)}) %collective-permute-start.7) | collective-permute-done | bytes 524320 | tf_op jit(solution)/shard_map/ppermute | solution.py:55
  152.9 6.5 %collective-permute-start.10 = (bf16[32,64,128]{2,1,0:T(8,128)(2,1)}, bf16[32,64,128]{2,1,0:T(8,128)(2,1)S(1)}, u32[]{:S(2)}, u32[]{:S(2)}) collective-permute-start(bf16[32,64,128]{2,1,0:T(8,128)(2,1)} %get-tuple-element.31), channel_id=1, source_target_pairs={{0,8},{8,0},{16,24},{24,16},{32,40},{40,32},{48,56},{56,48},{64,72... | collective-permute-start | bytes 1572872 | tf_op jit(solution)/shard_map/ppermute | solution.py:55
  160.8 3.6 %collective-permute-start.9 = (bf16[32,64,128]{2,1,0:T(8,128)(2,1)}, bf16[32,64,128]{2,1,0:T(8,128)(2,1)}, u32[]{:S(2)}, u32[]{:S(2)}) collective-permute-start(bf16[32,64,128]{2,1,0:T(8,128)(2,1)} %get-tuple-element.32), channel_id=1, source_target_pairs={{0,9},{1,8},{2,11},{3,10},{4,13},{5,12},{6,15},{7,14},{8,1},{9,0},... | collective-permute-start | bytes 1572872 | tf_op jit(solution)/shard_map/ppermute | solution.py:64
  169.3 3.1 %shard_map.84.rest_0_ = bf16[4,2,32,64,128]{4,3,2,1,0:T(8,128)(2,1)} custom-call(s32[1]{0:T(128)} %bitcast.k_ref, bf16[32,64,128]{2,1,0:T(8,128)(2,1)} %copy-done.4, bf16[3,256,256]{2,1,0:T(8,128)(2,1)} %pad_maximum_fusion.5.m_ref, bf16[4,2,32,64,128]{4,3,2,1,0:T(8,128)(2,1)} %shard_map.83.rest_0_), custom_call_target="tpu_custom_call", output_to_operand_aliasing={{}: (3, {})} | custom-call | tf_op jit(solution)/shard_map/pallas_call | solution.py:154
  173.2 3.1 %shard_map.85.rest_0_ = bf16[4,2,32,64,128]{4,3,2,1,0:T(8,128)(2,1)} custom-call(s32[1]{0:T(128)} %bitcast.k_ref, bf16[32,64,128]{2,1,0:T(8,128)(2,1)} %copy-done.2, bf16[3,256,256]{2,1,0:T(8,128)(2,1)} %pad_maximum_fusion.5.m_ref, bf16[4,2,32,64,128]{4,3,2,1,0:T(8,128)(2,1)} %shard_map.84.rest_0_), custom_call_target="tpu_custom_call", output_to_operand_aliasing={{}: (3, {})} | custom-call | tf_op jit(solution)/shard_map/pallas_call | solution.py:154
  183.3 3.1 %shard_map.88.rest_0_ = bf16[4,2,32,64,128]{4,3,2,1,0:T(8,128)(2,1)} custom-call(s32[1]{0:T(128)} %bitcast.k_ref, bf16[32,64,128]{2,1,0:T(8,128)(2,1)} %collective-permute-done.11.x_ref, bf16[3,256,256]{2,1,0:T(8,128)(2,1)} %pad_maximum_fusion.5.m_ref, bf16[4,2,32,64,128]{4,3,2,1,0:T(8,128)(2,1)} %shard_map.87.rest_0_), custom_call_target="tpu_custom_call", output_to_operand_aliasing={{}: (3, {})} | custom-call | tf_op jit(solution)/shard_map/pallas_call | solution.py:154
  190.3 4.3 %collective-permute-done.9.x_ref = bf16[32,64,128]{2,1,0:T(8,128)(2,1)} collective-permute-done((bf16[32,64,128]{2,1,0:T(8,128)(2,1)}, bf16[32,64,128]{2,1,0:T(8,128)(2,1)}, u32[]{:S(2)}, u32[]{:S(2)}) %collective-permute-start.9) | collective-permute-done | bytes 524320 | tf_op jit(solution)/shard_map/ppermute | solution.py:64
  (111 shorter events, 63.3 us)
Async XLA Ops:
  6.7 27.5 %collective-permute-start.12 = (bf16[32,64,128]{2,1,0:T(8,128)(2,1)}, bf16[32,64,128]{2,1,0:T(8,128)(2,1)}, u32[]{:S(2)}, u32[]{:S(2)}) collective-permute-start(bf16[32,64,128]{2,1,0:T(8,128)(2,1)} %shard_map.79), channel_id=1, source_target_pairs={{0,1},{1,0},{2,3},{3,2},{4,5},{5,4},{6,7},{7,6},{8,9},{9,8},{10,11... | collective-permute-start | bytes 1572872 | tf_op jit(solution)/shard_map/ppermute | solution.py:58
  12.2 23.1 %collective-permute-start.13 = (bf16[32,64,128]{2,1,0:T(8,128)(2,1)}, bf16[32,64,128]{2,1,0:T(8,128)(2,1)}, u32[]{:S(2)}, u32[]{:S(2)}) collective-permute-start(bf16[32,64,128]{2,1,0:T(8,128)(2,1)} %shard_map.80), channel_id=1, source_target_pairs={{0,8},{8,0},{16,24},{24,16},{32,40},{40,32},{48,56},{56,48},{64,72... | collective-permute-start | bytes 1572872 | tf_op jit(solution)/shard_map/ppermute | solution.py:55
  16.3 19.1 %collective-permute-start.14 = (bf16[32,64,128]{2,1,0:T(8,128)(2,1)}, bf16[32,64,128]{2,1,0:T(8,128)(2,1)}, u32[]{:S(2)}, u32[]{:S(2)}) collective-permute-start(bf16[32,64,128]{2,1,0:T(8,128)(2,1)} %shard_map.81), channel_id=1, source_target_pairs={{0,9},{1,8},{2,11},{3,10},{4,13},{5,12},{6,15},{7,14},{8,1},{9,0},... | collective-permute-start | bytes 1572872 | tf_op jit(solution)/shard_map/ppermute | solution.py:64
  19.4 25.9 %collective-permute-start.2 = (bf16[32,64,128]{2,1,0:T(8,128)(2,1)}, bf16[32,64,128]{2,1,0:T(8,128)(2,1)}, u32[]{:S(2)}, u32[]{:S(2)}) collective-permute-start(bf16[32,64,128]{2,1,0:T(8,128)(2,1)} %shard_map.76), channel_id=1, source_target_pairs={{0,9},{1,8},{2,11},{3,10},{4,13},{5,12},{6,15},{7,14},{8,1},{9,0},... | collective-permute-start | bytes 1572872 | tf_op jit(solution)/shard_map/ppermute | solution.py:64
  24.2 30.5 %collective-permute-start = (bf16[32,64,128]{2,1,0:T(8,128)(2,1)}, bf16[32,64,128]{2,1,0:T(8,128)(2,1)}, u32[]{:S(2)}, u32[]{:S(2)}) collective-permute-start(bf16[32,64,128]{2,1,0:T(8,128)(2,1)} %shard_map.74), channel_id=1, source_target_pairs={{0,1},{1,0},{2,3},{3,2},{4,5},{5,4},{6,7},{7,6},{8,9},{9,8},{10,11... | collective-permute-start | bytes 1572872 | tf_op jit(solution)/shard_map/ppermute | solution.py:58
  34.8 19.9 %collective-permute-start.1 = (bf16[32,64,128]{2,1,0:T(8,128)(2,1)S(1)}, bf16[32,64,128]{2,1,0:T(8,128)(2,1)S(1)}, u32[]{:S(2)}, u32[]{:S(2)}) collective-permute-start(bf16[32,64,128]{2,1,0:T(8,128)(2,1)S(1)} %copy-done.8), channel_id=1, source_target_pairs={{0,8},{8,0},{16,24},{24,16},{32,40},{40,32},{48,56},{56,48},{64,72... | collective-permute-start | bytes 1572872 | tf_op jit(solution)/shard_map/ppermute | solution.py:55
  38.7 27.6 %collective-permute-start.15 = (bf16[32,64,128]{2,1,0:T(8,128)(2,1)}, bf16[32,64,128]{2,1,0:T(8,128)(2,1)}, u32[]{:S(2)}, u32[]{:S(2)}) collective-permute-start(bf16[32,64,128]{2,1,0:T(8,128)(2,1)} %get-tuple-element.27), channel_id=1, source_target_pairs={{0,4},{1,5},{2,6},{3,7},{4,0},{5,1},{6,2},{7,3},{8,12},{9,13},{10,... | collective-permute-start | bytes 1572872 | tf_op jit(solution)/shard_map/ppermute | solution.py:58
  41.5 44.3 %collective-permute-start.16 = (bf16[32,64,128]{2,1,0:T(8,128)(2,1)}, bf16[32,64,128]{2,1,0:T(8,128)(2,1)}, u32[]{:S(2)}, u32[]{:S(2)}) collective-permute-start(bf16[32,64,128]{2,1,0:T(8,128)(2,1)} %get-tuple-element.26), channel_id=1, source_target_pairs={{0,64},{8,72},{16,80},{24,88},{32,96},{40,104},{48,112},{56,120},{... | collective-permute-start | bytes 1572872 | tf_op jit(solution)/shard_map/ppermute | solution.py:55
  45.3 40.6 %collective-permute-start.17 = (bf16[32,64,128]{2,1,0:T(8,128)(2,1)S(1)}, bf16[32,64,128]{2,1,0:T(8,128)(2,1)}, u32[]{:S(2)}, u32[]{:S(2)}) collective-permute-start(bf16[32,64,128]{2,1,0:T(8,128)(2,1)S(1)} %get-tuple-element.25), channel_id=1, source_target_pairs={{0,68},{1,69},{2,70},{3,71},{4,64},{5,65},{6,66},{7,67},{8,76},{9,... | collective-permute-start | bytes 1572872 | tf_op jit(solution)/shard_map/ppermute | solution.py:64
  57.9 46.5 %collective-permute-start.3 = (bf16[32,64,128]{2,1,0:T(8,128)(2,1)}, bf16[32,64,128]{2,1,0:T(8,128)(2,1)}, u32[]{:S(2)}, u32[]{:S(2)}) collective-permute-start(bf16[32,64,128]{2,1,0:T(8,128)(2,1)} %get-tuple-element.35), channel_id=1, source_target_pairs={{0,4},{1,5},{2,6},{3,7},{4,0},{5,1},{6,2},{7,3},{8,12},{9,13},{10,... | collective-permute-start | bytes 1572872 | tf_op jit(solution)/shard_map/ppermute | solution.py:58
  63.0 44.2 %collective-permute-start.4 = (bf16[32,64,128]{2,1,0:T(8,128)(2,1)}, bf16[32,64,128]{2,1,0:T(8,128)(2,1)S(1)}, u32[]{:S(2)}, u32[]{:S(2)}) collective-permute-start(bf16[32,64,128]{2,1,0:T(8,128)(2,1)} %get-tuple-element.34), channel_id=1, source_target_pairs={{0,64},{8,72},{16,80},{24,88},{32,96},{40,104},{48,112},{56,120},{... | collective-permute-start | bytes 1572872 | tf_op jit(solution)/shard_map/ppermute | solution.py:55
  66.3 41.0 %collective-permute-start.5 = (bf16[32,64,128]{2,1,0:T(8,128)(2,1)S(1)}, bf16[32,64,128]{2,1,0:T(8,128)(2,1)}, u32[]{:S(2)}, u32[]{:S(2)}) collective-permute-start(bf16[32,64,128]{2,1,0:T(8,128)(2,1)S(1)} %get-tuple-element.33), channel_id=1, source_target_pairs={{0,68},{1,69},{2,70},{3,71},{4,64},{5,65},{6,66},{7,67},{8,76},{9,... | collective-permute-start | bytes 1572872 | tf_op jit(solution)/shard_map/ppermute | solution.py:64
  95.8 25.1 %collective-permute-start.18 = (bf16[32,64,128]{2,1,0:T(8,128)(2,1)}, bf16[32,64,128]{2,1,0:T(8,128)(2,1)S(1)}, u32[]{:S(2)}, u32[]{:S(2)}) collective-permute-start(bf16[32,64,128]{2,1,0:T(8,128)(2,1)} %get-tuple-element.18), channel_id=1, source_target_pairs={{0,4},{1,5},{2,6},{3,7},{4,0},{5,1},{6,2},{7,3},{8,12},{9,13},{10,... | collective-permute-start | bytes 1572872 | tf_op jit(solution)/shard_map/ppermute | solution.py:58
  104.4 19.3 %collective-permute-start.19 = (bf16[32,64,128]{2,1,0:T(8,128)(2,1)}, bf16[32,64,128]{2,1,0:T(8,128)(2,1)}, u32[]{:S(2)}, u32[]{:S(2)}) collective-permute-start(bf16[32,64,128]{2,1,0:T(8,128)(2,1)} %get-tuple-element.19), channel_id=1, source_target_pairs={{0,64},{8,72},{16,80},{24,88},{32,96},{40,104},{48,112},{56,120},{... | collective-permute-start | bytes 1572872 | tf_op jit(solution)/shard_map/ppermute | solution.py:55
  104.4 20.1 %collective-permute-start.20 = (bf16[32,64,128]{2,1,0:T(8,128)(2,1)}, bf16[32,64,128]{2,1,0:T(8,128)(2,1)}, u32[]{:S(2)}, u32[]{:S(2)}) collective-permute-start(bf16[32,64,128]{2,1,0:T(8,128)(2,1)} %get-tuple-element.20), channel_id=1, source_target_pairs={{0,68},{1,69},{2,70},{3,71},{4,64},{5,65},{6,66},{7,67},{8,76},{9,... | collective-permute-start | bytes 1572872 | tf_op jit(solution)/shard_map/ppermute | solution.py:64
  118.0 20.1 %collective-permute-start.6 = (bf16[32,64,128]{2,1,0:T(8,128)(2,1)}, bf16[32,64,128]{2,1,0:T(8,128)(2,1)S(1)}, u32[]{:S(2)}, u32[]{:S(2)}) collective-permute-start(bf16[32,64,128]{2,1,0:T(8,128)(2,1)} %get-tuple-element.14), channel_id=1, source_target_pairs={{0,4},{1,5},{2,6},{3,7},{4,0},{5,1},{6,2},{7,3},{8,12},{9,13},{10,... | collective-permute-start | bytes 1572872 | tf_op jit(solution)/shard_map/ppermute | solution.py:58
  120.9 29.8 %collective-permute-start.7 = (bf16[32,64,128]{2,1,0:T(8,128)(2,1)}, bf16[32,64,128]{2,1,0:T(8,128)(2,1)S(1)}, u32[]{:S(2)}, u32[]{:S(2)}) collective-permute-start(bf16[32,64,128]{2,1,0:T(8,128)(2,1)} %get-tuple-element.15), channel_id=1, source_target_pairs={{0,64},{8,72},{16,80},{24,88},{32,96},{40,104},{48,112},{56,120},{... | collective-permute-start | bytes 1572872 | tf_op jit(solution)/shard_map/ppermute | solution.py:55
  120.9 29.8 %collective-permute-start.8 = (bf16[32,64,128]{2,1,0:T(8,128)(2,1)}, bf16[32,64,128]{2,1,0:T(8,128)(2,1)S(1)}, u32[]{:S(2)}, u32[]{:S(2)}) collective-permute-start(bf16[32,64,128]{2,1,0:T(8,128)(2,1)} %get-tuple-element.16), channel_id=1, source_target_pairs={{0,68},{1,69},{2,70},{3,71},{4,64},{5,65},{6,66},{7,67},{8,76},{9,... | collective-permute-start | bytes 1572872 | tf_op jit(solution)/shard_map/ppermute | solution.py:64
  127.8 33.0 %collective-permute-start.23 = (bf16[32,64,128]{2,1,0:T(8,128)(2,1)S(1)}, bf16[32,64,128]{2,1,0:T(8,128)(2,1)S(1)}, u32[]{:S(2)}, u32[]{:S(2)}) collective-permute-start(bf16[32,64,128]{2,1,0:T(8,128)(2,1)S(1)} %get-tuple-element.22), channel_id=1, source_target_pairs={{0,1},{1,0},{2,3},{3,2},{4,5},{5,4},{6,7},{7,6},{8,9},{9,8},{10,11... | collective-permute-start | bytes 1572872 | tf_op jit(solution)/shard_map/ppermute | solution.py:58
  127.8 44.6 %collective-permute-start.22 = (bf16[32,64,128]{2,1,0:T(8,128)(2,1)}, bf16[32,64,128]{2,1,0:T(8,128)(2,1)S(1)}, u32[]{:S(2)}, u32[]{:S(2)}) collective-permute-start(bf16[32,64,128]{2,1,0:T(8,128)(2,1)} %get-tuple-element.23), channel_id=1, source_target_pairs={{0,8},{8,0},{16,24},{24,16},{32,40},{40,32},{48,56},{56,48},{64,72... | collective-permute-start | bytes 1572872 | tf_op jit(solution)/shard_map/ppermute | solution.py:55
  138.1 38.2 %collective-permute-start.21 = (bf16[32,64,128]{2,1,0:T(8,128)(2,1)}, bf16[32,64,128]{2,1,0:T(8,128)(2,1)S(1)}, u32[]{:S(2)}, u32[]{:S(2)}) collective-permute-start(bf16[32,64,128]{2,1,0:T(8,128)(2,1)} %get-tuple-element.24), channel_id=1, source_target_pairs={{0,9},{1,8},{2,11},{3,10},{4,13},{5,12},{6,15},{7,14},{8,1},{9,0},... | collective-permute-start | bytes 1572872 | tf_op jit(solution)/shard_map/ppermute | solution.py:64
  152.9 30.4 %collective-permute-start.11 = (bf16[32,64,128]{2,1,0:T(8,128)(2,1)}, bf16[32,64,128]{2,1,0:T(8,128)(2,1)}, u32[]{:S(2)}, u32[]{:S(2)}) collective-permute-start(bf16[32,64,128]{2,1,0:T(8,128)(2,1)} %get-tuple-element.30), channel_id=1, source_target_pairs={{0,1},{1,0},{2,3},{3,2},{4,5},{5,4},{6,7},{7,6},{8,9},{9,8},{10,11... | collective-permute-start | bytes 1572872 | tf_op jit(solution)/shard_map/ppermute | solution.py:58
  152.9 33.5 %collective-permute-start.10 = (bf16[32,64,128]{2,1,0:T(8,128)(2,1)}, bf16[32,64,128]{2,1,0:T(8,128)(2,1)S(1)}, u32[]{:S(2)}, u32[]{:S(2)}) collective-permute-start(bf16[32,64,128]{2,1,0:T(8,128)(2,1)} %get-tuple-element.31), channel_id=1, source_target_pairs={{0,8},{8,0},{16,24},{24,16},{32,40},{40,32},{48,56},{56,48},{64,72... | collective-permute-start | bytes 1572872 | tf_op jit(solution)/shard_map/ppermute | solution.py:55
  160.8 33.8 %collective-permute-start.9 = (bf16[32,64,128]{2,1,0:T(8,128)(2,1)}, bf16[32,64,128]{2,1,0:T(8,128)(2,1)}, u32[]{:S(2)}, u32[]{:S(2)}) collective-permute-start(bf16[32,64,128]{2,1,0:T(8,128)(2,1)} %get-tuple-element.32), channel_id=1, source_target_pairs={{0,9},{1,8},{2,11},{3,10},{4,13},{5,12},{6,15},{7,14},{8,1},{9,0},... | collective-permute-start | bytes 1572872 | tf_op jit(solution)/shard_map/ppermute | solution.py:64
  (15 other events, 129.6 us)

commit v7 on v5

--- a/solution.py
+++ b/solution.py
@@ -252,7 +252,7 @@
             target=gradient,
         )
 
-    gradient = jnp.zeros(shape5, jnp.bfloat16)
+    gradient = None
     for m in range(CHUNKS):
         coef = [local_forward(m, f) for f in range(4)]
         pieces = exchange(coef, *shifts[0])

time: 195 us -> 195 us (level)
  local copies, waits for them, and re-layouts: 17.7 us -> 14.6 us
  waiting for transfers between devices: 50.7 us -> 53.7 us
    broadcast_in_dim x1 -> x0, local copies, waits for them, and re-layouts: 3.08 us -> none  [local(): gradient = jnp.zeros(shape5, jnp.bfloat16)]
    ppermute x8, waiting for transfers between devices: 6.05 us -> 9.12 us  [flip_send(): return lax.ppermute(value, ('qx', 'qy'), pairs)]
  transfers between devices with their start and end apart: 24 -> 24, of which waited for: 9 -> 9; matrix products, arithmetic and copies ran while one was open for 10% -> 8% of each run, Pallas kernels for 30% -> 30%
where the time goes in v7:
time: 195 us; the launch traced here: 194 us
  Pallas kernels  62.7 us (32%)
  waiting for transfers between devices  53.7 us (28%)
  starting transfers between devices  53.6 us (27%)
  local copies, waits for them, and re-layouts  14.6 us (7%)
  matrix products  6.8 us (3%)
  other arithmetic  2.27 us (1%)
    pallas_call x16, Pallas kernels, chain_call(): pl.pallas_call(functools.partial(chain_kernel, plan), grid_spec=pltpu.Pre...  42.9 us
    ppermute x8, waiting for transfers between devices, flip_send(): return lax.ppermute(value, 'qx', pairs)  28.8 us
    ppermute x8, starting transfers between devices, flip_send(): return lax.ppermute(value, ('qx', 'qy'), pairs)  23 us
    pallas_call x2, Pallas kernels, output_stage(): pl.pallas_call(output_stage_kernel, grid=(part // step,), in_specs=[piece...  19.9 us
    ppermute x8, starting transfers between devices, flip_send(): return lax.ppermute(value, 'qx', pairs)  16.3 us
    ppermute x8, waiting for transfers between devices, flip_send(): return lax.ppermute(value, 'qy', pairs)  15.8 us
    ppermute x8, starting transfers between devices, flip_send(): return lax.ppermute(value, 'qy', pairs)  14.3 us
    ppermute x8, waiting for transfers between devices, flip_send(): return lax.ppermute(value, ('qx', 'qy'), pairs)  9.12 us
  transfers between devices with their start and end apart: 24, of which 9 were waited for; matrix products, arithmetic and copies ran while one was open for 8% of the time, Pallas kernels for 30%

profile of v7, /device:TPU:1, one launch (start us, length us, event | category | flops | bytes accessed | tf_op | source)
XLA Modules:
  0.0 194.1 jit_solution(5095040863025572047)
XLA Ops:
  12.4 2.7 %shard_map.81 = bf16[32,64,128]{2,1,0:T(8,128)(2,1)} custom-call(s32[1]{0:T(128)} %bitcast.k_ref, bf16[4,2,32,64,128]{4,3,2,1,0:T(8,128)(2,1)} %bitcast.167, bf16[3,256,256]{2,1,0:T(8,128)(2,1)} %pad_maximum_fusion.4.m_ref), custom_call_target="tpu_custom_call" | custom-call | tf_op jit(solution)/shard_map/pallas_call | solution.py:154
  19.6 2.7 %shard_map.74 = bf16[32,64,128]{2,1,0:T(8,128)(2,1)} custom-call(s32[1]{0:T(128)} %bitcast.k_ref, bf16[4,2,32,64,128]{4,3,2,1,0:T(8,128)(2,1)} %bitcast.169, bf16[3,256,256]{2,1,0:T(8,128)(2,1)} %pad_maximum_fusion.4.m_ref), custom_call_target="tpu_custom_call" | custom-call | tf_op jit(solution)/shard_map/pallas_call | solution.py:154
  22.5 2.7 %shard_map.78 = bf16[32,64,128]{2,1,0:T(8,128)(2,1)} custom-call(s32[1]{0:T(128)} %bitcast.k_ref, bf16[4,2,32,64,128]{4,3,2,1,0:T(8,128)(2,1)} %bitcast.170, bf16[3,256,256]{2,1,0:T(8,128)(2,1)} %pad_maximum_fusion.4.m_ref), custom_call_target="tpu_custom_call" | custom-call | tf_op jit(solution)/shard_map/pallas_call | solution.py:154
  25.2 2.7 %shard_map.75 = bf16[32,64,128]{2,1,0:T(8,128)(2,1)} custom-call(s32[1]{0:T(128)} %bitcast.k_ref, bf16[4,2,32,64,128]{4,3,2,1,0:T(8,128)(2,1)} %bitcast.171, bf16[3,256,256]{2,1,0:T(8,128)(2,1)} %pad_maximum_fusion.4.m_ref), custom_call_target="tpu_custom_call" | custom-call | tf_op jit(solution)/shard_map/pallas_call | solution.py:154
  37.0 3.0 %collective-permute-start.15 = (bf16[32,64,128]{2,1,0:T(8,128)(2,1)}, bf16[32,64,128]{2,1,0:T(8,128)(2,1)}, u32[]{:S(2)}, u32[]{:S(2)}) collective-permute-start(bf16[32,64,128]{2,1,0:T(8,128)(2,1)} %get-tuple-element.27), channel_id=1, source_target_pairs={{0,4},{1,5},{2,6},{3,7},{4,0},{5,1},{6,2},{7,3},{8,12},{9,13},{10,... | collective-permute-start | bytes 1572872 | tf_op jit(solution)/shard_map/ppermute | solution.py:58
  40.0 3.6 %collective-permute-start.16 = (bf16[32,64,128]{2,1,0:T(8,128)(2,1)}, bf16[32,64,128]{2,1,0:T(8,128)(2,1)}, u32[]{:S(2)}, u32[]{:S(2)}) collective-permute-start(bf16[32,64,128]{2,1,0:T(8,128)(2,1)} %get-tuple-element.26), channel_id=1, source_target_pairs={{0,64},{8,72},{16,80},{24,88},{32,96},{40,104},{48,112},{56,120},{... | collective-permute-start | bytes 1572872 | tf_op jit(solution)/shard_map/ppermute | solution.py:55
  44.9 6.3 %collective-permute-start.17 = (bf16[32,64,128]{2,1,0:T(8,128)(2,1)S(1)}, bf16[32,64,128]{2,1,0:T(8,128)(2,1)}, u32[]{:S(2)}, u32[]{:S(2)}) collective-permute-start(bf16[32,64,128]{2,1,0:T(8,128)(2,1)S(1)} %get-tuple-element.25), channel_id=1, source_target_pairs={{0,68},{1,69},{2,70},{3,71},{4,64},{5,65},{6,66},{7,67},{8,76},{9,... | collective-permute-start | bytes 1572872 | tf_op jit(solution)/shard_map/ppermute | solution.py:64
  51.2 14.4 %collective-permute-done = bf16[32,64,128]{2,1,0:T(8,128)(2,1)} collective-permute-done((bf16[32,64,128]{2,1,0:T(8,128)(2,1)}, bf16[32,64,128]{2,1,0:T(8,128)(2,1)}, u32[]{:S(2)}, u32[]{:S(2)}) %collective-permute-start) | collective-permute-done | bytes 524320 | tf_op jit(solution)/shard_map/ppermute | solution.py:58
  68.8 2.8 %collective-permute-start.3 = (bf16[32,64,128]{2,1,0:T(8,128)(2,1)}, bf16[32,64,128]{2,1,0:T(8,128)(2,1)}, u32[]{:S(2)}, u32[]{:S(2)}) collective-permute-start(bf16[32,64,128]{2,1,0:T(8,128)(2,1)} %get-tuple-element.35), channel_id=1, source_target_pairs={{0,4},{1,5},{2,6},{3,7},{4,0},{5,1},{6,2},{7,3},{8,12},{9,13},{10,... | collective-permute-start | bytes 1572872 | tf_op jit(solution)/shard_map/ppermute | solution.py:58
  73.8 3.2 %collective-permute-start.4 = (bf16[32,64,128]{2,1,0:T(8,128)(2,1)}, bf16[32,64,128]{2,1,0:T(8,128)(2,1)S(1)}, u32[]{:S(2)}, u32[]{:S(2)}) collective-permute-start(bf16[32,64,128]{2,1,0:T(8,128)(2,1)} %get-tuple-element.34), channel_id=1, source_target_pairs={{0,64},{8,72},{16,80},{24,88},{32,96},{40,104},{48,112},{56,120},{... | collective-permute-start | bytes 1572872 | tf_op jit(solution)/shard_map/ppermute | solution.py:55
  77.1 2.8 %collective-permute-done.16.p2 = bf16[32,64,128]{2,1,0:T(8,128)(2,1)} collective-permute-done((bf16[32,64,128]{2,1,0:T(8,128)(2,1)}, bf16[32,64,128]{2,1,0:T(8,128)(2,1)}, u32[]{:S(2)}, u32[]{:S(2)}) %collective-permute-start.16) | collective-permute-done | bytes 524320 | tf_op jit(solution)/shard_map/ppermute | solution.py:55
  79.9 9.9 %shard_map.82 = (bf16[32,64,128]{2,1,0:T(8,128)(2,1)}, bf16[32,64,128]{2,1,0:T(8,128)(2,1)}, bf16[32,64,128]{2,1,0:T(8,128)(2,1)}, bf16[32,64,128]{2,1,0:T(8,128)(2,1)}) custom-call(bf16[32,64,128]{2,1,0:T(8,128)(2,1)} %get-tuple-element.28.p0, bf16[32,64,128]{2,1,0:T(8,128)(2,1)} %collective-permute-done.15.p1, ...), custom_call_target="tpu_custom_call" | custom-call | flops 2147483648 | bytes 10485760 | tf_op jit(solution)/shard_map/pallas_call | solution.py:173
  89.8 3.0 %collective-permute-start.18 = (bf16[32,64,128]{2,1,0:T(8,128)(2,1)}, bf16[32,64,128]{2,1,0:T(8,128)(2,1)S(1)}, u32[]{:S(2)}, u32[]{:S(2)}) collective-permute-start(bf16[32,64,128]{2,1,0:T(8,128)(2,1)} %get-tuple-element.18), channel_id=1, source_target_pairs={{0,4},{1,5},{2,6},{3,7},{4,0},{5,1},{6,2},{7,3},{8,12},{9,13},{10,... | collective-permute-start | bytes 1572872 | tf_op jit(solution)/shard_map/ppermute | solution.py:58
  92.8 2.8 %collective-permute-start.20 = (bf16[32,64,128]{2,1,0:T(8,128)(2,1)}, bf16[32,64,128]{2,1,0:T(8,128)(2,1)}, u32[]{:S(2)}, u32[]{:S(2)}) collective-permute-start(bf16[32,64,128]{2,1,0:T(8,128)(2,1)} %get-tuple-element.20), channel_id=1, source_target_pairs={{0,68},{1,69},{2,70},{3,71},{4,64},{5,65},{6,66},{7,67},{8,76},{9,... | collective-permute-start | bytes 1572872 | tf_op jit(solution)/shard_map/ppermute | solution.py:64
  95.6 6.6 %collective-permute-done.4.p2 = bf16[32,64,128]{2,1,0:T(8,128)(2,1)S(1)} collective-permute-done((bf16[32,64,128]{2,1,0:T(8,128)(2,1)}, bf16[32,64,128]{2,1,0:T(8,128)(2,1)S(1)}, u32[]{:S(2)}, u32[]{:S(2)}) %collective-permute-start.4) | collective-permute-done | bytes 524320 | tf_op jit(solution)/shard_map/ppermute | solution.py:55
  103.0 9.9 %shard_map.77 = (bf16[32,64,128]{2,1,0:T(8,128)(2,1)}, bf16[32,64,128]{2,1,0:T(8,128)(2,1)}, bf16[32,64,128]{2,1,0:T(8,128)(2,1)}, bf16[32,64,128]{2,1,0:T(8,128)(2,1)}) custom-call(bf16[32,64,128]{2,1,0:T(8,128)(2,1)} %get-tuple-element.36.p0, bf16[32,64,128]{2,1,0:T(8,128)(2,1)} %collective-permute-done.3.p1, bf16[32,64,128]{2,1,0:T(8,128)(2,1)} %copy-done.10, ...), custom_call_target="tpu_custom_call" | custom-call | flops 2147483648 | bytes 10485760 | tf_op jit(solution)/shard_map/pallas_call | solution.py:173
  113.0 3.0 %collective-permute-start.6 = (bf16[32,64,128]{2,1,0:T(8,128)(2,1)}, bf16[32,64,128]{2,1,0:T(8,128)(2,1)S(1)}, u32[]{:S(2)}, u32[]{:S(2)}) collective-permute-start(bf16[32,64,128]{2,1,0:T(8,128)(2,1)} %get-tuple-element.14), channel_id=1, source_target_pairs={{0,4},{1,5},{2,6},{3,7},{4,0},{5,1},{6,2},{7,3},{8,12},{9,13},{10,... | collective-permute-start | bytes 1572872 | tf_op jit(solution)/shard_map/ppermute | solution.py:58
  116.0 2.8 %collective-permute-start.8 = (bf16[32,64,128]{2,1,0:T(8,128)(2,1)}, bf16[32,64,128]{2,1,0:T(8,128)(2,1)S(1)}, u32[]{:S(2)}, u32[]{:S(2)}) collective-permute-start(bf16[32,64,128]{2,1,0:T(8,128)(2,1)} %get-tuple-element.16), channel_id=1, source_target_pairs={{0,68},{1,69},{2,70},{3,71},{4,64},{5,65},{6,66},{7,67},{8,76},{9,... | collective-permute-start | bytes 1572872 | tf_op jit(solution)/shard_map/ppermute | solution.py:64
  118.7 6.1 %collective-permute-done.19 = bf16[32,64,128]{2,1,0:T(8,128)(2,1)} collective-permute-done((bf16[32,64,128]{2,1,0:T(8,128)(2,1)}, bf16[32,64,128]{2,1,0:T(8,128)(2,1)}, u32[]{:S(2)}, u32[]{:S(2)}) %collective-permute-start.19) | collective-permute-done | bytes 524320 | tf_op jit(solution)/shard_map/ppermute | solution.py:55
  128.0 4.0 %collective-permute-start.22 = (bf16[32,64,128]{2,1,0:T(8,128)(2,1)}, bf16[32,64,128]{2,1,0:T(8,128)(2,1)S(1)}, u32[]{:S(2)}, u32[]{:S(2)}) collective-permute-start(bf16[32,64,128]{2,1,0:T(8,128)(2,1)} %get-tuple-element.23), channel_id=1, source_target_pairs={{0,8},{8,0},{16,24},{24,16},{32,40},{40,32},{48,56},{56,48},{64,72... | collective-permute-start | bytes 1572872 | tf_op jit(solution)/shard_map/ppermute | solution.py:55
  133.8 13.3 %collective-permute-done.7 = bf16[32,64,128]{2,1,0:T(8,128)(2,1)S(1)} collective-permute-done((bf16[32,64,128]{2,1,0:T(8,128)(2,1)}, bf16[32,64,128]{2,1,0:T(8,128)(2,1)S(1)}, u32[]{:S(2)}, u32[]{:S(2)}) %collective-permute-start.7) | collective-permute-done | bytes 524320 | tf_op jit(solution)/shard_map/ppermute | solution.py:55
  149.3 4.0 %collective-permute-start.10 = (bf16[32,64,128]{2,1,0:T(8,128)(2,1)}, bf16[32,64,128]{2,1,0:T(8,128)(2,1)S(1)}, u32[]{:S(2)}, u32[]{:S(2)}) collective-permute-start(bf16[32,64,128]{2,1,0:T(8,128)(2,1)} %get-tuple-element.31), channel_id=1, source_target_pairs={{0,8},{8,0},{16,24},{24,16},{32,40},{40,32},{48,56},{56,48},{64,72... | collective-permute-start | bytes 1572872 | tf_op jit(solution)/shard_map/ppermute | solution.py:55
  154.7 7.5 %collective-permute-start.9 = (bf16[32,64,128]{2,1,0:T(8,128)(2,1)}, bf16[32,64,128]{2,1,0:T(8,128)(2,1)}, u32[]{:S(2)}, u32[]{:S(2)}) collective-permute-start(bf16[32,64,128]{2,1,0:T(8,128)(2,1)} %get-tuple-element.32), channel_id=1, source_target_pairs={{0,9},{1,8},{2,11},{3,10},{4,13},{5,12},{6,15},{7,14},{8,1},{9,0},... | collective-permute-start | bytes 1572872 | tf_op jit(solution)/shard_map/ppermute | solution.py:64
  185.1 6.3 %collective-permute-done.9.x_ref = bf16[32,64,128]{2,1,0:T(8,128)(2,1)} collective-permute-done((bf16[32,64,128]{2,1,0:T(8,128)(2,1)}, bf16[32,64,128]{2,1,0:T(8,128)(2,1)}, u32[]{:S(2)}, u32[]{:S(2)}) %collective-permute-start.9) | collective-permute-done | bytes 524320 | tf_op jit(solution)/shard_map/ppermute | solution.py:64
  (111 shorter events, 67.6 us)
Async XLA Ops:
  6.3 24.7 %collective-permute-start.12 = (bf16[32,64,128]{2,1,0:T(8,128)(2,1)}, bf16[32,64,128]{2,1,0:T(8,128)(2,1)}, u32[]{:S(2)}, u32[]{:S(2)}) collective-permute-start(bf16[32,64,128]{2,1,0:T(8,128)(2,1)} %shard_map.79), channel_id=1, source_target_pairs={{0,1},{1,0},{2,3},{3,2},{4,5},{5,4},{6,7},{7,6},{8,9},{9,8},{10,11... | collective-permute-start | bytes 1572872 | tf_op jit(solution)/shard_map/ppermute | solution.py:58
  11.4 20.6 %collective-permute-start.13 = (bf16[32,64,128]{2,1,0:T(8,128)(2,1)}, bf16[32,64,128]{2,1,0:T(8,128)(2,1)}, u32[]{:S(2)}, u32[]{:S(2)}) collective-permute-start(bf16[32,64,128]{2,1,0:T(8,128)(2,1)} %shard_map.80), channel_id=1, source_target_pairs={{0,8},{8,0},{16,24},{24,16},{32,40},{40,32},{48,56},{56,48},{64,72... | collective-permute-start | bytes 1572872 | tf_op jit(solution)/shard_map/ppermute | solution.py:55
  15.1 18.5 %collective-permute-start.14 = (bf16[32,64,128]{2,1,0:T(8,128)(2,1)}, bf16[32,64,128]{2,1,0:T(8,128)(2,1)}, u32[]{:S(2)}, u32[]{:S(2)}) collective-permute-start(bf16[32,64,128]{2,1,0:T(8,128)(2,1)} %shard_map.81), channel_id=1, source_target_pairs={{0,9},{1,8},{2,11},{3,10},{4,13},{5,12},{6,15},{7,14},{8,1},{9,0},... | collective-permute-start | bytes 1572872 | tf_op jit(solution)/shard_map/ppermute | solution.py:64
  17.8 27.1 %collective-permute-start.2 = (bf16[32,64,128]{2,1,0:T(8,128)(2,1)}, bf16[32,64,128]{2,1,0:T(8,128)(2,1)}, u32[]{:S(2)}, u32[]{:S(2)}) collective-permute-start(bf16[32,64,128]{2,1,0:T(8,128)(2,1)} %shard_map.76), channel_id=1, source_target_pairs={{0,9},{1,8},{2,11},{3,10},{4,13},{5,12},{6,15},{7,14},{8,1},{9,0},... | collective-permute-start | bytes 1572872 | tf_op jit(solution)/shard_map/ppermute | solution.py:64
  22.3 43.3 %collective-permute-start = (bf16[32,64,128]{2,1,0:T(8,128)(2,1)}, bf16[32,64,128]{2,1,0:T(8,128)(2,1)}, u32[]{:S(2)}, u32[]{:S(2)}) collective-permute-start(bf16[32,64,128]{2,1,0:T(8,128)(2,1)} %shard_map.74), channel_id=1, source_target_pairs={{0,1},{1,0},{2,3},{3,2},{4,5},{5,4},{6,7},{7,6},{8,9},{9,8},{10,11... | collective-permute-start | bytes 1572872 | tf_op jit(solution)/shard_map/ppermute | solution.py:58
  31.6 34.0 %collective-permute-start.1 = (bf16[32,64,128]{2,1,0:T(8,128)(2,1)S(1)}, bf16[32,64,128]{2,1,0:T(8,128)(2,1)S(1)}, u32[]{:S(2)}, u32[]{:S(2)}) collective-permute-start(bf16[32,64,128]{2,1,0:T(8,128)(2,1)S(1)} %copy-done.8), channel_id=1, source_target_pairs={{0,8},{8,0},{16,24},{24,16},{32,40},{40,32},{48,56},{56,48},{64,72... | collective-permute-start | bytes 1572872 | tf_op jit(solution)/shard_map/ppermute | solution.py:55
  37.0 40.1 %collective-permute-start.15 = (bf16[32,64,128]{2,1,0:T(8,128)(2,1)}, bf16[32,64,128]{2,1,0:T(8,128)(2,1)}, u32[]{:S(2)}, u32[]{:S(2)}) collective-permute-start(bf16[32,64,128]{2,1,0:T(8,128)(2,1)} %get-tuple-element.27), channel_id=1, source_target_pairs={{0,4},{1,5},{2,6},{3,7},{4,0},{5,1},{6,2},{7,3},{8,12},{9,13},{10,... | collective-permute-start | bytes 1572872 | tf_op jit(solution)/shard_map/ppermute | solution.py:58
  40.0 39.9 %collective-permute-start.16 = (bf16[32,64,128]{2,1,0:T(8,128)(2,1)}, bf16[32,64,128]{2,1,0:T(8,128)(2,1)}, u32[]{:S(2)}, u32[]{:S(2)}) collective-permute-start(bf16[32,64,128]{2,1,0:T(8,128)(2,1)} %get-tuple-element.26), channel_id=1, source_target_pairs={{0,64},{8,72},{16,80},{24,88},{32,96},{40,104},{48,112},{56,120},{... | collective-permute-start | bytes 1572872 | tf_op jit(solution)/shard_map/ppermute | solution.py:55
  44.9 35.0 %collective-permute-start.17 = (bf16[32,64,128]{2,1,0:T(8,128)(2,1)S(1)}, bf16[32,64,128]{2,1,0:T(8,128)(2,1)}, u32[]{:S(2)}, u32[]{:S(2)}) collective-permute-start(bf16[32,64,128]{2,1,0:T(8,128)(2,1)S(1)} %get-tuple-element.25), channel_id=1, source_target_pairs={{0,68},{1,69},{2,70},{3,71},{4,64},{5,65},{6,66},{7,67},{8,76},{9,... | collective-permute-start | bytes 1572872 | tf_op jit(solution)/shard_map/ppermute | solution.py:64
  68.8 24.0 %collective-permute-start.3 = (bf16[32,64,128]{2,1,0:T(8,128)(2,1)}, bf16[32,64,128]{2,1,0:T(8,128)(2,1)}, u32[]{:S(2)}, u32[]{:S(2)}) collective-permute-start(bf16[32,64,128]{2,1,0:T(8,128)(2,1)} %get-tuple-element.35), channel_id=1, source_target_pairs={{0,4},{1,5},{2,6},{3,7},{4,0},{5,1},{6,2},{7,3},{8,12},{9,13},{10,... | collective-permute-start | bytes 1572872 | tf_op jit(solution)/shard_map/ppermute | solution.py:58
  73.8 28.4 %collective-permute-start.4 = (bf16[32,64,128]{2,1,0:T(8,128)(2,1)}, bf16[32,64,128]{2,1,0:T(8,128)(2,1)S(1)}, u32[]{:S(2)}, u32[]{:S(2)}) collective-permute-start(bf16[32,64,128]{2,1,0:T(8,128)(2,1)} %get-tuple-element.34), channel_id=1, source_target_pairs={{0,64},{8,72},{16,80},{24,88},{32,96},{40,104},{48,112},{56,120},{... | collective-permute-start | bytes 1572872 | tf_op jit(solution)/shard_map/ppermute | solution.py:55
  77.1 25.2 %collective-permute-start.5 = (bf16[32,64,128]{2,1,0:T(8,128)(2,1)S(1)}, bf16[32,64,128]{2,1,0:T(8,128)(2,1)}, u32[]{:S(2)}, u32[]{:S(2)}) collective-permute-start(bf16[32,64,128]{2,1,0:T(8,128)(2,1)S(1)} %get-tuple-element.33), channel_id=1, source_target_pairs={{0,68},{1,69},{2,70},{3,71},{4,64},{5,65},{6,66},{7,67},{8,76},{9,... | collective-permute-start | bytes 1572872 | tf_op jit(solution)/shard_map/ppermute | solution.py:64
  89.8 26.2 %collective-permute-start.18 = (bf16[32,64,128]{2,1,0:T(8,128)(2,1)}, bf16[32,64,128]{2,1,0:T(8,128)(2,1)S(1)}, u32[]{:S(2)}, u32[]{:S(2)}) collective-permute-start(bf16[32,64,128]{2,1,0:T(8,128)(2,1)} %get-tuple-element.18), channel_id=1, source_target_pairs={{0,4},{1,5},{2,6},{3,7},{4,0},{5,1},{6,2},{7,3},{8,12},{9,13},{10,... | collective-permute-start | bytes 1572872 | tf_op jit(solution)/shard_map/ppermute | solution.py:58
  92.8 32.0 %collective-permute-start.19 = (bf16[32,64,128]{2,1,0:T(8,128)(2,1)}, bf16[32,64,128]{2,1,0:T(8,128)(2,1)}, u32[]{:S(2)}, u32[]{:S(2)}) collective-permute-start(bf16[32,64,128]{2,1,0:T(8,128)(2,1)} %get-tuple-element.19), channel_id=1, source_target_pairs={{0,64},{8,72},{16,80},{24,88},{32,96},{40,104},{48,112},{56,120},{... | collective-permute-start | bytes 1572872 | tf_op jit(solution)/shard_map/ppermute | solution.py:55
  92.8 32.0 %collective-permute-start.20 = (bf16[32,64,128]{2,1,0:T(8,128)(2,1)}, bf16[32,64,128]{2,1,0:T(8,128)(2,1)}, u32[]{:S(2)}, u32[]{:S(2)}) collective-permute-start(bf16[32,64,128]{2,1,0:T(8,128)(2,1)} %get-tuple-element.20), channel_id=1, source_target_pairs={{0,68},{1,69},{2,70},{3,71},{4,64},{5,65},{6,66},{7,67},{8,76},{9,... | collective-permute-start | bytes 1572872 | tf_op jit(solution)/shard_map/ppermute | solution.py:64
  113.0 19.0 %collective-permute-start.6 = (bf16[32,64,128]{2,1,0:T(8,128)(2,1)}, bf16[32,64,128]{2,1,0:T(8,128)(2,1)S(1)}, u32[]{:S(2)}, u32[]{:S(2)}) collective-permute-start(bf16[32,64,128]{2,1,0:T(8,128)(2,1)} %get-tuple-element.14), channel_id=1, source_target_pairs={{0,4},{1,5},{2,6},{3,7},{4,0},{5,1},{6,2},{7,3},{8,12},{9,13},{10,... | collective-permute-start | bytes 1572872 | tf_op jit(solution)/shard_map/ppermute | solution.py:58
  116.0 31.2 %collective-permute-start.7 = (bf16[32,64,128]{2,1,0:T(8,128)(2,1)}, bf16[32,64,128]{2,1,0:T(8,128)(2,1)S(1)}, u32[]{:S(2)}, u32[]{:S(2)}) collective-permute-start(bf16[32,64,128]{2,1,0:T(8,128)(2,1)} %get-tuple-element.15), channel_id=1, source_target_pairs={{0,64},{8,72},{16,80},{24,88},{32,96},{40,104},{48,112},{56,120},{... | collective-permute-start | bytes 1572872 | tf_op jit(solution)/shard_map/ppermute | solution.py:55
  116.0 31.2 %collective-permute-start.8 = (bf16[32,64,128]{2,1,0:T(8,128)(2,1)}, bf16[32,64,128]{2,1,0:T(8,128)(2,1)S(1)}, u32[]{:S(2)}, u32[]{:S(2)}) collective-permute-start(bf16[32,64,128]{2,1,0:T(8,128)(2,1)} %get-tuple-element.16), channel_id=1, source_target_pairs={{0,68},{1,69},{2,70},{3,71},{4,64},{5,65},{6,66},{7,67},{8,76},{9,... | collective-permute-start | bytes 1572872 | tf_op jit(solution)/shard_map/ppermute | solution.py:64
  128.0 26.7 %collective-permute-start.23 = (bf16[32,64,128]{2,1,0:T(8,128)(2,1)S(1)}, bf16[32,64,128]{2,1,0:T(8,128)(2,1)S(1)}, u32[]{:S(2)}, u32[]{:S(2)}) collective-permute-start(bf16[32,64,128]{2,1,0:T(8,128)(2,1)S(1)} %get-tuple-element.22), channel_id=1, source_target_pairs={{0,1},{1,0},{2,3},{3,2},{4,5},{5,4},{6,7},{7,6},{8,9},{9,8},{10,11... | collective-permute-start | bytes 1572872 | tf_op jit(solution)/shard_map/ppermute | solution.py:58
  128.0 41.4 %collective-permute-start.22 = (bf16[32,64,128]{2,1,0:T(8,128)(2,1)}, bf16[32,64,128]{2,1,0:T(8,128)(2,1)S(1)}, u32[]{:S(2)}, u32[]{:S(2)}) collective-permute-start(bf16[32,64,128]{2,1,0:T(8,128)(2,1)} %get-tuple-element.23), channel_id=1, source_target_pairs={{0,8},{8,0},{16,24},{24,16},{32,40},{40,32},{48,56},{56,48},{64,72... | collective-permute-start | bytes 1572872 | tf_op jit(solution)/shard_map/ppermute | solution.py:55
  132.0 40.9 %collective-permute-start.21 = (bf16[32,64,128]{2,1,0:T(8,128)(2,1)}, bf16[32,64,128]{2,1,0:T(8,128)(2,1)S(1)}, u32[]{:S(2)}, u32[]{:S(2)}) collective-permute-start(bf16[32,64,128]{2,1,0:T(8,128)(2,1)} %get-tuple-element.24), channel_id=1, source_target_pairs={{0,9},{1,8},{2,11},{3,10},{4,13},{5,12},{6,15},{7,14},{8,1},{9,0},... | collective-permute-start | bytes 1572872 | tf_op jit(solution)/shard_map/ppermute | solution.py:64
  149.3 29.7 %collective-permute-start.11 = (bf16[32,64,128]{2,1,0:T(8,128)(2,1)}, bf16[32,64,128]{2,1,0:T(8,128)(2,1)}, u32[]{:S(2)}, u32[]{:S(2)}) collective-permute-start(bf16[32,64,128]{2,1,0:T(8,128)(2,1)} %get-tuple-element.30), channel_id=1, source_target_pairs={{0,1},{1,0},{2,3},{3,2},{4,5},{5,4},{6,7},{7,6},{8,9},{9,8},{10,11... | collective-permute-start | bytes 1572872 | tf_op jit(solution)/shard_map/ppermute | solution.py:58
  149.3 32.3 %collective-permute-start.10 = (bf16[32,64,128]{2,1,0:T(8,128)(2,1)}, bf16[32,64,128]{2,1,0:T(8,128)(2,1)S(1)}, u32[]{:S(2)}, u32[]{:S(2)}) collective-permute-start(bf16[32,64,128]{2,1,0:T(8,128)(2,1)} %get-tuple-element.31), channel_id=1, source_target_pairs={{0,8},{8,0},{16,24},{24,16},{32,40},{40,32},{48,56},{56,48},{64,72... | collective-permute-start | bytes 1572872 | tf_op jit(solution)/shard_map/ppermute | solution.py:55
  154.7 36.7 %collective-permute-start.9 = (bf16[32,64,128]{2,1,0:T(8,128)(2,1)}, bf16[32,64,128]{2,1,0:T(8,128)(2,1)}, u32[]{:S(2)}, u32[]{:S(2)}) collective-permute-start(bf16[32,64,128]{2,1,0:T(8,128)(2,1)} %get-tuple-element.32), channel_id=1, source_target_pairs={{0,9},{1,8},{2,11},{3,10},{4,13},{5,12},{6,15},{7,14},{8,1},{9,0},... | collective-permute-start | bytes 1572872 | tf_op jit(solution)/shard_map/ppermute | solution.py:64
  (15 other events, 114.5 us)

commit v8 on v7

--- a/solution.py
+++ b/solution.py
@@ -159,6 +159,73 @@
         out_shape=out_shape,
         input_output_aliases=aliases,
     )(*operands)
+
+
+def level0_kernel(plan, x_shift, y_shift, img_ref, mat_ref, out_ref, send_buf, send_sem,
+                  recv_sem):
+    t = lax.axis_index("qx")
+    u = lax.axis_index("qy")
+    k0 = 2 * (jnp.right_shift(t, x_shift) & 1) + (jnp.right_shift(u, y_shift) & 1)
+
+    def partner(f):
+        tt = jnp.bitwise_xor(t, 1 << x_shift) if f & 2 else t
+        uu = jnp.bitwise_xor(u, 1 << y_shift) if f & 1 else u
+        return (tt, uu)
+
+    barrier = pltpu.get_barrier_semaphore()
+    for f in (1, 2, 3):
+        pl.semaphore_signal(
+            barrier, inc=1, device_id=partner(f), device_id_type=pl.DeviceIdType.MESH
+        )
+    pl.semaphore_wait(barrier, 3)
+    chunks = img_ref.shape[1]
+    count = img_ref.shape[2]
+    copies = []
+    for m in range(chunks):
+        for f in (1, 2, 3, 0):
+            q = jnp.bitwise_xor(k0, f)
+            cur = [img_ref[q, m, g] for g in range(count)]
+            for index, sets in enumerate(plan):
+                cur = chain_stage(cur, mat_ref[index], sets)
+            if f == 0:
+                for g in range(count):
+                    out_ref[m, 0, g] = cur[g]
+                continue
+            for g in range(count):
+                send_buf[m, f - 1, g] = cur[g]
+            copy = pltpu.make_async_remote_copy(
+                src_ref=send_buf.at[m, f - 1],
+                dst_ref=out_ref.at[m, f],
+                send_sem=send_sem.at[m, f - 1],
+                recv_sem=recv_sem.at[m, f - 1],
+                device_id=partner(f),
+                device_id_type=pl.DeviceIdType.MESH,
+            )
+            copy.start()
+            copies.append(copy)
+    for copy in copies:
+        copy.wait()
+
+
+def level0_forward(plan, shifts, image, mats):
+    _, chunks, count, rank_size, inner_boxes = image.shape
+    vmem = pltpu.MemorySpace.VMEM if hasattr(pltpu, "MemorySpace") else pltpu.VMEM
+    return pl.pallas_call(
+        functools.partial(level0_kernel, plan, *shifts),
+        out_shape=jax.ShapeDtypeStruct(
+            (chunks, 4, count, rank_size, inner_boxes), jnp.bfloat16
+        ),
+        in_specs=[pl.BlockSpec(memory_space=vmem)] * 2,
+        out_specs=pl.BlockSpec(memory_space=vmem),
+        scratch_shapes=[
+            pltpu.VMEM((chunks, 3, count, rank_size, inner_boxes), jnp.bfloat16),
+            pltpu.SemaphoreType.DMA((chunks, 3)),
+            pltpu.SemaphoreType.DMA((chunks, 3)),
+        ],
+        compiler_params=pltpu.CompilerParams(
+            collective_id=0, has_side_effects=True, vmem_limit_bytes=48 * 1024 * 1024
+        ),
+    )(image, mats)
 
 
 def output_stage(pieces, wave, obs, chunk, w_mat, w_t, o_mat, o_t, step=8):
@@ -253,10 +320,9 @@
         )
 
     gradient = None
+    level0 = level0_forward(forward_plan, shifts[0], image, forward_mats)
     for m in range(CHUNKS):
-        coef = [local_forward(m, f) for f in range(4)]
-        pieces = exchange(coef, *shifts[0])
-        cur = mixing(w0, jnp.stack(pieces), "scor,cjrl->sjol")
+        cur = mixing(w0, level0[m], "scor,cjrl->sjol")
         pieces = exchange(cur, *shifts[1])
         terms = output_stage(pieces, wave, obs, m, w1_mat, w1_t, ow_mat, ow_t)
         back = exchange(terms, *shifts[1])

time: 195 us -> 207 us (1.062)
  Pallas kernels: 62.7 us -> 93.3 us
  starting transfers between devices: 53.6 us -> 33 us
  waiting for transfers between devices: 53.7 us -> 56.9 us
  matrix products: 6.8 us -> 4.22 us
  local copies, waits for them, and re-layouts: 14.6 us -> 17.1 us
    pallas_call x0 -> x1, Pallas kernels: none -> 52.2 us  [level0_forward(): pl.pallas_call(functools.partial(level0_kernel, plan, *shifts), out_shape...]
    pallas_call x16 -> x8, Pallas kernels: 42.9 us -> 21.3 us  [chain_call(): pl.pallas_call(functools.partial(chain_kernel, plan), grid_spec=pltpu.Pre...]
    ppermute x8 -> x6, waiting for transfers between devices: 9.12 us -> 22.8 us  [flip_send(): return lax.ppermute(value, ('qx', 'qy'), pairs)]
    ppermute x8 -> x6, waiting for transfers between devices: 28.8 us -> 16.2 us  [flip_send(): return lax.ppermute(value, 'qx', pairs)]
    ppermute x8 -> x6, starting transfers between devices: 16.3 us -> 4.21 us  [flip_send(): return lax.ppermute(value, 'qx', pairs)]
    ppermute x8 -> x6, starting transfers between devices: 14.3 us -> 8.43 us  [flip_send(): return lax.ppermute(value, 'qy', pairs)]
    ppermute x8 -> x6, starting transfers between devices: 23 us -> 20.3 us  [flip_send(): return lax.ppermute(value, ('qx', 'qy'), pairs)]
    dot_general x4, matrix products: 6.8 us -> 4.22 us  [mixing(): jnp.einsum(form, weight, data, preferred_element_type=jnp.float32)]
  transfers between devices with their start and end apart: 24 -> 18, of which waited for: 9 -> 9; matrix products, arithmetic and copies ran while one was open for 8% -> 5% of each run, Pallas kernels for 30% -> 19%
where the time goes in v8:
time: 207 us; the launch traced here: 206 us
  Pallas kernels  93.3 us (45%)
  waiting for transfers between devices  56.9 us (27%)
  starting transfers between devices  33 us (16%)
  local copies, waits for them, and re-layouts  17.1 us (8%)
  matrix products  4.22 us (2%)
    pallas_call x1, Pallas kernels, level0_forward(): pl.pallas_call(functools.partial(level0_kernel, plan, *shifts), out_shape...  52.2 us
    ppermute x6, waiting for transfers between devices, flip_send(): return lax.ppermute(value, ('qx', 'qy'), pairs)  22.8 us
    pallas_call x8, Pallas kernels, chain_call(): pl.pallas_call(functools.partial(chain_kernel, plan), grid_spec=pltpu.Pre...  21.3 us
    ppermute x6, starting transfers between devices, flip_send(): return lax.ppermute(value, ('qx', 'qy'), pairs)  20.3 us
    pallas_call x2, Pallas kernels, output_stage(): pl.pallas_call(output_stage_kernel, grid=(part // step,), in_specs=[piece...  19.8 us
    ppermute x6, waiting for transfers between devices, flip_send(): return lax.ppermute(value, 'qy', pairs)  17.9 us
    ppermute x6, waiting for transfers between devices, flip_send(): return lax.ppermute(value, 'qx', pairs)  16.2 us
    ppermute x6, starting transfers between devices, flip_send(): return lax.ppermute(value, 'qy', pairs)  8.43 us
  transfers between devices with their start and end apart: 18, of which 9 were waited for; matrix products, arithmetic and copies ran while one was open for 5% of the time, Pallas kernels for 19%

profile of v8, /device:TPU:1, one launch (start us, length us, event | category | flops | bytes accessed | tf_op | source)
XLA Modules:
  0.0 206.4 jit_solution(15707153695606264935)
XLA Ops:
  4.9 52.2 %shard_map.73 = bf16[2,4,32,64,128]{4,3,2,1,0:T(8,128)(2,1)S(1)} custom-call(bf16[4,2,32,64,128]{4,3,2,1,0:T(8,128)(2,1)} %bitcast.165, bf16[3,256,256]{2,1,0:T(8,128)(2,1)S(1)} %pad_maximum_fusion.2.mat_ref), custom_call_target="tpu_custom_call" | custom-call | tf_op jit(solution)/shard_map/pallas_call | solution.py:213
  60.3 5.9 %collective-permute-start.11 = (bf16[32,64,128]{2,1,0:T(8,128)(2,1)}, bf16[32,64,128]{2,1,0:T(8,128)(2,1)}, u32[]{:S(2)}, u32[]{:S(2)}) collective-permute-start(bf16[32,64,128]{2,1,0:T(8,128)(2,1)} %get-tuple-element.27), channel_id=1, source_target_pairs={{0,68},{1,69},{2,70},{3,71},{4,64},{5,65},{6,66},{7,67},{8,76},{9,... | collective-permute-start | bytes 1572872 | tf_op jit(solution)/shard_map/ppermute | solution.py:64
  68.2 5.4 %collective-permute-start.2 = (bf16[32,64,128]{2,1,0:T(8,128)(2,1)S(1)}, bf16[32,64,128]{2,1,0:T(8,128)(2,1)}, u32[]{:S(2)}, u32[]{:S(2)}) collective-permute-start(bf16[32,64,128]{2,1,0:T(8,128)(2,1)S(1)} %get-tuple-element.35), channel_id=1, source_target_pairs={{0,68},{1,69},{2,70},{3,71},{4,64},{5,65},{6,66},{7,67},{8,76},{9,... | collective-permute-start | bytes 1572872 | tf_op jit(solution)/shard_map/ppermute | solution.py:64
  75.8 2.9 %collective-permute-done.11.p3 = bf16[32,64,128]{2,1,0:T(8,128)(2,1)} collective-permute-done((bf16[32,64,128]{2,1,0:T(8,128)(2,1)}, bf16[32,64,128]{2,1,0:T(8,128)(2,1)}, u32[]{:S(2)}, u32[]{:S(2)}) %collective-permute-start.11) | collective-permute-done | bytes 524320 | tf_op jit(solution)/shard_map/ppermute | solution.py:64
  80.5 9.8 %collective-permute-done.10.p2 = bf16[32,64,128]{2,1,0:T(8,128)(2,1)} collective-permute-done((bf16[32,64,128]{2,1,0:T(8,128)(2,1)}, bf16[32,64,128]{2,1,0:T(8,128)(2,1)}, u32[]{:S(2)}, u32[]{:S(2)}) %collective-permute-start.10) | collective-permute-done | bytes 524320 | tf_op jit(solution)/shard_map/ppermute | solution.py:55
  90.3 9.9 %shard_map.75 = (bf16[32,64,128]{2,1,0:T(8,128)(2,1)}, bf16[32,64,128]{2,1,0:T(8,128)(2,1)}, bf16[32,64,128]{2,1,0:T(8,128)(2,1)}, bf16[32,64,128]{2,1,0:T(8,128)(2,1)}) custom-call(bf16[32,64,128]{2,1,0:T(8,128)(2,1)} %get-tuple-element.30.p0, bf16[32,64,128]{2,1,0:T(8,128)(2,1)} %collective-permute-done.9.p1, ...), custom_call_target="tpu_custom_call" | custom-call | flops 2147483648 | bytes 10485760 | tf_op jit(solution)/shard_map/pallas_call | solution.py:240
  100.2 2.9 %collective-permute-start.12 = (bf16[32,64,128]{2,1,0:T(8,128)(2,1)}, bf16[32,64,128]{2,1,0:T(8,128)(2,1)}, u32[]{:S(2)}, u32[]{:S(2)}) collective-permute-start(bf16[32,64,128]{2,1,0:T(8,128)(2,1)} %get-tuple-element.18), channel_id=1, source_target_pairs={{0,4},{1,5},{2,6},{3,7},{4,0},{5,1},{6,2},{7,3},{8,12},{9,13},{10,... | collective-permute-start | bytes 1572872 | tf_op jit(solution)/shard_map/ppermute | solution.py:58
  103.5 2.7 %collective-permute-start.14 = (bf16[32,64,128]{2,1,0:T(8,128)(2,1)}, bf16[32,64,128]{2,1,0:T(8,128)(2,1)S(1)}, u32[]{:S(2)}, u32[]{:S(2)}) collective-permute-start(bf16[32,64,128]{2,1,0:T(8,128)(2,1)} %get-tuple-element.20), channel_id=1, source_target_pairs={{0,68},{1,69},{2,70},{3,71},{4,64},{5,65},{6,66},{7,67},{8,76},{9,... | collective-permute-start | bytes 1572872 | tf_op jit(solution)/shard_map/ppermute | solution.py:64
  106.2 6.4 %collective-permute-done.1.p2 = bf16[32,64,128]{2,1,0:T(8,128)(2,1)} collective-permute-done((bf16[32,64,128]{2,1,0:T(8,128)(2,1)S(1)}, bf16[32,64,128]{2,1,0:T(8,128)(2,1)}, u32[]{:S(2)}, u32[]{:S(2)}) %collective-permute-start.1) | collective-permute-done | bytes 524320 | tf_op jit(solution)/shard_map/ppermute | solution.py:55
  113.4 9.9 %shard_map.74 = (bf16[32,64,128]{2,1,0:T(8,128)(2,1)}, bf16[32,64,128]{2,1,0:T(8,128)(2,1)}, bf16[32,64,128]{2,1,0:T(8,128)(2,1)}, bf16[32,64,128]{2,1,0:T(8,128)(2,1)}) custom-call(bf16[32,64,128]{2,1,0:T(8,128)(2,1)} %get-tuple-element.38.p0, bf16[32,64,128]{2,1,0:T(8,128)(2,1)} %copy-done.8, bf16[32,64,128]{2,1,0:T(8,128)(2,1)} %collective-permute-done.1.p2, ...), custom_call_target="tpu_custom_call" | custom-call | flops 2147483648 | bytes 10485760 | tf_op jit(solution)/shard_map/pallas_call | solution.py:240
  126.3 2.8 %collective-permute-start.5 = (bf16[32,64,128]{2,1,0:T(8,128)(2,1)}, bf16[32,64,128]{2,1,0:T(8,128)(2,1)S(1)}, u32[]{:S(2)}, u32[]{:S(2)}) collective-permute-start(bf16[32,64,128]{2,1,0:T(8,128)(2,1)} %get-tuple-element.16), channel_id=1, source_target_pairs={{0,68},{1,69},{2,70},{3,71},{4,64},{5,65},{6,66},{7,67},{8,76},{9,... | collective-permute-start | bytes 1572872 | tf_op jit(solution)/shard_map/ppermute | solution.py:64
  129.1 5.8 %collective-permute-done.14 = bf16[32,64,128]{2,1,0:T(8,128)(2,1)S(1)} collective-permute-done((bf16[32,64,128]{2,1,0:T(8,128)(2,1)}, bf16[32,64,128]{2,1,0:T(8,128)(2,1)S(1)}, u32[]{:S(2)}, u32[]{:S(2)}) %collective-permute-start.14) | collective-permute-done | bytes 524320 | tf_op jit(solution)/shard_map/ppermute | solution.py:64
  140.4 5.4 %collective-permute-done.3 = bf16[32,64,128]{2,1,0:T(8,128)(2,1)S(1)} collective-permute-done((bf16[32,64,128]{2,1,0:T(8,128)(2,1)}, bf16[32,64,128]{2,1,0:T(8,128)(2,1)S(1)}, u32[]{:S(2)}, u32[]{:S(2)}) %collective-permute-start.3) | collective-permute-done | bytes 524320 | tf_op jit(solution)/shard_map/ppermute | solution.py:58
  148.1 9.2 %collective-permute-done.5 = bf16[32,64,128]{2,1,0:T(8,128)(2,1)S(1)} collective-permute-done((bf16[32,64,128]{2,1,0:T(8,128)(2,1)}, bf16[32,64,128]{2,1,0:T(8,128)(2,1)S(1)}, u32[]{:S(2)}, u32[]{:S(2)}) %collective-permute-start.5) | collective-permute-done | bytes 524320 | tf_op jit(solution)/shard_map/ppermute | solution.py:64
  161.3 7.9 %collective-permute-done.17.x_ref = bf16[32,64,128]{2,1,0:T(8,128)(2,1)S(1)} collective-permute-done((bf16[32,64,128]{2,1,0:T(8,128)(2,1)S(1)}, bf16[32,64,128]{2,1,0:T(8,128)(2,1)S(1)}, u32[]{:S(2)}, u32[]{:S(2)}) %collective-permute-start.17) | collective-permute-done | bytes 524320 | tf_op jit(solution)/shard_map/ppermute | solution.py:58
  172.3 2.7 %shard_map.76.rest_0_ = bf16[4,2,32,64,128]{4,3,2,1,0:T(8,128)(2,1)} custom-call(s32[1]{0:T(128)} %bitcast.k_ref, bf16[32,64,128]{2,1,0:T(8,128)(2,1)} %get-tuple-element.23.x_ref, bf16[3,256,256]{2,1,0:T(8,128)(2,1)} %pad_maximum_fusion.3.m_ref), custom_call_target="tpu_custom_call" | custom-call | tf_op jit(solution)/shard_map/pallas_call | solution.py:154
  175.0 2.7 %shard_map.77.rest_0_ = bf16[4,2,32,64,128]{4,3,2,1,0:T(8,128)(2,1)} custom-call(s32[1]{0:T(128)} %bitcast.k_ref, bf16[32,64,128]{2,1,0:T(8,128)(2,1)} %copy-done.4, bf16[3,256,256]{2,1,0:T(8,128)(2,1)} %pad_maximum_fusion.3.m_ref, bf16[4,2,32,64,128]{4,3,2,1,0:T(8,128)(2,1)} %shard_map.76.rest_0_), custom_call_target="tpu_custom_call", output_to_operand_aliasing={{}: (3, {})} | custom-call | tf_op jit(solution)/shard_map/pallas_call | solution.py:154
  178.5 2.7 %shard_map.78.rest_0_ = bf16[4,2,32,64,128]{4,3,2,1,0:T(8,128)(2,1)} custom-call(s32[1]{0:T(128)} %bitcast.k_ref, bf16[32,64,128]{2,1,0:T(8,128)(2,1)} %copy-done.2, bf16[3,256,256]{2,1,0:T(8,128)(2,1)} %pad_maximum_fusion.3.m_ref, bf16[4,2,32,64,128]{4,3,2,1,0:T(8,128)(2,1)} %shard_map.77.rest_0_), custom_call_target="tpu_custom_call", output_to_operand_aliasing={{}: (3, {})} | custom-call | tf_op jit(solution)/shard_map/pallas_call | solution.py:154
  181.9 2.7 %shard_map.79.rest_0_ = bf16[4,2,32,64,128]{4,3,2,1,0:T(8,128)(2,1)} custom-call(s32[1]{0:T(128)} %bitcast.k_ref, bf16[32,64,128]{2,1,0:T(8,128)(2,1)} %copy-done.3, bf16[3,256,256]{2,1,0:T(8,128)(2,1)} %pad_maximum_fusion.3.m_ref, bf16[4,2,32,64,128]{4,3,2,1,0:T(8,128)(2,1)} %shard_map.78.rest_0_), custom_call_target="tpu_custom_call", output_to_operand_aliasing={{}: (3, {})} | custom-call | tf_op jit(solution)/shard_map/pallas_call | solution.py:154
  187.3 4.6 %collective-permute-done.8.x_ref = bf16[32,64,128]{2,1,0:T(8,128)(2,1)} collective-permute-done((bf16[32,64,128]{2,1,0:T(8,128)(2,1)}, bf16[32,64,128]{2,1,0:T(8,128)(2,1)}, u32[]{:S(2)}, u32[]{:S(2)}) %collective-permute-start.8) | collective-permute-done | bytes 524320 | tf_op jit(solution)/shard_map/ppermute | solution.py:58
  191.8 2.7 %shard_map.81.rest_0_ = bf16[4,2,32,64,128]{4,3,2,1,0:T(8,128)(2,1)} custom-call(s32[1]{0:T(128)} %bitcast.k_ref, bf16[32,64,128]{2,1,0:T(8,128)(2,1)} %collective-permute-done.8.x_ref, bf16[3,256,256]{2,1,0:T(8,128)(2,1)} %pad_maximum_fusion.3.m_ref, bf16[4,2,32,64,128]{4,3,2,1,0:T(8,128)(2,1)} %shard_map.80.rest_0_), custom_call_target="tpu_custom_call", output_to_operand_aliasing={{}: (3, {})} | custom-call | tf_op jit(solution)/shard_map/pallas_call | solution.py:154
  195.3 2.7 %shard_map.82.rest_0_ = bf16[4,2,32,64,128]{4,3,2,1,0:T(8,128)(2,1)} custom-call(s32[1]{0:T(128)} %bitcast.k_ref, bf16[32,64,128]{2,1,0:T(8,128)(2,1)} %copy-done.5, bf16[3,256,256]{2,1,0:T(8,128)(2,1)} %pad_maximum_fusion.3.m_ref, bf16[4,2,32,64,128]{4,3,2,1,0:T(8,128)(2,1)} %shard_map.81.rest_0_), custom_call_target="tpu_custom_call", output_to_operand_aliasing={{}: (3, {})} | custom-call | tf_op jit(solution)/shard_map/pallas_call | solution.py:154
  198.0 5.0 %collective-permute-done.6.x_ref = bf16[32,64,128]{2,1,0:T(8,128)(2,1)S(1)} collective-permute-done((bf16[32,64,128]{2,1,0:T(8,128)(2,1)}, bf16[32,64,128]{2,1,0:T(8,128)(2,1)S(1)}, u32[]{:S(2)}, u32[]{:S(2)}) %collective-permute-start.6) | collective-permute-done | bytes 524320 | tf_op jit(solution)/shard_map/ppermute | solution.py:64
  203.8 2.7 %shard_map.83 = bf16[4,2,32,64,128]{4,3,2,1,0:T(8,128)(2,1)} custom-call(s32[1]{0:T(128)} %bitcast.k_ref, bf16[32,64,128]{2,1,0:T(8,128)(2,1)} %copy-done.6, bf16[3,256,256]{2,1,0:T(8,128)(2,1)} %pad_maximum_fusion.3.m_ref, bf16[4,2,32,64,128]{4,3,2,1,0:T(8,128)(2,1)} %shard_map.82.rest_0_), custom_call_target="tpu_custom_call", output_to_operand_aliasing={{}: (3, {})} | custom-call | tf_op jit(solution)/shard_map/pallas_call | solution.py:154
  (85 shorter events, 38.8 us)
Async XLA Ops:
  0.0 4.2 %copy-start.7 = (bf16[1,1,2,4,4,64,64]{6,5,4,3,2,1,0:T(8,128)(2,1)S(1)}, bf16[1,1,2,4,4,64,64]{6,5,4,3,2,1,0:T(8,128)(2,1)}, u32[]{:S(2)}) copy-start(bf16[1,1,2,4,4,64,64]{6,5,4,3,2,1,0:T(8,128)(2,1)} %param.12) | copy-start | bytes 786436
  60.3 18.4 %collective-permute-start.11 = (bf16[32,64,128]{2,1,0:T(8,128)(2,1)}, bf16[32,64,128]{2,1,0:T(8,128)(2,1)}, u32[]{:S(2)}, u32[]{:S(2)}) collective-permute-start(bf16[32,64,128]{2,1,0:T(8,128)(2,1)} %get-tuple-element.27), channel_id=1, source_target_pairs={{0,68},{1,69},{2,70},{3,71},{4,64},{5,65},{6,66},{7,67},{8,76},{9,... | collective-permute-start | bytes 1572872 | tf_op jit(solution)/shard_map/ppermute | solution.py:64
  66.2 24.1 %collective-permute-start.10 = (bf16[32,64,128]{2,1,0:T(8,128)(2,1)}, bf16[32,64,128]{2,1,0:T(8,128)(2,1)}, u32[]{:S(2)}, u32[]{:S(2)}) collective-permute-start(bf16[32,64,128]{2,1,0:T(8,128)(2,1)} %get-tuple-element.28), channel_id=1, source_target_pairs={{0,64},{8,72},{16,80},{24,88},{32,96},{40,104},{48,112},{56,120},{... | collective-permute-start | bytes 1572872 | tf_op jit(solution)/shard_map/ppermute | solution.py:55
  66.2 24.1 %collective-permute-start.9 = (bf16[32,64,128]{2,1,0:T(8,128)(2,1)}, bf16[32,64,128]{2,1,0:T(8,128)(2,1)}, u32[]{:S(2)}, u32[]{:S(2)}) collective-permute-start(bf16[32,64,128]{2,1,0:T(8,128)(2,1)} %get-tuple-element.29), channel_id=1, source_target_pairs={{0,4},{1,5},{2,6},{3,7},{4,0},{5,1},{6,2},{7,3},{8,12},{9,13},{10,... | collective-permute-start | bytes 1572872 | tf_op jit(solution)/shard_map/ppermute | solution.py:58
  68.2 35.3 %collective-permute-start.2 = (bf16[32,64,128]{2,1,0:T(8,128)(2,1)S(1)}, bf16[32,64,128]{2,1,0:T(8,128)(2,1)}, u32[]{:S(2)}, u32[]{:S(2)}) collective-permute-start(bf16[32,64,128]{2,1,0:T(8,128)(2,1)S(1)} %get-tuple-element.35), channel_id=1, source_target_pairs={{0,68},{1,69},{2,70},{3,71},{4,64},{5,65},{6,66},{7,67},{8,76},{9,... | collective-permute-start | bytes 1572872 | tf_op jit(solution)/shard_map/ppermute | solution.py:64
  73.6 39.0 %collective-permute-start.1 = (bf16[32,64,128]{2,1,0:T(8,128)(2,1)S(1)}, bf16[32,64,128]{2,1,0:T(8,128)(2,1)}, u32[]{:S(2)}, u32[]{:S(2)}) collective-permute-start(bf16[32,64,128]{2,1,0:T(8,128)(2,1)S(1)} %get-tuple-element.36), channel_id=1, source_target_pairs={{0,64},{8,72},{16,80},{24,88},{32,96},{40,104},{48,112},{56,120},{... | collective-permute-start | bytes 1572872 | tf_op jit(solution)/shard_map/ppermute | solution.py:55
  73.8 16.5 %copy-start = (bf16[256,256]{0,1:T(8,128)(2,1)}, bf16[256,256]{0,1:T(8,128)(2,1)S(1)}, u32[]{:S(2)}) copy-start(bf16[256,256]{0,1:T(8,128)(2,1)S(1)} %reshape.52) | copy-start | bytes 393220
  75.0 15.3 %copy-start.1 = (bf16[256,256]{0,1:T(8,128)(2,1)}, bf16[256,256]{0,1:T(8,128)(2,1)S(1)}, u32[]{:S(2)}) copy-start(bf16[256,256]{0,1:T(8,128)(2,1)S(1)} %reshape.51) | copy-start | bytes 393220
  78.7 33.9 %collective-permute-start = (bf16[32,64,128]{2,1,0:T(8,128)(2,1)S(1)}, bf16[32,64,128]{2,1,0:T(8,128)(2,1)S(1)}, u32[]{:S(2)}, u32[]{:S(2)}) collective-permute-start(bf16[32,64,128]{2,1,0:T(8,128)(2,1)S(1)} %get-tuple-element.37), channel_id=1, source_target_pairs={{0,4},{1,5},{2,6},{3,7},{4,0},{5,1},{6,2},{7,3},{8,12},{9,13},{10,... | collective-permute-start | bytes 1572872 | tf_op jit(solution)/shard_map/ppermute | solution.py:58
  100.2 26.0 %collective-permute-start.12 = (bf16[32,64,128]{2,1,0:T(8,128)(2,1)}, bf16[32,64,128]{2,1,0:T(8,128)(2,1)}, u32[]{:S(2)}, u32[]{:S(2)}) collective-permute-start(bf16[32,64,128]{2,1,0:T(8,128)(2,1)} %get-tuple-element.18), channel_id=1, source_target_pairs={{0,4},{1,5},{2,6},{3,7},{4,0},{5,1},{6,2},{7,3},{8,12},{9,13},{10,... | collective-permute-start | bytes 1572872 | tf_op jit(solution)/shard_map/ppermute | solution.py:58
  103.1 25.9 %collective-permute-start.13 = (bf16[32,64,128]{2,1,0:T(8,128)(2,1)}, bf16[32,64,128]{2,1,0:T(8,128)(2,1)}, u32[]{:S(2)}, u32[]{:S(2)}) collective-permute-start(bf16[32,64,128]{2,1,0:T(8,128)(2,1)} %get-tuple-element.19), channel_id=1, source_target_pairs={{0,64},{8,72},{16,80},{24,88},{32,96},{40,104},{48,112},{56,120},{... | collective-permute-start | bytes 1572872 | tf_op jit(solution)/shard_map/ppermute | solution.py:55
  103.5 31.3 %collective-permute-start.14 = (bf16[32,64,128]{2,1,0:T(8,128)(2,1)}, bf16[32,64,128]{2,1,0:T(8,128)(2,1)S(1)}, u32[]{:S(2)}, u32[]{:S(2)}) collective-permute-start(bf16[32,64,128]{2,1,0:T(8,128)(2,1)} %get-tuple-element.20), channel_id=1, source_target_pairs={{0,68},{1,69},{2,70},{3,71},{4,64},{5,65},{6,66},{7,67},{8,76},{9,... | collective-permute-start | bytes 1572872 | tf_op jit(solution)/shard_map/ppermute | solution.py:64
  113.4 21.4 %copy-start.10 = (bf16[32,64,128]{2,1,0:T(8,128)(2,1)S(1)}, bf16[32,64,128]{2,1,0:T(8,128)(2,1)}, u32[]{:S(2)}) copy-start(bf16[32,64,128]{2,1,0:T(8,128)(2,1)} %get-tuple-element.17) | copy-start | bytes 1572868
  123.3 22.5 %collective-permute-start.3 = (bf16[32,64,128]{2,1,0:T(8,128)(2,1)}, bf16[32,64,128]{2,1,0:T(8,128)(2,1)S(1)}, u32[]{:S(2)}, u32[]{:S(2)}) collective-permute-start(bf16[32,64,128]{2,1,0:T(8,128)(2,1)} %get-tuple-element.14), channel_id=1, source_target_pairs={{0,4},{1,5},{2,6},{3,7},{4,0},{5,1},{6,2},{7,3},{8,12},{9,13},{10,... | collective-permute-start | bytes 1572872 | tf_op jit(solution)/shard_map/ppermute | solution.py:58
  125.9 22.3 %collective-permute-start.4 = (bf16[32,64,128]{2,1,0:T(8,128)(2,1)}, bf16[32,64,128]{2,1,0:T(8,128)(2,1)S(1)}, u32[]{:S(2)}, u32[]{:S(2)}) collective-permute-start(bf16[32,64,128]{2,1,0:T(8,128)(2,1)} %get-tuple-element.15), channel_id=1, source_target_pairs={{0,64},{8,72},{16,80},{24,88},{32,96},{40,104},{48,112},{56,120},{... | collective-permute-start | bytes 1572872 | tf_op jit(solution)/shard_map/ppermute | solution.py:55
  126.3 31.1 %collective-permute-start.5 = (bf16[32,64,128]{2,1,0:T(8,128)(2,1)}, bf16[32,64,128]{2,1,0:T(8,128)(2,1)S(1)}, u32[]{:S(2)}, u32[]{:S(2)}) collective-permute-start(bf16[32,64,128]{2,1,0:T(8,128)(2,1)} %get-tuple-element.16), channel_id=1, source_target_pairs={{0,68},{1,69},{2,70},{3,71},{4,64},{5,65},{6,66},{7,67},{8,76},{9,... | collective-permute-start | bytes 1572872 | tf_op jit(solution)/shard_map/ppermute | solution.py:64
  136.8 20.6 %copy-start.9 = (bf16[32,64,128]{2,1,0:T(8,128)(2,1)S(1)}, bf16[32,64,128]{2,1,0:T(8,128)(2,1)}, u32[]{:S(2)}) copy-start(bf16[32,64,128]{2,1,0:T(8,128)(2,1)} %get-tuple-element.13) | copy-start | bytes 1572868
  138.0 31.3 %collective-permute-start.17 = (bf16[32,64,128]{2,1,0:T(8,128)(2,1)S(1)}, bf16[32,64,128]{2,1,0:T(8,128)(2,1)S(1)}, u32[]{:S(2)}, u32[]{:S(2)}) collective-permute-start(bf16[32,64,128]{2,1,0:T(8,128)(2,1)S(1)} %get-tuple-element.24), channel_id=1, source_target_pairs={{0,1},{1,0},{2,3},{3,2},{4,5},{5,4},{6,7},{7,6},{8,9},{9,8},{10,11... | collective-permute-start | bytes 1572872 | tf_op jit(solution)/shard_map/ppermute | solution.py:58
  138.4 39.3 %collective-permute-start.16 = (bf16[32,64,128]{2,1,0:T(8,128)(2,1)}, bf16[32,64,128]{2,1,0:T(8,128)(2,1)S(1)}, u32[]{:S(2)}, u32[]{:S(2)}) collective-permute-start(bf16[32,64,128]{2,1,0:T(8,128)(2,1)} %get-tuple-element.25), channel_id=1, source_target_pairs={{0,8},{8,0},{16,24},{24,16},{32,40},{40,32},{48,56},{56,48},{64,72... | collective-permute-start | bytes 1572872 | tf_op jit(solution)/shard_map/ppermute | solution.py:55
  145.8 35.3 %collective-permute-start.15 = (bf16[32,64,128]{2,1,0:T(8,128)(2,1)}, bf16[32,64,128]{2,1,0:T(8,128)(2,1)S(1)}, u32[]{:S(2)}, u32[]{:S(2)}) collective-permute-start(bf16[32,64,128]{2,1,0:T(8,128)(2,1)} %get-tuple-element.26), channel_id=1, source_target_pairs={{0,9},{1,8},{2,11},{3,10},{4,13},{5,12},{6,15},{7,14},{8,1},{9,0},... | collective-permute-start | bytes 1572872 | tf_op jit(solution)/shard_map/ppermute | solution.py:64
  159.4 32.4 %collective-permute-start.8 = (bf16[32,64,128]{2,1,0:T(8,128)(2,1)}, bf16[32,64,128]{2,1,0:T(8,128)(2,1)}, u32[]{:S(2)}, u32[]{:S(2)}) collective-permute-start(bf16[32,64,128]{2,1,0:T(8,128)(2,1)} %get-tuple-element.32), channel_id=1, source_target_pairs={{0,1},{1,0},{2,3},{3,2},{4,5},{5,4},{6,7},{7,6},{8,9},{9,8},{10,11... | collective-permute-start | bytes 1572872 | tf_op jit(solution)/shard_map/ppermute | solution.py:58
  159.9 34.6 %collective-permute-start.7 = (bf16[32,64,128]{2,1,0:T(8,128)(2,1)}, bf16[32,64,128]{2,1,0:T(8,128)(2,1)S(1)}, u32[]{:S(2)}, u32[]{:S(2)}) collective-permute-start(bf16[32,64,128]{2,1,0:T(8,128)(2,1)} %get-tuple-element.33), channel_id=1, source_target_pairs={{0,8},{8,0},{16,24},{24,16},{32,40},{40,32},{48,56},{56,48},{64,72... | collective-permute-start | bytes 1572872 | tf_op jit(solution)/shard_map/ppermute | solution.py:55
  169.3 5.7 %copy-start.4 = (bf16[32,64,128]{2,1,0:T(8,128)(2,1)}, bf16[32,64,128]{2,1,0:T(8,128)(2,1)S(1)}, u32[]{:S(2)}) copy-start(bf16[32,64,128]{2,1,0:T(8,128)(2,1)S(1)} %collective-permute-done.17.x_ref) | copy-start | bytes 1572868
  169.3 33.7 %collective-permute-start.6 = (bf16[32,64,128]{2,1,0:T(8,128)(2,1)}, bf16[32,64,128]{2,1,0:T(8,128)(2,1)S(1)}, u32[]{:S(2)}, u32[]{:S(2)}) collective-permute-start(bf16[32,64,128]{2,1,0:T(8,128)(2,1)} %get-tuple-element.34), channel_id=1, source_target_pairs={{0,9},{1,8},{2,11},{3,10},{4,13},{5,12},{6,15},{7,14},{8,1},{9,0},... | collective-permute-start | bytes 1572872 | tf_op jit(solution)/shard_map/ppermute | solution.py:64
  (5 other events, 4.0 us)

commit v9 on v7

--- a/solution.py
+++ b/solution.py
@@ -200,12 +200,6 @@
         (jnp.right_shift(t, xs) & 1, jnp.right_shift(u, ys) & 1) for xs, ys in shifts
     ]
 
-    w0 = xor_order(xor_order(merges[0], 1, *bits[0]), 0, *bits[1])
-    w1 = xor_order(merges[1], 1, *bits[1])
-    w1_mat = jnp.transpose(w1, (0, 2, 1, 3)).reshape(4 * rank_size, 4 * rank_size)
-    w1_t = w1_mat.T
-    ow_mat = jnp.einsum("st,or->sotr", jnp.eye(4, dtype=output_weight.dtype), output_weight).reshape(4 * rank_size, 4 * rank_size)
-    ow_t = ow_mat.T
 
     shape5 = (4, CHUNKS, part, rank_size, inner_boxes)
     image = image_tiles[0, 0].reshape(shape5)
@@ -220,7 +214,6 @@
         for i in range(local_depth)
     ]
     forward_mats = jnp.stack([spread] + forward_levels)
-    adjoint_mats = jnp.stack([w.T for w in reversed(forward_levels)] + [spread.T])
     forward_plan = [chain_sets(part, 1)] + [chain_sets(part, 4**i) for i in range(local_depth)]
     adjoint_plan = [chain_sets(part, 4**i) for i in reversed(range(local_depth))] + [
         chain_sets(part, 1)
@@ -252,9 +245,21 @@
             target=gradient,
         )
 
+    first = local_forward(0, 1)
+    merges, output_weight, forward_levels, spread, first = lax.optimization_barrier(
+        (merges, output_weight, forward_levels, spread, first)
+    )
+    adjoint_mats = jnp.stack([w.T for w in reversed(forward_levels)] + [spread.T])
+    w0 = xor_order(xor_order(merges[0], 1, *bits[0]), 0, *bits[1])
+    w1 = xor_order(merges[1], 1, *bits[1])
+    w1_mat = jnp.transpose(w1, (0, 2, 1, 3)).reshape(4 * rank_size, 4 * rank_size)
+    w1_t = w1_mat.T
+    ow_mat = jnp.einsum("st,or->sotr", jnp.eye(4, dtype=output_weight.dtype), output_weight).reshape(4 * rank_size, 4 * rank_size)
+    ow_t = ow_mat.T
+
     gradient = None
     for m in range(CHUNKS):
-        coef = [local_forward(m, f) for f in range(4)]
+        coef = [first if (m, f) == (0, 1) else local_forward(m, f) for f in range(4)]
         pieces = exchange(coef, *shifts[0])
         cur = mixing(w0, jnp.stack(pieces), "scor,cjrl->sjol")
         pieces = exchange(cur, *shifts[1])

time: 195 us -> 196 us (level)
    unnamed x32 -> x33, local copies, waits for them, and re-layouts: 4.06 us -> 4.83 us
  transfers between devices with their start and end apart: 24 -> 24, of which waited for: 9 -> 10; matrix products, arithmetic and copies ran while one was open for 8% -> 8% of each run, Pallas kernels for 30% -> 29%
where the time goes in v9:
time: 196 us
  Pallas kernels  62.7 us (32%)
  waiting for transfers between devices  54.8 us (28%)
  starting transfers between devices  53.7 us (27%)
  local copies, waits for them, and re-layouts  15.4 us (8%)
  matrix products  6.47 us (3%)
  other arithmetic  2.3 us (1%)
    pallas_call x16, Pallas kernels, chain_call(): pl.pallas_call(functools.partial(chain_kernel, plan), grid_spec=pltpu.Pre...  42.8 us
    ppermute x8, waiting for transfers between devices, flip_send(): return lax.ppermute(value, 'qx', pairs)  29.3 us
    ppermute x8, starting transfers between devices, flip_send(): return lax.ppermute(value, ('qx', 'qy'), pairs)  22.9 us
    pallas_call x2, Pallas kernels, output_stage(): pl.pallas_call(output_stage_kernel, grid=(part // step,), in_specs=[piece...  19.8 us
    ppermute x8, starting transfers between devices, flip_send(): return lax.ppermute(value, 'qx', pairs)  16.5 us
    ppermute x8, waiting for transfers between devices, flip_send(): return lax.ppermute(value, 'qy', pairs)  16 us
    ppermute x8, starting transfers between devices, flip_send(): return lax.ppermute(value, 'qy', pairs)  14.3 us
    ppermute x8, waiting for transfers between devices, flip_send(): return lax.ppermute(value, ('qx', 'qy'), pairs)  9.54 us
  transfers between devices with their start and end apart: 24, of which 10 were waited for; matrix products, arithmetic and copies ran while one was open for 8% of the time, Pallas kernels for 29%

profile of v9, /device:TPU:1, one launch (start us, length us, event | category | flops | bytes accessed | tf_op | source)
XLA Modules:
  0.0 195.7 jit_solution(11926603807282333514)
XLA Ops:
  4.4 2.7 %shard_map.77 = bf16[32,64,128]{2,1,0:T(8,128)(2,1)} custom-call(s32[1]{0:T(128)} %bitcast.k_ref, bf16[4,2,32,64,128]{4,3,2,1,0:T(8,128)(2,1)} %bitcast.166, bf16[3,256,256]{2,1,0:T(8,128)(2,1)} %pad_maximum_fusion.4.m_ref), custom_call_target="tpu_custom_call" | custom-call | tf_op jit(solution)/shard_map/pallas_call | solution.py:154
  13.2 2.7 %shard_map.81 = bf16[32,64,128]{2,1,0:T(8,128)(2,1)} custom-call(s32[1]{0:T(128)} %bitcast.k_ref, bf16[4,2,32,64,128]{4,3,2,1,0:T(8,128)(2,1)} %bitcast.168, bf16[3,256,256]{2,1,0:T(8,128)(2,1)} %pad_maximum_fusion.4.m_ref), custom_call_target="tpu_custom_call" | custom-call | tf_op jit(solution)/shard_map/pallas_call | solution.py:154
  15.9 2.7 %shard_map.76 = bf16[32,64,128]{2,1,0:T(8,128)(2,1)} custom-call(s32[1]{0:T(128)} %bitcast.k_ref, bf16[4,2,32,64,128]{4,3,2,1,0:T(8,128)(2,1)} %bitcast.169, bf16[3,256,256]{2,1,0:T(8,128)(2,1)} %pad_maximum_fusion.4.m_ref), custom_call_target="tpu_custom_call" | custom-call | tf_op jit(solution)/shard_map/pallas_call | solution.py:154
  20.4 2.7 %shard_map.74 = bf16[32,64,128]{2,1,0:T(8,128)(2,1)} custom-call(s32[1]{0:T(128)} %bitcast.k_ref, bf16[4,2,32,64,128]{4,3,2,1,0:T(8,128)(2,1)} %bitcast.170, bf16[3,256,256]{2,1,0:T(8,128)(2,1)} %pad_maximum_fusion.4.m_ref), custom_call_target="tpu_custom_call" | custom-call | tf_op jit(solution)/shard_map/pallas_call | solution.py:154
  23.3 2.7 %shard_map.79 = bf16[32,64,128]{2,1,0:T(8,128)(2,1)} custom-call(s32[1]{0:T(128)} %bitcast.k_ref, bf16[4,2,32,64,128]{4,3,2,1,0:T(8,128)(2,1)} %bitcast.171, bf16[3,256,256]{2,1,0:T(8,128)(2,1)} %pad_maximum_fusion.4.m_ref), custom_call_target="tpu_custom_call" | custom-call | tf_op jit(solution)/shard_map/pallas_call | solution.py:154
  26.0 2.7 %shard_map.75 = bf16[32,64,128]{2,1,0:T(8,128)(2,1)} custom-call(s32[1]{0:T(128)} %bitcast.k_ref, bf16[4,2,32,64,128]{4,3,2,1,0:T(8,128)(2,1)} %bitcast.172, bf16[3,256,256]{2,1,0:T(8,128)(2,1)} %pad_maximum_fusion.4.m_ref), custom_call_target="tpu_custom_call" | custom-call | tf_op jit(solution)/shard_map/pallas_call | solution.py:154
  37.6 3.0 %collective-permute-start.15 = (bf16[32,64,128]{2,1,0:T(8,128)(2,1)}, bf16[32,64,128]{2,1,0:T(8,128)(2,1)}, u32[]{:S(2)}, u32[]{:S(2)}) collective-permute-start(bf16[32,64,128]{2,1,0:T(8,128)(2,1)} %get-tuple-element.39), channel_id=1, source_target_pairs={{0,4},{1,5},{2,6},{3,7},{4,0},{5,1},{6,2},{7,3},{8,12},{9,13},{10,... | collective-permute-start | bytes 1572872 | tf_op jit(solution)/shard_map/ppermute | solution.py:58
  40.6 3.6 %collective-permute-start.16 = (bf16[32,64,128]{2,1,0:T(8,128)(2,1)S(1)}, bf16[32,64,128]{2,1,0:T(8,128)(2,1)}, u32[]{:S(2)}, u32[]{:S(2)}) collective-permute-start(bf16[32,64,128]{2,1,0:T(8,128)(2,1)S(1)} %get-tuple-element.38), channel_id=1, source_target_pairs={{0,64},{8,72},{16,80},{24,88},{32,96},{40,104},{48,112},{56,120},{... | collective-permute-start | bytes 1572872 | tf_op jit(solution)/shard_map/ppermute | solution.py:55
  45.7 6.4 %collective-permute-start.17 = (bf16[32,64,128]{2,1,0:T(8,128)(2,1)S(1)}, bf16[32,64,128]{2,1,0:T(8,128)(2,1)}, u32[]{:S(2)}, u32[]{:S(2)}) collective-permute-start(bf16[32,64,128]{2,1,0:T(8,128)(2,1)S(1)} %get-tuple-element.37), channel_id=1, source_target_pairs={{0,68},{1,69},{2,70},{3,71},{4,64},{5,65},{6,66},{7,67},{8,76},{9,... | collective-permute-start | bytes 1572872 | tf_op jit(solution)/shard_map/ppermute | solution.py:64
  52.1 14.4 %collective-permute-done = bf16[32,64,128]{2,1,0:T(8,128)(2,1)} collective-permute-done((bf16[32,64,128]{2,1,0:T(8,128)(2,1)}, bf16[32,64,128]{2,1,0:T(8,128)(2,1)}, u32[]{:S(2)}, u32[]{:S(2)}) %collective-permute-start) | collective-permute-done | bytes 524320 | tf_op jit(solution)/shard_map/ppermute | solution.py:58
  69.6 2.8 %collective-permute-start.3 = (bf16[32,64,128]{2,1,0:T(8,128)(2,1)}, bf16[32,64,128]{2,1,0:T(8,128)(2,1)}, u32[]{:S(2)}, u32[]{:S(2)}) collective-permute-start(bf16[32,64,128]{2,1,0:T(8,128)(2,1)} %get-tuple-element.47), channel_id=1, source_target_pairs={{0,4},{1,5},{2,6},{3,7},{4,0},{5,1},{6,2},{7,3},{8,12},{9,13},{10,... | collective-permute-start | bytes 1572872 | tf_op jit(solution)/shard_map/ppermute | solution.py:58
  74.9 3.3 %collective-permute-start.4 = (bf16[32,64,128]{2,1,0:T(8,128)(2,1)S(1)}, bf16[32,64,128]{2,1,0:T(8,128)(2,1)}, u32[]{:S(2)}, u32[]{:S(2)}) collective-permute-start(bf16[32,64,128]{2,1,0:T(8,128)(2,1)S(1)} %get-tuple-element.46), channel_id=1, source_target_pairs={{0,64},{8,72},{16,80},{24,88},{32,96},{40,104},{48,112},{56,120},{... | collective-permute-start | bytes 1572872 | tf_op jit(solution)/shard_map/ppermute | solution.py:55
  80.7 9.9 %shard_map.82 = (bf16[32,64,128]{2,1,0:T(8,128)(2,1)}, bf16[32,64,128]{2,1,0:T(8,128)(2,1)}, bf16[32,64,128]{2,1,0:T(8,128)(2,1)}, bf16[32,64,128]{2,1,0:T(8,128)(2,1)}) custom-call(bf16[32,64,128]{2,1,0:T(8,128)(2,1)} %get-tuple-element.40.p0, bf16[32,64,128]{2,1,0:T(8,128)(2,1)} %collective-permute-done.15.p1, ...), custom_call_target="tpu_custom_call" | custom-call | flops 2147483648 | bytes 10485760 | tf_op jit(solution)/shard_map/pallas_call | solution.py:173
  90.6 3.0 %collective-permute-start.18 = (bf16[32,64,128]{2,1,0:T(8,128)(2,1)}, bf16[32,64,128]{2,1,0:T(8,128)(2,1)S(1)}, u32[]{:S(2)}, u32[]{:S(2)}) collective-permute-start(bf16[32,64,128]{2,1,0:T(8,128)(2,1)} %get-tuple-element.30), channel_id=1, source_target_pairs={{0,4},{1,5},{2,6},{3,7},{4,0},{5,1},{6,2},{7,3},{8,12},{9,13},{10,... | collective-permute-start | bytes 1572872 | tf_op jit(solution)/shard_map/ppermute | solution.py:58
  96.5 6.7 %collective-permute-done.4.p2 = bf16[32,64,128]{2,1,0:T(8,128)(2,1)} collective-permute-done((bf16[32,64,128]{2,1,0:T(8,128)(2,1)S(1)}, bf16[32,64,128]{2,1,0:T(8,128)(2,1)}, u32[]{:S(2)}, u32[]{:S(2)}) %collective-permute-start.4) | collective-permute-done | bytes 524320 | tf_op jit(solution)/shard_map/ppermute | solution.py:55
  103.2 9.9 %shard_map.78 = (bf16[32,64,128]{2,1,0:T(8,128)(2,1)}, bf16[32,64,128]{2,1,0:T(8,128)(2,1)}, bf16[32,64,128]{2,1,0:T(8,128)(2,1)}, bf16[32,64,128]{2,1,0:T(8,128)(2,1)}) custom-call(bf16[32,64,128]{2,1,0:T(8,128)(2,1)} %get-tuple-element.48.p0, bf16[32,64,128]{2,1,0:T(8,128)(2,1)} %collective-permute-done.3.p1, ...), custom_call_target="tpu_custom_call" | custom-call | flops 2147483648 | bytes 10485760 | tf_op jit(solution)/shard_map/pallas_call | solution.py:173
  113.1 3.0 %collective-permute-start.6 = (bf16[32,64,128]{2,1,0:T(8,128)(2,1)}, bf16[32,64,128]{2,1,0:T(8,128)(2,1)S(1)}, u32[]{:S(2)}, u32[]{:S(2)}) collective-permute-start(bf16[32,64,128]{2,1,0:T(8,128)(2,1)} %get-tuple-element.22), channel_id=1, source_target_pairs={{0,4},{1,5},{2,6},{3,7},{4,0},{5,1},{6,2},{7,3},{8,12},{9,13},{10,... | collective-permute-start | bytes 1572872 | tf_op jit(solution)/shard_map/ppermute | solution.py:58
  116.1 2.8 %collective-permute-start.8 = (bf16[32,64,128]{2,1,0:T(8,128)(2,1)}, bf16[32,64,128]{2,1,0:T(8,128)(2,1)S(1)}, u32[]{:S(2)}, u32[]{:S(2)}) collective-permute-start(bf16[32,64,128]{2,1,0:T(8,128)(2,1)} %get-tuple-element.24), channel_id=1, source_target_pairs={{0,68},{1,69},{2,70},{3,71},{4,64},{5,65},{6,66},{7,67},{8,76},{9,... | collective-permute-start | bytes 1572872 | tf_op jit(solution)/shard_map/ppermute | solution.py:64
  118.9 6.7 %collective-permute-done.19 = bf16[32,64,128]{2,1,0:T(8,128)(2,1)S(1)} collective-permute-done((bf16[32,64,128]{2,1,0:T(8,128)(2,1)}, bf16[32,64,128]{2,1,0:T(8,128)(2,1)S(1)}, u32[]{:S(2)}, u32[]{:S(2)}) %collective-permute-start.19) | collective-permute-done | bytes 524320 | tf_op jit(solution)/shard_map/ppermute | solution.py:55
  128.6 4.0 %collective-permute-start.22 = (bf16[32,64,128]{2,1,0:T(8,128)(2,1)}, bf16[32,64,128]{2,1,0:T(8,128)(2,1)S(1)}, u32[]{:S(2)}, u32[]{:S(2)}) collective-permute-start(bf16[32,64,128]{2,1,0:T(8,128)(2,1)} %get-tuple-element.35), channel_id=1, source_target_pairs={{0,8},{8,0},{16,24},{24,16},{32,40},{40,32},{48,56},{56,48},{64,72... | collective-permute-start | bytes 1572872 | tf_op jit(solution)/shard_map/ppermute | solution.py:55
  134.6 13.4 %collective-permute-done.7 = bf16[32,64,128]{2,1,0:T(8,128)(2,1)S(1)} collective-permute-done((bf16[32,64,128]{2,1,0:T(8,128)(2,1)}, bf16[32,64,128]{2,1,0:T(8,128)(2,1)S(1)}, u32[]{:S(2)}, u32[]{:S(2)}) %collective-permute-start.7) | collective-permute-done | bytes 524320 | tf_op jit(solution)/shard_map/ppermute | solution.py:55
  150.2 4.0 %collective-permute-start.10 = (bf16[32,64,128]{2,1,0:T(8,128)(2,1)}, bf16[32,64,128]{2,1,0:T(8,128)(2,1)S(1)}, u32[]{:S(2)}, u32[]{:S(2)}) collective-permute-start(bf16[32,64,128]{2,1,0:T(8,128)(2,1)} %get-tuple-element.43), channel_id=1, source_target_pairs={{0,8},{8,0},{16,24},{24,16},{32,40},{40,32},{48,56},{56,48},{64,72... | collective-permute-start | bytes 1572872 | tf_op jit(solution)/shard_map/ppermute | solution.py:55
  155.7 7.4 %collective-permute-start.9 = (bf16[32,64,128]{2,1,0:T(8,128)(2,1)}, bf16[32,64,128]{2,1,0:T(8,128)(2,1)S(1)}, u32[]{:S(2)}, u32[]{:S(2)}) collective-permute-start(bf16[32,64,128]{2,1,0:T(8,128)(2,1)} %get-tuple-element.44), channel_id=1, source_target_pairs={{0,9},{1,8},{2,11},{3,10},{4,13},{5,12},{6,15},{7,14},{8,1},{9,0},... | collective-permute-start | bytes 1572872 | tf_op jit(solution)/shard_map/ppermute | solution.py:64
  186.0 6.2 %collective-permute-done.9.x_ref = bf16[32,64,128]{2,1,0:T(8,128)(2,1)S(1)} collective-permute-done((bf16[32,64,128]{2,1,0:T(8,128)(2,1)}, bf16[32,64,128]{2,1,0:T(8,128)(2,1)S(1)}, u32[]{:S(2)}, u32[]{:S(2)}) %collective-permute-start.9) | collective-permute-done | bytes 524320 | tf_op jit(solution)/shard_map/ppermute | solution.py:64
  (114 shorter events, 68.7 us)
Async XLA Ops:
  7.1 24.7 %collective-permute-start.12 = (bf16[32,64,128]{2,1,0:T(8,128)(2,1)}, bf16[32,64,128]{2,1,0:T(8,128)(2,1)S(1)}, u32[]{:S(2)}, u32[]{:S(2)}) collective-permute-start(bf16[32,64,128]{2,1,0:T(8,128)(2,1)} %shard_map.77), channel_id=1, source_target_pairs={{0,1},{1,0},{2,3},{3,2},{4,5},{5,4},{6,7},{7,6},{8,9},{9,8},{10,11... | collective-permute-start | bytes 1572872 | tf_op jit(solution)/shard_map/ppermute | solution.py:58
  12.3 20.6 %collective-permute-start.13 = (bf16[32,64,128]{2,1,0:T(8,128)(2,1)}, bf16[32,64,128]{2,1,0:T(8,128)(2,1)}, u32[]{:S(2)}, u32[]{:S(2)}) collective-permute-start(bf16[32,64,128]{2,1,0:T(8,128)(2,1)} %shard_map.80), channel_id=1, source_target_pairs={{0,8},{8,0},{16,24},{24,16},{32,40},{40,32},{48,56},{56,48},{64,72... | collective-permute-start | bytes 1572872 | tf_op jit(solution)/shard_map/ppermute | solution.py:55
  15.9 18.5 %collective-permute-start.14 = (bf16[32,64,128]{2,1,0:T(8,128)(2,1)}, bf16[32,64,128]{2,1,0:T(8,128)(2,1)}, u32[]{:S(2)}, u32[]{:S(2)}) collective-permute-start(bf16[32,64,128]{2,1,0:T(8,128)(2,1)} %shard_map.81), channel_id=1, source_target_pairs={{0,9},{1,8},{2,11},{3,10},{4,13},{5,12},{6,15},{7,14},{8,1},{9,0},... | collective-permute-start | bytes 1572872 | tf_op jit(solution)/shard_map/ppermute | solution.py:64
  18.6 27.1 %collective-permute-start.2 = (bf16[32,64,128]{2,1,0:T(8,128)(2,1)}, bf16[32,64,128]{2,1,0:T(8,128)(2,1)}, u32[]{:S(2)}, u32[]{:S(2)}) collective-permute-start(bf16[32,64,128]{2,1,0:T(8,128)(2,1)} %shard_map.76), channel_id=1, source_target_pairs={{0,9},{1,8},{2,11},{3,10},{4,13},{5,12},{6,15},{7,14},{8,1},{9,0},... | collective-permute-start | bytes 1572872 | tf_op jit(solution)/shard_map/ppermute | solution.py:64
  23.1 43.4 %collective-permute-start = (bf16[32,64,128]{2,1,0:T(8,128)(2,1)}, bf16[32,64,128]{2,1,0:T(8,128)(2,1)}, u32[]{:S(2)}, u32[]{:S(2)}) collective-permute-start(bf16[32,64,128]{2,1,0:T(8,128)(2,1)} %shard_map.74), channel_id=1, source_target_pairs={{0,1},{1,0},{2,3},{3,2},{4,5},{5,4},{6,7},{7,6},{8,9},{9,8},{10,11... | collective-permute-start | bytes 1572872 | tf_op jit(solution)/shard_map/ppermute | solution.py:58
  32.4 34.0 %collective-permute-start.1 = (bf16[32,64,128]{2,1,0:T(8,128)(2,1)S(1)}, bf16[32,64,128]{2,1,0:T(8,128)(2,1)S(1)}, u32[]{:S(2)}, u32[]{:S(2)}) collective-permute-start(bf16[32,64,128]{2,1,0:T(8,128)(2,1)S(1)} %copy-done.10), channel_id=1, source_target_pairs={{0,8},{8,0},{16,24},{24,16},{32,40},{40,32},{48,56},{56,48},{64,72... | collective-permute-start | bytes 1572872 | tf_op jit(solution)/shard_map/ppermute | solution.py:55
  37.6 40.6 %collective-permute-start.15 = (bf16[32,64,128]{2,1,0:T(8,128)(2,1)}, bf16[32,64,128]{2,1,0:T(8,128)(2,1)}, u32[]{:S(2)}, u32[]{:S(2)}) collective-permute-start(bf16[32,64,128]{2,1,0:T(8,128)(2,1)} %get-tuple-element.39), channel_id=1, source_target_pairs={{0,4},{1,5},{2,6},{3,7},{4,0},{5,1},{6,2},{7,3},{8,12},{9,13},{10,... | collective-permute-start | bytes 1572872 | tf_op jit(solution)/shard_map/ppermute | solution.py:58
  40.6 40.1 %collective-permute-start.16 = (bf16[32,64,128]{2,1,0:T(8,128)(2,1)S(1)}, bf16[32,64,128]{2,1,0:T(8,128)(2,1)}, u32[]{:S(2)}, u32[]{:S(2)}) collective-permute-start(bf16[32,64,128]{2,1,0:T(8,128)(2,1)S(1)} %get-tuple-element.38), channel_id=1, source_target_pairs={{0,64},{8,72},{16,80},{24,88},{32,96},{40,104},{48,112},{56,120},{... | collective-permute-start | bytes 1572872 | tf_op jit(solution)/shard_map/ppermute | solution.py:55
  45.7 35.0 %collective-permute-start.17 = (bf16[32,64,128]{2,1,0:T(8,128)(2,1)S(1)}, bf16[32,64,128]{2,1,0:T(8,128)(2,1)}, u32[]{:S(2)}, u32[]{:S(2)}) collective-permute-start(bf16[32,64,128]{2,1,0:T(8,128)(2,1)S(1)} %get-tuple-element.37), channel_id=1, source_target_pairs={{0,68},{1,69},{2,70},{3,71},{4,64},{5,65},{6,66},{7,67},{8,76},{9,... | collective-permute-start | bytes 1572872 | tf_op jit(solution)/shard_map/ppermute | solution.py:64
  69.6 24.3 %collective-permute-start.3 = (bf16[32,64,128]{2,1,0:T(8,128)(2,1)}, bf16[32,64,128]{2,1,0:T(8,128)(2,1)}, u32[]{:S(2)}, u32[]{:S(2)}) collective-permute-start(bf16[32,64,128]{2,1,0:T(8,128)(2,1)} %get-tuple-element.47), channel_id=1, source_target_pairs={{0,4},{1,5},{2,6},{3,7},{4,0},{5,1},{6,2},{7,3},{8,12},{9,13},{10,... | collective-permute-start | bytes 1572872 | tf_op jit(solution)/shard_map/ppermute | solution.py:58
  74.9 28.3 %collective-permute-start.4 = (bf16[32,64,128]{2,1,0:T(8,128)(2,1)S(1)}, bf16[32,64,128]{2,1,0:T(8,128)(2,1)}, u32[]{:S(2)}, u32[]{:S(2)}) collective-permute-start(bf16[32,64,128]{2,1,0:T(8,128)(2,1)S(1)} %get-tuple-element.46), channel_id=1, source_target_pairs={{0,64},{8,72},{16,80},{24,88},{32,96},{40,104},{48,112},{56,120},{... | collective-permute-start | bytes 1572872 | tf_op jit(solution)/shard_map/ppermute | solution.py:55
  78.2 25.0 %collective-permute-start.5 = (bf16[32,64,128]{2,1,0:T(8,128)(2,1)S(1)}, bf16[32,64,128]{2,1,0:T(8,128)(2,1)}, u32[]{:S(2)}, u32[]{:S(2)}) collective-permute-start(bf16[32,64,128]{2,1,0:T(8,128)(2,1)S(1)} %get-tuple-element.45), channel_id=1, source_target_pairs={{0,68},{1,69},{2,70},{3,71},{4,64},{5,65},{6,66},{7,67},{8,76},{9,... | collective-permute-start | bytes 1572872 | tf_op jit(solution)/shard_map/ppermute | solution.py:64
  90.6 25.5 %collective-permute-start.18 = (bf16[32,64,128]{2,1,0:T(8,128)(2,1)}, bf16[32,64,128]{2,1,0:T(8,128)(2,1)S(1)}, u32[]{:S(2)}, u32[]{:S(2)}) collective-permute-start(bf16[32,64,128]{2,1,0:T(8,128)(2,1)} %get-tuple-element.30), channel_id=1, source_target_pairs={{0,4},{1,5},{2,6},{3,7},{4,0},{5,1},{6,2},{7,3},{8,12},{9,13},{10,... | collective-permute-start | bytes 1572872 | tf_op jit(solution)/shard_map/ppermute | solution.py:58
  93.7 31.9 %collective-permute-start.19 = (bf16[32,64,128]{2,1,0:T(8,128)(2,1)}, bf16[32,64,128]{2,1,0:T(8,128)(2,1)S(1)}, u32[]{:S(2)}, u32[]{:S(2)}) collective-permute-start(bf16[32,64,128]{2,1,0:T(8,128)(2,1)} %get-tuple-element.31), channel_id=1, source_target_pairs={{0,64},{8,72},{16,80},{24,88},{32,96},{40,104},{48,112},{56,120},{... | collective-permute-start | bytes 1572872 | tf_op jit(solution)/shard_map/ppermute | solution.py:55
  93.9 31.7 %collective-permute-start.20 = (bf16[32,64,128]{2,1,0:T(8,128)(2,1)}, bf16[32,64,128]{2,1,0:T(8,128)(2,1)}, u32[]{:S(2)}, u32[]{:S(2)}) collective-permute-start(bf16[32,64,128]{2,1,0:T(8,128)(2,1)} %get-tuple-element.32), channel_id=1, source_target_pairs={{0,68},{1,69},{2,70},{3,71},{4,64},{5,65},{6,66},{7,67},{8,76},{9,... | collective-permute-start | bytes 1572872 | tf_op jit(solution)/shard_map/ppermute | solution.py:64
  113.1 19.5 %collective-permute-start.6 = (bf16[32,64,128]{2,1,0:T(8,128)(2,1)}, bf16[32,64,128]{2,1,0:T(8,128)(2,1)S(1)}, u32[]{:S(2)}, u32[]{:S(2)}) collective-permute-start(bf16[32,64,128]{2,1,0:T(8,128)(2,1)} %get-tuple-element.22), channel_id=1, source_target_pairs={{0,4},{1,5},{2,6},{3,7},{4,0},{5,1},{6,2},{7,3},{8,12},{9,13},{10,... | collective-permute-start | bytes 1572872 | tf_op jit(solution)/shard_map/ppermute | solution.py:58
  116.1 31.9 %collective-permute-start.7 = (bf16[32,64,128]{2,1,0:T(8,128)(2,1)}, bf16[32,64,128]{2,1,0:T(8,128)(2,1)S(1)}, u32[]{:S(2)}, u32[]{:S(2)}) collective-permute-start(bf16[32,64,128]{2,1,0:T(8,128)(2,1)} %get-tuple-element.23), channel_id=1, source_target_pairs={{0,64},{8,72},{16,80},{24,88},{32,96},{40,104},{48,112},{56,120},{... | collective-permute-start | bytes 1572872 | tf_op jit(solution)/shard_map/ppermute | solution.py:55
  116.1 31.9 %collective-permute-start.8 = (bf16[32,64,128]{2,1,0:T(8,128)(2,1)}, bf16[32,64,128]{2,1,0:T(8,128)(2,1)S(1)}, u32[]{:S(2)}, u32[]{:S(2)}) collective-permute-start(bf16[32,64,128]{2,1,0:T(8,128)(2,1)} %get-tuple-element.24), channel_id=1, source_target_pairs={{0,68},{1,69},{2,70},{3,71},{4,64},{5,65},{6,66},{7,67},{8,76},{9,... | collective-permute-start | bytes 1572872 | tf_op jit(solution)/shard_map/ppermute | solution.py:64
  128.6 27.1 %collective-permute-start.23 = (bf16[32,64,128]{2,1,0:T(8,128)(2,1)S(1)}, bf16[32,64,128]{2,1,0:T(8,128)(2,1)S(1)}, u32[]{:S(2)}, u32[]{:S(2)}) collective-permute-start(bf16[32,64,128]{2,1,0:T(8,128)(2,1)S(1)} %get-tuple-element.34), channel_id=1, source_target_pairs={{0,1},{1,0},{2,3},{3,2},{4,5},{5,4},{6,7},{7,6},{8,9},{9,8},{10,11... | collective-permute-start | bytes 1572872 | tf_op jit(solution)/shard_map/ppermute | solution.py:58
  128.6 40.6 %collective-permute-start.22 = (bf16[32,64,128]{2,1,0:T(8,128)(2,1)}, bf16[32,64,128]{2,1,0:T(8,128)(2,1)S(1)}, u32[]{:S(2)}, u32[]{:S(2)}) collective-permute-start(bf16[32,64,128]{2,1,0:T(8,128)(2,1)} %get-tuple-element.35), channel_id=1, source_target_pairs={{0,8},{8,0},{16,24},{24,16},{32,40},{40,32},{48,56},{56,48},{64,72... | collective-permute-start | bytes 1572872 | tf_op jit(solution)/shard_map/ppermute | solution.py:55
  132.5 40.3 %collective-permute-start.21 = (bf16[32,64,128]{2,1,0:T(8,128)(2,1)}, bf16[32,64,128]{2,1,0:T(8,128)(2,1)S(1)}, u32[]{:S(2)}, u32[]{:S(2)}) collective-permute-start(bf16[32,64,128]{2,1,0:T(8,128)(2,1)} %get-tuple-element.36), channel_id=1, source_target_pairs={{0,9},{1,8},{2,11},{3,10},{4,13},{5,12},{6,15},{7,14},{8,1},{9,0},... | collective-permute-start | bytes 1572872 | tf_op jit(solution)/shard_map/ppermute | solution.py:64
  150.2 28.8 %collective-permute-start.11 = (bf16[32,64,128]{2,1,0:T(8,128)(2,1)}, bf16[32,64,128]{2,1,0:T(8,128)(2,1)S(1)}, u32[]{:S(2)}, u32[]{:S(2)}) collective-permute-start(bf16[32,64,128]{2,1,0:T(8,128)(2,1)} %get-tuple-element.42), channel_id=1, source_target_pairs={{0,1},{1,0},{2,3},{3,2},{4,5},{5,4},{6,7},{7,6},{8,9},{9,8},{10,11... | collective-permute-start | bytes 1572872 | tf_op jit(solution)/shard_map/ppermute | solution.py:58
  150.2 32.3 %collective-permute-start.10 = (bf16[32,64,128]{2,1,0:T(8,128)(2,1)}, bf16[32,64,128]{2,1,0:T(8,128)(2,1)S(1)}, u32[]{:S(2)}, u32[]{:S(2)}) collective-permute-start(bf16[32,64,128]{2,1,0:T(8,128)(2,1)} %get-tuple-element.43), channel_id=1, source_target_pairs={{0,8},{8,0},{16,24},{24,16},{32,40},{40,32},{48,56},{56,48},{64,72... | collective-permute-start | bytes 1572872 | tf_op jit(solution)/shard_map/ppermute | solution.py:55
  155.7 36.5 %collective-permute-start.9 = (bf16[32,64,128]{2,1,0:T(8,128)(2,1)}, bf16[32,64,128]{2,1,0:T(8,128)(2,1)S(1)}, u32[]{:S(2)}, u32[]{:S(2)}) collective-permute-start(bf16[32,64,128]{2,1,0:T(8,128)(2,1)} %get-tuple-element.44), channel_id=1, source_target_pairs={{0,9},{1,8},{2,11},{3,10},{4,13},{5,12},{6,15},{7,14},{8,1},{9,0},... | collective-permute-start | bytes 1572872 | tf_op jit(solution)/shard_map/ppermute | solution.py:64
  (16 other events, 118.1 us)

commit v10 on v9

--- a/solution.py
+++ b/solution.py
@@ -126,6 +126,57 @@
     return out
 
 
+def raw_stage(cur, block_of, sets):
+    size = cur[0].shape[0]
+    lanes = cur[0].shape[1]
+    wide = jnp.concatenate(
+        [jnp.concatenate([cur[g] for g in group], axis=0) for group in sets], axis=1
+    )
+    rows = []
+    for k in range(4):
+        total = None
+        for c in range(4):
+            block = block_of(k, c)
+            if block is None:
+                continue
+            term = jnp.dot(block, wide[c * size:(c + 1) * size], preferred_element_type=jnp.float32)
+            total = term if total is None else total + term
+        rows.append(total.astype(jnp.bfloat16))
+    mixed = jnp.concatenate(rows, axis=0)
+    out = list(cur)
+    for b, group in enumerate(sets):
+        for c, g in enumerate(group):
+            out[g] = mixed[c * size:(c + 1) * size, b * lanes:(b + 1) * lanes]
+    return out
+
+
+def raw_chain_kernel(plan, k_ref, x_ref, lv_ref, ip_ref, o_ref):
+    cur = [x_ref[g] for g in range(x_ref.shape[0])]
+    cur = raw_stage(cur, lambda k, c: ip_ref[...] if k == c else None, plan[0])
+    for index, sets in enumerate(plan[1:]):
+        cur = raw_stage(cur, lambda k, c: lv_ref[index, k, c], sets)
+    for g in range(len(cur)):
+        o_ref[g] = cur[g]
+
+
+def raw_chain_call(plan, k0, data, levels, interpolate, data_spec, out_shape, out_spec):
+    zeros = (0,) * levels.ndim
+    return pl.pallas_call(
+        functools.partial(raw_chain_kernel, plan),
+        grid_spec=pltpu.PrefetchScalarGridSpec(
+            num_scalar_prefetch=1,
+            grid=(1,),
+            in_specs=[
+                data_spec,
+                pl.BlockSpec(levels.shape, lambda i, k: zeros),
+                pl.BlockSpec(interpolate.shape, lambda i, k: (0, 0)),
+            ],
+            out_specs=out_spec,
+        ),
+        out_shape=out_shape,
+    )(k0, data, levels, interpolate)
+
+
 def chain_sets(count, stride):
     return [
         [a * 4 * stride + c * stride + e for c in range(4)]
@@ -245,7 +296,9 @@
             target=gradient,
         )
 
-    first = local_forward(0, 1)
+    first = raw_chain_call(
+        forward_plan, k0_ref, image, levels, interpolate, in_place(0, 1), piece_shape, whole_piece
+    )
     merges, output_weight, forward_levels, spread, first = lax.optimization_barrier(
         (merges, output_weight, forward_levels, spread, first)
     )

time: 196 us -> 200 us (1.020)
  waiting for transfers between devices: 54.8 us -> 60.8 us
  starting transfers between devices: 53.7 us -> 49.6 us
    ppermute x8, waiting for transfers between devices: 16 us -> 20.9 us  [flip_send(): return lax.ppermute(value, 'qy', pairs)]
    pallas_call x0 -> x1, Pallas kernels: none -> 3.53 us  [raw_chain_call(): pl.pallas_call(functools.partial(raw_chain_kernel, plan), grid_spec=pltpu...]
    pallas_call x16 -> x15, Pallas kernels: 42.8 us -> 40.1 us  [chain_call(): pl.pallas_call(functools.partial(chain_kernel, plan), grid_spec=pltpu.Pre...]
    ppermute x8, starting transfers between devices: 16.5 us -> 14 us  [flip_send(): return lax.ppermute(value, 'qx', pairs)]
    ppermute x8, starting transfers between devices: 14.3 us -> 11.9 us  [flip_send(): return lax.ppermute(value, 'qy', pairs)]
    unnamed x33 -> x31, local copies, waits for them, and re-layouts: 4.83 us -> 5.52 us
  transfers between devices with their start and end apart: 24 -> 24, of which waited for: 10 -> 11; matrix products, arithmetic and copies ran while one was open for 8% -> 8% of each run, Pallas kernels for 29% -> 29%
where the time goes in v10:
time: 200 us; the launch traced here: 199 us
  Pallas kernels  63.4 us (32%)
  waiting for transfers between devices  60.8 us (30%)
  starting transfers between devices  49.6 us (25%)
  local copies, waits for them, and re-layouts  16.1 us (8%)
  matrix products  6.47 us (3%)
  other arithmetic  2.31 us (1%)
    pallas_call x15, Pallas kernels, chain_call(): pl.pallas_call(functools.partial(chain_kernel, plan), grid_spec=pltpu.Pre...  40.1 us
    ppermute x8, waiting for transfers between devices, flip_send(): return lax.ppermute(value, 'qx', pairs)  30.2 us
    ppermute x8, starting transfers between devices, flip_send(): return lax.ppermute(value, ('qx', 'qy'), pairs)  23.7 us
    ppermute x8, waiting for transfers between devices, flip_send(): return lax.ppermute(value, 'qy', pairs)  20.9 us
    pallas_call x2, Pallas kernels, output_stage(): pl.pallas_call(output_stage_kernel, grid=(part // step,), in_specs=[piece...  19.8 us
    ppermute x8, starting transfers between devices, flip_send(): return lax.ppermute(value, 'qx', pairs)  14 us
    ppermute x8, starting transfers between devices, flip_send(): return lax.ppermute(value, 'qy', pairs)  11.9 us
    ppermute x8, waiting for transfers between devices, flip_send(): return lax.ppermute(value, ('qx', 'qy'), pairs)  9.66 us
  transfers between devices with their start and end apart: 24, of which 11 were waited for; matrix products, arithmetic and copies ran while one was open for 8% of the time, Pallas kernels for 29%

profile of v10, /device:TPU:1, one launch (start us, length us, event | category | flops | bytes accessed | tf_op | source)
XLA Modules:
  0.0 199.0 jit_solution(11920732766859243136)
XLA Ops:
  13.1 3.5 %shard_map.77 = bf16[32,64,128]{2,1,0:T(8,128)(2,1)} custom-call(s32[1]{0:T(128)} %bitcast.k_ref, bf16[4,2,32,64,128]{4,3,2,1,0:T(8,128)(2,1)} %bitcast.169, bf16[2,4,4,64,64]{4,3,2,1,0:T(8,128)(2,1)} %bitcast.179, bf16[64,64]{1,0:T(8,128)(2,1)} %ip_ref.1), custom_call_target="tpu_custom_call" | custom-call | tf_op jit(solution)/shard_map/pallas_call | solution.py:164
  22.0 2.7 %shard_map.74 = bf16[32,64,128]{2,1,0:T(8,128)(2,1)} custom-call(s32[1]{0:T(128)} %bitcast.k_ref, bf16[4,2,32,64,128]{4,3,2,1,0:T(8,128)(2,1)} %bitcast.171, bf16[3,256,256]{2,1,0:T(8,128)(2,1)} %pad_maximum_fusion.4.m_ref), custom_call_target="tpu_custom_call" | custom-call | tf_op jit(solution)/shard_map/pallas_call | solution.py:205
  24.8 2.7 %shard_map.79 = bf16[32,64,128]{2,1,0:T(8,128)(2,1)} custom-call(s32[1]{0:T(128)} %bitcast.k_ref, bf16[4,2,32,64,128]{4,3,2,1,0:T(8,128)(2,1)} %bitcast.172, bf16[3,256,256]{2,1,0:T(8,128)(2,1)} %pad_maximum_fusion.4.m_ref), custom_call_target="tpu_custom_call" | custom-call | tf_op jit(solution)/shard_map/pallas_call | solution.py:205
  27.6 2.7 %shard_map.75 = bf16[32,64,128]{2,1,0:T(8,128)(2,1)} custom-call(s32[1]{0:T(128)} %bitcast.k_ref, bf16[4,2,32,64,128]{4,3,2,1,0:T(8,128)(2,1)} %bitcast.173, bf16[3,256,256]{2,1,0:T(8,128)(2,1)} %pad_maximum_fusion.4.m_ref), custom_call_target="tpu_custom_call" | custom-call | tf_op jit(solution)/shard_map/pallas_call | solution.py:205
  39.4 2.9 %collective-permute-start.15 = (bf16[32,64,128]{2,1,0:T(8,128)(2,1)}, bf16[32,64,128]{2,1,0:T(8,128)(2,1)}, u32[]{:S(2)}, u32[]{:S(2)}) collective-permute-start(bf16[32,64,128]{2,1,0:T(8,128)(2,1)} %get-tuple-element.39), channel_id=1, source_target_pairs={{0,4},{1,5},{2,6},{3,7},{4,0},{5,1},{6,2},{7,3},{8,12},{9,13},{10,... | collective-permute-start | bytes 1572872 | tf_op jit(solution)/shard_map/ppermute | solution.py:58
  42.3 3.0 %collective-permute-start.16 = (bf16[32,64,128]{2,1,0:T(8,128)(2,1)S(1)}, bf16[32,64,128]{2,1,0:T(8,128)(2,1)}, u32[]{:S(2)}, u32[]{:S(2)}) collective-permute-start(bf16[32,64,128]{2,1,0:T(8,128)(2,1)S(1)} %get-tuple-element.38), channel_id=1, source_target_pairs={{0,64},{8,72},{16,80},{24,88},{32,96},{40,104},{48,112},{56,120},{... | collective-permute-start | bytes 1572872 | tf_op jit(solution)/shard_map/ppermute | solution.py:55
  45.3 2.8 %collective-permute-done.2 = bf16[32,64,128]{2,1,0:T(8,128)(2,1)} collective-permute-done((bf16[32,64,128]{2,1,0:T(8,128)(2,1)}, bf16[32,64,128]{2,1,0:T(8,128)(2,1)}, u32[]{:S(2)}, u32[]{:S(2)}) %collective-permute-start.2) | collective-permute-done | bytes 524320 | tf_op jit(solution)/shard_map/ppermute | solution.py:64
  48.2 6.3 %collective-permute-start.17 = (bf16[32,64,128]{2,1,0:T(8,128)(2,1)S(1)}, bf16[32,64,128]{2,1,0:T(8,128)(2,1)}, u32[]{:S(2)}, u32[]{:S(2)}) collective-permute-start(bf16[32,64,128]{2,1,0:T(8,128)(2,1)S(1)} %get-tuple-element.37), channel_id=1, source_target_pairs={{0,68},{1,69},{2,70},{3,71},{4,64},{5,65},{6,66},{7,67},{8,76},{9,... | collective-permute-start | bytes 1572872 | tf_op jit(solution)/shard_map/ppermute | solution.py:64
  54.4 15.6 %collective-permute-done = bf16[32,64,128]{2,1,0:T(8,128)(2,1)} collective-permute-done((bf16[32,64,128]{2,1,0:T(8,128)(2,1)}, bf16[32,64,128]{2,1,0:T(8,128)(2,1)}, u32[]{:S(2)}, u32[]{:S(2)}) %collective-permute-start) | collective-permute-done | bytes 524320 | tf_op jit(solution)/shard_map/ppermute | solution.py:58
  73.1 2.9 %collective-permute-start.3 = (bf16[32,64,128]{2,1,0:T(8,128)(2,1)}, bf16[32,64,128]{2,1,0:T(8,128)(2,1)}, u32[]{:S(2)}, u32[]{:S(2)}) collective-permute-start(bf16[32,64,128]{2,1,0:T(8,128)(2,1)} %get-tuple-element.47), channel_id=1, source_target_pairs={{0,4},{1,5},{2,6},{3,7},{4,0},{5,1},{6,2},{7,3},{8,12},{9,13},{10,... | collective-permute-start | bytes 1572872 | tf_op jit(solution)/shard_map/ppermute | solution.py:58
  78.5 3.0 %collective-permute-start.4 = (bf16[32,64,128]{2,1,0:T(8,128)(2,1)S(1)}, bf16[32,64,128]{2,1,0:T(8,128)(2,1)}, u32[]{:S(2)}, u32[]{:S(2)}) collective-permute-start(bf16[32,64,128]{2,1,0:T(8,128)(2,1)S(1)} %get-tuple-element.46), channel_id=1, source_target_pairs={{0,64},{8,72},{16,80},{24,88},{32,96},{40,104},{48,112},{56,120},{... | collective-permute-start | bytes 1572872 | tf_op jit(solution)/shard_map/ppermute | solution.py:55
  84.1 9.9 %shard_map.82 = (bf16[32,64,128]{2,1,0:T(8,128)(2,1)}, bf16[32,64,128]{2,1,0:T(8,128)(2,1)}, bf16[32,64,128]{2,1,0:T(8,128)(2,1)}, bf16[32,64,128]{2,1,0:T(8,128)(2,1)}) custom-call(bf16[32,64,128]{2,1,0:T(8,128)(2,1)} %get-tuple-element.40.p0, bf16[32,64,128]{2,1,0:T(8,128)(2,1)} %collective-permute-done.15.p1, ...), custom_call_target="tpu_custom_call" | custom-call | flops 2147483648 | bytes 10485760 | tf_op jit(solution)/shard_map/pallas_call | solution.py:224
  94.0 3.0 %collective-permute-start.18 = (bf16[32,64,128]{2,1,0:T(8,128)(2,1)}, bf16[32,64,128]{2,1,0:T(8,128)(2,1)S(1)}, u32[]{:S(2)}, u32[]{:S(2)}) collective-permute-start(bf16[32,64,128]{2,1,0:T(8,128)(2,1)} %get-tuple-element.30), channel_id=1, source_target_pairs={{0,4},{1,5},{2,6},{3,7},{4,0},{5,1},{6,2},{7,3},{8,12},{9,13},{10,... | collective-permute-start | bytes 1572872 | tf_op jit(solution)/shard_map/ppermute | solution.py:58
  99.8 6.8 %collective-permute-done.4.p2 = bf16[32,64,128]{2,1,0:T(8,128)(2,1)} collective-permute-done((bf16[32,64,128]{2,1,0:T(8,128)(2,1)S(1)}, bf16[32,64,128]{2,1,0:T(8,128)(2,1)}, u32[]{:S(2)}, u32[]{:S(2)}) %collective-permute-start.4) | collective-permute-done | bytes 524320 | tf_op jit(solution)/shard_map/ppermute | solution.py:55
  106.6 9.9 %shard_map.78 = (bf16[32,64,128]{2,1,0:T(8,128)(2,1)}, bf16[32,64,128]{2,1,0:T(8,128)(2,1)}, bf16[32,64,128]{2,1,0:T(8,128)(2,1)}, bf16[32,64,128]{2,1,0:T(8,128)(2,1)}) custom-call(bf16[32,64,128]{2,1,0:T(8,128)(2,1)} %get-tuple-element.48.p0, bf16[32,64,128]{2,1,0:T(8,128)(2,1)} %collective-permute-done.3.p1, ...), custom_call_target="tpu_custom_call" | custom-call | flops 2147483648 | bytes 10485760 | tf_op jit(solution)/shard_map/pallas_call | solution.py:224
  116.5 3.0 %collective-permute-start.6 = (bf16[32,64,128]{2,1,0:T(8,128)(2,1)}, bf16[32,64,128]{2,1,0:T(8,128)(2,1)S(1)}, u32[]{:S(2)}, u32[]{:S(2)}) collective-permute-start(bf16[32,64,128]{2,1,0:T(8,128)(2,1)} %get-tuple-element.22), channel_id=1, source_target_pairs={{0,4},{1,5},{2,6},{3,7},{4,0},{5,1},{6,2},{7,3},{8,12},{9,13},{10,... | collective-permute-start | bytes 1572872 | tf_op jit(solution)/shard_map/ppermute | solution.py:58
  119.5 2.8 %collective-permute-start.8 = (bf16[32,64,128]{2,1,0:T(8,128)(2,1)}, bf16[32,64,128]{2,1,0:T(8,128)(2,1)S(1)}, u32[]{:S(2)}, u32[]{:S(2)}) collective-permute-start(bf16[32,64,128]{2,1,0:T(8,128)(2,1)} %get-tuple-element.24), channel_id=1, source_target_pairs={{0,68},{1,69},{2,70},{3,71},{4,64},{5,65},{6,66},{7,67},{8,76},{9,... | collective-permute-start | bytes 1572872 | tf_op jit(solution)/shard_map/ppermute | solution.py:64
  122.2 6.7 %collective-permute-done.19 = bf16[32,64,128]{2,1,0:T(8,128)(2,1)S(1)} collective-permute-done((bf16[32,64,128]{2,1,0:T(8,128)(2,1)}, bf16[32,64,128]{2,1,0:T(8,128)(2,1)S(1)}, u32[]{:S(2)}, u32[]{:S(2)}) %collective-permute-start.19) | collective-permute-done | bytes 524320 | tf_op jit(solution)/shard_map/ppermute | solution.py:55
  132.0 2.9 %collective-permute-start.22 = (bf16[32,64,128]{2,1,0:T(8,128)(2,1)}, bf16[32,64,128]{2,1,0:T(8,128)(2,1)S(1)}, u32[]{:S(2)}, u32[]{:S(2)}) collective-permute-start(bf16[32,64,128]{2,1,0:T(8,128)(2,1)} %get-tuple-element.35), channel_id=1, source_target_pairs={{0,8},{8,0},{16,24},{24,16},{32,40},{40,32},{48,56},{56,48},{64,72... | collective-permute-start | bytes 1572872 | tf_op jit(solution)/shard_map/ppermute | solution.py:55
  137.3 14.1 %collective-permute-done.7 = bf16[32,64,128]{2,1,0:T(8,128)(2,1)S(1)} collective-permute-done((bf16[32,64,128]{2,1,0:T(8,128)(2,1)}, bf16[32,64,128]{2,1,0:T(8,128)(2,1)S(1)}, u32[]{:S(2)}, u32[]{:S(2)}) %collective-permute-start.7) | collective-permute-done | bytes 524320 | tf_op jit(solution)/shard_map/ppermute | solution.py:55
  153.6 2.9 %collective-permute-start.10 = (bf16[32,64,128]{2,1,0:T(8,128)(2,1)}, bf16[32,64,128]{2,1,0:T(8,128)(2,1)S(1)}, u32[]{:S(2)}, u32[]{:S(2)}) collective-permute-start(bf16[32,64,128]{2,1,0:T(8,128)(2,1)} %get-tuple-element.43), channel_id=1, source_target_pairs={{0,8},{8,0},{16,24},{24,16},{32,40},{40,32},{48,56},{56,48},{64,72... | collective-permute-start | bytes 1572872 | tf_op jit(solution)/shard_map/ppermute | solution.py:55
  156.5 3.1 %collective-permute-done.23.x_ref = bf16[32,64,128]{2,1,0:T(8,128)(2,1)S(1)} collective-permute-done((bf16[32,64,128]{2,1,0:T(8,128)(2,1)S(1)}, bf16[32,64,128]{2,1,0:T(8,128)(2,1)S(1)}, u32[]{:S(2)}, u32[]{:S(2)}) %collective-permute-start.23) | collective-permute-done | bytes 524320 | tf_op jit(solution)/shard_map/ppermute | solution.py:58
  159.6 6.0 %collective-permute-start.9 = (bf16[32,64,128]{2,1,0:T(8,128)(2,1)}, bf16[32,64,128]{2,1,0:T(8,128)(2,1)S(1)}, u32[]{:S(2)}, u32[]{:S(2)}) collective-permute-start(bf16[32,64,128]{2,1,0:T(8,128)(2,1)} %get-tuple-element.44), channel_id=1, source_target_pairs={{0,9},{1,8},{2,11},{3,10},{4,13},{5,12},{6,15},{7,14},{8,1},{9,0},... | collective-permute-start | bytes 1572872 | tf_op jit(solution)/shard_map/ppermute | solution.py:64
  189.1 6.5 %collective-permute-done.9.x_ref = bf16[32,64,128]{2,1,0:T(8,128)(2,1)S(1)} collective-permute-done((bf16[32,64,128]{2,1,0:T(8,128)(2,1)}, bf16[32,64,128]{2,1,0:T(8,128)(2,1)S(1)}, u32[]{:S(2)}, u32[]{:S(2)}) %collective-permute-start.9) | collective-permute-done | bytes 524320 | tf_op jit(solution)/shard_map/ppermute | solution.py:64
  (112 shorter events, 72.9 us)
Async XLA Ops:
  6.8 26.6 %collective-permute-start.13 = (bf16[32,64,128]{2,1,0:T(8,128)(2,1)}, bf16[32,64,128]{2,1,0:T(8,128)(2,1)S(1)}, u32[]{:S(2)}, u32[]{:S(2)}) collective-permute-start(bf16[32,64,128]{2,1,0:T(8,128)(2,1)} %shard_map.80), channel_id=1, source_target_pairs={{0,8},{8,0},{16,24},{24,16},{32,40},{40,32},{48,56},{56,48},{64,72... | collective-permute-start | bytes 1572872 | tf_op jit(solution)/shard_map/ppermute | solution.py:55
  10.9 23.6 %collective-permute-start.14 = (bf16[32,64,128]{2,1,0:T(8,128)(2,1)}, bf16[32,64,128]{2,1,0:T(8,128)(2,1)}, u32[]{:S(2)}, u32[]{:S(2)}) collective-permute-start(bf16[32,64,128]{2,1,0:T(8,128)(2,1)} %shard_map.81), channel_id=1, source_target_pairs={{0,9},{1,8},{2,11},{3,10},{4,13},{5,12},{6,15},{7,14},{8,1},{9,0},... | collective-permute-start | bytes 1572872 | tf_op jit(solution)/shard_map/ppermute | solution.py:64
  17.1 19.2 %collective-permute-start.12 = (bf16[32,64,128]{2,1,0:T(8,128)(2,1)}, bf16[32,64,128]{2,1,0:T(8,128)(2,1)}, u32[]{:S(2)}, u32[]{:S(2)}) collective-permute-start(bf16[32,64,128]{2,1,0:T(8,128)(2,1)} %shard_map.77), channel_id=1, source_target_pairs={{0,1},{1,0},{2,3},{3,2},{4,5},{5,4},{6,7},{7,6},{8,9},{9,8},{10,11... | collective-permute-start | bytes 1572872 | tf_op jit(solution)/shard_map/ppermute | solution.py:58
  19.9 28.2 %collective-permute-start.2 = (bf16[32,64,128]{2,1,0:T(8,128)(2,1)}, bf16[32,64,128]{2,1,0:T(8,128)(2,1)}, u32[]{:S(2)}, u32[]{:S(2)}) collective-permute-start(bf16[32,64,128]{2,1,0:T(8,128)(2,1)} %shard_map.76), channel_id=1, source_target_pairs={{0,9},{1,8},{2,11},{3,10},{4,13},{5,12},{6,15},{7,14},{8,1},{9,0},... | collective-permute-start | bytes 1572872 | tf_op jit(solution)/shard_map/ppermute | solution.py:64
  24.7 45.3 %collective-permute-start = (bf16[32,64,128]{2,1,0:T(8,128)(2,1)}, bf16[32,64,128]{2,1,0:T(8,128)(2,1)}, u32[]{:S(2)}, u32[]{:S(2)}) collective-permute-start(bf16[32,64,128]{2,1,0:T(8,128)(2,1)} %shard_map.74), channel_id=1, source_target_pairs={{0,1},{1,0},{2,3},{3,2},{4,5},{5,4},{6,7},{7,6},{8,9},{9,8},{10,11... | collective-permute-start | bytes 1572872 | tf_op jit(solution)/shard_map/ppermute | solution.py:58
  34.0 36.0 %collective-permute-start.1 = (bf16[32,64,128]{2,1,0:T(8,128)(2,1)S(1)}, bf16[32,64,128]{2,1,0:T(8,128)(2,1)S(1)}, u32[]{:S(2)}, u32[]{:S(2)}) collective-permute-start(bf16[32,64,128]{2,1,0:T(8,128)(2,1)S(1)} %copy-done.10), channel_id=1, source_target_pairs={{0,8},{8,0},{16,24},{24,16},{32,40},{40,32},{48,56},{56,48},{64,72... | collective-permute-start | bytes 1572872 | tf_op jit(solution)/shard_map/ppermute | solution.py:55
  39.4 42.1 %collective-permute-start.15 = (bf16[32,64,128]{2,1,0:T(8,128)(2,1)}, bf16[32,64,128]{2,1,0:T(8,128)(2,1)}, u32[]{:S(2)}, u32[]{:S(2)}) collective-permute-start(bf16[32,64,128]{2,1,0:T(8,128)(2,1)} %get-tuple-element.39), channel_id=1, source_target_pairs={{0,4},{1,5},{2,6},{3,7},{4,0},{5,1},{6,2},{7,3},{8,12},{9,13},{10,... | collective-permute-start | bytes 1572872 | tf_op jit(solution)/shard_map/ppermute | solution.py:58
  42.3 41.8 %collective-permute-start.16 = (bf16[32,64,128]{2,1,0:T(8,128)(2,1)S(1)}, bf16[32,64,128]{2,1,0:T(8,128)(2,1)}, u32[]{:S(2)}, u32[]{:S(2)}) collective-permute-start(bf16[32,64,128]{2,1,0:T(8,128)(2,1)S(1)} %get-tuple-element.38), channel_id=1, source_target_pairs={{0,64},{8,72},{16,80},{24,88},{32,96},{40,104},{48,112},{56,120},{... | collective-permute-start | bytes 1572872 | tf_op jit(solution)/shard_map/ppermute | solution.py:55
  48.2 36.0 %collective-permute-start.17 = (bf16[32,64,128]{2,1,0:T(8,128)(2,1)S(1)}, bf16[32,64,128]{2,1,0:T(8,128)(2,1)}, u32[]{:S(2)}, u32[]{:S(2)}) collective-permute-start(bf16[32,64,128]{2,1,0:T(8,128)(2,1)S(1)} %get-tuple-element.37), channel_id=1, source_target_pairs={{0,68},{1,69},{2,70},{3,71},{4,64},{5,65},{6,66},{7,67},{8,76},{9,... | collective-permute-start | bytes 1572872 | tf_op jit(solution)/shard_map/ppermute | solution.py:64
  73.1 24.1 %collective-permute-start.3 = (bf16[32,64,128]{2,1,0:T(8,128)(2,1)}, bf16[32,64,128]{2,1,0:T(8,128)(2,1)}, u32[]{:S(2)}, u32[]{:S(2)}) collective-permute-start(bf16[32,64,128]{2,1,0:T(8,128)(2,1)} %get-tuple-element.47), channel_id=1, source_target_pairs={{0,4},{1,5},{2,6},{3,7},{4,0},{5,1},{6,2},{7,3},{8,12},{9,13},{10,... | collective-permute-start | bytes 1572872 | tf_op jit(solution)/shard_map/ppermute | solution.py:58
  78.5 28.1 %collective-permute-start.4 = (bf16[32,64,128]{2,1,0:T(8,128)(2,1)S(1)}, bf16[32,64,128]{2,1,0:T(8,128)(2,1)}, u32[]{:S(2)}, u32[]{:S(2)}) collective-permute-start(bf16[32,64,128]{2,1,0:T(8,128)(2,1)S(1)} %get-tuple-element.46), channel_id=1, source_target_pairs={{0,64},{8,72},{16,80},{24,88},{32,96},{40,104},{48,112},{56,120},{... | collective-permute-start | bytes 1572872 | tf_op jit(solution)/shard_map/ppermute | solution.py:55
  81.6 25.0 %collective-permute-start.5 = (bf16[32,64,128]{2,1,0:T(8,128)(2,1)S(1)}, bf16[32,64,128]{2,1,0:T(8,128)(2,1)}, u32[]{:S(2)}, u32[]{:S(2)}) collective-permute-start(bf16[32,64,128]{2,1,0:T(8,128)(2,1)S(1)} %get-tuple-element.45), channel_id=1, source_target_pairs={{0,68},{1,69},{2,70},{3,71},{4,64},{5,65},{6,66},{7,67},{8,76},{9,... | collective-permute-start | bytes 1572872 | tf_op jit(solution)/shard_map/ppermute | solution.py:64
  94.0 25.4 %collective-permute-start.18 = (bf16[32,64,128]{2,1,0:T(8,128)(2,1)}, bf16[32,64,128]{2,1,0:T(8,128)(2,1)S(1)}, u32[]{:S(2)}, u32[]{:S(2)}) collective-permute-start(bf16[32,64,128]{2,1,0:T(8,128)(2,1)} %get-tuple-element.30), channel_id=1, source_target_pairs={{0,4},{1,5},{2,6},{3,7},{4,0},{5,1},{6,2},{7,3},{8,12},{9,13},{10,... | collective-permute-start | bytes 1572872 | tf_op jit(solution)/shard_map/ppermute | solution.py:58
  97.0 32.0 %collective-permute-start.19 = (bf16[32,64,128]{2,1,0:T(8,128)(2,1)}, bf16[32,64,128]{2,1,0:T(8,128)(2,1)S(1)}, u32[]{:S(2)}, u32[]{:S(2)}) collective-permute-start(bf16[32,64,128]{2,1,0:T(8,128)(2,1)} %get-tuple-element.31), channel_id=1, source_target_pairs={{0,64},{8,72},{16,80},{24,88},{32,96},{40,104},{48,112},{56,120},{... | collective-permute-start | bytes 1572872 | tf_op jit(solution)/shard_map/ppermute | solution.py:55
  97.2 31.7 %collective-permute-start.20 = (bf16[32,64,128]{2,1,0:T(8,128)(2,1)}, bf16[32,64,128]{2,1,0:T(8,128)(2,1)}, u32[]{:S(2)}, u32[]{:S(2)}) collective-permute-start(bf16[32,64,128]{2,1,0:T(8,128)(2,1)} %get-tuple-element.32), channel_id=1, source_target_pairs={{0,68},{1,69},{2,70},{3,71},{4,64},{5,65},{6,66},{7,67},{8,76},{9,... | collective-permute-start | bytes 1572872 | tf_op jit(solution)/shard_map/ppermute | solution.py:64
  116.5 18.4 %collective-permute-start.6 = (bf16[32,64,128]{2,1,0:T(8,128)(2,1)}, bf16[32,64,128]{2,1,0:T(8,128)(2,1)S(1)}, u32[]{:S(2)}, u32[]{:S(2)}) collective-permute-start(bf16[32,64,128]{2,1,0:T(8,128)(2,1)} %get-tuple-element.22), channel_id=1, source_target_pairs={{0,4},{1,5},{2,6},{3,7},{4,0},{5,1},{6,2},{7,3},{8,12},{9,13},{10,... | collective-permute-start | bytes 1572872 | tf_op jit(solution)/shard_map/ppermute | solution.py:58
  119.5 32.0 %collective-permute-start.7 = (bf16[32,64,128]{2,1,0:T(8,128)(2,1)}, bf16[32,64,128]{2,1,0:T(8,128)(2,1)S(1)}, u32[]{:S(2)}, u32[]{:S(2)}) collective-permute-start(bf16[32,64,128]{2,1,0:T(8,128)(2,1)} %get-tuple-element.23), channel_id=1, source_target_pairs={{0,64},{8,72},{16,80},{24,88},{32,96},{40,104},{48,112},{56,120},{... | collective-permute-start | bytes 1572872 | tf_op jit(solution)/shard_map/ppermute | solution.py:55
  119.5 32.0 %collective-permute-start.8 = (bf16[32,64,128]{2,1,0:T(8,128)(2,1)}, bf16[32,64,128]{2,1,0:T(8,128)(2,1)S(1)}, u32[]{:S(2)}, u32[]{:S(2)}) collective-permute-start(bf16[32,64,128]{2,1,0:T(8,128)(2,1)} %get-tuple-element.24), channel_id=1, source_target_pairs={{0,68},{1,69},{2,70},{3,71},{4,64},{5,65},{6,66},{7,67},{8,76},{9,... | collective-permute-start | bytes 1572872 | tf_op jit(solution)/shard_map/ppermute | solution.py:64
  132.0 27.6 %collective-permute-start.23 = (bf16[32,64,128]{2,1,0:T(8,128)(2,1)S(1)}, bf16[32,64,128]{2,1,0:T(8,128)(2,1)S(1)}, u32[]{:S(2)}, u32[]{:S(2)}) collective-permute-start(bf16[32,64,128]{2,1,0:T(8,128)(2,1)S(1)} %get-tuple-element.34), channel_id=1, source_target_pairs={{0,1},{1,0},{2,3},{3,2},{4,5},{5,4},{6,7},{7,6},{8,9},{9,8},{10,11... | collective-permute-start | bytes 1572872 | tf_op jit(solution)/shard_map/ppermute | solution.py:58
  132.0 39.8 %collective-permute-start.22 = (bf16[32,64,128]{2,1,0:T(8,128)(2,1)}, bf16[32,64,128]{2,1,0:T(8,128)(2,1)S(1)}, u32[]{:S(2)}, u32[]{:S(2)}) collective-permute-start(bf16[32,64,128]{2,1,0:T(8,128)(2,1)} %get-tuple-element.35), channel_id=1, source_target_pairs={{0,8},{8,0},{16,24},{24,16},{32,40},{40,32},{48,56},{56,48},{64,72... | collective-permute-start | bytes 1572872 | tf_op jit(solution)/shard_map/ppermute | solution.py:55
  134.9 40.7 %collective-permute-start.21 = (bf16[32,64,128]{2,1,0:T(8,128)(2,1)}, bf16[32,64,128]{2,1,0:T(8,128)(2,1)S(1)}, u32[]{:S(2)}, u32[]{:S(2)}) collective-permute-start(bf16[32,64,128]{2,1,0:T(8,128)(2,1)} %get-tuple-element.36), channel_id=1, source_target_pairs={{0,9},{1,8},{2,11},{3,10},{4,13},{5,12},{6,15},{7,14},{8,1},{9,0},... | collective-permute-start | bytes 1572872 | tf_op jit(solution)/shard_map/ppermute | solution.py:64
  153.6 28.5 %collective-permute-start.11 = (bf16[32,64,128]{2,1,0:T(8,128)(2,1)}, bf16[32,64,128]{2,1,0:T(8,128)(2,1)S(1)}, u32[]{:S(2)}, u32[]{:S(2)}) collective-permute-start(bf16[32,64,128]{2,1,0:T(8,128)(2,1)} %get-tuple-element.42), channel_id=1, source_target_pairs={{0,1},{1,0},{2,3},{3,2},{4,5},{5,4},{6,7},{7,6},{8,9},{9,8},{10,11... | collective-permute-start | bytes 1572872 | tf_op jit(solution)/shard_map/ppermute | solution.py:58
  153.6 32.0 %collective-permute-start.10 = (bf16[32,64,128]{2,1,0:T(8,128)(2,1)}, bf16[32,64,128]{2,1,0:T(8,128)(2,1)S(1)}, u32[]{:S(2)}, u32[]{:S(2)}) collective-permute-start(bf16[32,64,128]{2,1,0:T(8,128)(2,1)} %get-tuple-element.43), channel_id=1, source_target_pairs={{0,8},{8,0},{16,24},{24,16},{32,40},{40,32},{48,56},{56,48},{64,72... | collective-permute-start | bytes 1572872 | tf_op jit(solution)/shard_map/ppermute | solution.py:55
  159.6 35.9 %collective-permute-start.9 = (bf16[32,64,128]{2,1,0:T(8,128)(2,1)}, bf16[32,64,128]{2,1,0:T(8,128)(2,1)S(1)}, u32[]{:S(2)}, u32[]{:S(2)}) collective-permute-start(bf16[32,64,128]{2,1,0:T(8,128)(2,1)} %get-tuple-element.44), channel_id=1, source_target_pairs={{0,9},{1,8},{2,11},{3,10},{4,13},{5,12},{6,15},{7,14},{8,1},{9,0},... | collective-permute-start | bytes 1572872 | tf_op jit(solution)/shard_map/ppermute | solution.py:64
  (15 other events, 116.7 us)

commit v11 on v10

--- a/solution.py
+++ b/solution.py
@@ -296,9 +296,13 @@
             target=gradient,
         )
 
-    first = raw_chain_call(
-        forward_plan, k0_ref, image, levels, interpolate, in_place(0, 1), piece_shape, whole_piece
-    )
+    first = [
+        raw_chain_call(
+            forward_plan, k0_ref, image, levels, interpolate, in_place(0, f), piece_shape,
+            whole_piece,
+        )
+        for f in (1, 2, 3)
+    ]
     merges, output_weight, forward_levels, spread, first = lax.optimization_barrier(
         (merges, output_weight, forward_levels, spread, first)
     )
@@ -312,7 +316,7 @@
 
     gradient = None
     for m in range(CHUNKS):
-        coef = [first if (m, f) == (0, 1) else local_forward(m, f) for f in range(4)]
+        coef = [first[f - 1] if m == 0 and f else local_forward(m, f) for f in range(4)]
         pieces = exchange(coef, *shifts[0])
         cur = mixing(w0, jnp.stack(pieces), "scor,cjrl->sjol")
         pieces = exchange(cur, *shifts[1])

time: 200 us -> 201 us (level)
  starting transfers between devices: 49.6 us -> 53.9 us
  waiting for transfers between devices: 60.8 us -> 57.6 us
    pallas_call x1 -> x3, Pallas kernels: 3.53 us -> 10.6 us  [raw_chain_call(): pl.pallas_call(functools.partial(raw_chain_kernel, plan), grid_spec=pltpu...]
    pallas_call x15 -> x13, Pallas kernels: 40.1 us -> 34.8 us  [chain_call(): pl.pallas_call(functools.partial(chain_kernel, plan), grid_spec=pltpu.Pre...]
    ppermute x8, waiting for transfers between devices: 20.9 us -> 15.8 us  [flip_send(): return lax.ppermute(value, 'qy', pairs)]
    ppermute x8, waiting for transfers between devices: 9.66 us -> 12.4 us  [flip_send(): return lax.ppermute(value, ('qx', 'qy'), pairs)]
    ppermute x8, starting transfers between devices: 11.9 us -> 14.4 us  [flip_send(): return lax.ppermute(value, 'qy', pairs)]
    ppermute x8, starting transfers between devices: 14 us -> 16.3 us  [flip_send(): return lax.ppermute(value, 'qx', pairs)]
    unnamed x31 -> x39, local copies, waits for them, and re-layouts: 5.52 us -> 4.83 us
  transfers between devices with their start and end apart: 24 -> 24, of which waited for: 11 -> 10; matrix products, arithmetic and copies ran while one was open for 8% -> 9% of each run, Pallas kernels for 29% -> 26%
where the time goes in v11:
time: 201 us; the launch traced here: 200 us
  Pallas kernels  65.2 us (32%)
  waiting for transfers between devices  57.6 us (29%)
  starting transfers between devices  53.9 us (27%)
  local copies, waits for them, and re-layouts  14.4 us (7%)
  matrix products  6.78 us (3%)
  other arithmetic  2.3 us (1%)
    pallas_call x13, Pallas kernels, chain_call(): pl.pallas_call(functools.partial(chain_kernel, plan), grid_spec=pltpu.Pre...  34.8 us
    ppermute x8, waiting for transfers between devices, flip_send(): return lax.ppermute(value, 'qx', pairs)  29.3 us
    ppermute x8, starting transfers between devices, flip_send(): return lax.ppermute(value, ('qx', 'qy'), pairs)  23.1 us
    pallas_call x2, Pallas kernels, output_stage(): pl.pallas_call(output_stage_kernel, grid=(part // step,), in_specs=[piece...  19.8 us
    ppermute x8, starting transfers between devices, flip_send(): return lax.ppermute(value, 'qx', pairs)  16.3 us
    ppermute x8, waiting for transfers between devices, flip_send(): return lax.ppermute(value, 'qy', pairs)  15.8 us
    ppermute x8, starting transfers between devices, flip_send(): return lax.ppermute(value, 'qy', pairs)  14.4 us
    ppermute x8, waiting for transfers between devices, flip_send(): return lax.ppermute(value, ('qx', 'qy'), pairs)  12.4 us
  transfers between devices with their start and end apart: 24, of which 10 were waited for; matrix products, arithmetic and copies ran while one was open for 9% of the time, Pallas kernels for 26%

profile of v11, /device:TPU:1, one launch (start us, length us, event | category | flops | bytes accessed | tf_op | source)
XLA Modules:
  0.0 200.4 jit_solution(15414928876285418512)
XLA Ops:
  0.0 3.5 %shard_map.77 = bf16[32,64,128]{2,1,0:T(8,128)(2,1)} custom-call(s32[1]{0:T(128)} %bitcast.k_ref, bf16[4,2,32,64,128]{4,3,2,1,0:T(8,128)(2,1)} %bitcast.167, bf16[2,4,4,64,64]{4,3,2,1,0:T(8,128)(2,1)} %bitcast.179, bf16[64,64]{1,0:T(8,128)(2,1)} %ip_ref.5), custom_call_target="tpu_custom_call" | custom-call | tf_op jit(solution)/shard_map/pallas_call | solution.py:164
  3.5 3.5 %shard_map.78 = bf16[32,64,128]{2,1,0:T(8,128)(2,1)} custom-call(s32[1]{0:T(128)} %bitcast.k_ref, bf16[4,2,32,64,128]{4,3,2,1,0:T(8,128)(2,1)} %bitcast.168, bf16[2,4,4,64,64]{4,3,2,1,0:T(8,128)(2,1)} %bitcast.180, bf16[64,64]{1,0:T(8,128)(2,1)} %ip_ref.5), custom_call_target="tpu_custom_call" | custom-call | tf_op jit(solution)/shard_map/pallas_call | solution.py:164
  7.1 3.6 %shard_map.79 = bf16[32,64,128]{2,1,0:T(8,128)(2,1)} custom-call(s32[1]{0:T(128)} %bitcast.k_ref, bf16[4,2,32,64,128]{4,3,2,1,0:T(8,128)(2,1)} %bitcast.169, bf16[2,4,4,64,64]{4,3,2,1,0:T(8,128)(2,1)} %bitcast.181, bf16[64,64]{1,0:T(8,128)(2,1)} %ip_ref.5), custom_call_target="tpu_custom_call" | custom-call | tf_op jit(solution)/shard_map/pallas_call | solution.py:164
  22.0 2.7 %shard_map.74 = bf16[32,64,128]{2,1,0:T(8,128)(2,1)} custom-call(s32[1]{0:T(128)} %bitcast.k_ref, bf16[4,2,32,64,128]{4,3,2,1,0:T(8,128)(2,1)} %bitcast.171, bf16[3,256,256]{2,1,0:T(8,128)(2,1)} %pad_maximum_fusion.4.m_ref), custom_call_target="tpu_custom_call" | custom-call | tf_op jit(solution)/shard_map/pallas_call | solution.py:205
  24.9 2.7 %shard_map.81 = bf16[32,64,128]{2,1,0:T(8,128)(2,1)} custom-call(s32[1]{0:T(128)} %bitcast.k_ref, bf16[4,2,32,64,128]{4,3,2,1,0:T(8,128)(2,1)} %bitcast.172, bf16[3,256,256]{2,1,0:T(8,128)(2,1)} %pad_maximum_fusion.4.m_ref), custom_call_target="tpu_custom_call" | custom-call | tf_op jit(solution)/shard_map/pallas_call | solution.py:205
  34.5 4.8 %collective-permute-done.14 = bf16[32,64,128]{2,1,0:T(8,128)(2,1)} collective-permute-done((bf16[32,64,128]{2,1,0:T(8,128)(2,1)S(1)}, bf16[32,64,128]{2,1,0:T(8,128)(2,1)}, u32[]{:S(2)}, u32[]{:S(2)}) %collective-permute-start.14) | collective-permute-done | bytes 524320 | tf_op jit(solution)/shard_map/ppermute | solution.py:64
  42.7 3.0 %collective-permute-start.15 = (bf16[32,64,128]{2,1,0:T(8,128)(2,1)}, bf16[32,64,128]{2,1,0:T(8,128)(2,1)}, u32[]{:S(2)}, u32[]{:S(2)}) collective-permute-start(bf16[32,64,128]{2,1,0:T(8,128)(2,1)} %get-tuple-element.43), channel_id=1, source_target_pairs={{0,4},{1,5},{2,6},{3,7},{4,0},{5,1},{6,2},{7,3},{8,12},{9,13},{10,... | collective-permute-start | bytes 1572872 | tf_op jit(solution)/shard_map/ppermute | solution.py:58
  45.7 3.6 %collective-permute-start.16 = (bf16[32,64,128]{2,1,0:T(8,128)(2,1)S(1)}, bf16[32,64,128]{2,1,0:T(8,128)(2,1)}, u32[]{:S(2)}, u32[]{:S(2)}) collective-permute-start(bf16[32,64,128]{2,1,0:T(8,128)(2,1)S(1)} %get-tuple-element.42), channel_id=1, source_target_pairs={{0,64},{8,72},{16,80},{24,88},{32,96},{40,104},{48,112},{56,120},{... | collective-permute-start | bytes 1572872 | tf_op jit(solution)/shard_map/ppermute | solution.py:55
  50.5 6.3 %collective-permute-start.17 = (bf16[32,64,128]{2,1,0:T(8,128)(2,1)S(1)}, bf16[32,64,128]{2,1,0:T(8,128)(2,1)}, u32[]{:S(2)}, u32[]{:S(2)}) collective-permute-start(bf16[32,64,128]{2,1,0:T(8,128)(2,1)S(1)} %get-tuple-element.41), channel_id=1, source_target_pairs={{0,68},{1,69},{2,70},{3,71},{4,64},{5,65},{6,66},{7,67},{8,76},{9,... | collective-permute-start | bytes 1572872 | tf_op jit(solution)/shard_map/ppermute | solution.py:64
  56.9 14.4 %collective-permute-done = bf16[32,64,128]{2,1,0:T(8,128)(2,1)} collective-permute-done((bf16[32,64,128]{2,1,0:T(8,128)(2,1)}, bf16[32,64,128]{2,1,0:T(8,128)(2,1)}, u32[]{:S(2)}, u32[]{:S(2)}) %collective-permute-start) | collective-permute-done | bytes 524320 | tf_op jit(solution)/shard_map/ppermute | solution.py:58
  74.4 2.8 %collective-permute-start.3 = (bf16[32,64,128]{2,1,0:T(8,128)(2,1)}, bf16[32,64,128]{2,1,0:T(8,128)(2,1)}, u32[]{:S(2)}, u32[]{:S(2)}) collective-permute-start(bf16[32,64,128]{2,1,0:T(8,128)(2,1)} %get-tuple-element.51), channel_id=1, source_target_pairs={{0,4},{1,5},{2,6},{3,7},{4,0},{5,1},{6,2},{7,3},{8,12},{9,13},{10,... | collective-permute-start | bytes 1572872 | tf_op jit(solution)/shard_map/ppermute | solution.py:58
  79.7 3.2 %collective-permute-start.4 = (bf16[32,64,128]{2,1,0:T(8,128)(2,1)S(1)}, bf16[32,64,128]{2,1,0:T(8,128)(2,1)}, u32[]{:S(2)}, u32[]{:S(2)}) collective-permute-start(bf16[32,64,128]{2,1,0:T(8,128)(2,1)S(1)} %get-tuple-element.50), channel_id=1, source_target_pairs={{0,64},{8,72},{16,80},{24,88},{32,96},{40,104},{48,112},{56,120},{... | collective-permute-start | bytes 1572872 | tf_op jit(solution)/shard_map/ppermute | solution.py:55
  85.5 9.9 %shard_map.82 = (bf16[32,64,128]{2,1,0:T(8,128)(2,1)}, bf16[32,64,128]{2,1,0:T(8,128)(2,1)}, bf16[32,64,128]{2,1,0:T(8,128)(2,1)}, bf16[32,64,128]{2,1,0:T(8,128)(2,1)}) custom-call(bf16[32,64,128]{2,1,0:T(8,128)(2,1)} %get-tuple-element.44.p0, bf16[32,64,128]{2,1,0:T(8,128)(2,1)} %collective-permute-done.15.p1, ...), custom_call_target="tpu_custom_call" | custom-call | flops 2147483648 | bytes 10485760 | tf_op jit(solution)/shard_map/pallas_call | solution.py:224
  95.4 3.0 %collective-permute-start.18 = (bf16[32,64,128]{2,1,0:T(8,128)(2,1)}, bf16[32,64,128]{2,1,0:T(8,128)(2,1)S(1)}, u32[]{:S(2)}, u32[]{:S(2)}) collective-permute-start(bf16[32,64,128]{2,1,0:T(8,128)(2,1)} %get-tuple-element.34), channel_id=1, source_target_pairs={{0,4},{1,5},{2,6},{3,7},{4,0},{5,1},{6,2},{7,3},{8,12},{9,13},{10,... | collective-permute-start | bytes 1572872 | tf_op jit(solution)/shard_map/ppermute | solution.py:58
  101.2 6.8 %collective-permute-done.4.p2 = bf16[32,64,128]{2,1,0:T(8,128)(2,1)} collective-permute-done((bf16[32,64,128]{2,1,0:T(8,128)(2,1)S(1)}, bf16[32,64,128]{2,1,0:T(8,128)(2,1)}, u32[]{:S(2)}, u32[]{:S(2)}) %collective-permute-start.4) | collective-permute-done | bytes 524320 | tf_op jit(solution)/shard_map/ppermute | solution.py:55
  108.0 9.9 %shard_map.80 = (bf16[32,64,128]{2,1,0:T(8,128)(2,1)}, bf16[32,64,128]{2,1,0:T(8,128)(2,1)}, bf16[32,64,128]{2,1,0:T(8,128)(2,1)}, bf16[32,64,128]{2,1,0:T(8,128)(2,1)}) custom-call(bf16[32,64,128]{2,1,0:T(8,128)(2,1)} %get-tuple-element.52.p0, bf16[32,64,128]{2,1,0:T(8,128)(2,1)} %collective-permute-done.3.p1, ...), custom_call_target="tpu_custom_call" | custom-call | flops 2147483648 | bytes 10485760 | tf_op jit(solution)/shard_map/pallas_call | solution.py:224
  117.9 3.0 %collective-permute-start.6 = (bf16[32,64,128]{2,1,0:T(8,128)(2,1)}, bf16[32,64,128]{2,1,0:T(8,128)(2,1)S(1)}, u32[]{:S(2)}, u32[]{:S(2)}) collective-permute-start(bf16[32,64,128]{2,1,0:T(8,128)(2,1)} %get-tuple-element.24), channel_id=1, source_target_pairs={{0,4},{1,5},{2,6},{3,7},{4,0},{5,1},{6,2},{7,3},{8,12},{9,13},{10,... | collective-permute-start | bytes 1572872 | tf_op jit(solution)/shard_map/ppermute | solution.py:58
  120.9 2.8 %collective-permute-start.8 = (bf16[32,64,128]{2,1,0:T(8,128)(2,1)}, bf16[32,64,128]{2,1,0:T(8,128)(2,1)S(1)}, u32[]{:S(2)}, u32[]{:S(2)}) collective-permute-start(bf16[32,64,128]{2,1,0:T(8,128)(2,1)} %get-tuple-element.26), channel_id=1, source_target_pairs={{0,68},{1,69},{2,70},{3,71},{4,64},{5,65},{6,66},{7,67},{8,76},{9,... | collective-permute-start | bytes 1572872 | tf_op jit(solution)/shard_map/ppermute | solution.py:64
  123.7 6.7 %collective-permute-done.19 = bf16[32,64,128]{2,1,0:T(8,128)(2,1)S(1)} collective-permute-done((bf16[32,64,128]{2,1,0:T(8,128)(2,1)}, bf16[32,64,128]{2,1,0:T(8,128)(2,1)S(1)}, u32[]{:S(2)}, u32[]{:S(2)}) %collective-permute-start.19) | collective-permute-done | bytes 524320 | tf_op jit(solution)/shard_map/ppermute | solution.py:55
  133.4 4.0 %collective-permute-start.22 = (bf16[32,64,128]{2,1,0:T(8,128)(2,1)}, bf16[32,64,128]{2,1,0:T(8,128)(2,1)S(1)}, u32[]{:S(2)}, u32[]{:S(2)}) collective-permute-start(bf16[32,64,128]{2,1,0:T(8,128)(2,1)} %get-tuple-element.39), channel_id=1, source_target_pairs={{0,8},{8,0},{16,24},{24,16},{32,40},{40,32},{48,56},{56,48},{64,72... | collective-permute-start | bytes 1572872 | tf_op jit(solution)/shard_map/ppermute | solution.py:55
  139.5 13.3 %collective-permute-done.7 = bf16[32,64,128]{2,1,0:T(8,128)(2,1)S(1)} collective-permute-done((bf16[32,64,128]{2,1,0:T(8,128)(2,1)}, bf16[32,64,128]{2,1,0:T(8,128)(2,1)S(1)}, u32[]{:S(2)}, u32[]{:S(2)}) %collective-permute-start.7) | collective-permute-done | bytes 524320 | tf_op jit(solution)/shard_map/ppermute | solution.py:55
  155.0 4.0 %collective-permute-start.10 = (bf16[32,64,128]{2,1,0:T(8,128)(2,1)}, bf16[32,64,128]{2,1,0:T(8,128)(2,1)S(1)}, u32[]{:S(2)}, u32[]{:S(2)}) collective-permute-start(bf16[32,64,128]{2,1,0:T(8,128)(2,1)} %get-tuple-element.47), channel_id=1, source_target_pairs={{0,8},{8,0},{16,24},{24,16},{32,40},{40,32},{48,56},{56,48},{64,72... | collective-permute-start | bytes 1572872 | tf_op jit(solution)/shard_map/ppermute | solution.py:55
  160.3 7.5 %collective-permute-start.9 = (bf16[32,64,128]{2,1,0:T(8,128)(2,1)}, bf16[32,64,128]{2,1,0:T(8,128)(2,1)S(1)}, u32[]{:S(2)}, u32[]{:S(2)}) collective-permute-start(bf16[32,64,128]{2,1,0:T(8,128)(2,1)} %get-tuple-element.48), channel_id=1, source_target_pairs={{0,9},{1,8},{2,11},{3,10},{4,13},{5,12},{6,15},{7,14},{8,1},{9,0},... | collective-permute-start | bytes 1572872 | tf_op jit(solution)/shard_map/ppermute | solution.py:64
  190.9 6.1 %collective-permute-done.9.x_ref = bf16[32,64,128]{2,1,0:T(8,128)(2,1)S(1)} collective-permute-done((bf16[32,64,128]{2,1,0:T(8,128)(2,1)}, bf16[32,64,128]{2,1,0:T(8,128)(2,1)S(1)}, u32[]{:S(2)}, u32[]{:S(2)}) %collective-permute-start.9) | collective-permute-done | bytes 524320 | tf_op jit(solution)/shard_map/ppermute | solution.py:64
  (120 shorter events, 69.0 us)
Async XLA Ops:
  12.1 21.3 %collective-permute-start.12 = (bf16[32,64,128]{2,1,0:T(8,128)(2,1)S(1)}, bf16[32,64,128]{2,1,0:T(8,128)(2,1)}, u32[]{:S(2)}, u32[]{:S(2)}) collective-permute-start(bf16[32,64,128]{2,1,0:T(8,128)(2,1)S(1)} %copy-done.12), channel_id=1, source_target_pairs={{0,1},{1,0},{2,3},{3,2},{4,5},{5,4},{6,7},{7,6},{8,9},{9,8},{10,11... | collective-permute-start | bytes 1572872 | tf_op jit(solution)/shard_map/ppermute | solution.py:58
  14.6 19.8 %collective-permute-start.13 = (bf16[32,64,128]{2,1,0:T(8,128)(2,1)S(1)}, bf16[32,64,128]{2,1,0:T(8,128)(2,1)}, u32[]{:S(2)}, u32[]{:S(2)}) collective-permute-start(bf16[32,64,128]{2,1,0:T(8,128)(2,1)S(1)} %copy-done.11), channel_id=1, source_target_pairs={{0,8},{8,0},{16,24},{24,16},{32,40},{40,32},{48,56},{56,48},{64,72... | collective-permute-start | bytes 1572872 | tf_op jit(solution)/shard_map/ppermute | solution.py:55
  15.6 23.7 %collective-permute-start.14 = (bf16[32,64,128]{2,1,0:T(8,128)(2,1)S(1)}, bf16[32,64,128]{2,1,0:T(8,128)(2,1)}, u32[]{:S(2)}, u32[]{:S(2)}) collective-permute-start(bf16[32,64,128]{2,1,0:T(8,128)(2,1)S(1)} %copy-done.10), channel_id=1, source_target_pairs={{0,9},{1,8},{2,11},{3,10},{4,13},{5,12},{6,15},{7,14},{8,1},{9,0},... | collective-permute-start | bytes 1572872 | tf_op jit(solution)/shard_map/ppermute | solution.py:64
  20.2 30.3 %collective-permute-start.2 = (bf16[32,64,128]{2,1,0:T(8,128)(2,1)}, bf16[32,64,128]{2,1,0:T(8,128)(2,1)}, u32[]{:S(2)}, u32[]{:S(2)}) collective-permute-start(bf16[32,64,128]{2,1,0:T(8,128)(2,1)} %shard_map.76), channel_id=1, source_target_pairs={{0,9},{1,8},{2,11},{3,10},{4,13},{5,12},{6,15},{7,14},{8,1},{9,0},... | collective-permute-start | bytes 1572872 | tf_op jit(solution)/shard_map/ppermute | solution.py:64
  24.7 46.6 %collective-permute-start = (bf16[32,64,128]{2,1,0:T(8,128)(2,1)}, bf16[32,64,128]{2,1,0:T(8,128)(2,1)}, u32[]{:S(2)}, u32[]{:S(2)}) collective-permute-start(bf16[32,64,128]{2,1,0:T(8,128)(2,1)} %shard_map.74), channel_id=1, source_target_pairs={{0,1},{1,0},{2,3},{3,2},{4,5},{5,4},{6,7},{7,6},{8,9},{9,8},{10,11... | collective-permute-start | bytes 1572872 | tf_op jit(solution)/shard_map/ppermute | solution.py:58
  34.0 37.3 %collective-permute-start.1 = (bf16[32,64,128]{2,1,0:T(8,128)(2,1)S(1)}, bf16[32,64,128]{2,1,0:T(8,128)(2,1)S(1)}, u32[]{:S(2)}, u32[]{:S(2)}) collective-permute-start(bf16[32,64,128]{2,1,0:T(8,128)(2,1)S(1)} %copy-done.14), channel_id=1, source_target_pairs={{0,8},{8,0},{16,24},{24,16},{32,40},{40,32},{48,56},{56,48},{64,72... | collective-permute-start | bytes 1572872 | tf_op jit(solution)/shard_map/ppermute | solution.py:55
  42.7 40.2 %collective-permute-start.15 = (bf16[32,64,128]{2,1,0:T(8,128)(2,1)}, bf16[32,64,128]{2,1,0:T(8,128)(2,1)}, u32[]{:S(2)}, u32[]{:S(2)}) collective-permute-start(bf16[32,64,128]{2,1,0:T(8,128)(2,1)} %get-tuple-element.43), channel_id=1, source_target_pairs={{0,4},{1,5},{2,6},{3,7},{4,0},{5,1},{6,2},{7,3},{8,12},{9,13},{10,... | collective-permute-start | bytes 1572872 | tf_op jit(solution)/shard_map/ppermute | solution.py:58
  45.7 39.8 %collective-permute-start.16 = (bf16[32,64,128]{2,1,0:T(8,128)(2,1)S(1)}, bf16[32,64,128]{2,1,0:T(8,128)(2,1)}, u32[]{:S(2)}, u32[]{:S(2)}) collective-permute-start(bf16[32,64,128]{2,1,0:T(8,128)(2,1)S(1)} %get-tuple-element.42), channel_id=1, source_target_pairs={{0,64},{8,72},{16,80},{24,88},{32,96},{40,104},{48,112},{56,120},{... | collective-permute-start | bytes 1572872 | tf_op jit(solution)/shard_map/ppermute | solution.py:55
  50.5 35.0 %collective-permute-start.17 = (bf16[32,64,128]{2,1,0:T(8,128)(2,1)S(1)}, bf16[32,64,128]{2,1,0:T(8,128)(2,1)}, u32[]{:S(2)}, u32[]{:S(2)}) collective-permute-start(bf16[32,64,128]{2,1,0:T(8,128)(2,1)S(1)} %get-tuple-element.41), channel_id=1, source_target_pairs={{0,68},{1,69},{2,70},{3,71},{4,64},{5,65},{6,66},{7,67},{8,76},{9,... | collective-permute-start | bytes 1572872 | tf_op jit(solution)/shard_map/ppermute | solution.py:64
  74.4 24.2 %collective-permute-start.3 = (bf16[32,64,128]{2,1,0:T(8,128)(2,1)}, bf16[32,64,128]{2,1,0:T(8,128)(2,1)}, u32[]{:S(2)}, u32[]{:S(2)}) collective-permute-start(bf16[32,64,128]{2,1,0:T(8,128)(2,1)} %get-tuple-element.51), channel_id=1, source_target_pairs={{0,4},{1,5},{2,6},{3,7},{4,0},{5,1},{6,2},{7,3},{8,12},{9,13},{10,... | collective-permute-start | bytes 1572872 | tf_op jit(solution)/shard_map/ppermute | solution.py:58
  79.7 28.2 %collective-permute-start.4 = (bf16[32,64,128]{2,1,0:T(8,128)(2,1)S(1)}, bf16[32,64,128]{2,1,0:T(8,128)(2,1)}, u32[]{:S(2)}, u32[]{:S(2)}) collective-permute-start(bf16[32,64,128]{2,1,0:T(8,128)(2,1)S(1)} %get-tuple-element.50), channel_id=1, source_target_pairs={{0,64},{8,72},{16,80},{24,88},{32,96},{40,104},{48,112},{56,120},{... | collective-permute-start | bytes 1572872 | tf_op jit(solution)/shard_map/ppermute | solution.py:55
  82.9 25.0 %collective-permute-start.5 = (bf16[32,64,128]{2,1,0:T(8,128)(2,1)S(1)}, bf16[32,64,128]{2,1,0:T(8,128)(2,1)}, u32[]{:S(2)}, u32[]{:S(2)}) collective-permute-start(bf16[32,64,128]{2,1,0:T(8,128)(2,1)S(1)} %get-tuple-element.49), channel_id=1, source_target_pairs={{0,68},{1,69},{2,70},{3,71},{4,64},{5,65},{6,66},{7,67},{8,76},{9,... | collective-permute-start | bytes 1572872 | tf_op jit(solution)/shard_map/ppermute | solution.py:64
  95.4 25.5 %collective-permute-start.18 = (bf16[32,64,128]{2,1,0:T(8,128)(2,1)}, bf16[32,64,128]{2,1,0:T(8,128)(2,1)S(1)}, u32[]{:S(2)}, u32[]{:S(2)}) collective-permute-start(bf16[32,64,128]{2,1,0:T(8,128)(2,1)} %get-tuple-element.34), channel_id=1, source_target_pairs={{0,4},{1,5},{2,6},{3,7},{4,0},{5,1},{6,2},{7,3},{8,12},{9,13},{10,... | collective-permute-start | bytes 1572872 | tf_op jit(solution)/shard_map/ppermute | solution.py:58
  98.4 31.9 %collective-permute-start.19 = (bf16[32,64,128]{2,1,0:T(8,128)(2,1)}, bf16[32,64,128]{2,1,0:T(8,128)(2,1)S(1)}, u32[]{:S(2)}, u32[]{:S(2)}) collective-permute-start(bf16[32,64,128]{2,1,0:T(8,128)(2,1)} %get-tuple-element.35), channel_id=1, source_target_pairs={{0,64},{8,72},{16,80},{24,88},{32,96},{40,104},{48,112},{56,120},{... | collective-permute-start | bytes 1572872 | tf_op jit(solution)/shard_map/ppermute | solution.py:55
  98.6 31.8 %collective-permute-start.20 = (bf16[32,64,128]{2,1,0:T(8,128)(2,1)}, bf16[32,64,128]{2,1,0:T(8,128)(2,1)}, u32[]{:S(2)}, u32[]{:S(2)}) collective-permute-start(bf16[32,64,128]{2,1,0:T(8,128)(2,1)} %get-tuple-element.36), channel_id=1, source_target_pairs={{0,68},{1,69},{2,70},{3,71},{4,64},{5,65},{6,66},{7,67},{8,76},{9,... | collective-permute-start | bytes 1572872 | tf_op jit(solution)/shard_map/ppermute | solution.py:64
  117.9 19.5 %collective-permute-start.6 = (bf16[32,64,128]{2,1,0:T(8,128)(2,1)}, bf16[32,64,128]{2,1,0:T(8,128)(2,1)S(1)}, u32[]{:S(2)}, u32[]{:S(2)}) collective-permute-start(bf16[32,64,128]{2,1,0:T(8,128)(2,1)} %get-tuple-element.24), channel_id=1, source_target_pairs={{0,4},{1,5},{2,6},{3,7},{4,0},{5,1},{6,2},{7,3},{8,12},{9,13},{10,... | collective-permute-start | bytes 1572872 | tf_op jit(solution)/shard_map/ppermute | solution.py:58
  120.9 31.9 %collective-permute-start.7 = (bf16[32,64,128]{2,1,0:T(8,128)(2,1)}, bf16[32,64,128]{2,1,0:T(8,128)(2,1)S(1)}, u32[]{:S(2)}, u32[]{:S(2)}) collective-permute-start(bf16[32,64,128]{2,1,0:T(8,128)(2,1)} %get-tuple-element.25), channel_id=1, source_target_pairs={{0,64},{8,72},{16,80},{24,88},{32,96},{40,104},{48,112},{56,120},{... | collective-permute-start | bytes 1572872 | tf_op jit(solution)/shard_map/ppermute | solution.py:55
  120.9 31.9 %collective-permute-start.8 = (bf16[32,64,128]{2,1,0:T(8,128)(2,1)}, bf16[32,64,128]{2,1,0:T(8,128)(2,1)S(1)}, u32[]{:S(2)}, u32[]{:S(2)}) collective-permute-start(bf16[32,64,128]{2,1,0:T(8,128)(2,1)} %get-tuple-element.26), channel_id=1, source_target_pairs={{0,68},{1,69},{2,70},{3,71},{4,64},{5,65},{6,66},{7,67},{8,76},{9,... | collective-permute-start | bytes 1572872 | tf_op jit(solution)/shard_map/ppermute | solution.py:64
  133.4 27.0 %collective-permute-start.23 = (bf16[32,64,128]{2,1,0:T(8,128)(2,1)S(1)}, bf16[32,64,128]{2,1,0:T(8,128)(2,1)S(1)}, u32[]{:S(2)}, u32[]{:S(2)}) collective-permute-start(bf16[32,64,128]{2,1,0:T(8,128)(2,1)S(1)} %get-tuple-element.38), channel_id=1, source_target_pairs={{0,1},{1,0},{2,3},{3,2},{4,5},{5,4},{6,7},{7,6},{8,9},{9,8},{10,11... | collective-permute-start | bytes 1572872 | tf_op jit(solution)/shard_map/ppermute | solution.py:58
  133.4 40.6 %collective-permute-start.22 = (bf16[32,64,128]{2,1,0:T(8,128)(2,1)}, bf16[32,64,128]{2,1,0:T(8,128)(2,1)S(1)}, u32[]{:S(2)}, u32[]{:S(2)}) collective-permute-start(bf16[32,64,128]{2,1,0:T(8,128)(2,1)} %get-tuple-element.39), channel_id=1, source_target_pairs={{0,8},{8,0},{16,24},{24,16},{32,40},{40,32},{48,56},{56,48},{64,72... | collective-permute-start | bytes 1572872 | tf_op jit(solution)/shard_map/ppermute | solution.py:55
  137.4 40.4 %collective-permute-start.21 = (bf16[32,64,128]{2,1,0:T(8,128)(2,1)}, bf16[32,64,128]{2,1,0:T(8,128)(2,1)S(1)}, u32[]{:S(2)}, u32[]{:S(2)}) collective-permute-start(bf16[32,64,128]{2,1,0:T(8,128)(2,1)} %get-tuple-element.40), channel_id=1, source_target_pairs={{0,9},{1,8},{2,11},{3,10},{4,13},{5,12},{6,15},{7,14},{8,1},{9,0},... | collective-permute-start | bytes 1572872 | tf_op jit(solution)/shard_map/ppermute | solution.py:64
  155.0 28.9 %collective-permute-start.11 = (bf16[32,64,128]{2,1,0:T(8,128)(2,1)}, bf16[32,64,128]{2,1,0:T(8,128)(2,1)S(1)}, u32[]{:S(2)}, u32[]{:S(2)}) collective-permute-start(bf16[32,64,128]{2,1,0:T(8,128)(2,1)} %get-tuple-element.46), channel_id=1, source_target_pairs={{0,1},{1,0},{2,3},{3,2},{4,5},{5,4},{6,7},{7,6},{8,9},{9,8},{10,11... | collective-permute-start | bytes 1572872 | tf_op jit(solution)/shard_map/ppermute | solution.py:58
  155.0 32.4 %collective-permute-start.10 = (bf16[32,64,128]{2,1,0:T(8,128)(2,1)}, bf16[32,64,128]{2,1,0:T(8,128)(2,1)S(1)}, u32[]{:S(2)}, u32[]{:S(2)}) collective-permute-start(bf16[32,64,128]{2,1,0:T(8,128)(2,1)} %get-tuple-element.47), channel_id=1, source_target_pairs={{0,8},{8,0},{16,24},{24,16},{32,40},{40,32},{48,56},{56,48},{64,72... | collective-permute-start | bytes 1572872 | tf_op jit(solution)/shard_map/ppermute | solution.py:55
  160.3 36.6 %collective-permute-start.9 = (bf16[32,64,128]{2,1,0:T(8,128)(2,1)}, bf16[32,64,128]{2,1,0:T(8,128)(2,1)S(1)}, u32[]{:S(2)}, u32[]{:S(2)}) collective-permute-start(bf16[32,64,128]{2,1,0:T(8,128)(2,1)} %get-tuple-element.48), channel_id=1, source_target_pairs={{0,9},{1,8},{2,11},{3,10},{4,13},{5,12},{6,15},{7,14},{8,1},{9,0},... | collective-permute-start | bytes 1572872 | tf_op jit(solution)/shard_map/ppermute | solution.py:64
  (19 other events, 130.4 us)

commit v12 on v7

--- a/solution.py
+++ b/solution.py
@@ -215,12 +215,12 @@
 
     eye = jnp.eye(4, dtype=interpolate.dtype)
     spread = jnp.einsum("st,op->sotp", eye, interpolate).reshape(4 * rank_size, 4 * rank_size)
-    forward_levels = [
-        jnp.transpose(levels[i], (0, 2, 1, 3)).reshape(4 * rank_size, 4 * rank_size)
-        for i in range(local_depth)
-    ]
-    forward_mats = jnp.stack([spread] + forward_levels)
-    adjoint_mats = jnp.stack([w.T for w in reversed(forward_levels)] + [spread.T])
+    side = 4 * rank_size
+    forward_levels = jnp.transpose(levels, (0, 1, 3, 2, 4)).reshape(local_depth, side, side)
+    forward_mats = jnp.concatenate([spread[None], forward_levels], axis=0)
+    adjoint_mats = jnp.concatenate(
+        [jnp.swapaxes(forward_levels[::-1], 1, 2), spread.T[None]], axis=0
+    )
     forward_plan = [chain_sets(part, 1)] + [chain_sets(part, 4**i) for i in range(local_depth)]
     adjoint_plan = [chain_sets(part, 4**i) for i in reversed(range(local_depth))] + [
         chain_sets(part, 1)

time: 195 us -> 198 us (1.015)
  waiting for transfers between devices: 53.7 us -> 69.2 us
  starting transfers between devices: 53.6 us -> 40 us
  local copies, waits for them, and re-layouts: 14.6 us -> 16.7 us
    ppermute x8, waiting for transfers between devices: 9.12 us -> 23.4 us  [flip_send(): return lax.ppermute(value, ('qx', 'qy'), pairs)]
    ppermute x8, starting transfers between devices: 23 us -> 11.7 us  [flip_send(): return lax.ppermute(value, ('qx', 'qy'), pairs)]
    ppermute x8, starting transfers between devices: 16.3 us -> 12.7 us  [flip_send(): return lax.ppermute(value, 'qx', pairs)]
    ppermute x8, waiting for transfers between devices: 28.8 us -> 31.2 us  [flip_send(): return lax.ppermute(value, 'qx', pairs)]
    unnamed x32 -> x30, local copies, waits for them, and re-layouts: 4.06 us -> 6.29 us
  transfers between devices with their start and end apart: 24 -> 24, of which waited for: 9 -> 10; matrix products, arithmetic and copies ran while one was open for 8% -> 8% of each run, Pallas kernels for 30% -> 29%
where the time goes in v12:
time: 198 us; the launch traced here: 197 us
  waiting for transfers between devices  69.2 us (35%)
  Pallas kernels  62.7 us (32%)
  starting transfers between devices  40 us (20%)
  local copies, waits for them, and re-layouts  16.7 us (8%)
  matrix products  6.79 us (3%)
    pallas_call x16, Pallas kernels, chain_call(): pl.pallas_call(functools.partial(chain_kernel, plan), grid_spec=pltpu.Pre...  42.8 us
    ppermute x8, waiting for transfers between devices, flip_send(): return lax.ppermute(value, 'qx', pairs)  31.2 us
    ppermute x8, waiting for transfers between devices, flip_send(): return lax.ppermute(value, ('qx', 'qy'), pairs)  23.4 us
    pallas_call x2, Pallas kernels, output_stage(): pl.pallas_call(output_stage_kernel, grid=(part // step,), in_specs=[piece...  19.9 us
    ppermute x8, starting transfers between devices, flip_send(): return lax.ppermute(value, 'qy', pairs)  15.6 us
    ppermute x8, waiting for transfers between devices, flip_send(): return lax.ppermute(value, 'qy', pairs)  14.6 us
    ppermute x8, starting transfers between devices, flip_send(): return lax.ppermute(value, 'qx', pairs)  12.7 us
    ppermute x8, starting transfers between devices, flip_send(): return lax.ppermute(value, ('qx', 'qy'), pairs)  11.7 us
  transfers between devices with their start and end apart: 24, of which 10 were waited for; matrix products, arithmetic and copies ran while one was open for 8% of the time, Pallas kernels for 29%

profile of v12, /device:TPU:1, one launch (start us, length us, event | category | flops | bytes accessed | tf_op | source)
XLA Modules:
  0.0 197.0 jit_solution(5873417560587496937)
XLA Ops:
  4.8 2.7 %shard_map.79 = bf16[32,64,128]{2,1,0:T(8,128)(2,1)} custom-call(s32[1]{0:T(128)} %bitcast.k_ref, bf16[4,2,32,64,128]{4,3,2,1,0:T(8,128)(2,1)} %bitcast.154, bf16[3,256,256]{2,1,0:T(8,128)(2,1)} %copy.17.m_ref), custom_call_target="tpu_custom_call" | custom-call | tf_op jit(solution)/shard_map/pallas_call | solution.py:154
  9.9 2.7 %shard_map.80 = bf16[32,64,128]{2,1,0:T(8,128)(2,1)} custom-call(s32[1]{0:T(128)} %bitcast.k_ref, bf16[4,2,32,64,128]{4,3,2,1,0:T(8,128)(2,1)} %bitcast.155, bf16[3,256,256]{2,1,0:T(8,128)(2,1)} %copy.17.m_ref), custom_call_target="tpu_custom_call" | custom-call | tf_op jit(solution)/shard_map/pallas_call | solution.py:154
  13.6 2.7 %shard_map.81 = bf16[32,64,128]{2,1,0:T(8,128)(2,1)} custom-call(s32[1]{0:T(128)} %bitcast.k_ref, bf16[4,2,32,64,128]{4,3,2,1,0:T(8,128)(2,1)} %bitcast.156, bf16[3,256,256]{2,1,0:T(8,128)(2,1)} %copy.17.m_ref), custom_call_target="tpu_custom_call" | custom-call | tf_op jit(solution)/shard_map/pallas_call | solution.py:154
  16.3 2.7 %shard_map.74 = bf16[32,64,128]{2,1,0:T(8,128)(2,1)} custom-call(s32[1]{0:T(128)} %bitcast.k_ref, bf16[4,2,32,64,128]{4,3,2,1,0:T(8,128)(2,1)} %bitcast.157, bf16[3,256,256]{2,1,0:T(8,128)(2,1)} %copy.17.m_ref), custom_call_target="tpu_custom_call" | custom-call | tf_op jit(solution)/shard_map/pallas_call | solution.py:154
  20.3 2.7 %shard_map.75 = bf16[32,64,128]{2,1,0:T(8,128)(2,1)} custom-call(s32[1]{0:T(128)} %bitcast.k_ref, bf16[4,2,32,64,128]{4,3,2,1,0:T(8,128)(2,1)} %bitcast.158, bf16[3,256,256]{2,1,0:T(8,128)(2,1)} %copy.17.m_ref), custom_call_target="tpu_custom_call" | custom-call | tf_op jit(solution)/shard_map/pallas_call | solution.py:154
  24.0 2.7 %shard_map.78 = bf16[32,64,128]{2,1,0:T(8,128)(2,1)} custom-call(s32[1]{0:T(128)} %bitcast.k_ref, bf16[4,2,32,64,128]{4,3,2,1,0:T(8,128)(2,1)} %bitcast.159, bf16[3,256,256]{2,1,0:T(8,128)(2,1)} %copy.17.m_ref), custom_call_target="tpu_custom_call" | custom-call | tf_op jit(solution)/shard_map/pallas_call | solution.py:154
  26.7 2.7 %shard_map.76 = bf16[32,64,128]{2,1,0:T(8,128)(2,1)} custom-call(s32[1]{0:T(128)} %bitcast.k_ref, bf16[4,2,32,64,128]{4,3,2,1,0:T(8,128)(2,1)} %bitcast.160, bf16[3,256,256]{2,1,0:T(8,128)(2,1)} %copy.17.m_ref), custom_call_target="tpu_custom_call" | custom-call | tf_op jit(solution)/shard_map/pallas_call | solution.py:154
  29.3 2.7 %shard_map.73 = bf16[32,64,128]{2,1,0:T(8,128)(2,1)} custom-call(s32[1]{0:T(128)} %bitcast.k_ref, bf16[4,2,32,64,128]{4,3,2,1,0:T(8,128)(2,1)} %bitcast.161, bf16[3,256,256]{2,1,0:T(8,128)(2,1)} %copy.17.m_ref), custom_call_target="tpu_custom_call" | custom-call | tf_op jit(solution)/shard_map/pallas_call | solution.py:154
  37.9 3.0 %collective-permute-start.15 = (bf16[32,64,128]{2,1,0:T(8,128)(2,1)}, bf16[32,64,128]{2,1,0:T(8,128)(2,1)}, u32[]{:S(2)}, u32[]{:S(2)}) collective-permute-start(bf16[32,64,128]{2,1,0:T(8,128)(2,1)} %get-tuple-element.27), channel_id=1, source_target_pairs={{0,4},{1,5},{2,6},{3,7},{4,0},{5,1},{6,2},{7,3},{8,12},{9,13},{10,... | collective-permute-start | bytes 1572872 | tf_op jit(solution)/shard_map/ppermute | solution.py:58
  40.9 3.6 %collective-permute-start.16 = (bf16[32,64,128]{2,1,0:T(8,128)(2,1)}, bf16[32,64,128]{2,1,0:T(8,128)(2,1)}, u32[]{:S(2)}, u32[]{:S(2)}) collective-permute-start(bf16[32,64,128]{2,1,0:T(8,128)(2,1)} %get-tuple-element.26), channel_id=1, source_target_pairs={{0,64},{8,72},{16,80},{24,88},{32,96},{40,104},{48,112},{56,120},{... | collective-permute-start | bytes 1572872 | tf_op jit(solution)/shard_map/ppermute | solution.py:55
  44.5 5.6 %collective-permute-start.17 = (bf16[32,64,128]{2,1,0:T(8,128)(2,1)S(1)}, bf16[32,64,128]{2,1,0:T(8,128)(2,1)}, u32[]{:S(2)}, u32[]{:S(2)}) collective-permute-start(bf16[32,64,128]{2,1,0:T(8,128)(2,1)S(1)} %get-tuple-element.25), channel_id=1, source_target_pairs={{0,68},{1,69},{2,70},{3,71},{4,64},{5,65},{6,66},{7,67},{8,76},{9,... | collective-permute-start | bytes 1572872 | tf_op jit(solution)/shard_map/ppermute | solution.py:64
  50.1 18.2 %collective-permute-done.2 = bf16[32,64,128]{2,1,0:T(8,128)(2,1)S(1)} collective-permute-done((bf16[32,64,128]{2,1,0:T(8,128)(2,1)S(1)}, bf16[32,64,128]{2,1,0:T(8,128)(2,1)S(1)}, u32[]{:S(2)}, u32[]{:S(2)}) %collective-permute-start.2) | collective-permute-done | bytes 524320 | tf_op jit(solution)/shard_map/ppermute | solution.py:64
  71.4 2.9 %collective-permute-start.3 = (bf16[32,64,128]{2,1,0:T(8,128)(2,1)}, bf16[32,64,128]{2,1,0:T(8,128)(2,1)}, u32[]{:S(2)}, u32[]{:S(2)}) collective-permute-start(bf16[32,64,128]{2,1,0:T(8,128)(2,1)} %get-tuple-element.35), channel_id=1, source_target_pairs={{0,4},{1,5},{2,6},{3,7},{4,0},{5,1},{6,2},{7,3},{8,12},{9,13},{10,... | collective-permute-start | bytes 1572872 | tf_op jit(solution)/shard_map/ppermute | solution.py:58
  76.6 3.9 %collective-permute-start.4 = (bf16[32,64,128]{2,1,0:T(8,128)(2,1)}, bf16[32,64,128]{2,1,0:T(8,128)(2,1)S(1)}, u32[]{:S(2)}, u32[]{:S(2)}) collective-permute-start(bf16[32,64,128]{2,1,0:T(8,128)(2,1)} %get-tuple-element.34), channel_id=1, source_target_pairs={{0,64},{8,72},{16,80},{24,88},{32,96},{40,104},{48,112},{56,120},{... | collective-permute-start | bytes 1572872 | tf_op jit(solution)/shard_map/ppermute | solution.py:55
  81.0 9.9 %shard_map.82 = (bf16[32,64,128]{2,1,0:T(8,128)(2,1)}, bf16[32,64,128]{2,1,0:T(8,128)(2,1)}, bf16[32,64,128]{2,1,0:T(8,128)(2,1)}, bf16[32,64,128]{2,1,0:T(8,128)(2,1)}) custom-call(bf16[32,64,128]{2,1,0:T(8,128)(2,1)} %get-tuple-element.28.p0, bf16[32,64,128]{2,1,0:T(8,128)(2,1)} %collective-permute-done.15.p1, ...), custom_call_target="tpu_custom_call" | custom-call | flops 2147483648 | bytes 10485760 | tf_op jit(solution)/shard_map/pallas_call | solution.py:173
  91.0 3.0 %collective-permute-start.18 = (bf16[32,64,128]{2,1,0:T(8,128)(2,1)}, bf16[32,64,128]{2,1,0:T(8,128)(2,1)S(1)}, u32[]{:S(2)}, u32[]{:S(2)}) collective-permute-start(bf16[32,64,128]{2,1,0:T(8,128)(2,1)} %get-tuple-element.18), channel_id=1, source_target_pairs={{0,4},{1,5},{2,6},{3,7},{4,0},{5,1},{6,2},{7,3},{8,12},{9,13},{10,... | collective-permute-start | bytes 1572872 | tf_op jit(solution)/shard_map/ppermute | solution.py:58
  96.8 7.8 %collective-permute-done.4.p2 = bf16[32,64,128]{2,1,0:T(8,128)(2,1)S(1)} collective-permute-done((bf16[32,64,128]{2,1,0:T(8,128)(2,1)}, bf16[32,64,128]{2,1,0:T(8,128)(2,1)S(1)}, u32[]{:S(2)}, u32[]{:S(2)}) %collective-permute-start.4) | collective-permute-done | bytes 524320 | tf_op jit(solution)/shard_map/ppermute | solution.py:55
  105.3 9.9 %shard_map.77 = (bf16[32,64,128]{2,1,0:T(8,128)(2,1)}, bf16[32,64,128]{2,1,0:T(8,128)(2,1)}, bf16[32,64,128]{2,1,0:T(8,128)(2,1)}, bf16[32,64,128]{2,1,0:T(8,128)(2,1)}) custom-call(bf16[32,64,128]{2,1,0:T(8,128)(2,1)} %get-tuple-element.36.p0, bf16[32,64,128]{2,1,0:T(8,128)(2,1)} %collective-permute-done.3.p1, bf16[32,64,128]{2,1,0:T(8,128)(2,1)} %copy-done.11, ...), custom_call_target="tpu_custom_call" | custom-call | flops 2147483648 | bytes 10485760 | tf_op jit(solution)/shard_map/pallas_call | solution.py:173
  118.2 2.8 %collective-permute-start.8 = (bf16[32,64,128]{2,1,0:T(8,128)(2,1)}, bf16[32,64,128]{2,1,0:T(8,128)(2,1)S(1)}, u32[]{:S(2)}, u32[]{:S(2)}) collective-permute-start(bf16[32,64,128]{2,1,0:T(8,128)(2,1)} %get-tuple-element.16), channel_id=1, source_target_pairs={{0,68},{1,69},{2,70},{3,71},{4,64},{5,65},{6,66},{7,67},{8,76},{9,... | collective-permute-start | bytes 1572872 | tf_op jit(solution)/shard_map/ppermute | solution.py:64
  121.0 6.1 %collective-permute-done.19 = bf16[32,64,128]{2,1,0:T(8,128)(2,1)} collective-permute-done((bf16[32,64,128]{2,1,0:T(8,128)(2,1)}, bf16[32,64,128]{2,1,0:T(8,128)(2,1)}, u32[]{:S(2)}, u32[]{:S(2)}) %collective-permute-start.19) | collective-permute-done | bytes 524320 | tf_op jit(solution)/shard_map/ppermute | solution.py:55
  132.7 16.8 %collective-permute-done.7 = bf16[32,64,128]{2,1,0:T(8,128)(2,1)S(1)} collective-permute-done((bf16[32,64,128]{2,1,0:T(8,128)(2,1)}, bf16[32,64,128]{2,1,0:T(8,128)(2,1)S(1)}, u32[]{:S(2)}, u32[]{:S(2)}) %collective-permute-start.7) | collective-permute-done | bytes 524320 | tf_op jit(solution)/shard_map/ppermute | solution.py:55
  152.1 9.0 %collective-permute-done.23.x_ref = bf16[32,64,128]{2,1,0:T(8,128)(2,1)S(1)} collective-permute-done((bf16[32,64,128]{2,1,0:T(8,128)(2,1)S(1)}, bf16[32,64,128]{2,1,0:T(8,128)(2,1)S(1)}, u32[]{:S(2)}, u32[]{:S(2)}) %collective-permute-start.23) | collective-permute-done | bytes 524320 | tf_op jit(solution)/shard_map/ppermute | solution.py:58
  178.5 5.1 %collective-permute-done.11.x_ref = bf16[32,64,128]{2,1,0:T(8,128)(2,1)} collective-permute-done((bf16[32,64,128]{2,1,0:T(8,128)(2,1)}, bf16[32,64,128]{2,1,0:T(8,128)(2,1)}, u32[]{:S(2)}, u32[]{:S(2)}) %collective-permute-start.11) | collective-permute-done | bytes 524320 | tf_op jit(solution)/shard_map/ppermute | solution.py:58
  189.8 3.7 %collective-permute-done.9.x_ref = bf16[32,64,128]{2,1,0:T(8,128)(2,1)S(1)} collective-permute-done((bf16[32,64,128]{2,1,0:T(8,128)(2,1)}, bf16[32,64,128]{2,1,0:T(8,128)(2,1)S(1)}, u32[]{:S(2)}, u32[]{:S(2)}) %collective-permute-start.9) | collective-permute-done | bytes 524320 | tf_op jit(solution)/shard_map/ppermute | solution.py:64
  (103 shorter events, 63.7 us)
Async XLA Ops:
  7.5 25.0 %collective-permute-start.12 = (bf16[32,64,128]{2,1,0:T(8,128)(2,1)}, bf16[32,64,128]{2,1,0:T(8,128)(2,1)}, u32[]{:S(2)}, u32[]{:S(2)}) collective-permute-start(bf16[32,64,128]{2,1,0:T(8,128)(2,1)} %shard_map.79), channel_id=1, source_target_pairs={{0,1},{1,0},{2,3},{3,2},{4,5},{5,4},{6,7},{7,6},{8,9},{9,8},{10,11... | collective-permute-start | bytes 1572872 | tf_op jit(solution)/shard_map/ppermute | solution.py:58
  12.6 20.5 %collective-permute-start.13 = (bf16[32,64,128]{2,1,0:T(8,128)(2,1)}, bf16[32,64,128]{2,1,0:T(8,128)(2,1)}, u32[]{:S(2)}, u32[]{:S(2)}) collective-permute-start(bf16[32,64,128]{2,1,0:T(8,128)(2,1)} %shard_map.80), channel_id=1, source_target_pairs={{0,8},{8,0},{16,24},{24,16},{32,40},{40,32},{48,56},{56,48},{64,72... | collective-permute-start | bytes 1572872 | tf_op jit(solution)/shard_map/ppermute | solution.py:55
  16.3 18.3 %collective-permute-start.14 = (bf16[32,64,128]{2,1,0:T(8,128)(2,1)}, bf16[32,64,128]{2,1,0:T(8,128)(2,1)}, u32[]{:S(2)}, u32[]{:S(2)}) collective-permute-start(bf16[32,64,128]{2,1,0:T(8,128)(2,1)} %shard_map.81), channel_id=1, source_target_pairs={{0,9},{1,8},{2,11},{3,10},{4,13},{5,12},{6,15},{7,14},{8,1},{9,0},... | collective-permute-start | bytes 1572872 | tf_op jit(solution)/shard_map/ppermute | solution.py:64
  19.0 25.6 %collective-permute-start = (bf16[32,64,128]{2,1,0:T(8,128)(2,1)}, bf16[32,64,128]{2,1,0:T(8,128)(2,1)}, u32[]{:S(2)}, u32[]{:S(2)}) collective-permute-start(bf16[32,64,128]{2,1,0:T(8,128)(2,1)} %shard_map.74), channel_id=1, source_target_pairs={{0,1},{1,0},{2,3},{3,2},{4,5},{5,4},{6,7},{7,6},{8,9},{9,8},{10,11... | collective-permute-start | bytes 1572872 | tf_op jit(solution)/shard_map/ppermute | solution.py:58
  23.0 27.1 %collective-permute-start.1 = (bf16[32,64,128]{2,1,0:T(8,128)(2,1)}, bf16[32,64,128]{2,1,0:T(8,128)(2,1)}, u32[]{:S(2)}, u32[]{:S(2)}) collective-permute-start(bf16[32,64,128]{2,1,0:T(8,128)(2,1)} %shard_map.75), channel_id=1, source_target_pairs={{0,8},{8,0},{16,24},{24,16},{32,40},{40,32},{48,56},{56,48},{64,72... | collective-permute-start | bytes 1572872 | tf_op jit(solution)/shard_map/ppermute | solution.py:55
  33.1 35.2 %collective-permute-start.2 = (bf16[32,64,128]{2,1,0:T(8,128)(2,1)S(1)}, bf16[32,64,128]{2,1,0:T(8,128)(2,1)S(1)}, u32[]{:S(2)}, u32[]{:S(2)}) collective-permute-start(bf16[32,64,128]{2,1,0:T(8,128)(2,1)S(1)} %copy-done.9), channel_id=1, source_target_pairs={{0,9},{1,8},{2,11},{3,10},{4,13},{5,12},{6,15},{7,14},{8,1},{9,0},... | collective-permute-start | bytes 1572872 | tf_op jit(solution)/shard_map/ppermute | solution.py:64
  37.9 42.7 %collective-permute-start.15 = (bf16[32,64,128]{2,1,0:T(8,128)(2,1)}, bf16[32,64,128]{2,1,0:T(8,128)(2,1)}, u32[]{:S(2)}, u32[]{:S(2)}) collective-permute-start(bf16[32,64,128]{2,1,0:T(8,128)(2,1)} %get-tuple-element.27), channel_id=1, source_target_pairs={{0,4},{1,5},{2,6},{3,7},{4,0},{5,1},{6,2},{7,3},{8,12},{9,13},{10,... | collective-permute-start | bytes 1572872 | tf_op jit(solution)/shard_map/ppermute | solution.py:58
  40.9 40.2 %collective-permute-start.16 = (bf16[32,64,128]{2,1,0:T(8,128)(2,1)}, bf16[32,64,128]{2,1,0:T(8,128)(2,1)}, u32[]{:S(2)}, u32[]{:S(2)}) collective-permute-start(bf16[32,64,128]{2,1,0:T(8,128)(2,1)} %get-tuple-element.26), channel_id=1, source_target_pairs={{0,64},{8,72},{16,80},{24,88},{32,96},{40,104},{48,112},{56,120},{... | collective-permute-start | bytes 1572872 | tf_op jit(solution)/shard_map/ppermute | solution.py:55
  44.5 36.5 %collective-permute-start.17 = (bf16[32,64,128]{2,1,0:T(8,128)(2,1)S(1)}, bf16[32,64,128]{2,1,0:T(8,128)(2,1)}, u32[]{:S(2)}, u32[]{:S(2)}) collective-permute-start(bf16[32,64,128]{2,1,0:T(8,128)(2,1)S(1)} %get-tuple-element.25), channel_id=1, source_target_pairs={{0,68},{1,69},{2,70},{3,71},{4,64},{5,65},{6,66},{7,67},{8,76},{9,... | collective-permute-start | bytes 1572872 | tf_op jit(solution)/shard_map/ppermute | solution.py:64
  71.4 24.8 %collective-permute-start.3 = (bf16[32,64,128]{2,1,0:T(8,128)(2,1)}, bf16[32,64,128]{2,1,0:T(8,128)(2,1)}, u32[]{:S(2)}, u32[]{:S(2)}) collective-permute-start(bf16[32,64,128]{2,1,0:T(8,128)(2,1)} %get-tuple-element.35), channel_id=1, source_target_pairs={{0,4},{1,5},{2,6},{3,7},{4,0},{5,1},{6,2},{7,3},{8,12},{9,13},{10,... | collective-permute-start | bytes 1572872 | tf_op jit(solution)/shard_map/ppermute | solution.py:58
  76.6 27.9 %collective-permute-start.4 = (bf16[32,64,128]{2,1,0:T(8,128)(2,1)}, bf16[32,64,128]{2,1,0:T(8,128)(2,1)S(1)}, u32[]{:S(2)}, u32[]{:S(2)}) collective-permute-start(bf16[32,64,128]{2,1,0:T(8,128)(2,1)} %get-tuple-element.34), channel_id=1, source_target_pairs={{0,64},{8,72},{16,80},{24,88},{32,96},{40,104},{48,112},{56,120},{... | collective-permute-start | bytes 1572872 | tf_op jit(solution)/shard_map/ppermute | solution.py:55
  80.6 24.0 %collective-permute-start.5 = (bf16[32,64,128]{2,1,0:T(8,128)(2,1)S(1)}, bf16[32,64,128]{2,1,0:T(8,128)(2,1)}, u32[]{:S(2)}, u32[]{:S(2)}) collective-permute-start(bf16[32,64,128]{2,1,0:T(8,128)(2,1)S(1)} %get-tuple-element.33), channel_id=1, source_target_pairs={{0,68},{1,69},{2,70},{3,71},{4,64},{5,65},{6,66},{7,67},{8,76},{9,... | collective-permute-start | bytes 1572872 | tf_op jit(solution)/shard_map/ppermute | solution.py:64
  91.0 27.2 %collective-permute-start.18 = (bf16[32,64,128]{2,1,0:T(8,128)(2,1)}, bf16[32,64,128]{2,1,0:T(8,128)(2,1)S(1)}, u32[]{:S(2)}, u32[]{:S(2)}) collective-permute-start(bf16[32,64,128]{2,1,0:T(8,128)(2,1)} %get-tuple-element.18), channel_id=1, source_target_pairs={{0,4},{1,5},{2,6},{3,7},{4,0},{5,1},{6,2},{7,3},{8,12},{9,13},{10,... | collective-permute-start | bytes 1572872 | tf_op jit(solution)/shard_map/ppermute | solution.py:58
  94.0 33.1 %collective-permute-start.19 = (bf16[32,64,128]{2,1,0:T(8,128)(2,1)}, bf16[32,64,128]{2,1,0:T(8,128)(2,1)}, u32[]{:S(2)}, u32[]{:S(2)}) collective-permute-start(bf16[32,64,128]{2,1,0:T(8,128)(2,1)} %get-tuple-element.19), channel_id=1, source_target_pairs={{0,64},{8,72},{16,80},{24,88},{32,96},{40,104},{48,112},{56,120},{... | collective-permute-start | bytes 1572872 | tf_op jit(solution)/shard_map/ppermute | solution.py:55
  96.2 30.9 %collective-permute-start.20 = (bf16[32,64,128]{2,1,0:T(8,128)(2,1)}, bf16[32,64,128]{2,1,0:T(8,128)(2,1)}, u32[]{:S(2)}, u32[]{:S(2)}) collective-permute-start(bf16[32,64,128]{2,1,0:T(8,128)(2,1)} %get-tuple-element.20), channel_id=1, source_target_pairs={{0,68},{1,69},{2,70},{3,71},{4,64},{5,65},{6,66},{7,67},{8,76},{9,... | collective-permute-start | bytes 1572872 | tf_op jit(solution)/shard_map/ppermute | solution.py:64
  115.3 16.1 %collective-permute-start.6 = (bf16[32,64,128]{2,1,0:T(8,128)(2,1)}, bf16[32,64,128]{2,1,0:T(8,128)(2,1)S(1)}, u32[]{:S(2)}, u32[]{:S(2)}) collective-permute-start(bf16[32,64,128]{2,1,0:T(8,128)(2,1)} %get-tuple-element.14), channel_id=1, source_target_pairs={{0,4},{1,5},{2,6},{3,7},{4,0},{5,1},{6,2},{7,3},{8,12},{9,13},{10,... | collective-permute-start | bytes 1572872 | tf_op jit(solution)/shard_map/ppermute | solution.py:58
  117.2 32.3 %collective-permute-start.7 = (bf16[32,64,128]{2,1,0:T(8,128)(2,1)}, bf16[32,64,128]{2,1,0:T(8,128)(2,1)S(1)}, u32[]{:S(2)}, u32[]{:S(2)}) collective-permute-start(bf16[32,64,128]{2,1,0:T(8,128)(2,1)} %get-tuple-element.15), channel_id=1, source_target_pairs={{0,64},{8,72},{16,80},{24,88},{32,96},{40,104},{48,112},{56,120},{... | collective-permute-start | bytes 1572872 | tf_op jit(solution)/shard_map/ppermute | solution.py:55
  118.2 31.3 %collective-permute-start.8 = (bf16[32,64,128]{2,1,0:T(8,128)(2,1)}, bf16[32,64,128]{2,1,0:T(8,128)(2,1)S(1)}, u32[]{:S(2)}, u32[]{:S(2)}) collective-permute-start(bf16[32,64,128]{2,1,0:T(8,128)(2,1)} %get-tuple-element.16), channel_id=1, source_target_pairs={{0,68},{1,69},{2,70},{3,71},{4,64},{5,65},{6,66},{7,67},{8,76},{9,... | collective-permute-start | bytes 1572872 | tf_op jit(solution)/shard_map/ppermute | solution.py:64
  130.3 30.7 %collective-permute-start.23 = (bf16[32,64,128]{2,1,0:T(8,128)(2,1)S(1)}, bf16[32,64,128]{2,1,0:T(8,128)(2,1)S(1)}, u32[]{:S(2)}, u32[]{:S(2)}) collective-permute-start(bf16[32,64,128]{2,1,0:T(8,128)(2,1)S(1)} %get-tuple-element.22), channel_id=1, source_target_pairs={{0,1},{1,0},{2,3},{3,2},{4,5},{5,4},{6,7},{7,6},{8,9},{9,8},{10,11... | collective-permute-start | bytes 1572872 | tf_op jit(solution)/shard_map/ppermute | solution.py:58
  130.9 38.0 %collective-permute-start.22 = (bf16[32,64,128]{2,1,0:T(8,128)(2,1)}, bf16[32,64,128]{2,1,0:T(8,128)(2,1)S(1)}, u32[]{:S(2)}, u32[]{:S(2)}) collective-permute-start(bf16[32,64,128]{2,1,0:T(8,128)(2,1)} %get-tuple-element.23), channel_id=1, source_target_pairs={{0,8},{8,0},{16,24},{24,16},{32,40},{40,32},{48,56},{56,48},{64,72... | collective-permute-start | bytes 1572872 | tf_op jit(solution)/shard_map/ppermute | solution.py:55
  131.4 41.0 %collective-permute-start.21 = (bf16[32,64,128]{2,1,0:T(8,128)(2,1)}, bf16[32,64,128]{2,1,0:T(8,128)(2,1)S(1)}, u32[]{:S(2)}, u32[]{:S(2)}) collective-permute-start(bf16[32,64,128]{2,1,0:T(8,128)(2,1)} %get-tuple-element.24), channel_id=1, source_target_pairs={{0,9},{1,8},{2,11},{3,10},{4,13},{5,12},{6,15},{7,14},{8,1},{9,0},... | collective-permute-start | bytes 1572872 | tf_op jit(solution)/shard_map/ppermute | solution.py:64
  151.6 32.0 %collective-permute-start.11 = (bf16[32,64,128]{2,1,0:T(8,128)(2,1)}, bf16[32,64,128]{2,1,0:T(8,128)(2,1)}, u32[]{:S(2)}, u32[]{:S(2)}) collective-permute-start(bf16[32,64,128]{2,1,0:T(8,128)(2,1)} %get-tuple-element.30), channel_id=1, source_target_pairs={{0,1},{1,0},{2,3},{3,2},{4,5},{5,4},{6,7},{7,6},{8,9},{9,8},{10,11... | collective-permute-start | bytes 1572872 | tf_op jit(solution)/shard_map/ppermute | solution.py:58
  152.0 34.3 %collective-permute-start.10 = (bf16[32,64,128]{2,1,0:T(8,128)(2,1)}, bf16[32,64,128]{2,1,0:T(8,128)(2,1)S(1)}, u32[]{:S(2)}, u32[]{:S(2)}) collective-permute-start(bf16[32,64,128]{2,1,0:T(8,128)(2,1)} %get-tuple-element.31), channel_id=1, source_target_pairs={{0,8},{8,0},{16,24},{24,16},{32,40},{40,32},{48,56},{56,48},{64,72... | collective-permute-start | bytes 1572872 | tf_op jit(solution)/shard_map/ppermute | solution.py:55
  161.1 32.5 %collective-permute-start.9 = (bf16[32,64,128]{2,1,0:T(8,128)(2,1)}, bf16[32,64,128]{2,1,0:T(8,128)(2,1)S(1)}, u32[]{:S(2)}, u32[]{:S(2)}) collective-permute-start(bf16[32,64,128]{2,1,0:T(8,128)(2,1)} %get-tuple-element.32), channel_id=1, source_target_pairs={{0,9},{1,8},{2,11},{3,10},{4,13},{5,12},{6,15},{7,14},{8,1},{9,0},... | collective-permute-start | bytes 1572872 | tf_op jit(solution)/shard_map/ppermute | solution.py:64
  (14 other events, 102.8 us)

commit v13 on v7

--- a/solution.py
+++ b/solution.py
@@ -158,6 +158,13 @@
         ),
         out_shape=out_shape,
         input_output_aliases=aliases,
+        cost_estimate=pl.CostEstimate(
+            flops=2 * len(plan) * mats.shape[1] * mats.shape[2] * data_spec.block_shape[-1]
+            * data_spec.block_shape[-3],
+            bytes_accessed=mats.size * 2 + 4 * data_spec.block_shape[-1]
+            * data_spec.block_shape[-2] * data_spec.block_shape[-3],
+            transcendentals=0,
+        ),
     )(*operands)
 
 

time: 195 us -> 195 us (level)
    ppermute x8, waiting for transfers between devices: 9.12 us -> 13.2 us  [flip_send(): return lax.ppermute(value, ('qx', 'qy'), pairs)]
    unnamed x32 -> x34, local copies, waits for them, and re-layouts: 4.06 us -> 5.07 us
  transfers between devices with their start and end apart: 24 -> 24, of which waited for: 9 -> 9; matrix products, arithmetic and copies ran while one was open for 8% -> 8% of each run, Pallas kernels for 30% -> 29%
where the time goes in v13:
time: 195 us
  Pallas kernels  62.7 us (32%)
  waiting for transfers between devices  54.6 us (28%)
  starting transfers between devices  52.2 us (27%)
  local copies, waits for them, and re-layouts  15.6 us (8%)
  matrix products  6.79 us (3%)
  other arithmetic  2.28 us (1%)
    pallas_call x16, Pallas kernels, chain_call(): pl.pallas_call(functools.partial(chain_kernel, plan), grid_spec=pltpu.Pre...  42.9 us
    ppermute x8, waiting for transfers between devices, flip_send(): return lax.ppermute(value, 'qx', pairs)  27 us
    ppermute x8, starting transfers between devices, flip_send(): return lax.ppermute(value, ('qx', 'qy'), pairs)  22.2 us
    pallas_call x2, Pallas kernels, output_stage(): pl.pallas_call(output_stage_kernel, grid=(part // step,), in_specs=[piece...  19.8 us
    ppermute x8, starting transfers between devices, flip_send(): return lax.ppermute(value, 'qx', pairs)  15.7 us
    ppermute x8, waiting for transfers between devices, flip_send(): return lax.ppermute(value, 'qy', pairs)  14.4 us
    ppermute x8, starting transfers between devices, flip_send(): return lax.ppermute(value, 'qy', pairs)  14.3 us
    ppermute x8, waiting for transfers between devices, flip_send(): return lax.ppermute(value, ('qx', 'qy'), pairs)  13.2 us
  transfers between devices with their start and end apart: 24, of which 9 were waited for; matrix products, arithmetic and copies ran while one was open for 8% of the time, Pallas kernels for 29%

profile of v13, /device:TPU:1, one launch (start us, length us, event | category | flops | bytes accessed | tf_op | source)
XLA Modules:
  0.0 194.6 jit_solution(15853714649977879301)
XLA Ops:
  19.5 2.7 %shard_map.74 = bf16[32,64,128]{2,1,0:T(8,128)(2,1)} custom-call(s32[1]{0:T(128)} %bitcast.k_ref, bf16[4,2,32,64,128]{4,3,2,1,0:T(8,128)(2,1)} %bitcast.188, bf16[3,256,256]{2,1,0:T(8,128)(2,1)} %pad_maximum_fusion.4.m_ref), custom_call_target="tpu_custom_call" | custom-call | flops 1610612736 | bytes 1441792 | tf_op jit(solution)/shard_map/pallas_call | solution.py:154
  22.9 2.7 %shard_map.78 = bf16[32,64,128]{2,1,0:T(8,128)(2,1)} custom-call(s32[1]{0:T(128)} %bitcast.k_ref, bf16[4,2,32,64,128]{4,3,2,1,0:T(8,128)(2,1)} %bitcast.189, bf16[3,256,256]{2,1,0:T(8,128)(2,1)} %pad_maximum_fusion.4.m_ref), custom_call_target="tpu_custom_call" | custom-call | flops 1610612736 | bytes 1441792 | tf_op jit(solution)/shard_map/pallas_call | solution.py:154
  28.3 2.7 %shard_map.73 = bf16[32,64,128]{2,1,0:T(8,128)(2,1)} custom-call(s32[1]{0:T(128)} %bitcast.k_ref, bf16[4,2,32,64,128]{4,3,2,1,0:T(8,128)(2,1)} %bitcast.191, bf16[3,256,256]{2,1,0:T(8,128)(2,1)} %pad_maximum_fusion.4.m_ref), custom_call_target="tpu_custom_call" | custom-call | flops 1610612736 | bytes 1441792 | tf_op jit(solution)/shard_map/pallas_call | solution.py:154
  37.0 3.0 %collective-permute-start.15 = (bf16[32,64,128]{2,1,0:T(8,128)(2,1)}, bf16[32,64,128]{2,1,0:T(8,128)(2,1)}, u32[]{:S(2)}, u32[]{:S(2)}) collective-permute-start(bf16[32,64,128]{2,1,0:T(8,128)(2,1)} %get-tuple-element.27), channel_id=1, source_target_pairs={{0,4},{1,5},{2,6},{3,7},{4,0},{5,1},{6,2},{7,3},{8,12},{9,13},{10,... | collective-permute-start | bytes 1572872 | tf_op jit(solution)/shard_map/ppermute | solution.py:58
  40.0 3.6 %collective-permute-start.16 = (bf16[32,64,128]{2,1,0:T(8,128)(2,1)}, bf16[32,64,128]{2,1,0:T(8,128)(2,1)}, u32[]{:S(2)}, u32[]{:S(2)}) collective-permute-start(bf16[32,64,128]{2,1,0:T(8,128)(2,1)} %get-tuple-element.26), channel_id=1, source_target_pairs={{0,64},{8,72},{16,80},{24,88},{32,96},{40,104},{48,112},{56,120},{... | collective-permute-start | bytes 1572872 | tf_op jit(solution)/shard_map/ppermute | solution.py:55
  44.9 6.4 %collective-permute-start.17 = (bf16[32,64,128]{2,1,0:T(8,128)(2,1)S(1)}, bf16[32,64,128]{2,1,0:T(8,128)(2,1)}, u32[]{:S(2)}, u32[]{:S(2)}) collective-permute-start(bf16[32,64,128]{2,1,0:T(8,128)(2,1)S(1)} %get-tuple-element.25), channel_id=1, source_target_pairs={{0,68},{1,69},{2,70},{3,71},{4,64},{5,65},{6,66},{7,67},{8,76},{9,... | collective-permute-start | bytes 1572872 | tf_op jit(solution)/shard_map/ppermute | solution.py:64
  51.3 14.4 %collective-permute-done = bf16[32,64,128]{2,1,0:T(8,128)(2,1)} collective-permute-done((bf16[32,64,128]{2,1,0:T(8,128)(2,1)}, bf16[32,64,128]{2,1,0:T(8,128)(2,1)}, u32[]{:S(2)}, u32[]{:S(2)}) %collective-permute-start) | collective-permute-done | bytes 524320 | tf_op jit(solution)/shard_map/ppermute | solution.py:58
  68.8 2.8 %collective-permute-start.3 = (bf16[32,64,128]{2,1,0:T(8,128)(2,1)}, bf16[32,64,128]{2,1,0:T(8,128)(2,1)}, u32[]{:S(2)}, u32[]{:S(2)}) collective-permute-start(bf16[32,64,128]{2,1,0:T(8,128)(2,1)} %get-tuple-element.35), channel_id=1, source_target_pairs={{0,4},{1,5},{2,6},{3,7},{4,0},{5,1},{6,2},{7,3},{8,12},{9,13},{10,... | collective-permute-start | bytes 1572872 | tf_op jit(solution)/shard_map/ppermute | solution.py:58
  73.8 3.2 %collective-permute-start.4 = (bf16[32,64,128]{2,1,0:T(8,128)(2,1)S(1)}, bf16[32,64,128]{2,1,0:T(8,128)(2,1)S(1)}, u32[]{:S(2)}, u32[]{:S(2)}) collective-permute-start(bf16[32,64,128]{2,1,0:T(8,128)(2,1)S(1)} %get-tuple-element.34), channel_id=1, source_target_pairs={{0,64},{8,72},{16,80},{24,88},{32,96},{40,104},{48,112},{56,120},{... | collective-permute-start | bytes 1572872 | tf_op jit(solution)/shard_map/ppermute | solution.py:55
  77.1 2.8 %collective-permute-done.16.p2 = bf16[32,64,128]{2,1,0:T(8,128)(2,1)} collective-permute-done((bf16[32,64,128]{2,1,0:T(8,128)(2,1)}, bf16[32,64,128]{2,1,0:T(8,128)(2,1)}, u32[]{:S(2)}, u32[]{:S(2)}) %collective-permute-start.16) | collective-permute-done | bytes 524320 | tf_op jit(solution)/shard_map/ppermute | solution.py:55
  79.9 9.9 %shard_map.82 = (bf16[32,64,128]{2,1,0:T(8,128)(2,1)}, bf16[32,64,128]{2,1,0:T(8,128)(2,1)}, bf16[32,64,128]{2,1,0:T(8,128)(2,1)}, bf16[32,64,128]{2,1,0:T(8,128)(2,1)}) custom-call(bf16[32,64,128]{2,1,0:T(8,128)(2,1)} %get-tuple-element.28.p0, bf16[32,64,128]{2,1,0:T(8,128)(2,1)} %collective-permute-done.15.p1, ...), custom_call_target="tpu_custom_call" | custom-call | flops 2147483648 | bytes 10485760 | tf_op jit(solution)/shard_map/pallas_call | solution.py:180
  89.8 3.0 %collective-permute-start.18 = (bf16[32,64,128]{2,1,0:T(8,128)(2,1)}, bf16[32,64,128]{2,1,0:T(8,128)(2,1)S(1)}, u32[]{:S(2)}, u32[]{:S(2)}) collective-permute-start(bf16[32,64,128]{2,1,0:T(8,128)(2,1)} %get-tuple-element.18), channel_id=1, source_target_pairs={{0,4},{1,5},{2,6},{3,7},{4,0},{5,1},{6,2},{7,3},{8,12},{9,13},{10,... | collective-permute-start | bytes 1572872 | tf_op jit(solution)/shard_map/ppermute | solution.py:58
  92.8 2.8 %collective-permute-start.20 = (bf16[32,64,128]{2,1,0:T(8,128)(2,1)}, bf16[32,64,128]{2,1,0:T(8,128)(2,1)}, u32[]{:S(2)}, u32[]{:S(2)}) collective-permute-start(bf16[32,64,128]{2,1,0:T(8,128)(2,1)} %get-tuple-element.20), channel_id=1, source_target_pairs={{0,68},{1,69},{2,70},{3,71},{4,64},{5,65},{6,66},{7,67},{8,76},{9,... | collective-permute-start | bytes 1572872 | tf_op jit(solution)/shard_map/ppermute | solution.py:64
  97.4 4.8 %collective-permute-done.4.p2 = bf16[32,64,128]{2,1,0:T(8,128)(2,1)S(1)} collective-permute-done((bf16[32,64,128]{2,1,0:T(8,128)(2,1)S(1)}, bf16[32,64,128]{2,1,0:T(8,128)(2,1)S(1)}, u32[]{:S(2)}, u32[]{:S(2)}) %collective-permute-start.4) | collective-permute-done | bytes 524320 | tf_op jit(solution)/shard_map/ppermute | solution.py:55
  103.0 9.9 %shard_map.77 = (bf16[32,64,128]{2,1,0:T(8,128)(2,1)}, bf16[32,64,128]{2,1,0:T(8,128)(2,1)}, bf16[32,64,128]{2,1,0:T(8,128)(2,1)}, bf16[32,64,128]{2,1,0:T(8,128)(2,1)}) custom-call(bf16[32,64,128]{2,1,0:T(8,128)(2,1)} %get-tuple-element.36.p0, bf16[32,64,128]{2,1,0:T(8,128)(2,1)} %collective-permute-done.3.p1, bf16[32,64,128]{2,1,0:T(8,128)(2,1)} %copy-done.9, ...), custom_call_target="tpu_custom_call" | custom-call | flops 2147483648 | bytes 10485760 | tf_op jit(solution)/shard_map/pallas_call | solution.py:180
  113.0 3.0 %collective-permute-start.6 = (bf16[32,64,128]{2,1,0:T(8,128)(2,1)}, bf16[32,64,128]{2,1,0:T(8,128)(2,1)S(1)}, u32[]{:S(2)}, u32[]{:S(2)}) collective-permute-start(bf16[32,64,128]{2,1,0:T(8,128)(2,1)} %get-tuple-element.14), channel_id=1, source_target_pairs={{0,4},{1,5},{2,6},{3,7},{4,0},{5,1},{6,2},{7,3},{8,12},{9,13},{10,... | collective-permute-start | bytes 1572872 | tf_op jit(solution)/shard_map/ppermute | solution.py:58
  116.0 2.8 %collective-permute-start.8 = (bf16[32,64,128]{2,1,0:T(8,128)(2,1)}, bf16[32,64,128]{2,1,0:T(8,128)(2,1)S(1)}, u32[]{:S(2)}, u32[]{:S(2)}) collective-permute-start(bf16[32,64,128]{2,1,0:T(8,128)(2,1)} %get-tuple-element.16), channel_id=1, source_target_pairs={{0,68},{1,69},{2,70},{3,71},{4,64},{5,65},{6,66},{7,67},{8,76},{9,... | collective-permute-start | bytes 1572872 | tf_op jit(solution)/shard_map/ppermute | solution.py:64
  118.8 6.0 %collective-permute-done.19 = bf16[32,64,128]{2,1,0:T(8,128)(2,1)} collective-permute-done((bf16[32,64,128]{2,1,0:T(8,128)(2,1)}, bf16[32,64,128]{2,1,0:T(8,128)(2,1)}, u32[]{:S(2)}, u32[]{:S(2)}) %collective-permute-start.19) | collective-permute-done | bytes 524320 | tf_op jit(solution)/shard_map/ppermute | solution.py:55
  128.0 3.7 %collective-permute-start.22 = (bf16[32,64,128]{2,1,0:T(8,128)(2,1)}, bf16[32,64,128]{2,1,0:T(8,128)(2,1)S(1)}, u32[]{:S(2)}, u32[]{:S(2)}) collective-permute-start(bf16[32,64,128]{2,1,0:T(8,128)(2,1)} %get-tuple-element.23), channel_id=1, source_target_pairs={{0,8},{8,0},{16,24},{24,16},{32,40},{40,32},{48,56},{56,48},{64,72... | collective-permute-start | bytes 1572872 | tf_op jit(solution)/shard_map/ppermute | solution.py:55
  133.9 13.3 %collective-permute-done.7 = bf16[32,64,128]{2,1,0:T(8,128)(2,1)S(1)} collective-permute-done((bf16[32,64,128]{2,1,0:T(8,128)(2,1)}, bf16[32,64,128]{2,1,0:T(8,128)(2,1)S(1)}, u32[]{:S(2)}, u32[]{:S(2)}) %collective-permute-start.7) | collective-permute-done | bytes 524320 | tf_op jit(solution)/shard_map/ppermute | solution.py:55
  149.4 3.7 %collective-permute-start.10 = (bf16[32,64,128]{2,1,0:T(8,128)(2,1)}, bf16[32,64,128]{2,1,0:T(8,128)(2,1)S(1)}, u32[]{:S(2)}, u32[]{:S(2)}) collective-permute-start(bf16[32,64,128]{2,1,0:T(8,128)(2,1)} %get-tuple-element.31), channel_id=1, source_target_pairs={{0,8},{8,0},{16,24},{24,16},{32,40},{40,32},{48,56},{56,48},{64,72... | collective-permute-start | bytes 1572872 | tf_op jit(solution)/shard_map/ppermute | solution.py:55
  155.7 6.4 %collective-permute-start.9 = (bf16[32,64,128]{2,1,0:T(8,128)(2,1)}, bf16[32,64,128]{2,1,0:T(8,128)(2,1)S(1)}, u32[]{:S(2)}, u32[]{:S(2)}) collective-permute-start(bf16[32,64,128]{2,1,0:T(8,128)(2,1)} %get-tuple-element.32), channel_id=1, source_target_pairs={{0,9},{1,8},{2,11},{3,10},{4,13},{5,12},{6,15},{7,14},{8,1},{9,0},... | collective-permute-start | bytes 1572872 | tf_op jit(solution)/shard_map/ppermute | solution.py:64
  168.2 3.7 %collective-permute-done.21.x_ref = bf16[32,64,128]{2,1,0:T(8,128)(2,1)S(1)} collective-permute-done((bf16[32,64,128]{2,1,0:T(8,128)(2,1)}, bf16[32,64,128]{2,1,0:T(8,128)(2,1)S(1)}, u32[]{:S(2)}, u32[]{:S(2)}) %collective-permute-start.21) | collective-permute-done | bytes 524320 | tf_op jit(solution)/shard_map/ppermute | solution.py:64
  185.1 6.0 %collective-permute-done.9.x_ref = bf16[32,64,128]{2,1,0:T(8,128)(2,1)S(1)} collective-permute-done((bf16[32,64,128]{2,1,0:T(8,128)(2,1)}, bf16[32,64,128]{2,1,0:T(8,128)(2,1)S(1)}, u32[]{:S(2)}, u32[]{:S(2)}) %collective-permute-start.9) | collective-permute-done | bytes 524320 | tf_op jit(solution)/shard_map/ppermute | solution.py:64
  (113 shorter events, 70.7 us)
Async XLA Ops:
  6.3 24.7 %collective-permute-start.12 = (bf16[32,64,128]{2,1,0:T(8,128)(2,1)}, bf16[32,64,128]{2,1,0:T(8,128)(2,1)S(1)}, u32[]{:S(2)}, u32[]{:S(2)}) collective-permute-start(bf16[32,64,128]{2,1,0:T(8,128)(2,1)} %shard_map.79), channel_id=1, source_target_pairs={{0,1},{1,0},{2,3},{3,2},{4,5},{5,4},{6,7},{7,6},{8,9},{9,8},{10,11... | collective-permute-start | bytes 1572872 | tf_op jit(solution)/shard_map/ppermute | solution.py:58
  11.5 20.0 %collective-permute-start.13 = (bf16[32,64,128]{2,1,0:T(8,128)(2,1)}, bf16[32,64,128]{2,1,0:T(8,128)(2,1)}, u32[]{:S(2)}, u32[]{:S(2)}) collective-permute-start(bf16[32,64,128]{2,1,0:T(8,128)(2,1)} %shard_map.80), channel_id=1, source_target_pairs={{0,8},{8,0},{16,24},{24,16},{32,40},{40,32},{48,56},{56,48},{64,72... | collective-permute-start | bytes 1572872 | tf_op jit(solution)/shard_map/ppermute | solution.py:55
  15.1 18.6 %collective-permute-start.14 = (bf16[32,64,128]{2,1,0:T(8,128)(2,1)}, bf16[32,64,128]{2,1,0:T(8,128)(2,1)}, u32[]{:S(2)}, u32[]{:S(2)}) collective-permute-start(bf16[32,64,128]{2,1,0:T(8,128)(2,1)} %shard_map.81), channel_id=1, source_target_pairs={{0,9},{1,8},{2,11},{3,10},{4,13},{5,12},{6,15},{7,14},{8,1},{9,0},... | collective-permute-start | bytes 1572872 | tf_op jit(solution)/shard_map/ppermute | solution.py:64
  17.8 27.1 %collective-permute-start.2 = (bf16[32,64,128]{2,1,0:T(8,128)(2,1)}, bf16[32,64,128]{2,1,0:T(8,128)(2,1)}, u32[]{:S(2)}, u32[]{:S(2)}) collective-permute-start(bf16[32,64,128]{2,1,0:T(8,128)(2,1)} %shard_map.76), channel_id=1, source_target_pairs={{0,9},{1,8},{2,11},{3,10},{4,13},{5,12},{6,15},{7,14},{8,1},{9,0},... | collective-permute-start | bytes 1572872 | tf_op jit(solution)/shard_map/ppermute | solution.py:64
  22.2 43.4 %collective-permute-start = (bf16[32,64,128]{2,1,0:T(8,128)(2,1)}, bf16[32,64,128]{2,1,0:T(8,128)(2,1)}, u32[]{:S(2)}, u32[]{:S(2)}) collective-permute-start(bf16[32,64,128]{2,1,0:T(8,128)(2,1)} %shard_map.74), channel_id=1, source_target_pairs={{0,1},{1,0},{2,3},{3,2},{4,5},{5,4},{6,7},{7,6},{8,9},{9,8},{10,11... | collective-permute-start | bytes 1572872 | tf_op jit(solution)/shard_map/ppermute | solution.py:58
  31.0 34.6 %collective-permute-start.1 = (bf16[32,64,128]{2,1,0:T(8,128)(2,1)S(1)}, bf16[32,64,128]{2,1,0:T(8,128)(2,1)S(1)}, u32[]{:S(2)}, u32[]{:S(2)}) collective-permute-start(bf16[32,64,128]{2,1,0:T(8,128)(2,1)S(1)} %copy-done.14), channel_id=1, source_target_pairs={{0,8},{8,0},{16,24},{24,16},{32,40},{40,32},{48,56},{56,48},{64,72... | collective-permute-start | bytes 1572872 | tf_op jit(solution)/shard_map/ppermute | solution.py:55
  37.0 40.1 %collective-permute-start.15 = (bf16[32,64,128]{2,1,0:T(8,128)(2,1)}, bf16[32,64,128]{2,1,0:T(8,128)(2,1)}, u32[]{:S(2)}, u32[]{:S(2)}) collective-permute-start(bf16[32,64,128]{2,1,0:T(8,128)(2,1)} %get-tuple-element.27), channel_id=1, source_target_pairs={{0,4},{1,5},{2,6},{3,7},{4,0},{5,1},{6,2},{7,3},{8,12},{9,13},{10,... | collective-permute-start | bytes 1572872 | tf_op jit(solution)/shard_map/ppermute | solution.py:58
  40.0 39.9 %collective-permute-start.16 = (bf16[32,64,128]{2,1,0:T(8,128)(2,1)}, bf16[32,64,128]{2,1,0:T(8,128)(2,1)}, u32[]{:S(2)}, u32[]{:S(2)}) collective-permute-start(bf16[32,64,128]{2,1,0:T(8,128)(2,1)} %get-tuple-element.26), channel_id=1, source_target_pairs={{0,64},{8,72},{16,80},{24,88},{32,96},{40,104},{48,112},{56,120},{... | collective-permute-start | bytes 1572872 | tf_op jit(solution)/shard_map/ppermute | solution.py:55
  44.9 35.0 %collective-permute-start.17 = (bf16[32,64,128]{2,1,0:T(8,128)(2,1)S(1)}, bf16[32,64,128]{2,1,0:T(8,128)(2,1)}, u32[]{:S(2)}, u32[]{:S(2)}) collective-permute-start(bf16[32,64,128]{2,1,0:T(8,128)(2,1)S(1)} %get-tuple-element.25), channel_id=1, source_target_pairs={{0,68},{1,69},{2,70},{3,71},{4,64},{5,65},{6,66},{7,67},{8,76},{9,... | collective-permute-start | bytes 1572872 | tf_op jit(solution)/shard_map/ppermute | solution.py:64
  68.8 24.0 %collective-permute-start.3 = (bf16[32,64,128]{2,1,0:T(8,128)(2,1)}, bf16[32,64,128]{2,1,0:T(8,128)(2,1)}, u32[]{:S(2)}, u32[]{:S(2)}) collective-permute-start(bf16[32,64,128]{2,1,0:T(8,128)(2,1)} %get-tuple-element.35), channel_id=1, source_target_pairs={{0,4},{1,5},{2,6},{3,7},{4,0},{5,1},{6,2},{7,3},{8,12},{9,13},{10,... | collective-permute-start | bytes 1572872 | tf_op jit(solution)/shard_map/ppermute | solution.py:58
  73.8 28.4 %collective-permute-start.4 = (bf16[32,64,128]{2,1,0:T(8,128)(2,1)S(1)}, bf16[32,64,128]{2,1,0:T(8,128)(2,1)S(1)}, u32[]{:S(2)}, u32[]{:S(2)}) collective-permute-start(bf16[32,64,128]{2,1,0:T(8,128)(2,1)S(1)} %get-tuple-element.34), channel_id=1, source_target_pairs={{0,64},{8,72},{16,80},{24,88},{32,96},{40,104},{48,112},{56,120},{... | collective-permute-start | bytes 1572872 | tf_op jit(solution)/shard_map/ppermute | solution.py:55
  77.1 25.2 %collective-permute-start.5 = (bf16[32,64,128]{2,1,0:T(8,128)(2,1)S(1)}, bf16[32,64,128]{2,1,0:T(8,128)(2,1)}, u32[]{:S(2)}, u32[]{:S(2)}) collective-permute-start(bf16[32,64,128]{2,1,0:T(8,128)(2,1)S(1)} %get-tuple-element.33), channel_id=1, source_target_pairs={{0,68},{1,69},{2,70},{3,71},{4,64},{5,65},{6,66},{7,67},{8,76},{9,... | collective-permute-start | bytes 1572872 | tf_op jit(solution)/shard_map/ppermute | solution.py:64
  89.8 26.2 %collective-permute-start.18 = (bf16[32,64,128]{2,1,0:T(8,128)(2,1)}, bf16[32,64,128]{2,1,0:T(8,128)(2,1)S(1)}, u32[]{:S(2)}, u32[]{:S(2)}) collective-permute-start(bf16[32,64,128]{2,1,0:T(8,128)(2,1)} %get-tuple-element.18), channel_id=1, source_target_pairs={{0,4},{1,5},{2,6},{3,7},{4,0},{5,1},{6,2},{7,3},{8,12},{9,13},{10,... | collective-permute-start | bytes 1572872 | tf_op jit(solution)/shard_map/ppermute | solution.py:58
  92.8 32.0 %collective-permute-start.19 = (bf16[32,64,128]{2,1,0:T(8,128)(2,1)}, bf16[32,64,128]{2,1,0:T(8,128)(2,1)}, u32[]{:S(2)}, u32[]{:S(2)}) collective-permute-start(bf16[32,64,128]{2,1,0:T(8,128)(2,1)} %get-tuple-element.19), channel_id=1, source_target_pairs={{0,64},{8,72},{16,80},{24,88},{32,96},{40,104},{48,112},{56,120},{... | collective-permute-start | bytes 1572872 | tf_op jit(solution)/shard_map/ppermute | solution.py:55
  92.8 32.0 %collective-permute-start.20 = (bf16[32,64,128]{2,1,0:T(8,128)(2,1)}, bf16[32,64,128]{2,1,0:T(8,128)(2,1)}, u32[]{:S(2)}, u32[]{:S(2)}) collective-permute-start(bf16[32,64,128]{2,1,0:T(8,128)(2,1)} %get-tuple-element.20), channel_id=1, source_target_pairs={{0,68},{1,69},{2,70},{3,71},{4,64},{5,65},{6,66},{7,67},{8,76},{9,... | collective-permute-start | bytes 1572872 | tf_op jit(solution)/shard_map/ppermute | solution.py:64
  113.0 18.7 %collective-permute-start.6 = (bf16[32,64,128]{2,1,0:T(8,128)(2,1)}, bf16[32,64,128]{2,1,0:T(8,128)(2,1)S(1)}, u32[]{:S(2)}, u32[]{:S(2)}) collective-permute-start(bf16[32,64,128]{2,1,0:T(8,128)(2,1)} %get-tuple-element.14), channel_id=1, source_target_pairs={{0,4},{1,5},{2,6},{3,7},{4,0},{5,1},{6,2},{7,3},{8,12},{9,13},{10,... | collective-permute-start | bytes 1572872 | tf_op jit(solution)/shard_map/ppermute | solution.py:58
  116.0 31.2 %collective-permute-start.7 = (bf16[32,64,128]{2,1,0:T(8,128)(2,1)}, bf16[32,64,128]{2,1,0:T(8,128)(2,1)S(1)}, u32[]{:S(2)}, u32[]{:S(2)}) collective-permute-start(bf16[32,64,128]{2,1,0:T(8,128)(2,1)} %get-tuple-element.15), channel_id=1, source_target_pairs={{0,64},{8,72},{16,80},{24,88},{32,96},{40,104},{48,112},{56,120},{... | collective-permute-start | bytes 1572872 | tf_op jit(solution)/shard_map/ppermute | solution.py:55
  116.0 31.2 %collective-permute-start.8 = (bf16[32,64,128]{2,1,0:T(8,128)(2,1)}, bf16[32,64,128]{2,1,0:T(8,128)(2,1)S(1)}, u32[]{:S(2)}, u32[]{:S(2)}) collective-permute-start(bf16[32,64,128]{2,1,0:T(8,128)(2,1)} %get-tuple-element.16), channel_id=1, source_target_pairs={{0,68},{1,69},{2,70},{3,71},{4,64},{5,65},{6,66},{7,67},{8,76},{9,... | collective-permute-start | bytes 1572872 | tf_op jit(solution)/shard_map/ppermute | solution.py:64
  128.0 27.7 %collective-permute-start.23 = (bf16[32,64,128]{2,1,0:T(8,128)(2,1)S(1)}, bf16[32,64,128]{2,1,0:T(8,128)(2,1)S(1)}, u32[]{:S(2)}, u32[]{:S(2)}) collective-permute-start(bf16[32,64,128]{2,1,0:T(8,128)(2,1)S(1)} %get-tuple-element.22), channel_id=1, source_target_pairs={{0,1},{1,0},{2,3},{3,2},{4,5},{5,4},{6,7},{7,6},{8,9},{9,8},{10,11... | collective-permute-start | bytes 1572872 | tf_op jit(solution)/shard_map/ppermute | solution.py:58
  128.0 36.8 %collective-permute-start.22 = (bf16[32,64,128]{2,1,0:T(8,128)(2,1)}, bf16[32,64,128]{2,1,0:T(8,128)(2,1)S(1)}, u32[]{:S(2)}, u32[]{:S(2)}) collective-permute-start(bf16[32,64,128]{2,1,0:T(8,128)(2,1)} %get-tuple-element.23), channel_id=1, source_target_pairs={{0,8},{8,0},{16,24},{24,16},{32,40},{40,32},{48,56},{56,48},{64,72... | collective-permute-start | bytes 1572872 | tf_op jit(solution)/shard_map/ppermute | solution.py:55
  131.7 40.2 %collective-permute-start.21 = (bf16[32,64,128]{2,1,0:T(8,128)(2,1)}, bf16[32,64,128]{2,1,0:T(8,128)(2,1)S(1)}, u32[]{:S(2)}, u32[]{:S(2)}) collective-permute-start(bf16[32,64,128]{2,1,0:T(8,128)(2,1)} %get-tuple-element.24), channel_id=1, source_target_pairs={{0,9},{1,8},{2,11},{3,10},{4,13},{5,12},{6,15},{7,14},{8,1},{9,0},... | collective-permute-start | bytes 1572872 | tf_op jit(solution)/shard_map/ppermute | solution.py:64
  149.4 28.7 %collective-permute-start.11 = (bf16[32,64,128]{2,1,0:T(8,128)(2,1)}, bf16[32,64,128]{2,1,0:T(8,128)(2,1)S(1)}, u32[]{:S(2)}, u32[]{:S(2)}) collective-permute-start(bf16[32,64,128]{2,1,0:T(8,128)(2,1)} %get-tuple-element.30), channel_id=1, source_target_pairs={{0,1},{1,0},{2,3},{3,2},{4,5},{5,4},{6,7},{7,6},{8,9},{9,8},{10,11... | collective-permute-start | bytes 1572872 | tf_op jit(solution)/shard_map/ppermute | solution.py:58
  149.4 32.2 %collective-permute-start.10 = (bf16[32,64,128]{2,1,0:T(8,128)(2,1)}, bf16[32,64,128]{2,1,0:T(8,128)(2,1)S(1)}, u32[]{:S(2)}, u32[]{:S(2)}) collective-permute-start(bf16[32,64,128]{2,1,0:T(8,128)(2,1)} %get-tuple-element.31), channel_id=1, source_target_pairs={{0,8},{8,0},{16,24},{24,16},{32,40},{40,32},{48,56},{56,48},{64,72... | collective-permute-start | bytes 1572872 | tf_op jit(solution)/shard_map/ppermute | solution.py:55
  155.7 35.4 %collective-permute-start.9 = (bf16[32,64,128]{2,1,0:T(8,128)(2,1)}, bf16[32,64,128]{2,1,0:T(8,128)(2,1)S(1)}, u32[]{:S(2)}, u32[]{:S(2)}) collective-permute-start(bf16[32,64,128]{2,1,0:T(8,128)(2,1)} %get-tuple-element.32), channel_id=1, source_target_pairs={{0,9},{1,8},{2,11},{3,10},{4,13},{5,12},{6,15},{7,14},{8,1},{9,0},... | collective-permute-start | bytes 1572872 | tf_op jit(solution)/shard_map/ppermute | solution.py:64
  (16 other events, 109.2 us)

commit v14 on v7

--- a/solution.py
+++ b/solution.py
@@ -161,7 +161,7 @@
     )(*operands)
 
 
-def output_stage(pieces, wave, obs, chunk, w_mat, w_t, o_mat, o_t, step=8):
+def output_stage(pieces, wave, obs, chunk, w_mat, w_t, o_mat, o_t, step=16):
     part, rank_size, inner_boxes = pieces[0].shape
     piece_spec = pl.BlockSpec((step, rank_size, inner_boxes), lambda i: (i, 0, 0))
     field_spec = pl.BlockSpec(

time: 195 us -> 195 us (level)
  transfers between devices with their start and end apart: 24 -> 24, of which waited for: 9 -> 9; matrix products, arithmetic and copies ran while one was open for 8% -> 8% of each run, Pallas kernels for 30% -> 29%
where the time goes in v14:
time: 195 us; the launch traced here: 194 us
  Pallas kernels  61.8 us (32%)
  waiting for transfers between devices  54.3 us (28%)
  starting transfers between devices  53.9 us (28%)
  local copies, waits for them, and re-layouts  14.6 us (7%)
  matrix products  6.8 us (3%)
  other arithmetic  2.27 us (1%)
    pallas_call x16, Pallas kernels, chain_call(): pl.pallas_call(functools.partial(chain_kernel, plan), grid_spec=pltpu.Pre...  42.8 us
    ppermute x8, waiting for transfers between devices, flip_send(): return lax.ppermute(value, 'qx', pairs)  29.4 us
    ppermute x8, starting transfers between devices, flip_send(): return lax.ppermute(value, ('qx', 'qy'), pairs)  23.3 us
    pallas_call x2, Pallas kernels, output_stage(): pl.pallas_call(output_stage_kernel, grid=(part // step,), in_specs=[piece...  19 us
    ppermute x8, starting transfers between devices, flip_send(): return lax.ppermute(value, 'qx', pairs)  16.3 us
    ppermute x8, waiting for transfers between devices, flip_send(): return lax.ppermute(value, 'qy', pairs)  15.8 us
    ppermute x8, starting transfers between devices, flip_send(): return lax.ppermute(value, 'qy', pairs)  14.3 us
    ppermute x8, waiting for transfers between devices, flip_send(): return lax.ppermute(value, ('qx', 'qy'), pairs)  9.15 us
  transfers between devices with their start and end apart: 24, of which 9 were waited for; matrix products, arithmetic and copies ran while one was open for 8% of the time, Pallas kernels for 29%

profile of v14, /device:TPU:1, one launch (start us, length us, event | category | flops | bytes accessed | tf_op | source)
XLA Modules:
  0.0 194.1 jit_solution(10738438762744732850)
XLA Ops:
  12.4 2.7 %shard_map.81 = bf16[32,64,128]{2,1,0:T(8,128)(2,1)} custom-call(s32[1]{0:T(128)} %bitcast.k_ref, bf16[4,2,32,64,128]{4,3,2,1,0:T(8,128)(2,1)} %bitcast.167, bf16[3,256,256]{2,1,0:T(8,128)(2,1)} %pad_maximum_fusion.4.m_ref), custom_call_target="tpu_custom_call" | custom-call | tf_op jit(solution)/shard_map/pallas_call | solution.py:154
  19.6 2.7 %shard_map.74 = bf16[32,64,128]{2,1,0:T(8,128)(2,1)} custom-call(s32[1]{0:T(128)} %bitcast.k_ref, bf16[4,2,32,64,128]{4,3,2,1,0:T(8,128)(2,1)} %bitcast.169, bf16[3,256,256]{2,1,0:T(8,128)(2,1)} %pad_maximum_fusion.4.m_ref), custom_call_target="tpu_custom_call" | custom-call | tf_op jit(solution)/shard_map/pallas_call | solution.py:154
  22.5 2.7 %shard_map.78 = bf16[32,64,128]{2,1,0:T(8,128)(2,1)} custom-call(s32[1]{0:T(128)} %bitcast.k_ref, bf16[4,2,32,64,128]{4,3,2,1,0:T(8,128)(2,1)} %bitcast.170, bf16[3,256,256]{2,1,0:T(8,128)(2,1)} %pad_maximum_fusion.4.m_ref), custom_call_target="tpu_custom_call" | custom-call | tf_op jit(solution)/shard_map/pallas_call | solution.py:154
  25.2 2.7 %shard_map.75 = bf16[32,64,128]{2,1,0:T(8,128)(2,1)} custom-call(s32[1]{0:T(128)} %bitcast.k_ref, bf16[4,2,32,64,128]{4,3,2,1,0:T(8,128)(2,1)} %bitcast.171, bf16[3,256,256]{2,1,0:T(8,128)(2,1)} %pad_maximum_fusion.4.m_ref), custom_call_target="tpu_custom_call" | custom-call | tf_op jit(solution)/shard_map/pallas_call | solution.py:154
  37.0 3.0 %collective-permute-start.15 = (bf16[32,64,128]{2,1,0:T(8,128)(2,1)}, bf16[32,64,128]{2,1,0:T(8,128)(2,1)}, u32[]{:S(2)}, u32[]{:S(2)}) collective-permute-start(bf16[32,64,128]{2,1,0:T(8,128)(2,1)} %get-tuple-element.27), channel_id=1, source_target_pairs={{0,4},{1,5},{2,6},{3,7},{4,0},{5,1},{6,2},{7,3},{8,12},{9,13},{10,... | collective-permute-start | bytes 1572872 | tf_op jit(solution)/shard_map/ppermute | solution.py:58
  40.0 3.6 %collective-permute-start.16 = (bf16[32,64,128]{2,1,0:T(8,128)(2,1)}, bf16[32,64,128]{2,1,0:T(8,128)(2,1)}, u32[]{:S(2)}, u32[]{:S(2)}) collective-permute-start(bf16[32,64,128]{2,1,0:T(8,128)(2,1)} %get-tuple-element.26), channel_id=1, source_target_pairs={{0,64},{8,72},{16,80},{24,88},{32,96},{40,104},{48,112},{56,120},{... | collective-permute-start | bytes 1572872 | tf_op jit(solution)/shard_map/ppermute | solution.py:55
  44.9 6.3 %collective-permute-start.17 = (bf16[32,64,128]{2,1,0:T(8,128)(2,1)S(1)}, bf16[32,64,128]{2,1,0:T(8,128)(2,1)}, u32[]{:S(2)}, u32[]{:S(2)}) collective-permute-start(bf16[32,64,128]{2,1,0:T(8,128)(2,1)S(1)} %get-tuple-element.25), channel_id=1, source_target_pairs={{0,68},{1,69},{2,70},{3,71},{4,64},{5,65},{6,66},{7,67},{8,76},{9,... | collective-permute-start | bytes 1572872 | tf_op jit(solution)/shard_map/ppermute | solution.py:64
  51.2 14.4 %collective-permute-done = bf16[32,64,128]{2,1,0:T(8,128)(2,1)} collective-permute-done((bf16[32,64,128]{2,1,0:T(8,128)(2,1)}, bf16[32,64,128]{2,1,0:T(8,128)(2,1)}, u32[]{:S(2)}, u32[]{:S(2)}) %collective-permute-start) | collective-permute-done | bytes 524320 | tf_op jit(solution)/shard_map/ppermute | solution.py:58
  68.8 2.8 %collective-permute-start.3 = (bf16[32,64,128]{2,1,0:T(8,128)(2,1)}, bf16[32,64,128]{2,1,0:T(8,128)(2,1)}, u32[]{:S(2)}, u32[]{:S(2)}) collective-permute-start(bf16[32,64,128]{2,1,0:T(8,128)(2,1)} %get-tuple-element.35), channel_id=1, source_target_pairs={{0,4},{1,5},{2,6},{3,7},{4,0},{5,1},{6,2},{7,3},{8,12},{9,13},{10,... | collective-permute-start | bytes 1572872 | tf_op jit(solution)/shard_map/ppermute | solution.py:58
  73.8 3.2 %collective-permute-start.4 = (bf16[32,64,128]{2,1,0:T(8,128)(2,1)}, bf16[32,64,128]{2,1,0:T(8,128)(2,1)S(1)}, u32[]{:S(2)}, u32[]{:S(2)}) collective-permute-start(bf16[32,64,128]{2,1,0:T(8,128)(2,1)} %get-tuple-element.34), channel_id=1, source_target_pairs={{0,64},{8,72},{16,80},{24,88},{32,96},{40,104},{48,112},{56,120},{... | collective-permute-start | bytes 1572872 | tf_op jit(solution)/shard_map/ppermute | solution.py:55
  77.1 2.8 %collective-permute-done.16.p2 = bf16[32,64,128]{2,1,0:T(8,128)(2,1)} collective-permute-done((bf16[32,64,128]{2,1,0:T(8,128)(2,1)}, bf16[32,64,128]{2,1,0:T(8,128)(2,1)}, u32[]{:S(2)}, u32[]{:S(2)}) %collective-permute-start.16) | collective-permute-done | bytes 524320 | tf_op jit(solution)/shard_map/ppermute | solution.py:55
  79.9 9.5 %shard_map.82 = (bf16[32,64,128]{2,1,0:T(8,128)(2,1)}, bf16[32,64,128]{2,1,0:T(8,128)(2,1)}, bf16[32,64,128]{2,1,0:T(8,128)(2,1)}, bf16[32,64,128]{2,1,0:T(8,128)(2,1)}) custom-call(bf16[32,64,128]{2,1,0:T(8,128)(2,1)} %get-tuple-element.28.p0, bf16[32,64,128]{2,1,0:T(8,128)(2,1)} %collective-permute-done.15.p1, ...), custom_call_target="tpu_custom_call" | custom-call | flops 2147483648 | bytes 10485760 | tf_op jit(solution)/shard_map/pallas_call | solution.py:173
  89.3 3.0 %collective-permute-start.18 = (bf16[32,64,128]{2,1,0:T(8,128)(2,1)}, bf16[32,64,128]{2,1,0:T(8,128)(2,1)S(1)}, u32[]{:S(2)}, u32[]{:S(2)}) collective-permute-start(bf16[32,64,128]{2,1,0:T(8,128)(2,1)} %get-tuple-element.18), channel_id=1, source_target_pairs={{0,4},{1,5},{2,6},{3,7},{4,0},{5,1},{6,2},{7,3},{8,12},{9,13},{10,... | collective-permute-start | bytes 1572872 | tf_op jit(solution)/shard_map/ppermute | solution.py:58
  92.3 2.8 %collective-permute-start.20 = (bf16[32,64,128]{2,1,0:T(8,128)(2,1)}, bf16[32,64,128]{2,1,0:T(8,128)(2,1)}, u32[]{:S(2)}, u32[]{:S(2)}) collective-permute-start(bf16[32,64,128]{2,1,0:T(8,128)(2,1)} %get-tuple-element.20), channel_id=1, source_target_pairs={{0,68},{1,69},{2,70},{3,71},{4,64},{5,65},{6,66},{7,67},{8,76},{9,... | collective-permute-start | bytes 1572872 | tf_op jit(solution)/shard_map/ppermute | solution.py:64
  95.1 7.1 %collective-permute-done.4.p2 = bf16[32,64,128]{2,1,0:T(8,128)(2,1)S(1)} collective-permute-done((bf16[32,64,128]{2,1,0:T(8,128)(2,1)}, bf16[32,64,128]{2,1,0:T(8,128)(2,1)S(1)}, u32[]{:S(2)}, u32[]{:S(2)}) %collective-permute-start.4) | collective-permute-done | bytes 524320 | tf_op jit(solution)/shard_map/ppermute | solution.py:55
  103.0 9.5 %shard_map.77 = (bf16[32,64,128]{2,1,0:T(8,128)(2,1)}, bf16[32,64,128]{2,1,0:T(8,128)(2,1)}, bf16[32,64,128]{2,1,0:T(8,128)(2,1)}, bf16[32,64,128]{2,1,0:T(8,128)(2,1)}) custom-call(bf16[32,64,128]{2,1,0:T(8,128)(2,1)} %get-tuple-element.36.p0, bf16[32,64,128]{2,1,0:T(8,128)(2,1)} %collective-permute-done.3.p1, bf16[32,64,128]{2,1,0:T(8,128)(2,1)} %copy-done.10, ...), custom_call_target="tpu_custom_call" | custom-call | flops 2147483648 | bytes 10485760 | tf_op jit(solution)/shard_map/pallas_call | solution.py:173
  112.5 3.0 %collective-permute-start.6 = (bf16[32,64,128]{2,1,0:T(8,128)(2,1)}, bf16[32,64,128]{2,1,0:T(8,128)(2,1)S(1)}, u32[]{:S(2)}, u32[]{:S(2)}) collective-permute-start(bf16[32,64,128]{2,1,0:T(8,128)(2,1)} %get-tuple-element.14), channel_id=1, source_target_pairs={{0,4},{1,5},{2,6},{3,7},{4,0},{5,1},{6,2},{7,3},{8,12},{9,13},{10,... | collective-permute-start | bytes 1572872 | tf_op jit(solution)/shard_map/ppermute | solution.py:58
  115.6 2.8 %collective-permute-start.8 = (bf16[32,64,128]{2,1,0:T(8,128)(2,1)}, bf16[32,64,128]{2,1,0:T(8,128)(2,1)S(1)}, u32[]{:S(2)}, u32[]{:S(2)}) collective-permute-start(bf16[32,64,128]{2,1,0:T(8,128)(2,1)} %get-tuple-element.16), channel_id=1, source_target_pairs={{0,68},{1,69},{2,70},{3,71},{4,64},{5,65},{6,66},{7,67},{8,76},{9,... | collective-permute-start | bytes 1572872 | tf_op jit(solution)/shard_map/ppermute | solution.py:64
  118.3 6.5 %collective-permute-done.19 = bf16[32,64,128]{2,1,0:T(8,128)(2,1)} collective-permute-done((bf16[32,64,128]{2,1,0:T(8,128)(2,1)}, bf16[32,64,128]{2,1,0:T(8,128)(2,1)}, u32[]{:S(2)}, u32[]{:S(2)}) %collective-permute-start.19) | collective-permute-done | bytes 524320 | tf_op jit(solution)/shard_map/ppermute | solution.py:55
  128.0 4.0 %collective-permute-start.22 = (bf16[32,64,128]{2,1,0:T(8,128)(2,1)}, bf16[32,64,128]{2,1,0:T(8,128)(2,1)S(1)}, u32[]{:S(2)}, u32[]{:S(2)}) collective-permute-start(bf16[32,64,128]{2,1,0:T(8,128)(2,1)} %get-tuple-element.23), channel_id=1, source_target_pairs={{0,8},{8,0},{16,24},{24,16},{32,40},{40,32},{48,56},{56,48},{64,72... | collective-permute-start | bytes 1572872 | tf_op jit(solution)/shard_map/ppermute | solution.py:55
  134.2 13.0 %collective-permute-done.7 = bf16[32,64,128]{2,1,0:T(8,128)(2,1)S(1)} collective-permute-done((bf16[32,64,128]{2,1,0:T(8,128)(2,1)}, bf16[32,64,128]{2,1,0:T(8,128)(2,1)S(1)}, u32[]{:S(2)}, u32[]{:S(2)}) %collective-permute-start.7) | collective-permute-done | bytes 524320 | tf_op jit(solution)/shard_map/ppermute | solution.py:55
  149.3 4.0 %collective-permute-start.10 = (bf16[32,64,128]{2,1,0:T(8,128)(2,1)}, bf16[32,64,128]{2,1,0:T(8,128)(2,1)S(1)}, u32[]{:S(2)}, u32[]{:S(2)}) collective-permute-start(bf16[32,64,128]{2,1,0:T(8,128)(2,1)} %get-tuple-element.31), channel_id=1, source_target_pairs={{0,8},{8,0},{16,24},{24,16},{32,40},{40,32},{48,56},{56,48},{64,72... | collective-permute-start | bytes 1572872 | tf_op jit(solution)/shard_map/ppermute | solution.py:55
  154.7 7.5 %collective-permute-start.9 = (bf16[32,64,128]{2,1,0:T(8,128)(2,1)}, bf16[32,64,128]{2,1,0:T(8,128)(2,1)}, u32[]{:S(2)}, u32[]{:S(2)}) collective-permute-start(bf16[32,64,128]{2,1,0:T(8,128)(2,1)} %get-tuple-element.32), channel_id=1, source_target_pairs={{0,9},{1,8},{2,11},{3,10},{4,13},{5,12},{6,15},{7,14},{8,1},{9,0},... | collective-permute-start | bytes 1572872 | tf_op jit(solution)/shard_map/ppermute | solution.py:64
  185.1 6.3 %collective-permute-done.9.x_ref = bf16[32,64,128]{2,1,0:T(8,128)(2,1)} collective-permute-done((bf16[32,64,128]{2,1,0:T(8,128)(2,1)}, bf16[32,64,128]{2,1,0:T(8,128)(2,1)}, u32[]{:S(2)}, u32[]{:S(2)}) %collective-permute-start.9) | collective-permute-done | bytes 524320 | tf_op jit(solution)/shard_map/ppermute | solution.py:64
  (111 shorter events, 67.9 us)
Async XLA Ops:
  6.3 24.7 %collective-permute-start.12 = (bf16[32,64,128]{2,1,0:T(8,128)(2,1)}, bf16[32,64,128]{2,1,0:T(8,128)(2,1)}, u32[]{:S(2)}, u32[]{:S(2)}) collective-permute-start(bf16[32,64,128]{2,1,0:T(8,128)(2,1)} %shard_map.79), channel_id=1, source_target_pairs={{0,1},{1,0},{2,3},{3,2},{4,5},{5,4},{6,7},{7,6},{8,9},{9,8},{10,11... | collective-permute-start | bytes 1572872 | tf_op jit(solution)/shard_map/ppermute | solution.py:58
  11.4 20.6 %collective-permute-start.13 = (bf16[32,64,128]{2,1,0:T(8,128)(2,1)}, bf16[32,64,128]{2,1,0:T(8,128)(2,1)}, u32[]{:S(2)}, u32[]{:S(2)}) collective-permute-start(bf16[32,64,128]{2,1,0:T(8,128)(2,1)} %shard_map.80), channel_id=1, source_target_pairs={{0,8},{8,0},{16,24},{24,16},{32,40},{40,32},{48,56},{56,48},{64,72... | collective-permute-start | bytes 1572872 | tf_op jit(solution)/shard_map/ppermute | solution.py:55
  15.1 18.5 %collective-permute-start.14 = (bf16[32,64,128]{2,1,0:T(8,128)(2,1)}, bf16[32,64,128]{2,1,0:T(8,128)(2,1)}, u32[]{:S(2)}, u32[]{:S(2)}) collective-permute-start(bf16[32,64,128]{2,1,0:T(8,128)(2,1)} %shard_map.81), channel_id=1, source_target_pairs={{0,9},{1,8},{2,11},{3,10},{4,13},{5,12},{6,15},{7,14},{8,1},{9,0},... | collective-permute-start | bytes 1572872 | tf_op jit(solution)/shard_map/ppermute | solution.py:64
  17.8 27.1 %collective-permute-start.2 = (bf16[32,64,128]{2,1,0:T(8,128)(2,1)}, bf16[32,64,128]{2,1,0:T(8,128)(2,1)}, u32[]{:S(2)}, u32[]{:S(2)}) collective-permute-start(bf16[32,64,128]{2,1,0:T(8,128)(2,1)} %shard_map.76), channel_id=1, source_target_pairs={{0,9},{1,8},{2,11},{3,10},{4,13},{5,12},{6,15},{7,14},{8,1},{9,0},... | collective-permute-start | bytes 1572872 | tf_op jit(solution)/shard_map/ppermute | solution.py:64
  22.3 43.3 %collective-permute-start = (bf16[32,64,128]{2,1,0:T(8,128)(2,1)}, bf16[32,64,128]{2,1,0:T(8,128)(2,1)}, u32[]{:S(2)}, u32[]{:S(2)}) collective-permute-start(bf16[32,64,128]{2,1,0:T(8,128)(2,1)} %shard_map.74), channel_id=1, source_target_pairs={{0,1},{1,0},{2,3},{3,2},{4,5},{5,4},{6,7},{7,6},{8,9},{9,8},{10,11... | collective-permute-start | bytes 1572872 | tf_op jit(solution)/shard_map/ppermute | solution.py:58
  31.6 34.0 %collective-permute-start.1 = (bf16[32,64,128]{2,1,0:T(8,128)(2,1)S(1)}, bf16[32,64,128]{2,1,0:T(8,128)(2,1)S(1)}, u32[]{:S(2)}, u32[]{:S(2)}) collective-permute-start(bf16[32,64,128]{2,1,0:T(8,128)(2,1)S(1)} %copy-done.8), channel_id=1, source_target_pairs={{0,8},{8,0},{16,24},{24,16},{32,40},{40,32},{48,56},{56,48},{64,72... | collective-permute-start | bytes 1572872 | tf_op jit(solution)/shard_map/ppermute | solution.py:55
  37.0 40.1 %collective-permute-start.15 = (bf16[32,64,128]{2,1,0:T(8,128)(2,1)}, bf16[32,64,128]{2,1,0:T(8,128)(2,1)}, u32[]{:S(2)}, u32[]{:S(2)}) collective-permute-start(bf16[32,64,128]{2,1,0:T(8,128)(2,1)} %get-tuple-element.27), channel_id=1, source_target_pairs={{0,4},{1,5},{2,6},{3,7},{4,0},{5,1},{6,2},{7,3},{8,12},{9,13},{10,... | collective-permute-start | bytes 1572872 | tf_op jit(solution)/shard_map/ppermute | solution.py:58
  40.0 39.9 %collective-permute-start.16 = (bf16[32,64,128]{2,1,0:T(8,128)(2,1)}, bf16[32,64,128]{2,1,0:T(8,128)(2,1)}, u32[]{:S(2)}, u32[]{:S(2)}) collective-permute-start(bf16[32,64,128]{2,1,0:T(8,128)(2,1)} %get-tuple-element.26), channel_id=1, source_target_pairs={{0,64},{8,72},{16,80},{24,88},{32,96},{40,104},{48,112},{56,120},{... | collective-permute-start | bytes 1572872 | tf_op jit(solution)/shard_map/ppermute | solution.py:55
  44.9 35.0 %collective-permute-start.17 = (bf16[32,64,128]{2,1,0:T(8,128)(2,1)S(1)}, bf16[32,64,128]{2,1,0:T(8,128)(2,1)}, u32[]{:S(2)}, u32[]{:S(2)}) collective-permute-start(bf16[32,64,128]{2,1,0:T(8,128)(2,1)S(1)} %get-tuple-element.25), channel_id=1, source_target_pairs={{0,68},{1,69},{2,70},{3,71},{4,64},{5,65},{6,66},{7,67},{8,76},{9,... | collective-permute-start | bytes 1572872 | tf_op jit(solution)/shard_map/ppermute | solution.py:64
  68.8 23.6 %collective-permute-start.3 = (bf16[32,64,128]{2,1,0:T(8,128)(2,1)}, bf16[32,64,128]{2,1,0:T(8,128)(2,1)}, u32[]{:S(2)}, u32[]{:S(2)}) collective-permute-start(bf16[32,64,128]{2,1,0:T(8,128)(2,1)} %get-tuple-element.35), channel_id=1, source_target_pairs={{0,4},{1,5},{2,6},{3,7},{4,0},{5,1},{6,2},{7,3},{8,12},{9,13},{10,... | collective-permute-start | bytes 1572872 | tf_op jit(solution)/shard_map/ppermute | solution.py:58
  73.8 28.4 %collective-permute-start.4 = (bf16[32,64,128]{2,1,0:T(8,128)(2,1)}, bf16[32,64,128]{2,1,0:T(8,128)(2,1)S(1)}, u32[]{:S(2)}, u32[]{:S(2)}) collective-permute-start(bf16[32,64,128]{2,1,0:T(8,128)(2,1)} %get-tuple-element.34), channel_id=1, source_target_pairs={{0,64},{8,72},{16,80},{24,88},{32,96},{40,104},{48,112},{56,120},{... | collective-permute-start | bytes 1572872 | tf_op jit(solution)/shard_map/ppermute | solution.py:55
  77.1 25.2 %collective-permute-start.5 = (bf16[32,64,128]{2,1,0:T(8,128)(2,1)S(1)}, bf16[32,64,128]{2,1,0:T(8,128)(2,1)}, u32[]{:S(2)}, u32[]{:S(2)}) collective-permute-start(bf16[32,64,128]{2,1,0:T(8,128)(2,1)S(1)} %get-tuple-element.33), channel_id=1, source_target_pairs={{0,68},{1,69},{2,70},{3,71},{4,64},{5,65},{6,66},{7,67},{8,76},{9,... | collective-permute-start | bytes 1572872 | tf_op jit(solution)/shard_map/ppermute | solution.py:64
  89.3 26.2 %collective-permute-start.18 = (bf16[32,64,128]{2,1,0:T(8,128)(2,1)}, bf16[32,64,128]{2,1,0:T(8,128)(2,1)S(1)}, u32[]{:S(2)}, u32[]{:S(2)}) collective-permute-start(bf16[32,64,128]{2,1,0:T(8,128)(2,1)} %get-tuple-element.18), channel_id=1, source_target_pairs={{0,4},{1,5},{2,6},{3,7},{4,0},{5,1},{6,2},{7,3},{8,12},{9,13},{10,... | collective-permute-start | bytes 1572872 | tf_op jit(solution)/shard_map/ppermute | solution.py:58
  92.3 32.5 %collective-permute-start.19 = (bf16[32,64,128]{2,1,0:T(8,128)(2,1)}, bf16[32,64,128]{2,1,0:T(8,128)(2,1)}, u32[]{:S(2)}, u32[]{:S(2)}) collective-permute-start(bf16[32,64,128]{2,1,0:T(8,128)(2,1)} %get-tuple-element.19), channel_id=1, source_target_pairs={{0,64},{8,72},{16,80},{24,88},{32,96},{40,104},{48,112},{56,120},{... | collective-permute-start | bytes 1572872 | tf_op jit(solution)/shard_map/ppermute | solution.py:55
  92.3 32.5 %collective-permute-start.20 = (bf16[32,64,128]{2,1,0:T(8,128)(2,1)}, bf16[32,64,128]{2,1,0:T(8,128)(2,1)}, u32[]{:S(2)}, u32[]{:S(2)}) collective-permute-start(bf16[32,64,128]{2,1,0:T(8,128)(2,1)} %get-tuple-element.20), channel_id=1, source_target_pairs={{0,68},{1,69},{2,70},{3,71},{4,64},{5,65},{6,66},{7,67},{8,76},{9,... | collective-permute-start | bytes 1572872 | tf_op jit(solution)/shard_map/ppermute | solution.py:64
  112.5 19.4 %collective-permute-start.6 = (bf16[32,64,128]{2,1,0:T(8,128)(2,1)}, bf16[32,64,128]{2,1,0:T(8,128)(2,1)S(1)}, u32[]{:S(2)}, u32[]{:S(2)}) collective-permute-start(bf16[32,64,128]{2,1,0:T(8,128)(2,1)} %get-tuple-element.14), channel_id=1, source_target_pairs={{0,4},{1,5},{2,6},{3,7},{4,0},{5,1},{6,2},{7,3},{8,12},{9,13},{10,... | collective-permute-start | bytes 1572872 | tf_op jit(solution)/shard_map/ppermute | solution.py:58
  115.6 31.6 %collective-permute-start.7 = (bf16[32,64,128]{2,1,0:T(8,128)(2,1)}, bf16[32,64,128]{2,1,0:T(8,128)(2,1)S(1)}, u32[]{:S(2)}, u32[]{:S(2)}) collective-permute-start(bf16[32,64,128]{2,1,0:T(8,128)(2,1)} %get-tuple-element.15), channel_id=1, source_target_pairs={{0,64},{8,72},{16,80},{24,88},{32,96},{40,104},{48,112},{56,120},{... | collective-permute-start | bytes 1572872 | tf_op jit(solution)/shard_map/ppermute | solution.py:55
  115.6 31.6 %collective-permute-start.8 = (bf16[32,64,128]{2,1,0:T(8,128)(2,1)}, bf16[32,64,128]{2,1,0:T(8,128)(2,1)S(1)}, u32[]{:S(2)}, u32[]{:S(2)}) collective-permute-start(bf16[32,64,128]{2,1,0:T(8,128)(2,1)} %get-tuple-element.16), channel_id=1, source_target_pairs={{0,68},{1,69},{2,70},{3,71},{4,64},{5,65},{6,66},{7,67},{8,76},{9,... | collective-permute-start | bytes 1572872 | tf_op jit(solution)/shard_map/ppermute | solution.py:64
  128.0 26.7 %collective-permute-start.23 = (bf16[32,64,128]{2,1,0:T(8,128)(2,1)S(1)}, bf16[32,64,128]{2,1,0:T(8,128)(2,1)S(1)}, u32[]{:S(2)}, u32[]{:S(2)}) collective-permute-start(bf16[32,64,128]{2,1,0:T(8,128)(2,1)S(1)} %get-tuple-element.22), channel_id=1, source_target_pairs={{0,1},{1,0},{2,3},{3,2},{4,5},{5,4},{6,7},{7,6},{8,9},{9,8},{10,11... | collective-permute-start | bytes 1572872 | tf_op jit(solution)/shard_map/ppermute | solution.py:58
  128.0 41.4 %collective-permute-start.22 = (bf16[32,64,128]{2,1,0:T(8,128)(2,1)}, bf16[32,64,128]{2,1,0:T(8,128)(2,1)S(1)}, u32[]{:S(2)}, u32[]{:S(2)}) collective-permute-start(bf16[32,64,128]{2,1,0:T(8,128)(2,1)} %get-tuple-element.23), channel_id=1, source_target_pairs={{0,8},{8,0},{16,24},{24,16},{32,40},{40,32},{48,56},{56,48},{64,72... | collective-permute-start | bytes 1572872 | tf_op jit(solution)/shard_map/ppermute | solution.py:55
  132.0 40.9 %collective-permute-start.21 = (bf16[32,64,128]{2,1,0:T(8,128)(2,1)}, bf16[32,64,128]{2,1,0:T(8,128)(2,1)S(1)}, u32[]{:S(2)}, u32[]{:S(2)}) collective-permute-start(bf16[32,64,128]{2,1,0:T(8,128)(2,1)} %get-tuple-element.24), channel_id=1, source_target_pairs={{0,9},{1,8},{2,11},{3,10},{4,13},{5,12},{6,15},{7,14},{8,1},{9,0},... | collective-permute-start | bytes 1572872 | tf_op jit(solution)/shard_map/ppermute | solution.py:64
  149.3 29.6 %collective-permute-start.11 = (bf16[32,64,128]{2,1,0:T(8,128)(2,1)}, bf16[32,64,128]{2,1,0:T(8,128)(2,1)}, u32[]{:S(2)}, u32[]{:S(2)}) collective-permute-start(bf16[32,64,128]{2,1,0:T(8,128)(2,1)} %get-tuple-element.30), channel_id=1, source_target_pairs={{0,1},{1,0},{2,3},{3,2},{4,5},{5,4},{6,7},{7,6},{8,9},{9,8},{10,11... | collective-permute-start | bytes 1572872 | tf_op jit(solution)/shard_map/ppermute | solution.py:58
  149.3 32.3 %collective-permute-start.10 = (bf16[32,64,128]{2,1,0:T(8,128)(2,1)}, bf16[32,64,128]{2,1,0:T(8,128)(2,1)S(1)}, u32[]{:S(2)}, u32[]{:S(2)}) collective-permute-start(bf16[32,64,128]{2,1,0:T(8,128)(2,1)} %get-tuple-element.31), channel_id=1, source_target_pairs={{0,8},{8,0},{16,24},{24,16},{32,40},{40,32},{48,56},{56,48},{64,72... | collective-permute-start | bytes 1572872 | tf_op jit(solution)/shard_map/ppermute | solution.py:55
  154.7 36.7 %collective-permute-start.9 = (bf16[32,64,128]{2,1,0:T(8,128)(2,1)}, bf16[32,64,128]{2,1,0:T(8,128)(2,1)}, u32[]{:S(2)}, u32[]{:S(2)}) collective-permute-start(bf16[32,64,128]{2,1,0:T(8,128)(2,1)} %get-tuple-element.32), channel_id=1, source_target_pairs={{0,9},{1,8},{2,11},{3,10},{4,13},{5,12},{6,15},{7,14},{8,1},{9,0},... | collective-permute-start | bytes 1572872 | tf_op jit(solution)/shard_map/ppermute | solution.py:64
  (15 other events, 114.5 us)

commit v15 on v7

--- a/solution.py
+++ b/solution.py
@@ -252,6 +252,26 @@
             target=gradient,
         )
 
+    half = part // 2
+    half_plan = [chain_sets(half, 4**i) for i in reversed(range(local_depth))] + [
+        chain_sets(half, 1)
+    ]
+
+    def local_adjoint_half(gradient, piece, m, f, h):
+        return chain_call(
+            half_plan,
+            k0_ref,
+            piece,
+            adjoint_mats,
+            pl.BlockSpec((half, rank_size, inner_boxes), lambda i, k: (0, 0, 0)),
+            jax.ShapeDtypeStruct(shape5, jnp.bfloat16),
+            pl.BlockSpec(
+                (None, None, half, rank_size, inner_boxes),
+                lambda i, k: (jnp.bitwise_xor(k[0], f), m, h, 0, 0),
+            ),
+            target=gradient,
+        )
+
     gradient = None
     for m in range(CHUNKS):
         coef = [local_forward(m, f) for f in range(4)]
@@ -261,9 +281,15 @@
         terms = output_stage(pieces, wave, obs, m, w1_mat, w1_t, ow_mat, ow_t)
         back = exchange(terms, *shifts[1])
         terms = mixing(w0, jnp.stack(back), "scor,sjol->cjrl")
-        back = exchange(terms, *shifts[0])
-        for f in range(4):
-            gradient = local_adjoint(gradient, back[f], m, f)
+        if m < CHUNKS - 1:
+            back = exchange(terms, *shifts[0])
+            for f in range(4):
+                gradient = local_adjoint(gradient, back[f], m, f)
+            continue
+        for h in range(2):
+            back = exchange(terms[:, h * half:(h + 1) * half], *shifts[0])
+            for f in range(4):
+                gradient = local_adjoint_half(gradient, back[f], m, f, h)
     return gradient.reshape(groups, rank_size, inner_boxes)[None, None]
 
 

time: 195 us -> 210 us (1.077)
  waiting for transfers between devices: 53.7 us -> 64.5 us
  Pallas kernels: 62.7 us -> 71.3 us
  local copies, waits for them, and re-layouts: 14.6 us -> 11.6 us
    ppermute x8 -> x9, waiting for transfers between devices: 15.8 us -> 32.7 us  [flip_send(): return lax.ppermute(value, 'qy', pairs)]
    pallas_call x16 -> x20, Pallas kernels: 42.9 us -> 51.5 us  [chain_call(): pl.pallas_call(functools.partial(chain_kernel, plan), grid_spec=pltpu.Pre...]
    ppermute x8 -> x9, waiting for transfers between devices: 9.12 us -> 2.92 us  [flip_send(): return lax.ppermute(value, ('qx', 'qy'), pairs)]
    unnamed x32, local copies, waits for them, and re-layouts: 4.06 us -> 1.62 us
    ppermute x8 -> x9, starting transfers between devices: 23 us -> 21.4 us  [flip_send(): return lax.ppermute(value, ('qx', 'qy'), pairs)]
    ppermute x8 -> x9, starting transfers between devices: 14.3 us -> 15.1 us  [flip_send(): return lax.ppermute(value, 'qy', pairs)]
    ppermute x8 -> x9, starting transfers between devices: 16.3 us -> 16.1 us  [flip_send(): return lax.ppermute(value, 'qx', pairs)]
    ppermute x8 -> x9, waiting for transfers between devices: 28.8 us -> 28.9 us  [flip_send(): return lax.ppermute(value, 'qx', pairs)]
  transfers between devices with their start and end apart: 24 -> 27, of which waited for: 9 -> 8; matrix products, arithmetic and copies ran while one was open for 8% -> 8% of each run, Pallas kernels for 30% -> 32%
where the time goes in v15:
time: 210 us; the launch traced here: 209 us
  Pallas kernels  71.3 us (34%)
  waiting for transfers between devices  64.5 us (31%)
  starting transfers between devices  52.6 us (25%)
  local copies, waits for them, and re-layouts  11.6 us (6%)
  matrix products  6.79 us (3%)
  other arithmetic  2.27 us (1%)
    pallas_call x20, Pallas kernels, chain_call(): pl.pallas_call(functools.partial(chain_kernel, plan), grid_spec=pltpu.Pre...  51.5 us
    ppermute x9, waiting for transfers between devices, flip_send(): return lax.ppermute(value, 'qy', pairs)  32.7 us
    ppermute x9, waiting for transfers between devices, flip_send(): return lax.ppermute(value, 'qx', pairs)  28.9 us
    ppermute x9, starting transfers between devices, flip_send(): return lax.ppermute(value, ('qx', 'qy'), pairs)  21.4 us
    pallas_call x2, Pallas kernels, output_stage(): pl.pallas_call(output_stage_kernel, grid=(part // step,), in_specs=[piece...  19.8 us
    ppermute x9, starting transfers between devices, flip_send(): return lax.ppermute(value, 'qx', pairs)  16.1 us
    ppermute x9, starting transfers between devices, flip_send(): return lax.ppermute(value, 'qy', pairs)  15.1 us
    dot_general x4, matrix products, mixing(): jnp.einsum(form, weight, data, preferred_element_type=jnp.float32)  6.79 us
  transfers between devices with their start and end apart: 27, of which 8 were waited for; matrix products, arithmetic and copies ran while one was open for 8% of the time, Pallas kernels for 32%

profile of v15, /device:TPU:1, one launch (start us, length us, event | category | flops | bytes accessed | tf_op | source)
XLA Modules:
  0.0 209.4 jit_solution(1249621472584345353)
XLA Ops:
  8.7 2.7 %shard_map.80 = bf16[32,64,128]{2,1,0:T(8,128)(2,1)} custom-call(s32[1]{0:T(128)} %bitcast.k_ref, bf16[4,2,32,64,128]{4,3,2,1,0:T(8,128)(2,1)} %bitcast.174, bf16[3,256,256]{2,1,0:T(8,128)(2,1)} %pad_maximum_fusion.4.m_ref), custom_call_target="tpu_custom_call" | custom-call | tf_op jit(solution)/shard_map/pallas_call | solution.py:154
  12.4 2.7 %shard_map.81 = bf16[32,64,128]{2,1,0:T(8,128)(2,1)} custom-call(s32[1]{0:T(128)} %bitcast.k_ref, bf16[4,2,32,64,128]{4,3,2,1,0:T(8,128)(2,1)} %bitcast.175, bf16[3,256,256]{2,1,0:T(8,128)(2,1)} %pad_maximum_fusion.4.m_ref), custom_call_target="tpu_custom_call" | custom-call | tf_op jit(solution)/shard_map/pallas_call | solution.py:154
  19.5 2.7 %shard_map.74 = bf16[32,64,128]{2,1,0:T(8,128)(2,1)} custom-call(s32[1]{0:T(128)} %bitcast.k_ref, bf16[4,2,32,64,128]{4,3,2,1,0:T(8,128)(2,1)} %bitcast.177, bf16[3,256,256]{2,1,0:T(8,128)(2,1)} %pad_maximum_fusion.4.m_ref), custom_call_target="tpu_custom_call" | custom-call | tf_op jit(solution)/shard_map/pallas_call | solution.py:154
  22.4 2.7 %shard_map.78 = bf16[32,64,128]{2,1,0:T(8,128)(2,1)} custom-call(s32[1]{0:T(128)} %bitcast.k_ref, bf16[4,2,32,64,128]{4,3,2,1,0:T(8,128)(2,1)} %bitcast.178, bf16[3,256,256]{2,1,0:T(8,128)(2,1)} %pad_maximum_fusion.4.m_ref), custom_call_target="tpu_custom_call" | custom-call | tf_op jit(solution)/shard_map/pallas_call | solution.py:154
  36.9 3.0 %collective-permute-start.18 = (bf16[32,64,128]{2,1,0:T(8,128)(2,1)}, bf16[32,64,128]{2,1,0:T(8,128)(2,1)}, u32[]{:S(2)}, u32[]{:S(2)}) collective-permute-start(bf16[32,64,128]{2,1,0:T(8,128)(2,1)} %get-tuple-element.27), channel_id=1, source_target_pairs={{0,4},{1,5},{2,6},{3,7},{4,0},{5,1},{6,2},{7,3},{8,12},{9,13},{10,... | collective-permute-start | bytes 1572872 | tf_op jit(solution)/shard_map/ppermute | solution.py:58
  39.9 3.6 %collective-permute-start.19 = (bf16[32,64,128]{2,1,0:T(8,128)(2,1)}, bf16[32,64,128]{2,1,0:T(8,128)(2,1)}, u32[]{:S(2)}, u32[]{:S(2)}) collective-permute-start(bf16[32,64,128]{2,1,0:T(8,128)(2,1)} %get-tuple-element.26), channel_id=1, source_target_pairs={{0,64},{8,72},{16,80},{24,88},{32,96},{40,104},{48,112},{56,120},{... | collective-permute-start | bytes 1572872 | tf_op jit(solution)/shard_map/ppermute | solution.py:55
  44.8 6.4 %collective-permute-start.20 = (bf16[32,64,128]{2,1,0:T(8,128)(2,1)S(1)}, bf16[32,64,128]{2,1,0:T(8,128)(2,1)}, u32[]{:S(2)}, u32[]{:S(2)}) collective-permute-start(bf16[32,64,128]{2,1,0:T(8,128)(2,1)S(1)} %get-tuple-element.25), channel_id=1, source_target_pairs={{0,68},{1,69},{2,70},{3,71},{4,64},{5,65},{6,66},{7,67},{8,76},{9,... | collective-permute-start | bytes 1572872 | tf_op jit(solution)/shard_map/ppermute | solution.py:64
  51.2 14.4 %collective-permute-done = bf16[32,64,128]{2,1,0:T(8,128)(2,1)} collective-permute-done((bf16[32,64,128]{2,1,0:T(8,128)(2,1)}, bf16[32,64,128]{2,1,0:T(8,128)(2,1)}, u32[]{:S(2)}, u32[]{:S(2)}) %collective-permute-start) | collective-permute-done | bytes 524320 | tf_op jit(solution)/shard_map/ppermute | solution.py:58
  68.8 2.8 %collective-permute-start.3 = (bf16[32,64,128]{2,1,0:T(8,128)(2,1)}, bf16[32,64,128]{2,1,0:T(8,128)(2,1)}, u32[]{:S(2)}, u32[]{:S(2)}) collective-permute-start(bf16[32,64,128]{2,1,0:T(8,128)(2,1)} %get-tuple-element.39), channel_id=1, source_target_pairs={{0,4},{1,5},{2,6},{3,7},{4,0},{5,1},{6,2},{7,3},{8,12},{9,13},{10,... | collective-permute-start | bytes 1572872 | tf_op jit(solution)/shard_map/ppermute | solution.py:58
  73.8 3.2 %collective-permute-start.4 = (bf16[32,64,128]{2,1,0:T(8,128)(2,1)}, bf16[32,64,128]{2,1,0:T(8,128)(2,1)S(1)}, u32[]{:S(2)}, u32[]{:S(2)}) collective-permute-start(bf16[32,64,128]{2,1,0:T(8,128)(2,1)} %get-tuple-element.38), channel_id=1, source_target_pairs={{0,64},{8,72},{16,80},{24,88},{32,96},{40,104},{48,112},{56,120},{... | collective-permute-start | bytes 1572872 | tf_op jit(solution)/shard_map/ppermute | solution.py:55
  77.0 2.8 %collective-permute-done.19.p2 = bf16[32,64,128]{2,1,0:T(8,128)(2,1)} collective-permute-done((bf16[32,64,128]{2,1,0:T(8,128)(2,1)}, bf16[32,64,128]{2,1,0:T(8,128)(2,1)}, u32[]{:S(2)}, u32[]{:S(2)}) %collective-permute-start.19) | collective-permute-done | bytes 524320 | tf_op jit(solution)/shard_map/ppermute | solution.py:55
  79.9 9.9 %shard_map.82 = (bf16[32,64,128]{2,1,0:T(8,128)(2,1)}, bf16[32,64,128]{2,1,0:T(8,128)(2,1)}, bf16[32,64,128]{2,1,0:T(8,128)(2,1)}, bf16[32,64,128]{2,1,0:T(8,128)(2,1)}) custom-call(bf16[32,64,128]{2,1,0:T(8,128)(2,1)} %get-tuple-element.28.p0, bf16[32,64,128]{2,1,0:T(8,128)(2,1)} %collective-permute-done.18.p1, ...), custom_call_target="tpu_custom_call" | custom-call | flops 2147483648 | bytes 10485760 | tf_op jit(solution)/shard_map/pallas_call | solution.py:173
  89.8 3.0 %collective-permute-start.21 = (bf16[32,64,128]{2,1,0:T(8,128)(2,1)}, bf16[32,64,128]{2,1,0:T(8,128)(2,1)S(1)}, u32[]{:S(2)}, u32[]{:S(2)}) collective-permute-start(bf16[32,64,128]{2,1,0:T(8,128)(2,1)} %get-tuple-element.18), channel_id=1, source_target_pairs={{0,4},{1,5},{2,6},{3,7},{4,0},{5,1},{6,2},{7,3},{8,12},{9,13},{10,... | collective-permute-start | bytes 1572872 | tf_op jit(solution)/shard_map/ppermute | solution.py:58
  92.8 2.8 %collective-permute-start.23 = (bf16[32,64,128]{2,1,0:T(8,128)(2,1)}, bf16[32,64,128]{2,1,0:T(8,128)(2,1)}, u32[]{:S(2)}, u32[]{:S(2)}) collective-permute-start(bf16[32,64,128]{2,1,0:T(8,128)(2,1)} %get-tuple-element.20), channel_id=1, source_target_pairs={{0,68},{1,69},{2,70},{3,71},{4,64},{5,65},{6,66},{7,67},{8,76},{9,... | collective-permute-start | bytes 1572872 | tf_op jit(solution)/shard_map/ppermute | solution.py:64
  95.5 6.7 %collective-permute-done.4.p2 = bf16[32,64,128]{2,1,0:T(8,128)(2,1)S(1)} collective-permute-done((bf16[32,64,128]{2,1,0:T(8,128)(2,1)}, bf16[32,64,128]{2,1,0:T(8,128)(2,1)S(1)}, u32[]{:S(2)}, u32[]{:S(2)}) %collective-permute-start.4) | collective-permute-done | bytes 524320 | tf_op jit(solution)/shard_map/ppermute | solution.py:55
  103.0 9.9 %shard_map.77 = (bf16[32,64,128]{2,1,0:T(8,128)(2,1)}, bf16[32,64,128]{2,1,0:T(8,128)(2,1)}, bf16[32,64,128]{2,1,0:T(8,128)(2,1)}, bf16[32,64,128]{2,1,0:T(8,128)(2,1)}) custom-call(bf16[32,64,128]{2,1,0:T(8,128)(2,1)} %get-tuple-element.40.p0, bf16[32,64,128]{2,1,0:T(8,128)(2,1)} %collective-permute-done.3.p1, bf16[32,64,128]{2,1,0:T(8,128)(2,1)} %copy-done.9, ...), custom_call_target="tpu_custom_call" | custom-call | flops 2147483648 | bytes 10485760 | tf_op jit(solution)/shard_map/pallas_call | solution.py:173
  112.9 3.0 %collective-permute-start.6 = (bf16[32,64,128]{2,1,0:T(8,128)(2,1)}, bf16[32,64,128]{2,1,0:T(8,128)(2,1)S(1)}, u32[]{:S(2)}, u32[]{:S(2)}) collective-permute-start(bf16[32,64,128]{2,1,0:T(8,128)(2,1)} %get-tuple-element.14), channel_id=1, source_target_pairs={{0,4},{1,5},{2,6},{3,7},{4,0},{5,1},{6,2},{7,3},{8,12},{9,13},{10,... | collective-permute-start | bytes 1572872 | tf_op jit(solution)/shard_map/ppermute | solution.py:58
  115.9 2.8 %collective-permute-start.8 = (bf16[32,64,128]{2,1,0:T(8,128)(2,1)}, bf16[32,64,128]{2,1,0:T(8,128)(2,1)S(1)}, u32[]{:S(2)}, u32[]{:S(2)}) collective-permute-start(bf16[32,64,128]{2,1,0:T(8,128)(2,1)} %get-tuple-element.16), channel_id=1, source_target_pairs={{0,68},{1,69},{2,70},{3,71},{4,64},{5,65},{6,66},{7,67},{8,76},{9,... | collective-permute-start | bytes 1572872 | tf_op jit(solution)/shard_map/ppermute | solution.py:64
  118.7 6.1 %collective-permute-done.22 = bf16[32,64,128]{2,1,0:T(8,128)(2,1)} collective-permute-done((bf16[32,64,128]{2,1,0:T(8,128)(2,1)}, bf16[32,64,128]{2,1,0:T(8,128)(2,1)}, u32[]{:S(2)}, u32[]{:S(2)}) %collective-permute-start.22) | collective-permute-done | bytes 524320 | tf_op jit(solution)/shard_map/ppermute | solution.py:55
  127.7 3.9 %collective-permute-start.25 = (bf16[32,64,128]{2,1,0:T(8,128)(2,1)S(1)}, bf16[32,64,128]{2,1,0:T(8,128)(2,1)S(1)}, u32[]{:S(2)}, u32[]{:S(2)}) collective-permute-start(bf16[32,64,128]{2,1,0:T(8,128)(2,1)S(1)} %get-tuple-element.23), channel_id=1, source_target_pairs={{0,8},{8,0},{16,24},{24,16},{32,40},{40,32},{48,56},{56,48},{64,72... | collective-permute-start | bytes 1572872 | tf_op jit(solution)/shard_map/ppermute | solution.py:55
  133.9 13.3 %collective-permute-done.7 = bf16[32,64,128]{2,1,0:T(8,128)(2,1)S(1)} collective-permute-done((bf16[32,64,128]{2,1,0:T(8,128)(2,1)}, bf16[32,64,128]{2,1,0:T(8,128)(2,1)S(1)}, u32[]{:S(2)}, u32[]{:S(2)}) %collective-permute-start.7) | collective-permute-done | bytes 524320 | tf_op jit(solution)/shard_map/ppermute | solution.py:55
  149.0 3.9 %collective-permute-start.13 = (bf16[16,64,128]{2,1,0:T(8,128)(2,1)}, bf16[16,64,128]{2,1,0:T(8,128)(2,1)}, u32[]{:S(2)}, u32[]{:S(2)}) collective-permute-start(bf16[16,64,128]{2,1,0:T(8,128)(2,1)} %get-tuple-element.31), channel_id=1, source_target_pairs={{0,8},{8,0},{16,24},{24,16},{32,40},{40,32},{48,56},{56,48},{64,72... | collective-permute-start | bytes 786440 | tf_op jit(solution)/shard_map/ppermute | solution.py:55
  153.0 18.3 %collective-permute-done.14.x_ref = bf16[16,64,128]{2,1,0:T(8,128)(2,1)S(1)} collective-permute-done((bf16[16,64,128]{2,1,0:T(8,128)(2,1)S(1)}, bf16[16,64,128]{2,1,0:T(8,128)(2,1)S(1)}, u32[]{:S(2)}, u32[]{:S(2)}) %collective-permute-start.14) | collective-permute-done | bytes 262176 | tf_op jit(solution)/shard_map/ppermute | solution.py:58
  171.2 4.5 %collective-permute-start.12 = (bf16[16,64,128]{2,1,0:T(8,128)(2,1)}, bf16[16,64,128]{2,1,0:T(8,128)(2,1)}, u32[]{:S(2)}, u32[]{:S(2)}) collective-permute-start(bf16[16,64,128]{2,1,0:T(8,128)(2,1)} %get-tuple-element.32), channel_id=1, source_target_pairs={{0,9},{1,8},{2,11},{3,10},{4,13},{5,12},{6,15},{7,14},{8,1},{9,0},... | collective-permute-start | bytes 786440 | tf_op jit(solution)/shard_map/ppermute | solution.py:64
  (121 shorter events, 74.0 us)
Async XLA Ops:
  6.2 24.7 %collective-permute-start.15 = (bf16[32,64,128]{2,1,0:T(8,128)(2,1)}, bf16[32,64,128]{2,1,0:T(8,128)(2,1)}, u32[]{:S(2)}, u32[]{:S(2)}) collective-permute-start(bf16[32,64,128]{2,1,0:T(8,128)(2,1)} %shard_map.79), channel_id=1, source_target_pairs={{0,1},{1,0},{2,3},{3,2},{4,5},{5,4},{6,7},{7,6},{8,9},{9,8},{10,11... | collective-permute-start | bytes 1572872 | tf_op jit(solution)/shard_map/ppermute | solution.py:58
  17.8 27.1 %collective-permute-start.2 = (bf16[32,64,128]{2,1,0:T(8,128)(2,1)}, bf16[32,64,128]{2,1,0:T(8,128)(2,1)}, u32[]{:S(2)}, u32[]{:S(2)}) collective-permute-start(bf16[32,64,128]{2,1,0:T(8,128)(2,1)} %shard_map.76), channel_id=1, source_target_pairs={{0,9},{1,8},{2,11},{3,10},{4,13},{5,12},{6,15},{7,14},{8,1},{9,0},... | collective-permute-start | bytes 1572872 | tf_op jit(solution)/shard_map/ppermute | solution.py:64
  22.2 43.4 %collective-permute-start = (bf16[32,64,128]{2,1,0:T(8,128)(2,1)}, bf16[32,64,128]{2,1,0:T(8,128)(2,1)}, u32[]{:S(2)}, u32[]{:S(2)}) collective-permute-start(bf16[32,64,128]{2,1,0:T(8,128)(2,1)} %shard_map.74), channel_id=1, source_target_pairs={{0,1},{1,0},{2,3},{3,2},{4,5},{5,4},{6,7},{7,6},{8,9},{9,8},{10,11... | collective-permute-start | bytes 1572872 | tf_op jit(solution)/shard_map/ppermute | solution.py:58
  31.5 34.1 %collective-permute-start.1 = (bf16[32,64,128]{2,1,0:T(8,128)(2,1)S(1)}, bf16[32,64,128]{2,1,0:T(8,128)(2,1)S(1)}, u32[]{:S(2)}, u32[]{:S(2)}) collective-permute-start(bf16[32,64,128]{2,1,0:T(8,128)(2,1)S(1)} %copy-done.7), channel_id=1, source_target_pairs={{0,8},{8,0},{16,24},{24,16},{32,40},{40,32},{48,56},{56,48},{64,72... | collective-permute-start | bytes 1572872 | tf_op jit(solution)/shard_map/ppermute | solution.py:55
  36.9 40.1 %collective-permute-start.18 = (bf16[32,64,128]{2,1,0:T(8,128)(2,1)}, bf16[32,64,128]{2,1,0:T(8,128)(2,1)}, u32[]{:S(2)}, u32[]{:S(2)}) collective-permute-start(bf16[32,64,128]{2,1,0:T(8,128)(2,1)} %get-tuple-element.27), channel_id=1, source_target_pairs={{0,4},{1,5},{2,6},{3,7},{4,0},{5,1},{6,2},{7,3},{8,12},{9,13},{10,... | collective-permute-start | bytes 1572872 | tf_op jit(solution)/shard_map/ppermute | solution.py:58
  39.9 39.9 %collective-permute-start.19 = (bf16[32,64,128]{2,1,0:T(8,128)(2,1)}, bf16[32,64,128]{2,1,0:T(8,128)(2,1)}, u32[]{:S(2)}, u32[]{:S(2)}) collective-permute-start(bf16[32,64,128]{2,1,0:T(8,128)(2,1)} %get-tuple-element.26), channel_id=1, source_target_pairs={{0,64},{8,72},{16,80},{24,88},{32,96},{40,104},{48,112},{56,120},{... | collective-permute-start | bytes 1572872 | tf_op jit(solution)/shard_map/ppermute | solution.py:55
  44.8 35.0 %collective-permute-start.20 = (bf16[32,64,128]{2,1,0:T(8,128)(2,1)S(1)}, bf16[32,64,128]{2,1,0:T(8,128)(2,1)}, u32[]{:S(2)}, u32[]{:S(2)}) collective-permute-start(bf16[32,64,128]{2,1,0:T(8,128)(2,1)S(1)} %get-tuple-element.25), channel_id=1, source_target_pairs={{0,68},{1,69},{2,70},{3,71},{4,64},{5,65},{6,66},{7,67},{8,76},{9,... | collective-permute-start | bytes 1572872 | tf_op jit(solution)/shard_map/ppermute | solution.py:64
  68.8 24.0 %collective-permute-start.3 = (bf16[32,64,128]{2,1,0:T(8,128)(2,1)}, bf16[32,64,128]{2,1,0:T(8,128)(2,1)}, u32[]{:S(2)}, u32[]{:S(2)}) collective-permute-start(bf16[32,64,128]{2,1,0:T(8,128)(2,1)} %get-tuple-element.39), channel_id=1, source_target_pairs={{0,4},{1,5},{2,6},{3,7},{4,0},{5,1},{6,2},{7,3},{8,12},{9,13},{10,... | collective-permute-start | bytes 1572872 | tf_op jit(solution)/shard_map/ppermute | solution.py:58
  73.8 28.4 %collective-permute-start.4 = (bf16[32,64,128]{2,1,0:T(8,128)(2,1)}, bf16[32,64,128]{2,1,0:T(8,128)(2,1)S(1)}, u32[]{:S(2)}, u32[]{:S(2)}) collective-permute-start(bf16[32,64,128]{2,1,0:T(8,128)(2,1)} %get-tuple-element.38), channel_id=1, source_target_pairs={{0,64},{8,72},{16,80},{24,88},{32,96},{40,104},{48,112},{56,120},{... | collective-permute-start | bytes 1572872 | tf_op jit(solution)/shard_map/ppermute | solution.py:55
  77.0 25.2 %collective-permute-start.5 = (bf16[32,64,128]{2,1,0:T(8,128)(2,1)S(1)}, bf16[32,64,128]{2,1,0:T(8,128)(2,1)}, u32[]{:S(2)}, u32[]{:S(2)}) collective-permute-start(bf16[32,64,128]{2,1,0:T(8,128)(2,1)S(1)} %get-tuple-element.37), channel_id=1, source_target_pairs={{0,68},{1,69},{2,70},{3,71},{4,64},{5,65},{6,66},{7,67},{8,76},{9,... | collective-permute-start | bytes 1572872 | tf_op jit(solution)/shard_map/ppermute | solution.py:64
  89.8 26.1 %collective-permute-start.21 = (bf16[32,64,128]{2,1,0:T(8,128)(2,1)}, bf16[32,64,128]{2,1,0:T(8,128)(2,1)S(1)}, u32[]{:S(2)}, u32[]{:S(2)}) collective-permute-start(bf16[32,64,128]{2,1,0:T(8,128)(2,1)} %get-tuple-element.18), channel_id=1, source_target_pairs={{0,4},{1,5},{2,6},{3,7},{4,0},{5,1},{6,2},{7,3},{8,12},{9,13},{10,... | collective-permute-start | bytes 1572872 | tf_op jit(solution)/shard_map/ppermute | solution.py:58
  92.8 32.0 %collective-permute-start.22 = (bf16[32,64,128]{2,1,0:T(8,128)(2,1)}, bf16[32,64,128]{2,1,0:T(8,128)(2,1)}, u32[]{:S(2)}, u32[]{:S(2)}) collective-permute-start(bf16[32,64,128]{2,1,0:T(8,128)(2,1)} %get-tuple-element.19), channel_id=1, source_target_pairs={{0,64},{8,72},{16,80},{24,88},{32,96},{40,104},{48,112},{56,120},{... | collective-permute-start | bytes 1572872 | tf_op jit(solution)/shard_map/ppermute | solution.py:55
  92.8 32.0 %collective-permute-start.23 = (bf16[32,64,128]{2,1,0:T(8,128)(2,1)}, bf16[32,64,128]{2,1,0:T(8,128)(2,1)}, u32[]{:S(2)}, u32[]{:S(2)}) collective-permute-start(bf16[32,64,128]{2,1,0:T(8,128)(2,1)} %get-tuple-element.20), channel_id=1, source_target_pairs={{0,68},{1,69},{2,70},{3,71},{4,64},{5,65},{6,66},{7,67},{8,76},{9,... | collective-permute-start | bytes 1572872 | tf_op jit(solution)/shard_map/ppermute | solution.py:64
  115.9 31.3 %collective-permute-start.7 = (bf16[32,64,128]{2,1,0:T(8,128)(2,1)}, bf16[32,64,128]{2,1,0:T(8,128)(2,1)S(1)}, u32[]{:S(2)}, u32[]{:S(2)}) collective-permute-start(bf16[32,64,128]{2,1,0:T(8,128)(2,1)} %get-tuple-element.15), channel_id=1, source_target_pairs={{0,64},{8,72},{16,80},{24,88},{32,96},{40,104},{48,112},{56,120},{... | collective-permute-start | bytes 1572872 | tf_op jit(solution)/shard_map/ppermute | solution.py:55
  115.9 31.2 %collective-permute-start.8 = (bf16[32,64,128]{2,1,0:T(8,128)(2,1)}, bf16[32,64,128]{2,1,0:T(8,128)(2,1)S(1)}, u32[]{:S(2)}, u32[]{:S(2)}) collective-permute-start(bf16[32,64,128]{2,1,0:T(8,128)(2,1)} %get-tuple-element.16), channel_id=1, source_target_pairs={{0,68},{1,69},{2,70},{3,71},{4,64},{5,65},{6,66},{7,67},{8,76},{9,... | collective-permute-start | bytes 1572872 | tf_op jit(solution)/shard_map/ppermute | solution.py:64
  127.7 48.0 %collective-permute-start.26 = (bf16[32,64,128]{2,1,0:T(8,128)(2,1)S(1)}, bf16[32,64,128]{2,1,0:T(8,128)(2,1)S(1)}, u32[]{:S(2)}, u32[]{:S(2)}) collective-permute-start(bf16[32,64,128]{2,1,0:T(8,128)(2,1)S(1)} %get-tuple-element.22), channel_id=1, source_target_pairs={{0,1},{1,0},{2,3},{3,2},{4,5},{5,4},{6,7},{7,6},{8,9},{9,8},{10,11... | collective-permute-start | bytes 1572872 | tf_op jit(solution)/shard_map/ppermute | solution.py:58
  127.7 48.7 %collective-permute-start.25 = (bf16[32,64,128]{2,1,0:T(8,128)(2,1)S(1)}, bf16[32,64,128]{2,1,0:T(8,128)(2,1)S(1)}, u32[]{:S(2)}, u32[]{:S(2)}) collective-permute-start(bf16[32,64,128]{2,1,0:T(8,128)(2,1)S(1)} %get-tuple-element.23), channel_id=1, source_target_pairs={{0,8},{8,0},{16,24},{24,16},{32,40},{40,32},{48,56},{56,48},{64,72... | collective-permute-start | bytes 1572872 | tf_op jit(solution)/shard_map/ppermute | solution.py:55
  131.7 44.8 %collective-permute-start.24 = (bf16[32,64,128]{2,1,0:T(8,128)(2,1)S(1)}, bf16[32,64,128]{2,1,0:T(8,128)(2,1)S(1)}, u32[]{:S(2)}, u32[]{:S(2)}) collective-permute-start(bf16[32,64,128]{2,1,0:T(8,128)(2,1)S(1)} %get-tuple-element.24), channel_id=1, source_target_pairs={{0,9},{1,8},{2,11},{3,10},{4,13},{5,12},{6,15},{7,14},{8,1},{9,0},... | collective-permute-start | bytes 1572872 | tf_op jit(solution)/shard_map/ppermute | solution.py:64
  149.0 22.2 %collective-permute-start.14 = (bf16[16,64,128]{2,1,0:T(8,128)(2,1)S(1)}, bf16[16,64,128]{2,1,0:T(8,128)(2,1)S(1)}, u32[]{:S(2)}, u32[]{:S(2)}) collective-permute-start(bf16[16,64,128]{2,1,0:T(8,128)(2,1)S(1)} %get-tuple-element.30), channel_id=1, source_target_pairs={{0,1},{1,0},{2,3},{3,2},{4,5},{5,4},{6,7},{7,6},{8,9},{9,8},{10,11... | collective-permute-start | bytes 786440 | tf_op jit(solution)/shard_map/ppermute | solution.py:58
  149.0 45.9 %collective-permute-start.13 = (bf16[16,64,128]{2,1,0:T(8,128)(2,1)}, bf16[16,64,128]{2,1,0:T(8,128)(2,1)}, u32[]{:S(2)}, u32[]{:S(2)}) collective-permute-start(bf16[16,64,128]{2,1,0:T(8,128)(2,1)} %get-tuple-element.31), channel_id=1, source_target_pairs={{0,8},{8,0},{16,24},{24,16},{32,40},{40,32},{48,56},{56,48},{64,72... | collective-permute-start | bytes 786440 | tf_op jit(solution)/shard_map/ppermute | solution.py:55
  171.2 26.1 %collective-permute-start.12 = (bf16[16,64,128]{2,1,0:T(8,128)(2,1)}, bf16[16,64,128]{2,1,0:T(8,128)(2,1)}, u32[]{:S(2)}, u32[]{:S(2)}) collective-permute-start(bf16[16,64,128]{2,1,0:T(8,128)(2,1)} %get-tuple-element.32), channel_id=1, source_target_pairs={{0,9},{1,8},{2,11},{3,10},{4,13},{5,12},{6,15},{7,14},{8,1},{9,0},... | collective-permute-start | bytes 786440 | tf_op jit(solution)/shard_map/ppermute | solution.py:64
  175.7 26.4 %collective-permute-start.11 = (bf16[16,64,128]{2,1,0:T(8,128)(2,1)}, bf16[16,64,128]{2,1,0:T(8,128)(2,1)}, u32[]{:S(2)}, u32[]{:S(2)}) collective-permute-start(bf16[16,64,128]{2,1,0:T(8,128)(2,1)} %get-tuple-element.34), channel_id=1, source_target_pairs={{0,1},{1,0},{2,3},{3,2},{4,5},{5,4},{6,7},{7,6},{8,9},{9,8},{10,11... | collective-permute-start | bytes 786440 | tf_op jit(solution)/shard_map/ppermute | solution.py:58
  176.5 28.1 %collective-permute-start.10 = (bf16[16,64,128]{2,1,0:T(8,128)(2,1)S(1)}, bf16[16,64,128]{2,1,0:T(8,128)(2,1)}, u32[]{:S(2)}, u32[]{:S(2)}) collective-permute-start(bf16[16,64,128]{2,1,0:T(8,128)(2,1)S(1)} %get-tuple-element.35), channel_id=1, source_target_pairs={{0,8},{8,0},{16,24},{24,16},{32,40},{40,32},{48,56},{56,48},{64,72... | collective-permute-start | bytes 786440 | tf_op jit(solution)/shard_map/ppermute | solution.py:55
  176.5 30.5 %collective-permute-start.9 = (bf16[16,64,128]{2,1,0:T(8,128)(2,1)S(1)}, bf16[16,64,128]{2,1,0:T(8,128)(2,1)}, u32[]{:S(2)}, u32[]{:S(2)}) collective-permute-start(bf16[16,64,128]{2,1,0:T(8,128)(2,1)S(1)} %get-tuple-element.36), channel_id=1, source_target_pairs={{0,9},{1,8},{2,11},{3,10},{4,13},{5,12},{6,15},{7,14},{8,1},{9,0},... | collective-permute-start | bytes 786440 | tf_op jit(solution)/shard_map/ppermute | solution.py:64
  (18 other events, 182.2 us)

commit v16 on v7

--- a/solution.py
+++ b/solution.py
@@ -112,6 +112,38 @@
             terms[f][j] = out[f * size:(f + 1) * size, j * lanes:(j + 1) * lanes]
 
 
+def mix4_kernel(p0, p1, p2, p3, w_ref, t0, t1, t2, t3):
+    size = p0.shape[1]
+    lanes = p0.shape[2]
+    step = p0.shape[0]
+    pieces = (p0, p1, p2, p3)
+    terms = (t0, t1, t2, t3)
+    stacked = jnp.concatenate(
+        [jnp.concatenate([p[j] for p in pieces], axis=0) for j in range(step)], axis=1
+    )
+    out = jnp.dot(w_ref[...], stacked, preferred_element_type=jnp.float32).astype(jnp.bfloat16)
+    for f in range(4):
+        for j in range(step):
+            terms[f][j] = out[f * size:(f + 1) * size, j * lanes:(j + 1) * lanes]
+
+
+def mix4(pieces, w_mat, step=8):
+    part, rank_size, inner_boxes = pieces[0].shape
+    piece_spec = pl.BlockSpec((step, rank_size, inner_boxes), lambda i: (i, 0, 0))
+    return pl.pallas_call(
+        mix4_kernel,
+        grid=(part // step,),
+        in_specs=[piece_spec] * 4 + [pl.BlockSpec(w_mat.shape, lambda i: (0, 0))],
+        out_specs=[piece_spec] * 4,
+        out_shape=[jax.ShapeDtypeStruct(pieces[0].shape, jnp.bfloat16)] * 4,
+        cost_estimate=pl.CostEstimate(
+            flops=2 * part * inner_boxes * w_mat.shape[0] * w_mat.shape[1],
+            bytes_accessed=8 * part * rank_size * inner_boxes * 2,
+            transcendentals=0,
+        ),
+    )(*pieces, w_mat)
+
+
 def chain_stage(cur, matrix, sets):
     size = cur[0].shape[0]
     lanes = cur[0].shape[1]
@@ -204,6 +236,8 @@
     w1 = xor_order(merges[1], 1, *bits[1])
     w1_mat = jnp.transpose(w1, (0, 2, 1, 3)).reshape(4 * rank_size, 4 * rank_size)
     w1_t = w1_mat.T
+    w0_mat = jnp.transpose(w0, (0, 2, 1, 3)).reshape(4 * rank_size, 4 * rank_size)
+    w0_t = w0_mat.T
     ow_mat = jnp.einsum("st,or->sotr", jnp.eye(4, dtype=output_weight.dtype), output_weight).reshape(4 * rank_size, 4 * rank_size)
     ow_t = ow_mat.T
 
@@ -256,11 +290,11 @@
     for m in range(CHUNKS):
         coef = [local_forward(m, f) for f in range(4)]
         pieces = exchange(coef, *shifts[0])
-        cur = mixing(w0, jnp.stack(pieces), "scor,cjrl->sjol")
+        cur = mix4(pieces, w0_mat)
         pieces = exchange(cur, *shifts[1])
         terms = output_stage(pieces, wave, obs, m, w1_mat, w1_t, ow_mat, ow_t)
         back = exchange(terms, *shifts[1])
-        terms = mixing(w0, jnp.stack(back), "scor,sjol->cjrl")
+        terms = mix4(back, w0_t)
         back = exchange(terms, *shifts[0])
         for f in range(4):
             gradient = local_adjoint(gradient, back[f], m, f)

time: 195 us -> 199 us (1.021)
  Pallas kernels: 62.7 us -> 80.5 us
  starting transfers between devices: 53.6 us -> 39.1 us
  waiting for transfers between devices: 53.7 us -> 61.4 us
  matrix products: 6.8 us -> 0 us
    pallas_call x0 -> x4, Pallas kernels: none -> 17.8 us  [mix4(): pl.pallas_call(mix4_kernel, grid=(part // step,), in_specs=[piece_spec] *...]
    ppermute x8, waiting for transfers between devices: 9.12 us -> 21.3 us  [flip_send(): return lax.ppermute(value, ('qx', 'qy'), pairs)]
    ppermute x8, starting transfers between devices: 23 us -> 10.9 us  [flip_send(): return lax.ppermute(value, ('qx', 'qy'), pairs)]
    dot_general x4 -> x0, matrix products: 6.8 us -> none  [mixing(): jnp.einsum(form, weight, data, preferred_element_type=jnp.float32)]
    ppermute x8, waiting for transfers between devices: 15.8 us -> 10.8 us  [flip_send(): return lax.ppermute(value, 'qy', pairs)]
    squeeze x4 -> x0, local copies, waits for them, and re-layouts: 4.97 us -> none  [the longest x2 2.59 us: exchange(): relative[0]]
    unnamed x32 -> x34, local copies, waits for them, and re-layouts: 4.06 us -> 6.5 us
    ppermute x8, starting transfers between devices: 16.3 us -> 14.1 us  [flip_send(): return lax.ppermute(value, 'qx', pairs)]
  transfers between devices with their start and end apart: 24 -> 24, of which waited for: 9 -> 8; matrix products, arithmetic and copies ran while one was open for 8% -> 3% of each run, Pallas kernels for 30% -> 38%
where the time goes in v16:
time: 199 us; the launch traced here: 198 us
  Pallas kernels  80.5 us (40%)
  waiting for transfers between devices  61.4 us (31%)
  starting transfers between devices  39.1 us (20%)
  local copies, waits for them, and re-layouts  14.1 us (7%)
  other arithmetic  2.25 us (1%)
    pallas_call x16, Pallas kernels, chain_call(): pl.pallas_call(functools.partial(chain_kernel, plan), grid_spec=pltpu.Pre...  42.8 us
    ppermute x8, waiting for transfers between devices, flip_send(): return lax.ppermute(value, 'qx', pairs)  29.3 us
    ppermute x8, waiting for transfers between devices, flip_send(): return lax.ppermute(value, ('qx', 'qy'), pairs)  21.3 us
    pallas_call x2, Pallas kernels, output_stage(): pl.pallas_call(output_stage_kernel, grid=(part // step,), in_specs=[piece...  19.8 us
    pallas_call x4, Pallas kernels, mix4(): pl.pallas_call(mix4_kernel, grid=(part // step,), in_specs=[piece_spec] *...  17.8 us
    ppermute x8, starting transfers between devices, flip_send(): return lax.ppermute(value, 'qx', pairs)  14.1 us
    ppermute x8, starting transfers between devices, flip_send(): return lax.ppermute(value, 'qy', pairs)  14.1 us
    ppermute x8, starting transfers between devices, flip_send(): return lax.ppermute(value, ('qx', 'qy'), pairs)  10.9 us
  transfers between devices with their start and end apart: 24, of which 8 were waited for; matrix products, arithmetic and copies ran while one was open for 3% of the time, Pallas kernels for 38%

profile of v16, /device:TPU:1, one launch (start us, length us, event | category | flops | bytes accessed | tf_op | source)
XLA Modules:
  0.0 197.7 jit_solution(11971312891252008626)
XLA Ops:
  5.0 2.7 %shard_map.81 = bf16[32,64,128]{2,1,0:T(8,128)(2,1)} custom-call(s32[1]{0:T(128)} %bitcast.k_ref, bf16[4,2,32,64,128]{4,3,2,1,0:T(8,128)(2,1)} %bitcast.63, bf16[3,256,256]{2,1,0:T(8,128)(2,1)} %pad_maximum_fusion.m_ref), custom_call_target="tpu_custom_call" | custom-call | tf_op jit(solution)/shard_map/pallas_call | solution.py:186
  20.5 2.7 %shard_map.75 = bf16[32,64,128]{2,1,0:T(8,128)(2,1)} custom-call(s32[1]{0:T(128)} %bitcast.k_ref, bf16[4,2,32,64,128]{4,3,2,1,0:T(8,128)(2,1)} %bitcast.67, bf16[3,256,256]{2,1,0:T(8,128)(2,1)} %pad_maximum_fusion.m_ref), custom_call_target="tpu_custom_call" | custom-call | tf_op jit(solution)/shard_map/pallas_call | solution.py:186
  25.2 2.7 %shard_map.76 = bf16[32,64,128]{2,1,0:T(8,128)(2,1)} custom-call(s32[1]{0:T(128)} %bitcast.k_ref, bf16[4,2,32,64,128]{4,3,2,1,0:T(8,128)(2,1)} %bitcast.68, bf16[3,256,256]{2,1,0:T(8,128)(2,1)} %pad_maximum_fusion.m_ref), custom_call_target="tpu_custom_call" | custom-call | tf_op jit(solution)/shard_map/pallas_call | solution.py:186
  28.9 2.7 %shard_map.80.p0 = bf16[32,64,128]{2,1,0:T(8,128)(2,1)} custom-call(s32[1]{0:T(128)} %bitcast.k_ref, bf16[4,2,32,64,128]{4,3,2,1,0:T(8,128)(2,1)} %bitcast.69, bf16[3,256,256]{2,1,0:T(8,128)(2,1)} %pad_maximum_fusion.m_ref), custom_call_target="tpu_custom_call" | custom-call | tf_op jit(solution)/shard_map/pallas_call | solution.py:186
  34.7 4.5 %shard_map.84 = (bf16[32,64,128]{2,1,0:T(8,128)(2,1)}, bf16[32,64,128]{2,1,0:T(8,128)(2,1)}, bf16[32,64,128]{2,1,0:T(8,128)(2,1)}, bf16[32,64,128]{2,1,0:T(8,128)(2,1)}) custom-call(bf16[32,64,128]{2,1,0:T(8,128)(2,1)} %shard_map.80.p0, bf16[32,64,128]{2,1,0:T(8,128)(2,1)} %copy-done.5, bf16[32,64,128]{2,1,0:T(8,128)(2,1)} %collective-permute-done.13.p2, ...), custom_call_target="tpu_custom_call" | custom-call | flops 536870912 | bytes 4194304 | tf_op jit(solution)/shard_map/pallas_call | solution.py:133
  39.2 3.0 %collective-permute-start.15 = (bf16[32,64,128]{2,1,0:T(8,128)(2,1)}, bf16[32,64,128]{2,1,0:T(8,128)(2,1)S(1)}, u32[]{:S(2)}, u32[]{:S(2)}) collective-permute-start(bf16[32,64,128]{2,1,0:T(8,128)(2,1)} %get-tuple-element.42), channel_id=1, source_target_pairs={{0,4},{1,5},{2,6},{3,7},{4,0},{5,1},{6,2},{7,3},{8,12},{9,13},{10,... | collective-permute-start | bytes 1572872 | tf_op jit(solution)/shard_map/ppermute | solution.py:58
  42.2 3.7 %collective-permute-start.16 = (bf16[32,64,128]{2,1,0:T(8,128)(2,1)}, bf16[32,64,128]{2,1,0:T(8,128)(2,1)}, u32[]{:S(2)}, u32[]{:S(2)}) collective-permute-start(bf16[32,64,128]{2,1,0:T(8,128)(2,1)} %get-tuple-element.43), channel_id=1, source_target_pairs={{0,64},{8,72},{16,80},{24,88},{32,96},{40,104},{48,112},{56,120},{... | collective-permute-start | bytes 1572872 | tf_op jit(solution)/shard_map/ppermute | solution.py:55
  45.9 4.3 %collective-permute-start.17 = (bf16[32,64,128]{2,1,0:T(8,128)(2,1)}, bf16[32,64,128]{2,1,0:T(8,128)(2,1)}, u32[]{:S(2)}, u32[]{:S(2)}) collective-permute-start(bf16[32,64,128]{2,1,0:T(8,128)(2,1)} %get-tuple-element.44), channel_id=1, source_target_pairs={{0,68},{1,69},{2,70},{3,71},{4,64},{5,65},{6,66},{7,67},{8,76},{9,... | collective-permute-start | bytes 1572872 | tf_op jit(solution)/shard_map/ppermute | solution.py:64
  52.9 15.8 %collective-permute-done.2.p3 = bf16[32,64,128]{2,1,0:T(8,128)(2,1)} collective-permute-done((bf16[32,64,128]{2,1,0:T(8,128)(2,1)}, bf16[32,64,128]{2,1,0:T(8,128)(2,1)}, u32[]{:S(2)}, u32[]{:S(2)}) %collective-permute-start.2) | collective-permute-done | bytes 524320 | tf_op jit(solution)/shard_map/ppermute | solution.py:64
  68.7 4.5 %shard_map.77 = (bf16[32,64,128]{2,1,0:T(8,128)(2,1)}, bf16[32,64,128]{2,1,0:T(8,128)(2,1)}, bf16[32,64,128]{2,1,0:T(8,128)(2,1)}, bf16[32,64,128]{2,1,0:T(8,128)(2,1)}) custom-call(bf16[32,64,128]{2,1,0:T(8,128)(2,1)} %shard_map.73.p0, bf16[32,64,128]{2,1,0:T(8,128)(2,1)} %copy-done.3, bf16[32,64,128]{2,1,0:T(8,128)(2,1)} %copy-done.4, ...), custom_call_target="tpu_custom_call" | custom-call | flops 536870912 | bytes 4194304 | tf_op jit(solution)/shard_map/pallas_call | solution.py:133
  73.2 3.1 %collective-permute-start.3 = (bf16[32,64,128]{2,1,0:T(8,128)(2,1)}, bf16[32,64,128]{2,1,0:T(8,128)(2,1)S(1)}, u32[]{:S(2)}, u32[]{:S(2)}) collective-permute-start(bf16[32,64,128]{2,1,0:T(8,128)(2,1)} %get-tuple-element.30), channel_id=1, source_target_pairs={{0,4},{1,5},{2,6},{3,7},{4,0},{5,1},{6,2},{7,3},{8,12},{9,13},{10,... | collective-permute-start | bytes 1572872 | tf_op jit(solution)/shard_map/ppermute | solution.py:58
  78.5 3.6 %collective-permute-start.4 = (bf16[32,64,128]{2,1,0:T(8,128)(2,1)}, bf16[32,64,128]{2,1,0:T(8,128)(2,1)}, u32[]{:S(2)}, u32[]{:S(2)}) collective-permute-start(bf16[32,64,128]{2,1,0:T(8,128)(2,1)} %get-tuple-element.31), channel_id=1, source_target_pairs={{0,64},{8,72},{16,80},{24,88},{32,96},{40,104},{48,112},{56,120},{... | collective-permute-start | bytes 1572872 | tf_op jit(solution)/shard_map/ppermute | solution.py:55
  82.9 9.9 %shard_map.85 = (bf16[32,64,128]{2,1,0:T(8,128)(2,1)}, bf16[32,64,128]{2,1,0:T(8,128)(2,1)}, bf16[32,64,128]{2,1,0:T(8,128)(2,1)}, bf16[32,64,128]{2,1,0:T(8,128)(2,1)}) custom-call(bf16[32,64,128]{2,1,0:T(8,128)(2,1)} %get-tuple-element.41.p0, bf16[32,64,128]{2,1,0:T(8,128)(2,1)} %copy-done.14, bf16[32,64,128]{2,1,0:T(8,128)(2,1)} %collective-permute-done.16.p2, ...), custom_call_target="tpu_custom_call" | custom-call | flops 2147483648 | bytes 10485760 | tf_op jit(solution)/shard_map/pallas_call | solution.py:205
  95.2 2.7 %collective-permute-start.19 = (bf16[32,64,128]{2,1,0:T(8,128)(2,1)}, bf16[32,64,128]{2,1,0:T(8,128)(2,1)S(1)}, u32[]{:S(2)}, u32[]{:S(2)}) collective-permute-start(bf16[32,64,128]{2,1,0:T(8,128)(2,1)} %get-tuple-element.47), channel_id=1, source_target_pairs={{0,64},{8,72},{16,80},{24,88},{32,96},{40,104},{48,112},{56,120},{... | collective-permute-start | bytes 1572872 | tf_op jit(solution)/shard_map/ppermute | solution.py:55
  98.6 7.5 %collective-permute-done.4.p2 = bf16[32,64,128]{2,1,0:T(8,128)(2,1)} collective-permute-done((bf16[32,64,128]{2,1,0:T(8,128)(2,1)}, bf16[32,64,128]{2,1,0:T(8,128)(2,1)}, u32[]{:S(2)}, u32[]{:S(2)}) %collective-permute-start.4) | collective-permute-done | bytes 524320 | tf_op jit(solution)/shard_map/ppermute | solution.py:55
  106.2 9.9 %shard_map.78 = (bf16[32,64,128]{2,1,0:T(8,128)(2,1)}, bf16[32,64,128]{2,1,0:T(8,128)(2,1)}, bf16[32,64,128]{2,1,0:T(8,128)(2,1)}, bf16[32,64,128]{2,1,0:T(8,128)(2,1)}) custom-call(bf16[32,64,128]{2,1,0:T(8,128)(2,1)} %get-tuple-element.29.p0, bf16[32,64,128]{2,1,0:T(8,128)(2,1)} %copy-done.15, bf16[32,64,128]{2,1,0:T(8,128)(2,1)} %collective-permute-done.4.p2, ...), custom_call_target="tpu_custom_call" | custom-call | flops 2147483648 | bytes 10485760 | tf_op jit(solution)/shard_map/pallas_call | solution.py:205
  119.0 2.9 %collective-permute-start.8 = (bf16[32,64,128]{2,1,0:T(8,128)(2,1)}, bf16[32,64,128]{2,1,0:T(8,128)(2,1)}, u32[]{:S(2)}, u32[]{:S(2)}) collective-permute-start(bf16[32,64,128]{2,1,0:T(8,128)(2,1)} %get-tuple-element.36), channel_id=1, source_target_pairs={{0,68},{1,69},{2,70},{3,71},{4,64},{5,65},{6,66},{7,67},{8,76},{9,... | collective-permute-start | bytes 1572872 | tf_op jit(solution)/shard_map/ppermute | solution.py:64
  121.8 6.7 %collective-permute-done.19.p2 = bf16[32,64,128]{2,1,0:T(8,128)(2,1)S(1)} collective-permute-done((bf16[32,64,128]{2,1,0:T(8,128)(2,1)}, bf16[32,64,128]{2,1,0:T(8,128)(2,1)S(1)}, u32[]{:S(2)}, u32[]{:S(2)}) %collective-permute-start.19) | collective-permute-done | bytes 524320 | tf_op jit(solution)/shard_map/ppermute | solution.py:55
  129.5 4.4 %shard_map.86 = (bf16[32,64,128]{2,1,0:T(8,128)(2,1)}, bf16[32,64,128]{2,1,0:T(8,128)(2,1)}, bf16[32,64,128]{2,1,0:T(8,128)(2,1)}, bf16[32,64,128]{2,1,0:T(8,128)(2,1)}) custom-call(bf16[32,64,128]{2,1,0:T(8,128)(2,1)} %get-tuple-element.45.p0, bf16[32,64,128]{2,1,0:T(8,128)(2,1)} %copy-done.8, bf16[32,64,128]{2,1,0:T(8,128)(2,1)} %copy-done.10, ...), custom_call_target="tpu_custom_call" | custom-call | flops 536870912 | bytes 4194304 | tf_op jit(solution)/shard_map/pallas_call | solution.py:133
  136.1 15.0 %collective-permute-done.7.p2 = bf16[32,64,128]{2,1,0:T(8,128)(2,1)} collective-permute-done((bf16[32,64,128]{2,1,0:T(8,128)(2,1)}, bf16[32,64,128]{2,1,0:T(8,128)(2,1)}, u32[]{:S(2)}, u32[]{:S(2)}) %collective-permute-start.7) | collective-permute-done | bytes 524320 | tf_op jit(solution)/shard_map/ppermute | solution.py:55
  151.1 4.5 %shard_map.79 = (bf16[32,64,128]{2,1,0:T(8,128)(2,1)}, bf16[32,64,128]{2,1,0:T(8,128)(2,1)}, bf16[32,64,128]{2,1,0:T(8,128)(2,1)}, bf16[32,64,128]{2,1,0:T(8,128)(2,1)}) custom-call(bf16[32,64,128]{2,1,0:T(8,128)(2,1)} %get-tuple-element.33.p0, bf16[32,64,128]{2,1,0:T(8,128)(2,1)} %copy-done.11, bf16[32,64,128]{2,1,0:T(8,128)(2,1)} %collective-permute-done.7.p2, ...), custom_call_target="tpu_custom_call" | custom-call | flops 536870912 | bytes 4194304 | tf_op jit(solution)/shard_map/pallas_call | solution.py:133
  156.1 6.6 %collective-permute-done.23.x_ref = bf16[32,64,128]{2,1,0:T(8,128)(2,1)S(1)} collective-permute-done((bf16[32,64,128]{2,1,0:T(8,128)(2,1)}, bf16[32,64,128]{2,1,0:T(8,128)(2,1)S(1)}, u32[]{:S(2)}, u32[]{:S(2)}) %collective-permute-start.23) | collective-permute-done | bytes 524320 | tf_op jit(solution)/shard_map/ppermute | solution.py:58
  181.0 4.2 %collective-permute-done.11.x_ref = bf16[32,64,128]{2,1,0:T(8,128)(2,1)} collective-permute-done((bf16[32,64,128]{2,1,0:T(8,128)(2,1)}, bf16[32,64,128]{2,1,0:T(8,128)(2,1)}, u32[]{:S(2)}, u32[]{:S(2)}) %collective-permute-start.11) | collective-permute-done | bytes 524320 | tf_op jit(solution)/shard_map/ppermute | solution.py:58
  191.4 3.6 %collective-permute-done.9.x_ref = bf16[32,64,128]{2,1,0:T(8,128)(2,1)} collective-permute-done((bf16[32,64,128]{2,1,0:T(8,128)(2,1)}, bf16[32,64,128]{2,1,0:T(8,128)(2,1)}, u32[]{:S(2)}, u32[]{:S(2)}) %collective-permute-start.9) | collective-permute-done | bytes 524320 | tf_op jit(solution)/shard_map/ppermute | solution.py:64
  (111 shorter events, 66.1 us)
Async XLA Ops:
  7.7 20.3 %collective-permute-start.12 = (bf16[32,64,128]{2,1,0:T(8,128)(2,1)}, bf16[32,64,128]{2,1,0:T(8,128)(2,1)S(1)}, u32[]{:S(2)}, u32[]{:S(2)}) collective-permute-start(bf16[32,64,128]{2,1,0:T(8,128)(2,1)} %shard_map.81), channel_id=1, source_target_pairs={{0,1},{1,0},{2,3},{3,2},{4,5},{5,4},{6,7},{7,6},{8,9},{9,8},{10,11... | collective-permute-start | bytes 1572872 | tf_op jit(solution)/shard_map/ppermute | solution.py:58
  12.8 20.0 %collective-permute-start.13 = (bf16[32,64,128]{2,1,0:T(8,128)(2,1)}, bf16[32,64,128]{2,1,0:T(8,128)(2,1)}, u32[]{:S(2)}, u32[]{:S(2)}) collective-permute-start(bf16[32,64,128]{2,1,0:T(8,128)(2,1)} %shard_map.82), channel_id=1, source_target_pairs={{0,8},{8,0},{16,24},{24,16},{32,40},{40,32},{48,56},{56,48},{64,72... | collective-permute-start | bytes 1572872 | tf_op jit(solution)/shard_map/ppermute | solution.py:55
  16.4 18.3 %collective-permute-start.14 = (bf16[32,64,128]{2,1,0:T(8,128)(2,1)}, bf16[32,64,128]{2,1,0:T(8,128)(2,1)}, u32[]{:S(2)}, u32[]{:S(2)}) collective-permute-start(bf16[32,64,128]{2,1,0:T(8,128)(2,1)} %shard_map.83), channel_id=1, source_target_pairs={{0,9},{1,8},{2,11},{3,10},{4,13},{5,12},{6,15},{7,14},{8,1},{9,0},... | collective-permute-start | bytes 1572872 | tf_op jit(solution)/shard_map/ppermute | solution.py:64
  19.1 26.7 %collective-permute-start = (bf16[32,64,128]{2,1,0:T(8,128)(2,1)}, bf16[32,64,128]{2,1,0:T(8,128)(2,1)S(1)}, u32[]{:S(2)}, u32[]{:S(2)}) collective-permute-start(bf16[32,64,128]{2,1,0:T(8,128)(2,1)} %shard_map.74), channel_id=1, source_target_pairs={{0,1},{1,0},{2,3},{3,2},{4,5},{5,4},{6,7},{7,6},{8,9},{9,8},{10,11... | collective-permute-start | bytes 1572872 | tf_op jit(solution)/shard_map/ppermute | solution.py:58
  23.2 29.7 %collective-permute-start.1 = (bf16[32,64,128]{2,1,0:T(8,128)(2,1)}, bf16[32,64,128]{2,1,0:T(8,128)(2,1)S(1)}, u32[]{:S(2)}, u32[]{:S(2)}) collective-permute-start(bf16[32,64,128]{2,1,0:T(8,128)(2,1)} %shard_map.75), channel_id=1, source_target_pairs={{0,8},{8,0},{16,24},{24,16},{32,40},{40,32},{48,56},{56,48},{64,72... | collective-permute-start | bytes 1572872 | tf_op jit(solution)/shard_map/ppermute | solution.py:55
  27.9 40.8 %collective-permute-start.2 = (bf16[32,64,128]{2,1,0:T(8,128)(2,1)}, bf16[32,64,128]{2,1,0:T(8,128)(2,1)}, u32[]{:S(2)}, u32[]{:S(2)}) collective-permute-start(bf16[32,64,128]{2,1,0:T(8,128)(2,1)} %shard_map.76), channel_id=1, source_target_pairs={{0,9},{1,8},{2,11},{3,10},{4,13},{5,12},{6,15},{7,14},{8,1},{9,0},... | collective-permute-start | bytes 1572872 | tf_op jit(solution)/shard_map/ppermute | solution.py:64
  39.2 43.0 %collective-permute-start.15 = (bf16[32,64,128]{2,1,0:T(8,128)(2,1)}, bf16[32,64,128]{2,1,0:T(8,128)(2,1)S(1)}, u32[]{:S(2)}, u32[]{:S(2)}) collective-permute-start(bf16[32,64,128]{2,1,0:T(8,128)(2,1)} %get-tuple-element.42), channel_id=1, source_target_pairs={{0,4},{1,5},{2,6},{3,7},{4,0},{5,1},{6,2},{7,3},{8,12},{9,13},{10,... | collective-permute-start | bytes 1572872 | tf_op jit(solution)/shard_map/ppermute | solution.py:58
  42.2 40.0 %collective-permute-start.16 = (bf16[32,64,128]{2,1,0:T(8,128)(2,1)}, bf16[32,64,128]{2,1,0:T(8,128)(2,1)}, u32[]{:S(2)}, u32[]{:S(2)}) collective-permute-start(bf16[32,64,128]{2,1,0:T(8,128)(2,1)} %get-tuple-element.43), channel_id=1, source_target_pairs={{0,64},{8,72},{16,80},{24,88},{32,96},{40,104},{48,112},{56,120},{... | collective-permute-start | bytes 1572872 | tf_op jit(solution)/shard_map/ppermute | solution.py:55
  45.9 36.3 %collective-permute-start.17 = (bf16[32,64,128]{2,1,0:T(8,128)(2,1)}, bf16[32,64,128]{2,1,0:T(8,128)(2,1)}, u32[]{:S(2)}, u32[]{:S(2)}) collective-permute-start(bf16[32,64,128]{2,1,0:T(8,128)(2,1)} %get-tuple-element.44), channel_id=1, source_target_pairs={{0,68},{1,69},{2,70},{3,71},{4,64},{5,65},{6,66},{7,67},{8,76},{9,... | collective-permute-start | bytes 1572872 | tf_op jit(solution)/shard_map/ppermute | solution.py:64
  73.2 24.7 %collective-permute-start.3 = (bf16[32,64,128]{2,1,0:T(8,128)(2,1)}, bf16[32,64,128]{2,1,0:T(8,128)(2,1)S(1)}, u32[]{:S(2)}, u32[]{:S(2)}) collective-permute-start(bf16[32,64,128]{2,1,0:T(8,128)(2,1)} %get-tuple-element.30), channel_id=1, source_target_pairs={{0,4},{1,5},{2,6},{3,7},{4,0},{5,1},{6,2},{7,3},{8,12},{9,13},{10,... | collective-permute-start | bytes 1572872 | tf_op jit(solution)/shard_map/ppermute | solution.py:58
  78.5 27.7 %collective-permute-start.4 = (bf16[32,64,128]{2,1,0:T(8,128)(2,1)}, bf16[32,64,128]{2,1,0:T(8,128)(2,1)}, u32[]{:S(2)}, u32[]{:S(2)}) collective-permute-start(bf16[32,64,128]{2,1,0:T(8,128)(2,1)} %get-tuple-element.31), channel_id=1, source_target_pairs={{0,64},{8,72},{16,80},{24,88},{32,96},{40,104},{48,112},{56,120},{... | collective-permute-start | bytes 1572872 | tf_op jit(solution)/shard_map/ppermute | solution.py:55
  82.2 24.0 %collective-permute-start.5 = (bf16[32,64,128]{2,1,0:T(8,128)(2,1)}, bf16[32,64,128]{2,1,0:T(8,128)(2,1)}, u32[]{:S(2)}, u32[]{:S(2)}) collective-permute-start(bf16[32,64,128]{2,1,0:T(8,128)(2,1)} %get-tuple-element.32), channel_id=1, source_target_pairs={{0,68},{1,69},{2,70},{3,71},{4,64},{5,65},{6,66},{7,67},{8,76},{9,... | collective-permute-start | bytes 1572872 | tf_op jit(solution)/shard_map/ppermute | solution.py:64
  92.9 26.1 %collective-permute-start.18 = (bf16[32,64,128]{2,1,0:T(8,128)(2,1)}, bf16[32,64,128]{2,1,0:T(8,128)(2,1)S(1)}, u32[]{:S(2)}, u32[]{:S(2)}) collective-permute-start(bf16[32,64,128]{2,1,0:T(8,128)(2,1)} %get-tuple-element.46), channel_id=1, source_target_pairs={{0,4},{1,5},{2,6},{3,7},{4,0},{5,1},{6,2},{7,3},{8,12},{9,13},{10,... | collective-permute-start | bytes 1572872 | tf_op jit(solution)/shard_map/ppermute | solution.py:58
  95.2 33.4 %collective-permute-start.19 = (bf16[32,64,128]{2,1,0:T(8,128)(2,1)}, bf16[32,64,128]{2,1,0:T(8,128)(2,1)S(1)}, u32[]{:S(2)}, u32[]{:S(2)}) collective-permute-start(bf16[32,64,128]{2,1,0:T(8,128)(2,1)} %get-tuple-element.47), channel_id=1, source_target_pairs={{0,64},{8,72},{16,80},{24,88},{32,96},{40,104},{48,112},{56,120},{... | collective-permute-start | bytes 1572872 | tf_op jit(solution)/shard_map/ppermute | solution.py:55
  97.9 30.7 %collective-permute-start.20 = (bf16[32,64,128]{2,1,0:T(8,128)(2,1)}, bf16[32,64,128]{2,1,0:T(8,128)(2,1)S(1)}, u32[]{:S(2)}, u32[]{:S(2)}) collective-permute-start(bf16[32,64,128]{2,1,0:T(8,128)(2,1)} %get-tuple-element.48), channel_id=1, source_target_pairs={{0,68},{1,69},{2,70},{3,71},{4,64},{5,65},{6,66},{7,67},{8,76},{9,... | collective-permute-start | bytes 1572872 | tf_op jit(solution)/shard_map/ppermute | solution.py:64
  116.1 18.8 %collective-permute-start.6 = (bf16[32,64,128]{2,1,0:T(8,128)(2,1)}, bf16[32,64,128]{2,1,0:T(8,128)(2,1)S(1)}, u32[]{:S(2)}, u32[]{:S(2)}) collective-permute-start(bf16[32,64,128]{2,1,0:T(8,128)(2,1)} %get-tuple-element.34), channel_id=1, source_target_pairs={{0,4},{1,5},{2,6},{3,7},{4,0},{5,1},{6,2},{7,3},{8,12},{9,13},{10,... | collective-permute-start | bytes 1572872 | tf_op jit(solution)/shard_map/ppermute | solution.py:58
  116.6 34.5 %collective-permute-start.7 = (bf16[32,64,128]{2,1,0:T(8,128)(2,1)}, bf16[32,64,128]{2,1,0:T(8,128)(2,1)}, u32[]{:S(2)}, u32[]{:S(2)}) collective-permute-start(bf16[32,64,128]{2,1,0:T(8,128)(2,1)} %get-tuple-element.35), channel_id=1, source_target_pairs={{0,64},{8,72},{16,80},{24,88},{32,96},{40,104},{48,112},{56,120},{... | collective-permute-start | bytes 1572872 | tf_op jit(solution)/shard_map/ppermute | solution.py:55
  119.0 32.2 %collective-permute-start.8 = (bf16[32,64,128]{2,1,0:T(8,128)(2,1)}, bf16[32,64,128]{2,1,0:T(8,128)(2,1)}, u32[]{:S(2)}, u32[]{:S(2)}) collective-permute-start(bf16[32,64,128]{2,1,0:T(8,128)(2,1)} %get-tuple-element.36), channel_id=1, source_target_pairs={{0,68},{1,69},{2,70},{3,71},{4,64},{5,65},{6,66},{7,67},{8,76},{9,... | collective-permute-start | bytes 1572872 | tf_op jit(solution)/shard_map/ppermute | solution.py:64
  134.0 28.7 %collective-permute-start.23 = (bf16[32,64,128]{2,1,0:T(8,128)(2,1)}, bf16[32,64,128]{2,1,0:T(8,128)(2,1)S(1)}, u32[]{:S(2)}, u32[]{:S(2)}) collective-permute-start(bf16[32,64,128]{2,1,0:T(8,128)(2,1)} %get-tuple-element.51), channel_id=1, source_target_pairs={{0,1},{1,0},{2,3},{3,2},{4,5},{5,4},{6,7},{7,6},{8,9},{9,8},{10,11... | collective-permute-start | bytes 1572872 | tf_op jit(solution)/shard_map/ppermute | solution.py:58
  134.8 36.6 %collective-permute-start.22 = (bf16[32,64,128]{2,1,0:T(8,128)(2,1)}, bf16[32,64,128]{2,1,0:T(8,128)(2,1)S(1)}, u32[]{:S(2)}, u32[]{:S(2)}) collective-permute-start(bf16[32,64,128]{2,1,0:T(8,128)(2,1)} %get-tuple-element.50), channel_id=1, source_target_pairs={{0,8},{8,0},{16,24},{24,16},{32,40},{40,32},{48,56},{56,48},{64,72... | collective-permute-start | bytes 1572872 | tf_op jit(solution)/shard_map/ppermute | solution.py:55
  134.9 40.1 %collective-permute-start.21 = (bf16[32,64,128]{2,1,0:T(8,128)(2,1)}, bf16[32,64,128]{2,1,0:T(8,128)(2,1)S(1)}, u32[]{:S(2)}, u32[]{:S(2)}) collective-permute-start(bf16[32,64,128]{2,1,0:T(8,128)(2,1)} %get-tuple-element.49), channel_id=1, source_target_pairs={{0,9},{1,8},{2,11},{3,10},{4,13},{5,12},{6,15},{7,14},{8,1},{9,0},... | collective-permute-start | bytes 1572872 | tf_op jit(solution)/shard_map/ppermute | solution.py:64
  155.6 29.7 %collective-permute-start.11 = (bf16[32,64,128]{2,1,0:T(8,128)(2,1)}, bf16[32,64,128]{2,1,0:T(8,128)(2,1)}, u32[]{:S(2)}, u32[]{:S(2)}) collective-permute-start(bf16[32,64,128]{2,1,0:T(8,128)(2,1)} %get-tuple-element.39), channel_id=1, source_target_pairs={{0,1},{1,0},{2,3},{3,2},{4,5},{5,4},{6,7},{7,6},{8,9},{9,8},{10,11... | collective-permute-start | bytes 1572872 | tf_op jit(solution)/shard_map/ppermute | solution.py:58
  156.0 31.9 %collective-permute-start.10 = (bf16[32,64,128]{2,1,0:T(8,128)(2,1)}, bf16[32,64,128]{2,1,0:T(8,128)(2,1)S(1)}, u32[]{:S(2)}, u32[]{:S(2)}) collective-permute-start(bf16[32,64,128]{2,1,0:T(8,128)(2,1)} %get-tuple-element.38), channel_id=1, source_target_pairs={{0,8},{8,0},{16,24},{24,16},{32,40},{40,32},{48,56},{56,48},{64,72... | collective-permute-start | bytes 1572872 | tf_op jit(solution)/shard_map/ppermute | solution.py:55
  162.7 32.4 %collective-permute-start.9 = (bf16[32,64,128]{2,1,0:T(8,128)(2,1)}, bf16[32,64,128]{2,1,0:T(8,128)(2,1)}, u32[]{:S(2)}, u32[]{:S(2)}) collective-permute-start(bf16[32,64,128]{2,1,0:T(8,128)(2,1)} %get-tuple-element.37), channel_id=1, source_target_pairs={{0,9},{1,8},{2,11},{3,10},{4,13},{5,12},{6,15},{7,14},{8,1},{9,0},... | collective-permute-start | bytes 1572872 | tf_op jit(solution)/shard_map/ppermute | solution.py:64
  (16 other events, 135.8 us)
